TPU v7x, 32 devices: a whole 2x2x4 slice. The times are simulated.
32 devices in a mesh: dp: 8 (over z, y), seq: 4 (over x, core).
Axes of the slice: x: 2, y: 2, z: 4, core: 2. Of those that a mesh axis runs over, the one named last changes fastest.
Arguments:
- hidden_in: bfloat16 [8, 2048, 768], P('dp', 'seq'), may hold values from -6 to 6
- prev_logits: float32 [8, 2048, 12], P('dp', 'seq'), may hold values from -6 to 6
- segments: int32 [8, 2048], P('dp'), may hold values from 0 to 15, never falling along the last dimension, each value on 1 to 1024 neighbouring positions
- routes: int32 [8, 2048, 2], P('dp', 'seq'), may hold values from 0 to 11, all different within a row; in each aligned block of 512 rows (0 to 511, 512 to 1023, ..., all dimensions but the last counted through in order) at most 128 rows name the same one
- attn_gain: bfloat16 [768], P('dp'), may hold values from 0.5 to 1.5
- w_qkv: bfloat16 [768, 2304], P('dp'), may hold values from -0.21875 to 0.21875
- w_out: bfloat16 [768, 768], P('dp'), may hold values from -1.75 to 1.75
- moe_gain: bfloat16 [768], P('dp'), may hold values from 0.5 to 1.5
- w_router: bfloat16 [768, 12], P('dp'), may hold values from -0.109375 to 0.109375
- w_carry: bfloat16 [12, 12], replicated, may hold values from -0.875 to 0.875
- const_vec: bfloat16 [2, 768], P(None, 'dp'), may hold values from -6 to 6
- const_mix: bfloat16 [2, 2, 768], P(None, None, 'dp'), may hold values from -0.21875 to 0.21875
- experts: bfloat16 [3, 16384, 768], P(None, 'dp'), may hold values from -0.21875 to 0.21875
- cotangent: bfloat16 [8, 2048, 768], P('dp', 'seq'), may hold values from -6 to 6
Outputs:
- block_out: bfloat16 [8, 2048, 768], P('dp', 'seq')
- d_input: float32 [8, 2048, 768], P('dp', 'seq')
- d_prev: float32 [8, 2048, 12], P('dp', 'seq')
- d_attn_gain: float32 [768], P('dp')
- d_w_qkv: float32 [768, 2304], P('dp')
- d_w_out: float32 [768, 768], P('dp')
- d_moe_gain: float32 [768], P('dp')
- d_w_router: float32 [768, 12], P('dp')
- d_w_carry: float32 [12, 12], replicated
- d_const_vec: float32 [2, 768], P(None, 'dp')
- d_const_mix: float32 [2, 2, 768], P(None, None, 'dp')
- d_experts: float32 [3, 16384, 768], P(None, 'dp')
Inputs may be any that keep to these rules, and one draw needn't show every extreme that they name: `routes`: each token names two different experts: numbers below 8 are feed-forward experts, 8 the zero expert, 9 the copy expert, 10 and 11 the constant experts. Among the 512 tokens of one device no expert is named more than 128 times, and some expert of some device is named exactly 128 times. `segments`: within a sequence the numbers start at 0 and never fall; a document has 1 to 1024 tokens, and one has exactly that many.
All inputs are finite; a program needn't handle non-finite values.
Results may differ from a plain program's by a relative error of at most 0.013.
The roundings to bfloat16 on the way count: a program that leaves them out, or rounds other values in their place, can miss the bound.
Values may be sent and summed in bfloat16 or wider, within the bound.
A program may use at most 192 MiB of HBM per device.

v0:
```python
import math

import jax
import jax.numpy as jnp
from jax import lax
from jax.sharding import PartitionSpec as P

D = 768
H = 12
HD = 64
E = 8
CAP = 128


exact_prec = lax.Precision.HIGHEST
neg_large = -1e30
contract_rows = (((0,), (0,)), ((), ()))
contract_cols = (((1,), (1,)), ((), ()))


def rms_scale(values, gain_vec):
    mean_square = jnp.mean(values * values, axis=-1, keepdims=True)
    return values * lax.rsqrt(mean_square + 1e-06) * gain_vec


def rope_tables(positions):
    freq_index = jnp.arange(HD // 2, dtype=jnp.float32)
    inv_freq = jnp.exp(freq_index * (-2.0 * math.log(10000.0) / HD))
    angles = positions.astype(jnp.float32)[:, None] * inv_freq[None, :]
    return (jnp.cos(angles)[:, None, :], jnp.sin(angles)[:, None, :])


def rotate_half(values, cos_part, sin_part):
    half_size = values.shape[-1] // 2
    first_half = values[..., :half_size]
    second_half = values[..., half_size:]
    return jnp.concatenate(
        [
            first_half * cos_part - second_half * sin_part,
            first_half * sin_part + second_half * cos_part,
        ],
        axis=-1,
    )


def slot_layout(route_rows, slots_each):
    flat_routes = route_rows.reshape(-1)
    expert_hot = (flat_routes[:, None] == jnp.arange(E, dtype=jnp.int32)[None, :]).astype(jnp.int32)
    ranks = jnp.sum((jnp.cumsum(expert_hot, axis=0) - expert_hot) * expert_hot, axis=1)
    return jnp.where(flat_routes < E, flat_routes * slots_each + ranks, E * slots_each)


def combine(normed, logits, vec_f, mix_f, ffn_rows, route_rows):
    tok_count = normed.shape[0]
    chosen = jnp.take_along_axis(logits, route_rows, axis=1)
    gate_exp = jnp.exp(chosen - jnp.max(chosen, axis=1, keepdims=True))
    gates = gate_exp / jnp.sum(gate_exp, axis=1, keepdims=True)
    const_logits = jnp.einsum("td,jcd->tjc", normed, mix_f, precision=exact_prec)
    const_exp = jnp.exp(const_logits - jnp.max(const_logits, axis=2, keepdims=True))
    alphas = const_exp / jnp.sum(const_exp, axis=2, keepdims=True)
    const_out = alphas[:, :, 0:1] * normed[:, None, :] + alphas[:, :, 1:2] * vec_f[None, :, :]
    slot_rows = ffn_rows.reshape(tok_count, 2, normed.shape[1])
    route_cube = route_rows[:, :, None]
    slot_rows = slot_rows + jnp.where(route_cube == E + 1, normed[:, None, :], 0.0)
    slot_rows = slot_rows + jnp.where(route_cube == E + 2, const_out[:, 0:1, :], 0.0)
    slot_rows = slot_rows + jnp.where(route_cube == E + 3, const_out[:, 1:2, :], 0.0)
    return jnp.sum(gates[:, :, None] * slot_rows, axis=1)


def to_slots(slot_values, slot_index):
    row_width = slot_values.shape[1]
    buffer_rows = (
        jnp.zeros((E * CAP + 1, row_width), slot_values.dtype).at[slot_index].add(slot_values)
    )
    return buffer_rows[: E * CAP].reshape(E, CAP, row_width)


def from_slots(grouped, slot_index):
    flat_rows = grouped.reshape(E * CAP, grouped.shape[-1])
    padded = jnp.concatenate(
        [flat_rows, jnp.zeros((1, flat_rows.shape[1]), flat_rows.dtype)], axis=0
    )
    return padded[slot_index]


def block_plan(seq_len):
    block_rows = min(512, seq_len)
    return (block_rows, seq_len // block_rows)


def block_scores(queries, keys_all, seg_row, row_start, block_rows):
    q_blk = lax.dynamic_slice_in_dim(queries, row_start, block_rows, 0)
    key_pos = jnp.arange(seg_row.shape[0], dtype=jnp.int32)
    query_pos = row_start + jnp.arange(block_rows, dtype=jnp.int32)
    query_seg = lax.dynamic_slice_in_dim(seg_row, row_start, block_rows, 0)
    allowed = (key_pos[None, :] <= query_pos[:, None]) & (seg_row[None, :] == query_seg[:, None])
    scores = jnp.einsum("qhd,khd->hqk", q_blk, keys_all, preferred_element_type=jnp.float32) * 0.125
    return (q_blk, jnp.where(allowed[None], scores, neg_large))


def forward_pass(
    hidden_in,
    prev_logits,
    segments,
    routes,
    attn_gain,
    w_qkv,
    w_out,
    moe_gain,
    w_router,
    w_carry,
    const_vec,
    const_mix,
    experts,
):
    gathered = (
        lax.all_gather(attn_gain, "dp", axis=0, tiled=True),
        lax.all_gather(w_qkv, "dp", axis=0, tiled=True),
        lax.all_gather(w_out, "dp", axis=0, tiled=True),
        lax.all_gather(moe_gain, "dp", axis=0, tiled=True),
        lax.all_gather(w_router, "dp", axis=0, tiled=True),
        lax.all_gather(const_vec, "dp", axis=1, tiled=True),
        lax.all_gather(const_mix, "dp", axis=2, tiled=True),
    )
    gain_one, qkv_weight, out_weight, gain_two, router_weight, vec_const, mix_const = gathered
    tok_count = hidden_in.shape[1]
    seq_parts = lax.axis_size("seq")
    owners = lax.axis_size("dp") // E
    heads_here = H // seq_parts
    head_width = heads_here * HD
    tokens_f = hidden_in[0].astype(jnp.float32)
    attn_in = rms_scale(tokens_f, gain_one.astype(jnp.float32)).astype(jnp.bfloat16)
    qkv_pre = jnp.dot(attn_in, qkv_weight, preferred_element_type=jnp.float32).reshape(
        tok_count, 3, H, HD
    )
    positions = lax.axis_index("seq") * tok_count + jnp.arange(tok_count, dtype=jnp.int32)
    cos_part, sin_part = rope_tables(positions)
    rotated = jnp.stack(
        [
            rotate_half(qkv_pre[:, 0], cos_part, sin_part),
            rotate_half(qkv_pre[:, 1], cos_part, sin_part),
            qkv_pre[:, 2],
        ],
        axis=1,
    )
    outgoing = rotated.astype(jnp.bfloat16).reshape(tok_count, 3, seq_parts, head_width)
    head_rows = lax.all_to_all(outgoing, "seq", split_axis=2, concat_axis=0, tiled=True)
    seq_len = head_rows.shape[0]
    head_rows = head_rows.reshape(seq_len, 3, heads_here, HD)
    queries = head_rows[:, 0]
    keys_all = head_rows[:, 1]
    values_all = head_rows[:, 2]
    seg_row = segments[0]
    block_rows, count_blocks = block_plan(seq_len)

    def attend(block_index):
        unused_q, scores = block_scores(
            queries, keys_all, seg_row, block_index * block_rows, block_rows
        )
        top_score = jnp.max(scores, axis=-1, keepdims=True)
        weights = jnp.exp(scores - top_score)
        row_total = jnp.sum(weights, axis=-1, keepdims=True)
        probabilities = weights / row_total
        attended = jnp.einsum(
            "hqk,khd->qhd",
            probabilities.astype(jnp.bfloat16),
            values_all,
            preferred_element_type=jnp.float32,
        )
        return (attended.astype(jnp.bfloat16), (top_score + jnp.log(row_total))[:, :, 0])

    attended, log_totals = lax.map(attend, jnp.arange(count_blocks, dtype=jnp.int32))
    head_out = attended.reshape(seq_len, 1, head_width)
    token_heads = lax.all_to_all(head_out, "seq", split_axis=0, concat_axis=1, tiled=True).reshape(
        tok_count, H * HD
    )
    attn_out = jnp.dot(token_heads, out_weight, preferred_element_type=jnp.float32)
    resid_mid = tokens_f + attn_out
    normed = rms_scale(resid_mid, gain_two.astype(jnp.float32))
    normed_low = normed.astype(jnp.bfloat16)
    logits = jnp.dot(normed_low, router_weight, preferred_element_type=jnp.float32) + jnp.dot(
        prev_logits[0], w_carry.astype(jnp.float32), precision=exact_prec
    )
    route_rows = routes[0]
    slot_index = slot_layout(route_rows, CAP)
    token_of = jnp.arange(2 * tok_count, dtype=jnp.int32) // 2
    grouped = to_slots(normed_low[token_of], slot_index)
    sending = jnp.repeat(grouped, owners, axis=0)
    arrived = lax.all_to_all(sending, "dp", split_axis=0, concat_axis=0, tiled=True)
    flat_rows = arrived.reshape(-1, D)
    gate_pre = lax.dot_general(
        flat_rows, experts[0], contract_cols, preferred_element_type=jnp.float32
    )
    up_pre = lax.dot_general(
        flat_rows, experts[1], contract_cols, preferred_element_type=jnp.float32
    )
    hidden = (jax.nn.silu(gate_pre) * up_pre).astype(jnp.bfloat16)
    partial_rows = jnp.dot(hidden, experts[2], preferred_element_type=jnp.float32).astype(
        jnp.bfloat16
    )
    returned = lax.all_to_all(
        partial_rows.reshape(arrived.shape), "dp", split_axis=0, concat_axis=0, tiled=True
    )
    hidden_shape = (arrived.shape[0], arrived.shape[1], gate_pre.shape[1])
    returned, arrived, gate_pre, up_pre = (
        returned,
        arrived,
        gate_pre.reshape(hidden_shape),
        up_pre.reshape(hidden_shape),
    )
    expert_sum = jnp.sum(returned.astype(jnp.float32).reshape(E, owners, CAP, D), axis=1)
    ffn_rows = from_slots(expert_sum, slot_index)
    mixed = combine(
        normed,
        logits,
        vec_const.astype(jnp.float32),
        mix_const.astype(jnp.float32),
        ffn_rows,
        route_rows,
    )
    result = (resid_mid + mixed).astype(jnp.bfloat16)[None]
    return (
        result,
        gathered,
        tokens_f,
        attn_in,
        cos_part,
        sin_part,
        queries,
        keys_all,
        values_all,
        log_totals,
        token_heads,
        resid_mid,
        normed,
        normed_low,
        logits,
        slot_index,
        arrived,
        gate_pre,
        up_pre,
        ffn_rows,
    )


def per_device(
    hidden_in,
    prev_logits,
    segments,
    routes,
    attn_gain,
    w_qkv,
    w_out,
    moe_gain,
    w_router,
    w_carry,
    const_vec,
    const_mix,
    experts,
    cotangent,
):
    forward_out = forward_pass(
        hidden_in,
        prev_logits,
        segments,
        routes,
        attn_gain,
        w_qkv,
        w_out,
        moe_gain,
        w_router,
        w_carry,
        const_vec,
        const_mix,
        experts,
    )
    block_out = forward_out[0]
    fresh_args = lax.optimization_barrier(
        (
            hidden_in,
            prev_logits,
            segments,
            routes,
            attn_gain,
            w_qkv,
            w_out,
            moe_gain,
            w_router,
            w_carry,
            const_vec,
            const_mix,
            experts,
        )
    )
    forward_out = forward_pass(*fresh_args)
    (
        unused_out,
        gathered,
        tokens_f,
        attn_in,
        cos_part,
        sin_part,
        queries,
        keys_all,
        values_all,
        log_totals,
        token_heads,
        resid_mid,
        normed,
        normed_low,
        logits,
        slot_index,
        arrived,
        gate_pre,
        up_pre,
        ffn_rows,
    ) = forward_out
    gain_one, qkv_weight, out_weight, gain_two, router_weight, vec_const, mix_const = gathered
    tok_count = hidden_in.shape[1]
    seq_parts = lax.axis_size("seq")
    owners = lax.axis_size("dp") // E
    heads_here = H // seq_parts
    head_width = heads_here * HD
    seq_len = queries.shape[0]
    block_rows, count_blocks = block_plan(seq_len)
    seg_row = segments[0]
    route_rows = routes[0]
    prev_rows = prev_logits[0]
    grad_top = cotangent[0].astype(jnp.float32)

    def mixing(normed_in, logits_in, vec_in, mix_in, rows_in):
        return combine(normed_in, logits_in, vec_in, mix_in, rows_in, route_rows)

    unused_mix, mix_pull = jax.vjp(
        mixing,
        normed,
        logits,
        vec_const.astype(jnp.float32),
        mix_const.astype(jnp.float32),
        ffn_rows,
    )
    grad_normed, grad_logits, grad_vec, grad_mix, grad_slot_rows = mix_pull(grad_top)
    grad_normed = grad_normed + jnp.dot(
        grad_logits, router_weight.astype(jnp.float32).T, precision=exact_prec
    )
    grad_router = jnp.dot(normed_low.astype(jnp.float32).T, grad_logits, precision=exact_prec)
    grad_carry = jnp.dot(prev_rows.T, grad_logits, precision=exact_prec)
    grad_prev = jnp.dot(grad_logits, w_carry.astype(jnp.float32).T, precision=exact_prec)
    grad_slots = to_slots(grad_slot_rows.astype(jnp.bfloat16), slot_index)
    arrived_grad = lax.all_to_all(
        jnp.repeat(grad_slots, owners, axis=0), "dp", split_axis=0, concat_axis=0, tiled=True
    )
    flat_grad = arrived_grad.reshape(-1, D)
    flat_rows = arrived.reshape(-1, D)
    gate_flat = gate_pre.reshape(flat_rows.shape[0], -1)
    up_flat = up_pre.reshape(flat_rows.shape[0], -1)
    sig_gate = jax.nn.sigmoid(gate_flat)
    silu_gate = gate_flat * sig_gate
    hidden = (silu_gate * up_flat).astype(jnp.bfloat16)
    grad_hidden = lax.dot_general(
        flat_grad, experts[2], contract_cols, preferred_element_type=jnp.float32
    )
    grad_down = lax.dot_general(
        hidden, flat_grad, contract_rows, preferred_element_type=jnp.float32
    )
    grad_gate_pre = (
        grad_hidden * up_flat * sig_gate * (1.0 + gate_flat * (1.0 - sig_gate))
    ).astype(jnp.bfloat16)
    grad_up_pre = (grad_hidden * silu_gate).astype(jnp.bfloat16)
    grad_piece = jnp.dot(grad_gate_pre, experts[0], preferred_element_type=jnp.float32) + jnp.dot(
        grad_up_pre, experts[1], preferred_element_type=jnp.float32
    )
    grad_gate_w = lax.dot_general(
        grad_gate_pre, flat_rows, contract_rows, preferred_element_type=jnp.float32
    )
    grad_up_w = lax.dot_general(
        grad_up_pre, flat_rows, contract_rows, preferred_element_type=jnp.float32
    )
    expert_grads = jnp.stack([grad_gate_w, grad_up_w, grad_down], axis=0)
    back_rows = lax.all_to_all(
        grad_piece.astype(jnp.bfloat16).reshape(arrived_grad.shape),
        "dp",
        split_axis=0,
        concat_axis=0,
        tiled=True,
    )
    grad_slot_sum = jnp.sum(back_rows.astype(jnp.float32).reshape(E, owners, CAP, D), axis=1)
    grad_normed = grad_normed + jnp.sum(
        from_slots(grad_slot_sum, slot_index).reshape(tok_count, 2, D), axis=1
    )
    unused_norm, norm_pull = jax.vjp(rms_scale, resid_mid, gain_two.astype(jnp.float32))
    grad_resid, grad_gain_two = norm_pull(grad_normed)
    grad_resid = grad_resid + grad_top
    grad_attn = grad_resid.astype(jnp.bfloat16)
    grad_out_w = lax.dot_general(
        token_heads, grad_attn, contract_rows, preferred_element_type=jnp.float32
    )
    grad_heads_tok = lax.dot_general(
        grad_attn, out_weight, contract_cols, preferred_element_type=jnp.float32
    ).astype(jnp.bfloat16)
    grad_heads = lax.all_to_all(
        grad_heads_tok.reshape(tok_count, seq_parts, head_width),
        "seq",
        split_axis=1,
        concat_axis=0,
        tiled=True,
    ).reshape(seq_len, heads_here, HD)

    def attend_back(carry_pair, block_index):
        grad_keys, grad_values = carry_pair
        row_start = block_index * block_rows
        q_blk, scores = block_scores(queries, keys_all, seg_row, row_start, block_rows)
        grad_blk = lax.dynamic_slice_in_dim(grad_heads, row_start, block_rows, 0)
        log_blk = lax.dynamic_index_in_dim(log_totals, block_index, 0, keepdims=False)
        probabilities = jnp.exp(scores - log_blk[:, :, None])
        grad_probs = jnp.einsum(
            "qhd,khd->hqk", grad_blk, values_all, preferred_element_type=jnp.float32
        )
        row_dot = jnp.sum(probabilities * grad_probs, axis=-1, keepdims=True)
        grad_scores = (probabilities * (grad_probs - row_dot)).astype(jnp.bfloat16)
        grad_q = (
            jnp.einsum("hqk,khd->qhd", grad_scores, keys_all, preferred_element_type=jnp.float32)
            * 0.125
        )
        grad_keys = (
            grad_keys
            + jnp.einsum("hqk,qhd->khd", grad_scores, q_blk, preferred_element_type=jnp.float32)
            * 0.125
        )
        grad_values = grad_values + jnp.einsum(
            "hqk,qhd->khd",
            probabilities.astype(jnp.bfloat16),
            grad_blk,
            preferred_element_type=jnp.float32,
        )
        return ((grad_keys, grad_values), grad_q)

    zero_heads = jnp.zeros((seq_len, heads_here, HD), jnp.float32)
    (grad_keys, grad_values), grad_q_blocks = lax.scan(
        attend_back, (zero_heads, zero_heads), jnp.arange(count_blocks, dtype=jnp.int32)
    )
    grad_queries = grad_q_blocks.reshape(seq_len, heads_here, HD)
    grad_heads_all = (
        jnp.stack([grad_queries, grad_keys, grad_values], axis=1)
        .astype(jnp.bfloat16)
        .reshape(seq_len, 3, 1, head_width)
    )
    grad_tok = lax.all_to_all(
        grad_heads_all, "seq", split_axis=0, concat_axis=2, tiled=True
    ).reshape(tok_count, 3, H, HD)
    grad_q_tok = rotate_half(grad_tok[:, 0].astype(jnp.float32), cos_part, -sin_part).astype(
        jnp.bfloat16
    )
    grad_k_tok = rotate_half(grad_tok[:, 1].astype(jnp.float32), cos_part, -sin_part).astype(
        jnp.bfloat16
    )
    grad_qkv = jnp.stack([grad_q_tok, grad_k_tok, grad_tok[:, 2]], axis=1).reshape(
        tok_count, 3 * H * HD
    )
    grad_qkv_w = lax.dot_general(
        attn_in, grad_qkv, contract_rows, preferred_element_type=jnp.float32
    )
    grad_attn_in = lax.dot_general(
        grad_qkv, qkv_weight, contract_cols, preferred_element_type=jnp.float32
    )
    unused_first, first_pull = jax.vjp(rms_scale, tokens_f, gain_one.astype(jnp.float32))
    grad_tokens_norm, grad_gain_one = first_pull(grad_attn_in)
    grad_input = grad_resid + grad_tokens_norm
    shard_gain_one, shard_qkv, shard_out, shard_gain_two, shard_router, shard_vec, shard_mix = (
        lax.psum_scatter(grad_gain_one, "dp", scatter_dimension=0, tiled=True),
        lax.psum_scatter(grad_qkv_w, "dp", scatter_dimension=0, tiled=True),
        lax.psum_scatter(grad_out_w, "dp", scatter_dimension=0, tiled=True),
        lax.psum_scatter(grad_gain_two, "dp", scatter_dimension=0, tiled=True),
        lax.psum_scatter(grad_router, "dp", scatter_dimension=0, tiled=True),
        lax.psum_scatter(grad_vec, "dp", scatter_dimension=1, tiled=True),
        lax.psum_scatter(grad_mix, "dp", scatter_dimension=2, tiled=True),
    )
    summed = lax.psum(
        (
            shard_gain_one,
            shard_qkv,
            shard_out,
            shard_gain_two,
            shard_router,
            shard_vec,
            shard_mix,
            expert_grads,
        ),
        "seq",
    )
    carry_total = lax.psum(grad_carry, ("dp", "seq"))
    return (
        block_out,
        grad_input[None],
        grad_prev[None],
        summed[0],
        summed[1],
        summed[2],
        summed[3],
        summed[4],
        carry_total,
        summed[5],
        summed[6],
        summed[7],
    )


def solution(mesh):
    return jax.shard_map(
        per_device,
        mesh=mesh,
        in_specs=(
            P("dp", "seq", None),
            P("dp", "seq", None),
            P("dp", None),
            P("dp", "seq", None),
            P("dp"),
            P("dp", None),
            P("dp", None),
            P("dp"),
            P("dp", None),
            P(),
            P(None, "dp"),
            P(None, None, "dp"),
            P(None, "dp", None),
            P("dp", "seq", None),
        ),
        out_specs=(
            P("dp", "seq", None),
            P("dp", "seq", None),
            P("dp", "seq", None),
            P("dp"),
            P("dp", None),
            P("dp", None),
            P("dp"),
            P("dp", None),
            P(),
            P(None, "dp"),
            P(None, None, "dp"),
            P(None, "dp", None),
        ),
        check_vma=False,
    )
```

profile of v0, /device:TPU:13, one launch (start us, length us, event | category | flops | bytes accessed | tf_op | source)
XLA Modules:
  0.0 1868.3 jit_solution(9835863920703674466)
XLA Ops:
  18.8 12.9 all-reduce.16
  34.5 25.1 %all-gather.2 = bf16[8,96,12]{1,2,0:T(8,128)(2,1)S(1)} all-gather(bf16[1,96,12]{1,2,0:T(8,128)(2,1)S(1)} %bitcast.533), channel_id=1, replica_groups=mesh['dp'=8,'seq'=4] {'dp'}, dimensions={0}, use_global_device_ids=true | all-gather | bytes 20736 | tf_op jit(solution)/shard_map/all_gather | solution.py:121
  62.5 23.1 %all-gather = bf16[8,96,12]{1,2,0:T(8,128)(2,1)S(1)} all-gather(bf16[1,96,12]{1,2,0:T(8,128)(2,1)S(1)} %bitcast.534), channel_id=1, replica_groups=mesh['dp'=8,'seq'=4] {'dp'}, dimensions={0}, use_global_device_ids=true | all-gather | bytes 20736 | tf_op jit(solution)/shard_map/all_gather | solution.py:121
  86.4 17.4 all-gather.1
  104.4 27.0 %all_gather.47 = bf16[2,2,768]{1,0,2:T(2,128)(2,1)} all-gather(bf16[2,2,96]{1,0,2:T(2,128)(2,1)S(1)} %copy.275), channel_id=1, replica_groups=mesh['dp'=8,'seq'=4] {'dp'}, dimensions={2}, use_global_device_ids=true | all-gather | bytes 6912 | tf_op jit(solution)/shard_map/all_gather | solution.py:123
  147.9 24.3 %all_gather.54 = bf16[2,2,768]{1,0,2:T(2,128)(2,1)S(1)} all-gather(bf16[2,2,96]{1,0,2:T(2,128)(2,1)S(1)} %copy.290), channel_id=1, replica_groups=mesh['dp'=8,'seq'=4] {'dp'}, dimensions={2}, use_global_device_ids=true | all-gather | bytes 6912 | tf_op jit(solution)/shard_map/all_gather | solution.py:123
  173.1 15.7 all-gather.3
  221.3 39.3 %all-to-all-start = ((bf16[512,3,4,192]{0,3,1,2:T(8,128)(2,1)}), bf16[512,3,4,192]{0,3,1,2:T(8,128)(2,1)S(1)}, u32[]{:S(2)}, u32[]{:S(2)}) async-start(bf16[512,3,4,192]{0,3,1,2:T(8,128)(2,1)} %pad_maximum_fusion.1), calls=%async_computation | async-start | bytes 4718592 | tf_op jit(solution)/shard_map/all_to_all | solution.py:147
  266.7 21.6 %all-to-all-done = bf16[512,3,4,192]{0,3,1,2:T(8,128)(2,1)S(1)} async-done(((bf16[512,3,4,192]{0,3,1,2:T(8,128)(2,1)}), bf16[512,3,4,192]{0,3,1,2:T(8,128)(2,1)S(1)}, u32[]{:S(2)}, u32[]{:S(2)}) %all-to-all-start) | async-done | bytes 2359328 | tf_op jit(solution)/shard_map/all_to_all | solution.py:147
  309.5 80.7 %while.37 = (s32[]{:T(128)}, bf16[4,512,3,64]{1,3,2,0:T(8,128)(2,1)}, s32[4]{0:T(128)S(1)}, s32[1,2048]{1,0:T(1,128)S(1)}, s32[2048]{0:T(1024)S(1)}, /*index=5*/...) while((s32[]{:T(128)}, ...), condition=%wide.region_4.5_spmd, body=%wide.region_1.4_spmd.sunk | while | flops 827427328 | bytes 29259976 | solution.py:172
  311.8 10.3 fusion.297
  416.5 90.7 %while.38 = (s32[]{:T(128)}, bf16[4,512,3,64]{1,3,2,0:T(8,128)(2,1)S(1)}, f32[4,3,512]{2,1,0:T(4,128)}, s32[4]{0:T(128)S(1)}, s32[1,2048]{1,0:T(1,128)S(1)}, /*i...) while((s32[]{:T(128)}, ...), condition=%wide.region_19.20_spmd, body=%wide.region_16.19_spmd.sunk | while | flops 846298112 | bytes 43983060 | solution.py:172
  533.7 14.2 scatter_custom_fusion
  619.6 17.1 scatter_custom_fusion.1
  671.3 13.7 fusion.104
  685.0 11.6 all-to-all-done.6
  714.0 13.5 multiply_convert_fusion.3
  767.0 13.0 all-to-all-done.9
  811.0 24.6 %fusion.67 = (f32[512,768]{1,0:T(8,128)}, f32[512,768]{1,0:T(8,128)}, f32[512,768]{1,0:T(8,128)}, f32[512,768]{1,0:T(8,128)}) fusion(pred[512,2]{1,0:T(8,128)(4,1)} %get-tuple-element.465, f32[512,768]{1,0:T(8,128)S(1)} %copy-done.14, f32[512,2]{1,0:T(8,128)} %get-tuple-element.475, pred[512,2]{1,0:T(8,128)(4,1)} %get-tuple-element.464, ...), kind=kLoop, calls=%fused_computation.97 | loop fusion | flops 10223616 | bytes 15739904 | tf_op jit(solution)/shard_map/transpose(jvp(jit(_where)))/reduce_sum | solution.py:66
  853.7 21.5 %multiply_reduce_fusion.1 = (f32[2,768]{1,0:T(2,128)}, f32[512,2]{1,0:T(8,128)}, f32[512,2]{1,0:T(8,128)}, f32[512,768]{1,0:T(8,128)}, f32[512,2]{1,0:T(8,128)S(1)}) fusion(f32[512,2]{1,0:T(8,128)} %bitcast.513, f32[512,1,768]{2,1,0:T(1,128)} %broadcast_in_dim.292, f32[512,1,768]{2,1,0:T(1,128)} %broadcast_in_dim.291, f32[2,768]{1,0:T(2,128)S(1)} %bitcast.530, ...), kind=kLoop, calls=%fused_computation.116 | loop fusion | flops 12971520 | bytes 14191616 | tf_op jit(solution)/shard_map/transpose(jvp())/reduce_sum | solution.py:61
  917.6 177.5 %while.39 = (s32[]{:T(128)}, f32[2048,3,64]{0,2,1:T(8,128)}, f32[2048,3,64]{0,2,1:T(8,128)}, bf16[4,512,3,64]{1,3,2,0:T(8,128)(2,1)}, s32[4]{0:T(128)S(1)}, /*in...) while((s32[]{:T(128)}, f32[2048,3,64]{0,2,1:T(8,128)}, ...), condition=%wide.region_48.49_spmd.clone, body=%wide.region_46.48_spmd.clone.sunk | while | flops 2065660928 | bytes 191296128 | solution.py:439
  1106.2 53.8 %all_to_all.120 = bf16[2048,3,1,192]{3,1,2,0:T(4,128)(2,1)} all-to-all(bf16[2048,3,1,192]{3,1,2,0:T(4,128)(2,1)} %copy.306), channel_id=1, replica_groups=mesh['dp'=8,'seq'=4] {'seq'}, dimensions={0} | all-to-all | bytes 4718592 | tf_op jit(solution)/shard_map/all_to_all | solution.py:448
  1202.1 14.9 pad_maximum_fusion
  1217.0 87.5 %reduce-scatter.12.cloned.1.call-done = f32[96,2304]{1,0:T(8,128)} async-done(((f32[768,2304]{1,0:T(8,128)}), f32[96,2304]{1,0:T(8,128)}) %reduce-scatter.12.cloned.1.call-update) | async-done | bytes 884752 | tf_op jit(solution)/shard_map/reduce_scatter | solution.py:471
  1306.2 39.6 %psum.68 = f32[12,12]{0,1:T(8,128)S(1)} all-reduce(f32[12,12]{0,1:T(8,128)S(1)} %convolution_bitcast_fusion.4), channel_id=1, replica_groups=mesh['dp'=8,'seq'=4] {'dp','seq'}, use_global_device_ids=true, to_apply=%region_62.63 | all-reduce | flops 144 | bytes 1152 | tf_op jit(solution)/shard_map/psum | solution.py:491
  1349.0 18.4 reduce-scatter.18.cloned.1.call-done
  1368.3 63.2 %reduce-scatter.20.cloned.1.call-done = f32[96,4]{1,0:T(8,128)} async-done(((f32[768,4]{1,0:T(8,128)}), f32[96,4]{1,0:T(8,128)}) %reduce-scatter.20.cloned.1.call-update) | async-done | bytes 1552
  1432.5 63.6 %reduce-scatter.16.cloned.1.call-done = f32[96,12]{1,0:T(8,128)} async-done(((f32[768,12]{1,0:T(8,128)}), f32[96,12]{1,0:T(8,128)}) %reduce-scatter.16.cloned.1.call-update) | async-done | bytes 4624
  1503.2 12.7 all-reduce.13
  1516.0 16.4 all-reduce.14
  1535.4 307.4 %all-reduce.19.cloned.1.call-done = (f32[96,2304]{1,0:T(8,128)}, f32[96,768]{1,0:T(8,128)}, f32[3,2048,768]{2,1,0:T(8,128)}) async-done(((f32[96,2304]{1,0:T(8,128)}, f32[96,768]{1,0:T(8,128)}, f32[3,2048,768]{2,1,0:T(8,128)}), (f32[96,2304]{1,0:T(8,128)}, f32[96,768]{1,0:T(8,128)}, f32[3,2048,768]{2,1,0:T(8,128)})) %all-reduce.19.cloned.1.call-update) | async-done | bytes 20054032 | tf_op jit(solution)/shard_map/psum | solution.py:478
  1846.6 14.4 copy.405
  (753 shorter events, 796.0 us)
Async XLA Ops:
  7.2 565.2 %copy-start = (bf16[12,12]{1,0:T(8,128)(2,1)S(1)}, bf16[12,12]{1,0:T(8,128)(2,1)}, u32[]{:S(2)}) copy-start(bf16[12,12]{1,0:T(8,128)(2,1)} %param.29) | copy-start | bytes 868
  7.3 185.9 %all-gather.9.cloned.1.call-start = ((), (), s32[]{:S(2)}) async-start(), calls=%async_computation.17 | async-start | bytes 3981312 | tf_op jit(solution)/shard_map/all_gather | solution.py:118
  8.0 196.8 %all-gather.13.cloned.1.call-start = ((), (), s32[]{:S(2)}) async-start(), calls=%async_computation.19 | async-start | bytes 3981312 | tf_op jit(solution)/shard_map/all_gather | solution.py:118
  8.7 521.0 %all-gather.11.cloned.1.call-start = ((), (), s32[]{:S(2)}) async-start(), calls=%async_computation.18 | async-start | bytes 1327104 | tf_op jit(solution)/shard_map/all_gather | solution.py:119
  9.5 557.5 %all-gather.15.cloned.1.call-start = ((), (), s32[]{:S(2)}) async-start(), calls=%async_computation.20 | async-start | bytes 1327104 | tf_op jit(solution)/shard_map/all_gather | solution.py:119
  12.8 249.8 %copy-start.29 = (s32[1,512,2]{2,1,0:T(8,128)}, s32[1,512,2]{2,1,0:T(8,128)S(1)}, u32[]{:S(2)}) copy-start(s32[1,512,2]{2,1,0:T(8,128)S(1)} %copy.268) | copy-start | bytes 12292
  16.1 118.9 %copy-start.83 = (s32[1024]{0:T(1024)}, s32[1024]{0:T(1024)S(1)}, u32[]{:S(2)}) copy-start(s32[1024]{0:T(1024)S(1)} %eq.161) | copy-start | bytes 12292
  32.9 177.6 %copy-start.78 = (f32[768]{0:T(1024)}, f32[768]{0:T(1024)S(1)}, u32[]{:S(2)}) copy-start(f32[768]{0:T(1024)S(1)} %convert_element_type.218) | copy-start | bytes 9220
  33.1 53.3 %copy-start.102 = (f32[512]{0:T(512)}, f32[512]{0:T(512)S(1)}, u32[]{:S(2)}) copy-start(f32[512]{0:T(512)S(1)} %fusion.115) | copy-start | bytes 6148
  33.1 177.4 %copy-start.94 = (f32[512]{0:T(512)}, f32[512]{0:T(512)S(1)}, u32[]{:S(2)}) copy-start(f32[512]{0:T(512)S(1)} %fusion.190) | copy-start | bytes 6148
  33.8 107.4 %copy-start.13 = (f32[512,768]{1,0:T(8,128)}, f32[512,768]{1,0:T(8,128)S(1)}, u32[]{:S(2)}) copy-start(f32[512,768]{1,0:T(8,128)S(1)} %bitcast_convert_fusion) | copy-start | bytes 4718596
  141.3 50.9 %copy-start.114 = (f32[512]{0:T(512)S(1)}, f32[512]{0:T(512)}, u32[]{:S(2)}) copy-start(f32[512]{0:T(512)} %add_convert_fusion.8) | copy-start | bytes 6148
  141.3 50.9 %copy-start.122 = (f32[32]{0:T(128)S(1)}, f32[32]{0:T(128)}, u32[]{:S(2)}) copy-start(f32[32]{0:T(128)} %multiply_exponential_fusion) | copy-start | bytes 388
  221.3 43.5 %copy-start.49 = (bf16[512,12,32]{0,2,1:T(8,128)(2,1)S(1)}, bf16[512,12,32]{0,2,1:T(8,128)(2,1)}, u32[]{:S(2)}) copy-start(bf16[512,12,32]{0,2,1:T(8,128)(2,1)} %get-tuple-element.453) | copy-start | bytes 1179652
  221.3 43.5 %copy-start.50 = (bf16[512,12,32]{0,2,1:T(8,128)(2,1)S(1)}, bf16[512,12,32]{0,2,1:T(8,128)(2,1)}, u32[]{:S(2)}) copy-start(bf16[512,12,32]{0,2,1:T(8,128)(2,1)} %get-tuple-element.454) | copy-start | bytes 1179652
  221.3 66.9 %all-to-all-start = ((bf16[512,3,4,192]{0,3,1,2:T(8,128)(2,1)}), bf16[512,3,4,192]{0,3,1,2:T(8,128)(2,1)S(1)}, u32[]{:S(2)}, u32[]{:S(2)}) async-start(bf16[512,3,4,192]{0,3,1,2:T(8,128)(2,1)} %pad_maximum_fusion.1), calls=%async_computation | async-start | bytes 4718592 | tf_op jit(solution)/shard_map/all_to_all | solution.py:147
  289.7 111.6 %all-to-all-start.4 = ((bf16[512,3,4,192]{0,3,1,2:T(8,128)(2,1)}), bf16[512,3,4,192]{0,3,1,2:T(8,128)(2,1)S(1)}, u32[]{:S(2)}, u32[]{:S(2)}) async-start(bf16[512,3,4,192]{0,3,1,2:T(8,128)(2,1)} %pad_maximum_fusion.2), calls=%async_computation.4 | async-start | bytes 4718592 | tf_op jit(solution)/shard_map/all_to_all | solution.py:147
  401.3 115.3 %all-to-all-start.1 = ((bf16[4,2,49152]{2,1,0:T(2,128)(2,1)}), bf16[4,2,49152]{2,1,0:T(2,128)(2,1)}, u32[]{:S(2)}, u32[]{:S(2)}) async-start(bf16[4,2,49152]{2,1,0:T(2,128)(2,1)} %reshape.1229), calls=%async_computation.1 | async-start | bytes 1572864 | tf_op jit(solution)/shard_map/all_to_all | solution.py:174
  516.7 32.6 %all-to-all-start.5 = ((bf16[4,2,49152]{2,1,0:T(2,128)(2,1)}), bf16[4,2,49152]{2,1,0:T(2,128)(2,1)}, u32[]{:S(2)}, u32[]{:S(2)}) async-start(bf16[4,2,49152]{2,1,0:T(2,128)(2,1)} %reshape.1231), calls=%async_computation.5 | async-start | bytes 1572864 | tf_op jit(solution)/shard_map/all_to_all | solution.py:174
  549.2 61.8 %all-to-all-start.2 = ((bf16[8,128,768]{2,1,0:T(8,128)(2,1)}), bf16[8,128,768]{2,1,0:T(8,128)(2,1)}, u32[]{:S(2)}, u32[]{:S(2)}) async-start(bf16[8,128,768]{2,1,0:T(8,128)(2,1)} %bitcast.481), calls=%async_computation.2 | async-start | bytes 3145728 | tf_op jit(solution)/shard_map/all_to_all | solution.py:189
  611.1 45.3 %all-to-all-start.8 = ((bf16[8,128,768]{2,1,0:T(8,128)(2,1)}), bf16[8,128,768]{2,1,0:T(8,128)(2,1)}, u32[]{:S(2)}, u32[]{:S(2)}) async-start(bf16[8,128,768]{2,1,0:T(8,128)(2,1)} %bitcast.96), calls=%async_computation.8 | async-start | bytes 3145728 | tf_op jit(solution)/shard_map/all_to_all | solution.py:350
  656.4 40.2 %all-to-all-start.6 = ((bf16[8,128,768]{2,1,0:T(8,128)(2,1)}), bf16[8,128,768]{2,1,0:T(8,128)(2,1)S(1)}, u32[]{:S(2)}, u32[]{:S(2)}) async-start(bf16[8,128,768]{2,1,0:T(8,128)(2,1)} %bitcast.88), calls=%async_computation.6 | async-start | bytes 3145728 | tf_op jit(solution)/shard_map/all_to_all | solution.py:189
  697.7 41.3 %all-to-all-start.3 = ((bf16[8,128,768]{2,1,0:T(8,128)(2,1)}), bf16[8,128,768]{2,1,0:T(8,128)(2,1)S(1)}, u32[]{:S(2)}, u32[]{:S(2)}) async-start(bf16[8,128,768]{2,1,0:T(8,128)(2,1)} %bitcast.521), calls=%async_computation.3 | async-start | bytes 3145728 | tf_op jit(solution)/shard_map/all_to_all | solution.py:201
  739.0 41.0 %all-to-all-start.9 = ((bf16[8,128,768]{2,1,0:T(8,128)(2,1)}), bf16[8,128,768]{2,1,0:T(8,128)(2,1)}, u32[]{:S(2)}, u32[]{:S(2)}) async-start(bf16[8,128,768]{2,1,0:T(8,128)(2,1)} %bitcast.520), calls=%async_computation.9 | async-start | bytes 3145728 | tf_op jit(solution)/shard_map/all_to_all | solution.py:380
  780.0 61.5 %all-to-all-start.7 = ((bf16[8,128,768]{2,1,0:T(8,128)(2,1)}), bf16[8,128,768]{2,1,0:T(8,128)(2,1)}, u32[]{:S(2)}, u32[]{:S(2)}) async-start(bf16[8,128,768]{2,1,0:T(8,128)(2,1)} %bitcast.93), calls=%async_computation.7 | async-start | bytes 3145728 | tf_op jit(solution)/shard_map/all_to_all | solution.py:201
  899.6 15.9 all-to-all-start.10
  904.7 312.3 %reduce-scatter.14.cloned.1.call-start = ((), (), s32[]{:S(2)}) async-start(), calls=%async_computation.22 | async-start | bytes 2654208 | tf_op jit(solution)/shard_map/reduce_scatter | solution.py:472
  907.0 397.5 %reduce-scatter.12.cloned.1.call-start = ((), (), s32[]{:S(2)}) async-start(), calls=%async_computation.21 | async-start | bytes 7962624 | tf_op jit(solution)/shard_map/reduce_scatter | solution.py:471
  1176.1 191.3 %reduce-scatter.18.cloned.1.call-start = ((), (), s32[]{:S(2)}) async-start(), calls=%async_computation.24 | async-start | bytes 442368
  1197.6 233.9 %reduce-scatter.20.cloned.1.call-start = ((), (), s32[]{:S(2)}) async-start(), calls=%async_computation.25 | async-start | bytes 442368
  1200.3 295.8 %reduce-scatter.16.cloned.1.call-start = ((), (), s32[]{:S(2)}) async-start(), calls=%async_computation.23 | async-start | bytes 442368
  1202.0 640.8 %all-reduce.19.cloned.1.call-start = ((), (), s32[]{:S(2)}) async-start(), calls=%async_computation.26 | async-start | bytes 40108032 | tf_op jit(solution)/shard_map/psum | solution.py:478
  (162 other events, 1268.5 us)
Sparse Core Ops, SparseCore 0:
  10.3 65.0 all-gather.8
  77.6 68.1 all-gather.12
  148.0 40.7 all-gather.10
  190.8 40.1 all-gather.14
  908.7 67.3 reduce-scatter.13
  1176.2 128.2 reduce-scatter.11
  1308.1 59.2 reduce-scatter.17
  1371.0 60.3 reduce-scatter.19
  1435.6 60.3 reduce-scatter.15
  1499.5 343.2 all-reduce.18
where the time goes:
time: 1880 us; the launch traced here: 1870 us
  waiting for transfers between devices  599 us (32%)
  matrix products  376 us (20%)
  blocking collectives  268 us (14%)
  local copies, waits for them, and re-layouts  248 us (13%)
  other arithmetic  244 us (13%)
  starting transfers between devices  98.4 us (5%)
    psum x1, waiting for transfers between devices, per_device(): lax.psum((shard_gain_one, shard_qkv, shard_out, shard_gain_two, shard_rou...  307 us
    unnamed x13, waiting for transfers between devices  148 us
    reduce_scatter x1, waiting for transfers between devices, per_device(): lax.psum_scatter(grad_qkv_w, 'dp', scatter_dimension=0, tiled=True)  87.5 us
    unnamed x298, local copies, waits for them, and re-layouts  59.8 us
    dot_general x8, matrix products, attend(): jnp.einsum('hqk,khd->qhd', probabilities.astype(jnp.bfloat16), values_all...  57.1 us
    dot_general x8, matrix products, block_scores(): jnp.einsum('qhd,khd->hqk', q_blk, keys_all, preferred_element_type=jnp.fl...  55.2 us
    all_to_all x1, blocking collectives, per_device(): lax.all_to_all(grad_heads_all, 'seq', split_axis=0, concat_axis=2, tiled=...  53.8 us
    all_gather x2, blocking collectives, forward_pass(): lax.all_gather(const_mix, 'dp', axis=2, tiled=True)  51.3 us
  transfers between devices with their start and end apart: 21, of which 10 were waited for; matrix products, arithmetic and copies ran while one was open for 41% of the time, Pallas kernels for 0%

commit v1 on v0

v1 whole, which is shorter than its diff:
```python
import functools
import math

import jax
import jax.numpy as jnp
from jax import lax
from jax.experimental import pallas as pl
from jax.experimental.pallas import tpu as pltpu
from jax.sharding import PartitionSpec as P

D = 768
H = 12
HD = 64
E = 8
CAP = 128
BLK = 256

exact_prec = lax.Precision.HIGHEST
neg_large = -1e30
score_scale = 0.125 * math.log2(math.e)
f32 = jnp.float32
bf16 = jnp.bfloat16

NN = (((1,), (0,)), ((), ()))
NT = (((1,), (1,)), ((), ()))
TN = (((0,), (0,)), ((), ()))


def mm(a, b, dims):
    return lax.dot_general(a, b, dims, preferred_element_type=f32)


def swap(value, axis, bit):
    size = lax.axis_size(axis)
    return lax.ppermute(value, axis, [(i, i ^ bit) for i in range(size)])


def bits_high_first(size):
    bit = size // 2
    while bit >= 1:
        yield bit
        bit //= 2


def gather_relative(value, axis):
    held = {0: value}
    for bit in bits_high_first(lax.axis_size(axis)):
        for place in list(held):
            held[place ^ bit] = swap(held[place], axis, bit)
    return [held[place] for place in range(len(held))]


def sum_relative(blocks, axis):
    held = {place: block.astype(f32) for place, block in enumerate(blocks)}
    bit = 1
    while bit < lax.axis_size(axis):
        for place in [p for p in held if p & bit]:
            arrived = swap(held.pop(place).astype(bf16), axis, bit)
            held[place ^ bit] = held[place ^ bit] + arrived.astype(f32)
        bit *= 2
    return held[0]


def qkv_kernel(me_ref, h_ref, gain_ref, w_ref, cos_ref, sin_ref, attn_ref, out_ref, wt_ref):
    @pl.when((pl.program_id(0) == 0) & (pl.program_id(1) == 0))
    def _():
        wt_ref[...] = w_ref[...].T

    x = h_ref[0].astype(f32)
    mean_square = jnp.mean(x * x, axis=-1, keepdims=True)
    attn = (x * lax.rsqrt(mean_square + 1e-06) * gain_ref[...]).astype(bf16)
    attn_ref[...] = attn
    y = mm(wt_ref[...], attn, NT)
    cos, sin = cos_ref[...], sin_ref[...]
    rows = y.shape[0]
    half = HD // 2
    for head in range(2 * rows // (3 * HD)):
        a = y[head * HD : head * HD + half]
        b = y[head * HD + half : (head + 1) * HD]
        out_ref[head * HD : head * HD + half] = (a * cos - b * sin).astype(bf16)
        out_ref[head * HD + half : (head + 1) * HD] = (a * sin + b * cos).astype(bf16)
    out_ref[2 * rows // 3 :] = y[2 * rows // 3 :].astype(bf16)


def qkv_call(me, blocks, gain, w, cos_t, sin_t):
    parts, tok, _ = blocks.shape
    seq_len, width = parts * tok, w.shape[1]
    per = tok // BLK
    return pl.pallas_call(
        qkv_kernel,
        out_shape=(
            jax.ShapeDtypeStruct((seq_len, D), bf16),
            jax.ShapeDtypeStruct((width, seq_len), bf16),
        ),
        grid_spec=pltpu.PrefetchScalarGridSpec(
            num_scalar_prefetch=1,
            grid=(parts, per),
            in_specs=[
                pl.BlockSpec((1, BLK, D), lambda b, t, me_ref: (b ^ me_ref[0], t, 0)),
                pl.BlockSpec((1, D), lambda b, t, me_ref: (0, 0)),
                pl.BlockSpec((D, width), lambda b, t, me_ref: (0, 0)),
                pl.BlockSpec((HD // 2, BLK), lambda b, t, me_ref: (0, b * per + t)),
                pl.BlockSpec((HD // 2, BLK), lambda b, t, me_ref: (0, b * per + t)),
            ],
            out_specs=[
                pl.BlockSpec((BLK, D), lambda b, t, me_ref: (b * per + t, 0)),
                pl.BlockSpec((width, BLK), lambda b, t, me_ref: (0, b * per + t)),
            ],
            scratch_shapes=[pltpu.VMEM((width, D), bf16)],
        ),
        name="qkv",
    )(me, blocks, gain, w, cos_t, sin_t)


def allowed_block(key_block, query_block, start_row):
    key_pos = key_block * BLK + lax.broadcasted_iota(jnp.int32, (BLK, BLK), 0)
    query_pos = query_block * BLK + lax.broadcasted_iota(jnp.int32, (BLK, BLK), 1)
    return (key_pos >= start_row) & (key_pos <= query_pos)


def attn_kernel(lo_ref, qkv_ref, start_ref, out_ref, exact_ref, log_ref, keys_ref):
    heads, seq_len, _ = keys_ref.shape
    width = heads * HD
    qb = pl.program_id(0)

    @pl.when(qb == 0)
    def _():
        for h in range(heads):
            keys_ref[h] = qkv_ref[width + h * HD : width + (h + 1) * HD, :].T

    here = pl.ds(pl.multiple_of(qb * BLK, BLK), BLK)
    start_row = start_ref[...]

    def step(kb, carry):
        there = pl.ds(pl.multiple_of(kb * BLK, BLK), BLK)
        allowed = allowed_block(kb, qb, start_row)
        new = []
        for h in range(heads):
            top, total, acc = carry[h]
            scores = mm(keys_ref[h, there, :], qkv_ref[h * HD : (h + 1) * HD, here], NN)
            scores = jnp.where(allowed, scores * score_scale, neg_large)
            new_top = jnp.maximum(top, jnp.max(scores, axis=0, keepdims=True))
            fade = jnp.exp2(top - new_top)
            weights = jnp.exp2(scores - new_top)
            total = total * fade + jnp.sum(weights, axis=0, keepdims=True)
            values = qkv_ref[2 * width + h * HD : 2 * width + (h + 1) * HD, there]
            acc = acc * fade + mm(values, weights.astype(bf16), NN)
            new.append((new_top, total, acc))
        return tuple(new)

    first = tuple(
        (
            jnp.full((1, BLK), neg_large, f32),
            jnp.zeros((1, BLK), f32),
            jnp.zeros((HD, BLK), f32),
        )
        for _ in range(heads)
    )
    done = lax.fori_loop(lo_ref[qb], qb + 1, step, first)
    for h in range(heads):
        top, total, acc = done[h]
        attended = acc / total
        exact_ref[h * HD : (h + 1) * HD, :] = attended
        out_ref[0, h * HD : (h + 1) * HD, :] = attended.astype(bf16)
        log_ref[h : h + 1, :] = top + jnp.log2(total)


def attn_call(lows, qkv, start_row, tok):
    width3, seq_len = qkv.shape
    width = width3 // 3
    heads = width // HD
    per = tok // BLK
    return pl.pallas_call(
        attn_kernel,
        out_shape=(
            jax.ShapeDtypeStruct((seq_len // tok, width, tok), bf16),
            jax.ShapeDtypeStruct((width, seq_len), f32),
            jax.ShapeDtypeStruct((heads, seq_len), f32),
        ),
        grid_spec=pltpu.PrefetchScalarGridSpec(
            num_scalar_prefetch=1,
            grid=(seq_len // BLK,),
            in_specs=[
                pl.BlockSpec((width3, seq_len), lambda i, lo: (0, 0)),
                pl.BlockSpec((1, BLK), lambda i, lo: (0, i)),
            ],
            out_specs=[
                pl.BlockSpec((1, width, BLK), lambda i, lo: (i // per, 0, i % per)),
                pl.BlockSpec((width, BLK), lambda i, lo: (0, i)),
                pl.BlockSpec((heads, BLK), lambda i, lo: (0, i)),
            ],
            scratch_shapes=[pltpu.VMEM((heads, seq_len, HD), bf16)],
        ),
        name="attend",
    )(lows, qkv, start_row)


def attn_back_kernel(
    lo_ref, qkv_ref, go_ref, exact_ref, log_ref, start_ref, cos_ref, sin_ref, out_ref,
    keys_ref, values_ref, dk_ref, dv_ref,
):
    heads, seq_len, _ = keys_ref.shape
    width = heads * HD
    half = HD // 2
    qb = pl.program_id(0)

    @pl.when(qb == 0)
    def _():
        for h in range(heads):
            keys_ref[h] = qkv_ref[width + h * HD : width + (h + 1) * HD, :].T
            values_ref[h] = qkv_ref[2 * width + h * HD : 2 * width + (h + 1) * HD, :].T
        dk_ref[...] = jnp.zeros_like(dk_ref)
        dv_ref[...] = jnp.zeros_like(dv_ref)

    here = pl.ds(pl.multiple_of(qb * BLK, BLK), BLK)
    start_row = start_ref[...]
    grad = go_ref[0]
    deltas = [
        jnp.sum(
            exact_ref[h * HD : (h + 1) * HD, :] * grad[h * HD : (h + 1) * HD].astype(f32),
            axis=0,
            keepdims=True,
        )
        for h in range(heads)
    ]

    def step(kb, carry):
        there = pl.ds(pl.multiple_of(kb * BLK, BLK), BLK)
        allowed = allowed_block(kb, qb, start_row)
        new = []
        for h in range(heads):
            rows = slice(h * HD, (h + 1) * HD)
            queries = qkv_ref[rows, here]
            scores = mm(keys_ref[h, there, :], queries, NN)
            scores = jnp.where(allowed, scores * score_scale, neg_large)
            probs = jnp.exp2(scores - log_ref[h : h + 1, :])
            grad_probs = mm(values_ref[h, there, :], grad[rows], NN)
            grad_scores = (probs * (grad_probs - deltas[h])).astype(bf16)
            dv_ref[rows, there] += mm(grad[rows], probs.astype(bf16), NT)
            dk_ref[rows, there] += mm(queries, grad_scores, NT)
            keys = qkv_ref[width + h * HD : width + (h + 1) * HD, there]
            new.append(carry[h] + mm(keys, grad_scores, NN))
        return tuple(new)

    grads = lax.fori_loop(
        lo_ref[qb], qb + 1, step, tuple(jnp.zeros((HD, BLK), f32) for _ in range(heads))
    )

    def turn_back(value, cos, sin):
        value = value.astype(bf16).astype(f32)
        a, b = value[:half], value[half:]
        return (a * cos + b * sin).astype(bf16), (b * cos - a * sin).astype(bf16)

    for h in range(heads):
        a, b = turn_back(grads[h] * 0.125, cos_ref[:, here], sin_ref[:, here])
        out_ref[h * HD : h * HD + half, here] = a
        out_ref[h * HD + half : (h + 1) * HD, here] = b

    @pl.when(qb == pl.num_programs(0) - 1)
    def _():
        cos, sin = cos_ref[...], sin_ref[...]
        for h in range(heads):
            a, b = turn_back(dk_ref[h * HD : (h + 1) * HD, :] * 0.125, cos, sin)
            out_ref[width + h * HD : width + h * HD + half, :] = a
            out_ref[width + h * HD + half : width + (h + 1) * HD, :] = b
        out_ref[2 * width :, :] = dv_ref[...].astype(bf16)


def attn_back_call(lows, qkv, grad_out, exact, logs, start_row, cos_t, sin_t):
    width3, seq_len = qkv.shape
    width = width3 // 3
    heads = width // HD
    per = grad_out.shape[2] // BLK
    return pl.pallas_call(
        attn_back_kernel,
        out_shape=jax.ShapeDtypeStruct((width3, seq_len), bf16),
        grid_spec=pltpu.PrefetchScalarGridSpec(
            num_scalar_prefetch=1,
            grid=(seq_len // BLK,),
            in_specs=[
                pl.BlockSpec((width3, seq_len), lambda i, lo: (0, 0)),
                pl.BlockSpec((1, width, BLK), lambda i, lo: (i // per, 0, i % per)),
                pl.BlockSpec((width, BLK), lambda i, lo: (0, i)),
                pl.BlockSpec((heads, BLK), lambda i, lo: (0, i)),
                pl.BlockSpec((1, BLK), lambda i, lo: (0, i)),
                pl.BlockSpec((HD // 2, seq_len), lambda i, lo: (0, 0)),
                pl.BlockSpec((HD // 2, seq_len), lambda i, lo: (0, 0)),
            ],
            out_specs=pl.BlockSpec((width3, seq_len), lambda i, lo: (0, 0)),
            scratch_shapes=[
                pltpu.VMEM((heads, seq_len, HD), bf16),
                pltpu.VMEM((heads, seq_len, HD), bf16),
                pltpu.VMEM((width, seq_len), f32),
                pltpu.VMEM((width, seq_len), f32),
            ],
        ),
        name="attend_back",
    )(lows, qkv, grad_out, exact, logs, start_row, cos_t, sin_t)


def expert_kernel(
    x_ref, g_ref, gate_ref, w_ref, out_ref, piece_ref, dot_ref, dw_ref, gs_ref, oacc_ref, pacc_ref
):
    i = pl.program_id(0)

    @pl.when(i == 0)
    def _():
        gs_ref[...] = (g_ref[...].astype(f32) * gate_ref[...]).astype(bf16)
        oacc_ref[...] = jnp.zeros_like(oacc_ref)
        pacc_ref[...] = jnp.zeros_like(pacc_ref)

    x, gs = x_ref[...], gs_ref[...]
    gate_pre = mm(x, w_ref[0], NT)
    up_pre = mm(x, w_ref[1], NT)
    sig = 1.0 / (1.0 + jnp.exp(-gate_pre))
    silu = gate_pre * sig
    hidden = (silu * up_pre).astype(bf16)
    oacc_ref[...] += mm(hidden, w_ref[2], NN)
    dw_ref[2] = mm(hidden, gs, TN).astype(dw_ref.dtype)
    grad_hidden = mm(gs, w_ref[2], NT)
    grad_gate = (grad_hidden * up_pre * sig * (1.0 + gate_pre * (1.0 - sig))).astype(bf16)
    grad_up = (grad_hidden * silu).astype(bf16)
    pacc_ref[...] += mm(grad_gate, w_ref[0], NN) + mm(grad_up, w_ref[1], NN)
    dw_ref[0] = mm(grad_gate, x, TN).astype(dw_ref.dtype)
    dw_ref[1] = mm(grad_up, x, TN).astype(dw_ref.dtype)

    @pl.when(i == pl.num_programs(0) - 1)
    def _():
        out = oacc_ref[...].astype(bf16)
        out_ref[...] = out
        piece_ref[...] = pacc_ref[...].astype(bf16)
        dot_ref[...] = jnp.sum(out.astype(f32) * g_ref[...].astype(f32), axis=-1, keepdims=True)


def expert_plain(x, g, gate, weights):
    gs = (g.astype(f32) * gate).astype(bf16)
    gate_pre = mm(x, weights[0], NT)
    up_pre = mm(x, weights[1], NT)
    sig = 1.0 / (1.0 + jnp.exp(-gate_pre))
    silu = gate_pre * sig
    hidden = (silu * up_pre).astype(bf16)
    out = mm(hidden, weights[2], NN).astype(bf16)
    grad_hidden = mm(gs, weights[2], NT)
    grad_gate = (grad_hidden * up_pre * sig * (1.0 + gate_pre * (1.0 - sig))).astype(bf16)
    grad_up = (grad_hidden * silu).astype(bf16)
    piece = (mm(grad_gate, weights[0], NN) + mm(grad_up, weights[1], NN)).astype(bf16)
    dw = jnp.stack([mm(grad_gate, x, TN), mm(grad_up, x, TN), mm(hidden, gs, TN)]).astype(bf16)
    dots = jnp.sum(out.astype(f32) * g.astype(f32), axis=-1, keepdims=True)
    return out, piece, dots, dw


def expert_call(x, g, gate, weights):
    rows, units = x.shape[0], weights.shape[1]
    if rows > 1024:
        return expert_plain(x, g, gate, weights)
    tile = min(256, units)
    whole = pl.BlockSpec((rows, D), lambda i: (0, 0))
    column = pl.BlockSpec((rows, 1), lambda i: (0, 0))
    return pl.pallas_call(
        expert_kernel,
        out_shape=(
            jax.ShapeDtypeStruct((rows, D), bf16),
            jax.ShapeDtypeStruct((rows, D), bf16),
            jax.ShapeDtypeStruct((rows, 1), f32),
            jax.ShapeDtypeStruct(weights.shape, bf16),
        ),
        grid=(units // tile,),
        in_specs=[whole, whole, column, pl.BlockSpec((3, tile, D), lambda i: (0, i, 0))],
        out_specs=[whole, whole, column, pl.BlockSpec((3, tile, D), lambda i: (0, i, 0))],
        scratch_shapes=[
            pltpu.VMEM((rows, D), bf16),
            pltpu.VMEM((rows, D), f32),
            pltpu.VMEM((rows, D), f32),
        ],
        name="experts",
    )(x, g, gate, weights)


def rope_tables(seq_len):
    freq_index = jnp.arange(HD // 2, dtype=f32)
    inv_freq = jnp.exp(freq_index * (-2.0 * math.log(10000.0) / HD))
    angles = jnp.arange(seq_len, dtype=jnp.int32).astype(f32)[None, :] * inv_freq[:, None]
    return jnp.cos(angles), jnp.sin(angles)


def norm_back(values, gain, grad):
    rate = lax.rsqrt(jnp.mean(values * values, axis=-1, keepdims=True) + 1e-06)
    scaled = gain * grad
    inner = jnp.mean(values * scaled, axis=-1, keepdims=True)
    return rate * scaled - values * (rate * rate * rate) * inner, rate


def per_device(
    hidden_in,
    prev_logits,
    segments,
    routes,
    attn_gain,
    w_qkv,
    w_out,
    moe_gain,
    w_router,
    w_carry,
    const_vec,
    const_mix,
    experts,
    cotangent,
):
    n_seq, n_dp = lax.axis_size("seq"), lax.axis_size("dp")
    owners = n_dp // E
    me = lax.axis_index("seq")
    me_arr = me.astype(jnp.int32).reshape(1)
    tok = hidden_in.shape[1]
    seq_len = tok * n_seq
    shard = w_qkv.shape[0]
    heads_here = H // n_seq
    width = heads_here * HD
    hidden = hidden_in[0]
    tokens_f = hidden.astype(f32)
    grad_low = cotangent[0]
    grad_top = grad_low.astype(f32)
    prev_rows = prev_logits[0]
    route_rows = routes[0]
    carry_f = w_carry.astype(f32)

    blocks = jnp.stack(gather_relative(hidden, "seq"))
    w_mine = lax.dynamic_slice_in_dim(
        w_qkv.reshape(shard, 3, n_seq, width), me, 1, axis=2
    ).reshape(shard, 3 * width)
    small = jnp.concatenate(
        [
            attn_gain[:, None],
            moe_gain[:, None],
            const_vec.T,
            const_mix.reshape(4, shard).T,
            w_router,
        ],
        axis=1,
    )
    first = lax.all_gather(jnp.concatenate([w_mine, small], axis=1), "dp", axis=0, tiled=True)
    w_slice = first[:, : 3 * width]
    small_t = first[:, 3 * width :].astype(f32).T
    gain_one, gain_two = small_t[0:1], small_t[1:2]
    vec_f, mix_f, router_t = small_t[2:4], small_t[4:8], small_t[8:20]
    dp_me = lax.axis_index("dp")
    out_parts = [w_out] + [
        lax.ppermute(w_out, "dp", [(i, (i + k) % n_dp) for i in range(n_dp)])
        for k in range(1, n_dp)
    ]
    out_weight = jnp.zeros((n_dp, shard, D), bf16)
    for k, part in enumerate(out_parts):
        out_weight = lax.dynamic_update_index_in_dim(
            out_weight, part, lax.rem(dp_me + n_dp - k, n_dp), 0
        )
    out_weight = out_weight.reshape(D, D)

    named = [
        (route_rows[:, k : k + 1] == jnp.arange(E, dtype=jnp.int32)[None, :]) for k in range(2)
    ]
    earlier = (
        jnp.arange(tok, dtype=jnp.int32)[None, :] < jnp.arange(tok, dtype=jnp.int32)[:, None]
    ).astype(bf16)
    ranks = mm(earlier, (named[0] | named[1]).astype(bf16), NN)
    slot_of = [
        jnp.where(
            route_rows[:, k] < E,
            route_rows[:, k] * CAP
            + jnp.sum(jnp.where(named[k], ranks, 0.0), axis=1).astype(jnp.int32),
            E * CAP,
        )
        for k in range(2)
    ]
    slots = jnp.arange(E * CAP, dtype=jnp.int32)[None, :]
    picks = [slot_of[k][:, None] == slots for k in range(2)]
    pick_low = [p.astype(bf16) for p in picks]
    pick_any = (picks[0] | picks[1]).astype(bf16)

    def dispatch(rows):
        grouped = mm(pick_any, rows, TN).astype(bf16).reshape(E, CAP, D)
        return lax.all_to_all(
            jnp.repeat(grouped, owners, axis=0), "dp", split_axis=0, concat_axis=0, tiled=True
        )

    def back_to_source(values):
        return lax.all_to_all(values, "dp", split_axis=0, concat_axis=0, tiled=True)

    arrived_grad = dispatch(grad_low)

    cos_t, sin_t = rope_tables(seq_len)
    seg_row = segments[0]
    doc_ids = jnp.arange(16, dtype=jnp.int32)
    doc_start = jnp.sum((seg_row[None, :] < doc_ids[:, None]).astype(jnp.int32), axis=1)
    start = jnp.sum(jnp.where(seg_row[None, :] == doc_ids[:, None], doc_start[:, None], 0), axis=0)
    start_row = start.astype(jnp.int32)[None, :]
    lows = start[::BLK].astype(jnp.int32) // BLK
    attn_in, qkv = qkv_call(me_arr, blocks, gain_one, w_slice, cos_t, sin_t)
    attended, attended_exact, logs = attn_call(lows, qkv, start_row, tok)
    heads_t = lax.all_to_all(attended, "seq", split_axis=0, concat_axis=0, tiled=True).reshape(
        D, tok
    )

    resid_mid = tokens_f + mm(heads_t, out_weight, TN)
    rate_two = lax.rsqrt(jnp.mean(resid_mid * resid_mid, axis=-1, keepdims=True) + 1e-06)
    normed = resid_mid * rate_two * gain_two
    normed_low = normed.astype(bf16)
    logits = mm(normed_low, router_t.astype(bf16), NT) + jnp.dot(
        prev_rows, carry_f, precision=exact_prec
    )
    all_ids = jnp.arange(H, dtype=jnp.int32)[None, :]
    hot = [route_rows[:, k : k + 1] == all_ids for k in range(2)]
    chosen = [jnp.sum(jnp.where(hot[k], logits, 0.0), axis=1, keepdims=True) for k in range(2)]
    top_logit = jnp.maximum(chosen[0], chosen[1])
    gate_exp = [jnp.exp(c - top_logit) for c in chosen]
    gate_sum = gate_exp[0] + gate_exp[1]
    gates = [g / gate_sum for g in gate_exp]

    arrived = dispatch(normed_low)
    gate_slots = jnp.sum(
        jnp.where(picks[0], gates[0], 0.0) + jnp.where(picks[1], gates[1], 0.0), axis=0
    ).reshape(E, 1, CAP)
    arrived_gate = lax.all_to_all(
        jnp.repeat(gate_slots, owners, axis=0), "dp", split_axis=0, concat_axis=0, tiled=True
    )
    rows = n_dp * CAP
    partial, piece, dots, dw = expert_call(
        arrived.reshape(rows, D),
        arrived_grad.reshape(rows, D),
        arrived_gate.reshape(rows, 1),
        experts,
    )
    back_piece = back_to_source(piece.reshape(n_dp, CAP, D))
    back_dots = back_to_source(dots.reshape(n_dp, 1, CAP))
    partial, back_piece = lax.optimization_barrier((partial, back_piece))
    back_out = back_to_source(partial.reshape(n_dp, CAP, D))

    def owner_rows(values, owner):
        return values.reshape(E, owners, CAP, -1)[:, owner].reshape(E * CAP, -1)

    half = dw.shape[1] // 2
    core = me & 1
    kept = lax.dynamic_slice_in_dim(dw, core * half, half, 1)
    given = lax.dynamic_slice_in_dim(dw, (1 - core) * half, half, 1)
    summed = (kept.astype(f32) + swap(given, "seq", 1).astype(f32)).astype(bf16)
    bit = 2
    total = summed.astype(f32)
    while bit < n_seq:
        low = total.astype(bf16)
        total = low.astype(f32) + swap(low, "seq", bit).astype(f32)
        bit *= 2
    mine = total.astype(bf16)
    other = swap(mine, "seq", 1)
    d_experts = jnp.concatenate(
        [jnp.where(core == 0, mine, other), jnp.where(core == 0, other, mine)], axis=1
    ).astype(f32)

    const_logits = lax.dot_general(normed, mix_f, NT, precision=exact_prec)
    grad_normed_dot = jnp.sum(grad_top * normed, axis=1, keepdims=True)
    grad_vec_dot = lax.dot_general(grad_top, vec_f, NT, precision=exact_prec)
    alphas = []
    for j in range(2):
        pair = const_logits[:, 2 * j : 2 * j + 2]
        pair_exp = jnp.exp(pair - jnp.max(pair, axis=1, keepdims=True))
        alphas.append(pair_exp / jnp.sum(pair_exp, axis=1, keepdims=True))
    const_dot = [
        alphas[j][:, 0:1] * grad_normed_dot + alphas[j][:, 1:2] * grad_vec_dot[:, j : j + 1]
        for j in range(2)
    ]
    slot_dots = jnp.sum(back_dots.reshape(E, owners, CAP), axis=1).reshape(1, E * CAP)
    out_dots = []
    for k in range(2):
        route = route_rows[:, k : k + 1]
        value = jnp.sum(jnp.where(picks[k], slot_dots, 0.0), axis=1, keepdims=True)
        value = value + jnp.where(route == E + 1, grad_normed_dot, 0.0)
        for j in range(2):
            value = value + jnp.where(route == E + 2 + j, const_dot[j], 0.0)
        out_dots.append(value)
    mean_dot = gates[0] * out_dots[0] + gates[1] * out_dots[1]
    grad_logits = sum(
        jnp.where(hot[k], gates[k] * (out_dots[k] - mean_dot), 0.0) for k in range(2)
    )

    def gate_of(expert):
        return sum(
            jnp.where(route_rows[:, k : k + 1] == expert, gates[k], 0.0) for k in range(2)
        )

    copy_gate = gate_of(E + 1)
    const_gate = [gate_of(E + 2 + j) for j in range(2)]
    mix_grads = []
    for j in range(2):
        terms = [grad_normed_dot, grad_vec_dot[:, j : j + 1]]
        for c in range(2):
            mix_grads.append(
                const_gate[j] * alphas[j][:, c : c + 1] * (terms[c] - const_dot[j])
            )
    mix_grads = jnp.concatenate(mix_grads, axis=1)
    normed_gate = copy_gate + sum(const_gate[j] * alphas[j][:, 0:1] for j in range(2))
    vec_gate = jnp.concatenate([const_gate[j] * alphas[j][:, 1:2] for j in range(2)], axis=1)

    mixed = normed * normed_gate + jnp.dot(vec_gate, vec_f, precision=exact_prec)
    for k in range(2):
        picked = sum(mm(pick_low[k], owner_rows(back_out, o), NN) for o in range(owners))
        mixed = mixed + gates[k] * picked
    block_out = (resid_mid + mixed).astype(bf16)

    grad_normed = grad_top * normed_gate
    grad_normed = grad_normed + jnp.dot(
        jnp.concatenate([grad_logits, mix_grads], axis=1),
        jnp.concatenate([router_t, mix_f], axis=0),
        precision=exact_prec,
    )
    for o in range(owners):
        grad_normed = grad_normed + mm(pick_any, owner_rows(back_piece, o), NN)
    grad_mid, _ = norm_back(resid_mid, gain_two, grad_normed)
    grad_resid = grad_top + grad_mid
    grad_attn = grad_resid.astype(bf16)
    grad_heads = mm(out_weight, grad_attn, NT).astype(bf16)
    grad_out = lax.all_to_all(
        grad_heads.reshape(n_seq, width, tok), "seq", split_axis=0, concat_axis=0, tiled=True
    )

    d_prev = jnp.dot(grad_logits, carry_f.T, precision=exact_prec)
    grad_router = jnp.dot(grad_logits.T, normed_low.astype(f32), precision=exact_prec)
    grad_carry = jnp.dot(prev_rows.T, grad_logits, precision=exact_prec)
    grad_gain_two = jnp.sum(grad_normed * resid_mid * rate_two, axis=0, keepdims=True)
    grad_vec = jnp.dot(vec_gate.T, grad_top, precision=exact_prec)
    grad_mix = jnp.dot(mix_grads.T, normed, precision=exact_prec)
    packed = jnp.concatenate([grad_router, grad_gain_two, grad_vec, grad_mix], axis=0)
    lines = packed.shape[0]
    packed = packed.reshape(lines, n_dp, shard).swapaxes(0, 1).reshape(n_dp, lines * shard)
    packed = jnp.concatenate(
        [packed, jnp.broadcast_to(grad_carry.reshape(1, H * H), (n_dp, H * H))], axis=1
    )
    packed = lax.all_to_all(packed, "dp", split_axis=0, concat_axis=0, tiled=True)
    packed = jnp.sum(packed, axis=0, keepdims=True)
    for bit in bits_high_first(n_seq):
        packed = packed + swap(packed, "seq", bit)
    lined = packed[0, : lines * shard].reshape(lines, shard)
    d_router, d_moe_gain = lined[:H].T, lined[H]
    d_vec, d_mix = lined[H + 1 : H + 3], lined[H + 3 : H + 7].reshape(2, 2, shard)
    d_carry = packed[0, lines * shard :].reshape(H, H)

    grad_out_w = mm(heads_t, grad_attn, NN)
    blocks_out = grad_out_w.reshape(D, n_seq, width).swapaxes(0, 1)
    blocks_out = blocks_out[jnp.arange(n_seq) ^ me]
    mine_out = sum_relative([blocks_out[r] for r in range(n_seq)], "seq").astype(bf16)

    def reduce_rows(value):
        value = value.reshape(n_dp, -1, value.shape[-1])
        value = lax.all_to_all(value, "dp", split_axis=0, concat_axis=0, tiled=True)
        return jnp.sum(value.astype(f32), axis=0)

    def collect_columns(value):
        parts = jnp.stack(gather_relative(value, "seq"))
        return parts[jnp.arange(n_seq) ^ me]

    d_out = collect_columns(reduce_rows(mine_out)).swapaxes(0, 1).reshape(shard, D)

    grad_qkv = attn_back_call(
        lows, qkv, grad_out, attended_exact, logs, start_row, cos_t, sin_t
    )
    grad_w = lax.dot_general(
        attn_in, grad_qkv, (((0,), (1,)), ((), ())), preferred_element_type=f32
    )
    rows_w = collect_columns(reduce_rows(grad_w.astype(bf16)))
    d_qkv = (
        rows_w.reshape(n_seq, shard, 3, width).transpose(1, 2, 0, 3).reshape(shard, 3 * D)
    )
    d_attn_gain = jnp.sum(d_qkv * w_qkv.astype(f32), axis=1) / attn_gain.astype(f32)

    grad_in = lax.dot_general(
        grad_qkv, w_slice, (((0,), (1,)), ((), ())), preferred_element_type=f32
    ).astype(bf16)
    grad_in = grad_in.reshape(n_seq, tok, D)[jnp.arange(n_seq) ^ me]
    grad_attn_in = sum_relative([grad_in[r] for r in range(n_seq)], "seq")
    grad_first, _ = norm_back(tokens_f, gain_one, grad_attn_in)
    d_input = grad_resid + grad_first
    return (
        block_out[None],
        d_input[None],
        d_prev[None],
        d_attn_gain,
        d_qkv,
        d_out,
        d_moe_gain,
        d_router,
        d_carry,
        d_vec,
        d_mix,
        d_experts,
    )


def solution(mesh):
    return jax.shard_map(
        per_device,
        mesh=mesh,
        in_specs=(
            P("dp", "seq", None),
            P("dp", "seq", None),
            P("dp", None),
            P("dp", "seq", None),
            P("dp"),
            P("dp", None),
            P("dp", None),
            P("dp"),
            P("dp", None),
            P(),
            P(None, "dp"),
            P(None, None, "dp"),
            P(None, "dp", None),
            P("dp", "seq", None),
        ),
        out_specs=(
            P("dp", "seq", None),
            P("dp", "seq", None),
            P("dp", "seq", None),
            P("dp"),
            P("dp", None),
            P("dp", None),
            P("dp"),
            P("dp", None),
            P(),
            P(None, "dp"),
            P(None, None, "dp"),
            P(None, "dp", None),
        ),
        check_vma=False,
    )
```

time: 1880 us -> 598 us (0.32)
  waiting for transfers between devices: 599 us -> 184 us
  matrix products: 376 us -> 45 us
  blocking collectives: 268 us -> 24.8 us
  other arithmetic: 244 us -> 64.4 us
  local copies, waits for them, and re-layouts: 248 us -> 68.6 us
  Pallas kernels: 0 us -> 99.8 us
    psum x1 -> x0, waiting for transfers between devices: 307 us -> none  [per_device(): lax.psum((shard_gain_one, shard_qkv, shard_out, shard_gain_two, shard_rou...]
    dot_general x61 -> x21, matrix products: 333 us -> 44.8 us  [the longest x10 22.1 us: mm(): return lax.dot_general(a, b, dims, preferred_element_type=f32)]
    unnamed x13 -> x0, waiting for transfers between devices: 148 us -> none
    all_gather x6 -> x1, blocking collectives: 133 us -> 24.8 us  [per_device(): lax.all_gather(jnp.concatenate([w_mine, small], axis=1), 'dp', axis=0, ti...]
    pallas_call x0 -> x4, Pallas kernels: none -> 99.8 us  [the longest x1 41.7 us: expert_call(): pl.pallas_call(expert_kernel, out_shape=(jax.ShapeDtypeStruct((rows, D),...]
    ppermute x0 -> x27, waiting for transfers between devices: none -> 88 us  [the longest x20 82.5 us: swap(): return lax.ppermute(value, axis, [(i, i ^ bit) for i in range(size)])]
    reduce_scatter x2 -> x0, waiting for transfers between devices: 87.5 us -> none  [the longest x1 87.5 us: per_device(): lax.psum_scatter(grad_qkv_w, 'dp', scatter_dimension=0, tiled=True)]
    reduce_sum x18 -> x11, other arithmetic: 84.7 us -> 8.82 us  [the longest x1 2.38 us: norm_back(): rate = lax.rsqrt(jnp.mean(values * values, axis=-1, keepdims=True) + 1e-06)]
  transfers between devices with their start and end apart: 21 -> 38, of which waited for: 10 -> 10; matrix products, arithmetic and copies ran while one was open for 41% -> 25% of each run, Pallas kernels for 0% -> 10%
where the time goes in v1:
time: 598 us; the launch traced here: 587 us
  waiting for transfers between devices  184 us (31%)
  Pallas kernels  99.8 us (17%)
  starting transfers between devices  98.5 us (16%)
  local copies, waits for them, and re-layouts  68.6 us (11%)
  other arithmetic  64.4 us (11%)
  matrix products  45 us (8%)
  blocking collectives  24.8 us (4%)
    ppermute x20, waiting for transfers between devices, swap(): return lax.ppermute(value, axis, [(i, i ^ bit) for i in range(size)])  82.5 us
    all_to_all x2, waiting for transfers between devices, dispatch(): lax.all_to_all(jnp.repeat(grouped, owners, axis=0), 'dp', split_axis=0, c...  64.1 us
    pallas_call x1, Pallas kernels, expert_call(): pl.pallas_call(expert_kernel, out_shape=(jax.ShapeDtypeStruct((rows, D),...  41.7 us
    pallas_call x1, Pallas kernels, attn_back_call(): pl.pallas_call(attn_back_kernel, out_shape=jax.ShapeDtypeStruct((width3,...  25.6 us
    all_to_all x3, waiting for transfers between devices, back_to_source(): return lax.all_to_all(values, 'dp', split_axis=0, concat_axis=0, tiled=True)  25.1 us
    all_gather x1, blocking collectives, per_device(): lax.all_gather(jnp.concatenate([w_mine, small], axis=1), 'dp', axis=0, ti...  24.8 us
    pallas_call x1, Pallas kernels, attn_call(): pl.pallas_call(attn_kernel, out_shape=(jax.ShapeDtypeStruct((seq_len // t...  23.6 us
    ppermute x20, starting transfers between devices, swap(): return lax.ppermute(value, axis, [(i, i ^ bit) for i in range(size)])  23.2 us
  transfers between devices with their start and end apart: 38, of which 10 were waited for; matrix products, arithmetic and copies ran while one was open for 25% of the time, Pallas kernels for 10%

profile of v1, /device:TPU:13, one launch (start us, length us, event | category | flops | bytes accessed | tf_op | source)
XLA Modules:
  0.0 586.6 jit_solution(8300600459058545691)
XLA Ops:
  19.0 24.8 %all_gather.3 = bf16[768,596]{1,0:T(8,128)(2,1)S(1)} all-gather(bf16[96,596]{1,0:T(8,128)(2,1)S(1)} %concatenate.32), channel_id=1, replica_groups=mesh['dp'=8,'seq'=4] {'dp'}, dimensions={0}, use_global_device_ids=true | all-gather | bytes 1029888 | tf_op jit(solution)/shard_map/all_gather | solution.py:440
  50.3 5.7 collective-permute-start
  61.8 5.5 collective-permute-done.5
  67.9 4.5 collective-permute-start.8
  76.3 8.8 %qkv.1 = (bf16[2048,768]{1,0:T(8,128)(2,1)}, bf16[576,2048]{1,0:T(8,128)(2,1)}) custom-call(s32[1]{0:T(128)} %bitcast.2.me_ref, bf16[4,512,768]{2,1,0:T(8,128)(2,1)} %pad_maximum_fusion.h_ref, f32[1,768]{1,0:T(1,128)} %copy.107.gain_ref, bf16[768,576]{1,0:T(8,128)(2,1)} %bitcast.191, f32[32,2048]{1,0:T(8,128)} %get-tuple-element.137.cos_ref, ...), custom_call_target="tpu_custom_call" | custom-call | tf_op jit(solution)/shard_map/qkv/pallas_call | solution.py:89
  85.1 23.6 %attend.1 = (bf16[4,192,512]{2,1,0:T(8,128)(2,1)}, f32[192,2048]{1,0:T(8,128)}, f32[3,2048]{1,0:T(4,128)}) custom-call(s32[8]{0:T(128)} %and_select_fusion.lo_ref, bf16[576,2048]{1,0:T(8,128)(2,1)} %get-tuple-element.23.qkv_ref, s32[1,2048]{1,0:T(1,128)} %bitcast.223), custom_call_target="tpu_custom_call" | custom-call | tf_op jit(solution)/shard_map/attend/pallas_call | solution.py:173
  108.7 4.5 all-to-all-start
  117.9 6.0 %all-to-all-done = bf16[4,192,512]{2,1,0:T(8,128)(2,1)S(1)} async-done(((bf16[4,192,512]{2,1,0:T(8,128)(2,1)}), bf16[4,192,512]{2,1,0:T(8,128)(2,1)S(1)}, u32[]{:S(2)}, u32[]{:S(2)}) %all-to-all-start) | async-done | bytes 786464 | tf_op jit(solution)/shard_map/all_to_all | solution.py:498
  138.7 6.1 %all-to-all-start.2 = ((bf16[8,128,768]{2,1,0:T(8,128)(2,1)}), bf16[8,128,768]{2,1,0:T(8,128)(2,1)}, u32[]{:S(2)}, u32[]{:S(2)}) async-start(bf16[8,128,768]{2,1,0:T(8,128)(2,1)} %bitcast.200), calls=%async_computation.2 | async-start | bytes 3145728 | tf_op jit(solution)/shard_map/all_to_all | solution.py:480
  147.9 31.4 %all-to-all-done.2 = bf16[8,128,768]{2,1,0:T(8,128)(2,1)} async-done(((bf16[8,128,768]{2,1,0:T(8,128)(2,1)}), bf16[8,128,768]{2,1,0:T(8,128)(2,1)}, u32[]{:S(2)}, u32[]{:S(2)}) %all-to-all-start.2) | async-done | bytes 1572896 | tf_op jit(solution)/shard_map/all_to_all | solution.py:480
  179.3 7.0 %all-to-all-start.1 = ((bf16[8,128,768]{2,1,0:T(8,128)(2,1)}), bf16[8,128,768]{2,1,0:T(8,128)(2,1)}, u32[]{:S(2)}, u32[]{:S(2)}) async-start(bf16[8,128,768]{2,1,0:T(8,128)(2,1)} %bitcast.199), calls=%async_computation.1 | async-start | bytes 3145728 | tf_op jit(solution)/shard_map/all_to_all | solution.py:480
  188.0 32.7 %all-to-all-done.1 = bf16[8,128,768]{2,1,0:T(8,128)(2,1)} async-done(((bf16[8,128,768]{2,1,0:T(8,128)(2,1)}), bf16[8,128,768]{2,1,0:T(8,128)(2,1)}, u32[]{:S(2)}, u32[]{:S(2)}) %all-to-all-start.1) | async-done | bytes 1572896 | tf_op jit(solution)/shard_map/all_to_all | solution.py:480
  220.7 41.7 %experts.1 = (bf16[1024,768]{1,0:T(8,128)(2,1)}, bf16[1024,768]{1,0:T(8,128)(2,1)}, f32[1024,1]{1,0:T(8,128)}, bf16[3,2048,768]{2,1,0:T(8,128)(2,1)}) custom-call(bf16[1024,768]{1,0:T(8,128)(2,1)} %bitcast.35.x_ref, bf16[1024,768]{1,0:T(8,128)(2,1)} %bitcast.38.g_ref, f32[1024,1]{1,0:T(8,128)} %copy.108.gate_ref, bf16[3,2048,768]{2,1,0:T(8,128)(2,1)} %w_ref.1), custom_call_target="tpu_custom_call" | custom-call | tf_op jit(solution)/shard_map/experts/pallas_call | solution.py:359
  262.4 4.8 constant_dynamic-slice_fusion.1
  277.1 6.5 %all-to-all-start.6 = ((f32[8,1,128]{2,1,0:T(1,128)}), f32[8,1,128]{2,1,0:T(1,128)S(1)}, u32[]{:S(2)}, u32[]{:S(2)}) async-start(f32[8,1,128]{2,1,0:T(1,128)} %bitcast.45), calls=%async_computation.6 | async-start | bytes 8192 | tf_op jit(solution)/shard_map/all_to_all | solution.py:485
  286.8 6.5 %all-to-all-start.4 = ((bf16[8,128,768]{2,1,0:T(8,128)(2,1)}), bf16[8,128,768]{2,1,0:T(8,128)(2,1)}, u32[]{:S(2)}, u32[]{:S(2)}) async-start(bf16[8,128,768]{2,1,0:T(8,128)(2,1)} %bitcast.198), calls=%async_computation.4 | async-start | bytes 3145728 | tf_op jit(solution)/shard_map/all_to_all | solution.py:485
  296.2 7.0 %add_convert_fusion.1 = bf16[3,1024,768]{2,1,0:T(8,128)(2,1)} fusion(bf16[3,1024,768]{2,1,0:T(8,128)(2,1)} %collective-permute-done.24, bf16[3,2048,768]{2,1,0:T(8,128)(2,1)} %get-tuple-element.33, s32[]{:T(128)S(6)} %select_n.186), kind=kLoop, calls=%fused_computation.6 | loop fusion | flops 9437184 | bytes 14155780 | tf_op jit(solution)/shard_map/convert_element_type | solution.py:543
  305.7 22.0 %all-to-all-done.4 = bf16[8,128,768]{2,1,0:T(8,128)(2,1)} async-done(((bf16[8,128,768]{2,1,0:T(8,128)(2,1)}), bf16[8,128,768]{2,1,0:T(8,128)(2,1)}, u32[]{:S(2)}, u32[]{:S(2)}) %all-to-all-start.4) | async-done | bytes 1572896 | tf_op jit(solution)/shard_map/all_to_all | solution.py:485
  356.3 63.4 %collective-permute-done.18 = bf16[768,192]{0,1:T(8,128)(2,1)S(1)} collective-permute-done((bf16[768,192]{0,1:T(8,128)(2,1)S(1)}, bf16[768,192]{0,1:T(8,128)(2,1)S(1)}, u32[]{:S(2)}, u32[]{:S(2)}) %collective-permute-start.18) | collective-permute-done | bytes 294944 | tf_op jit(solution)/shard_map/ppermute | solution.py:35
  422.2 5.7 all-to-all-start.10
  427.9 25.6 %attend_back.1 = bf16[576,2048]{1,0:T(8,128)(2,1)} custom-call(s32[8]{0:T(128)} %and_select_fusion.lo_ref, bf16[576,2048]{1,0:T(8,128)(2,1)} %get-tuple-element.23.qkv_ref, bf16[4,192,512]{2,1,0:T(8,128)(2,1)} %copy-done.9, f32[192,2048]{1,0:T(8,128)} %get-tuple-element.30.exact_ref, f32[3,2048]{1,0:T(4,128)} %get-tuple-element.31.log_ref, ...), custom_call_target="tpu_custom_call" | custom-call | tf_op jit(solution)/shard_map/attend_back/pallas_call | solution.py:274
  453.5 4.6 convolution_convert_fusion.3
  459.4 4.5 all-to-all-start.9
  464.0 7.0 %add_convert_fusion = bf16[3,1024,768]{2,1,0:T(8,128)(2,1)} fusion(bf16[3,1024,768]{2,1,0:T(8,128)(2,1)} %collective-permute-done.25, bf16[3,1024,768]{2,1,0:T(8,128)(2,1)} %add_convert_fusion.1), kind=kLoop, calls=%fused_computation.5 | loop fusion | flops 9437184 | bytes 14155776 | tf_op jit(solution)/shard_map/convert_element_type | solution.py:550
  475.6 5.4 all-to-all-start.8
  481.0 6.1 %convolution_convert_fusion = bf16[2048,768]{1,0:T(8,128)(2,1)} fusion(bf16[576,2048]{1,0:T(8,128)(2,1)} %attend_back.1, bf16[768,596]{1,0:T(8,128)(2,1)S(1)} %copy-done.7), kind=kOutput, calls=%fused_computation.9 | convolution fusion | flops 1813512192 | bytes 6420480 | tf_op jit(solution)/shard_map/dot_general | solution.py:671
  487.1 4.4 gather_fusion
  502.9 6.8 %all-to-all-start.5 = ((bf16[8,128,768]{2,1,0:T(8,128)(2,1)}), bf16[8,128,768]{2,1,0:T(8,128)(2,1)}, u32[]{:S(2)}, u32[]{:S(2)}) async-start(bf16[8,128,768]{2,1,0:T(8,128)(2,1)} %bitcast.197), calls=%async_computation.5 | async-start | bytes 3145728 | tf_op jit(solution)/shard_map/all_to_all | solution.py:485
  517.8 14.5 %collective-permute-done.20 = f32[96,192]{1,0:T(8,128)S(1)} collective-permute-done((f32[96,192]{1,0:T(8,128)S(1)}, f32[96,192]{1,0:T(8,128)S(1)}, u32[]{:S(2)}, u32[]{:S(2)}) %collective-permute-start.20) | collective-permute-done | bytes 73760 | tf_op jit(solution)/shard_map/ppermute | solution.py:35
  546.5 4.5 collective-permute-done.14
  569.6 6.6 %broadcast_select_fusion.1 = (bf16[3,1024,768]{2,1,0:T(8,128)(2,1)S(1)}, bf16[3,1024,768]{2,1,0:T(8,128)(2,1)}) fusion(bf16[3,1024,768]{2,1,0:T(8,128)(2,1)} %add_convert_fusion, bf16[3,1024,768]{2,1,0:T(8,128)(2,1)} %collective-permute-done.26, pred[]{:T(512)S(6)} %eq.164), kind=kLoop, calls=%fused_computation.8 | loop fusion | flops 4718592 | bytes 18874368 | tf_op jit(solution)/shard_map/jit(_where)/select_n | solution.py:553
  576.2 9.9 %maximum_convert_fusion = f32[3,2048,768]{2,1,0:T(8,128)} fusion(bf16[3,1024,768]{2,1,0:T(8,128)(2,1)} %get-tuple-element.126, bf16[3,1024,768]{2,1,0:T(8,128)(2,1)S(1)} %get-tuple-element.125), kind=kLoop, calls=%fused_computation.4 | loop fusion | flops 18874368 | bytes 28311552 | tf_op jit(solution)/shard_map/convert_element_type | solution.py:554
  (314 shorter events, 166.3 us)
Async XLA Ops:
  0.7 112.5 %collective-permute-start.7 = (bf16[96,768]{1,0:T(8,128)(2,1)}, bf16[96,768]{1,0:T(8,128)(2,1)}, u32[]{:S(2)}, u32[]{:S(2)}) collective-permute-start(bf16[96,768]{1,0:T(8,128)(2,1)} %param.20), channel_id=1, source_target_pairs={{0,20},{4,24},{8,28},{12,0},{16,4},{20,8},{24,12},{28,16},{1,21},{... | collective-permute-start | bytes 442376 | tf_op jit(solution)/shard_map/ppermute | solution.py:447
  0.7 67.2 %collective-permute-start.6 = (bf16[96,768]{1,0:T(8,128)(2,1)}, bf16[96,768]{1,0:T(8,128)(2,1)}, u32[]{:S(2)}, u32[]{:S(2)}) collective-permute-start(bf16[96,768]{1,0:T(8,128)(2,1)} %param.20), channel_id=1, source_target_pairs={{0,16},{4,20},{8,24},{12,28},{16,0},{20,4},{24,8},{28,12},{1,17},{... | collective-permute-start | bytes 442376 | tf_op jit(solution)/shard_map/ppermute | solution.py:447
  3.1 54.4 %collective-permute-start.4 = (bf16[96,768]{1,0:T(8,128)(2,1)}, bf16[96,768]{1,0:T(8,128)(2,1)}, u32[]{:S(2)}, u32[]{:S(2)}) collective-permute-start(bf16[96,768]{1,0:T(8,128)(2,1)} %param.20), channel_id=1, source_target_pairs={{0,8},{4,12},{8,16},{12,20},{16,24},{20,28},{24,0},{28,4},{1,9},{5... | collective-permute-start | bytes 442376 | tf_op jit(solution)/shard_map/ppermute | solution.py:447
  5.3 44.9 %collective-permute-start.3 = (bf16[96,768]{1,0:T(8,128)(2,1)}, bf16[96,768]{1,0:T(8,128)(2,1)S(1)}, u32[]{:S(2)}, u32[]{:S(2)}) collective-permute-start(bf16[96,768]{1,0:T(8,128)(2,1)} %param.20), channel_id=1, source_target_pairs={{0,4},{4,8},{8,12},{12,16},{16,20},{20,24},{24,28},{28,0},{1,5},{5... | collective-permute-start | bytes 442376 | tf_op jit(solution)/shard_map/ppermute | solution.py:447
  6.6 49.4 %collective-permute-start.1 = (bf16[512,768]{1,0:T(8,128)(2,1)}, bf16[512,768]{1,0:T(8,128)(2,1)S(1)}, u32[]{:S(2)}, u32[]{:S(2)}) collective-permute-start(bf16[512,768]{1,0:T(8,128)(2,1)} %bitcast.188), channel_id=1, source_target_pairs={{0,2},{1,3},{2,0},{3,1},{4,6},{5,7},{6,4},{7,5},{8,10},{9,11},{10,... | collective-permute-start | bytes 2359304 | tf_op jit(solution)/shard_map/ppermute | solution.py:35
  50.3 23.1 %collective-permute-start = (bf16[512,768]{1,0:T(8,128)(2,1)S(1)}, bf16[512,768]{1,0:T(8,128)(2,1)S(1)}, u32[]{:S(2)}, u32[]{:S(2)}) collective-permute-start(bf16[512,768]{1,0:T(8,128)(2,1)S(1)} %bitcast.189), channel_id=1, source_target_pairs={{0,1},{1,0},{2,3},{3,2},{4,5},{5,4},{6,7},{7,6},{8,9},{9,8},{10,11... | collective-permute-start | bytes 2359304 | tf_op jit(solution)/shard_map/ppermute | solution.py:35
  56.0 18.4 %collective-permute-start.2 = (bf16[512,768]{1,0:T(8,128)(2,1)S(1)}, bf16[512,768]{1,0:T(8,128)(2,1)S(1)}, u32[]{:S(2)}, u32[]{:S(2)}) collective-permute-start(bf16[512,768]{1,0:T(8,128)(2,1)S(1)} %collective-permute-done.1), channel_id=1, source_target_pairs={{0,1},{1,0},{2,3},{3,2},{4,5},{5,4},{6,7},{7,6},{8,9},{9,8},{10,11... | collective-permute-start | bytes 2359304 | tf_op jit(solution)/shard_map/ppermute | solution.py:35
  57.5 9.7 %collective-permute-start.5 = (bf16[96,768]{1,0:T(8,128)(2,1)}, bf16[96,768]{1,0:T(8,128)(2,1)S(1)}, u32[]{:S(2)}, u32[]{:S(2)}) collective-permute-start(bf16[96,768]{1,0:T(8,128)(2,1)} %param.20), channel_id=1, source_target_pairs={{0,12},{4,16},{8,20},{12,24},{16,28},{20,0},{24,4},{28,8},{1,13},{... | collective-permute-start | bytes 442376 | tf_op jit(solution)/shard_map/ppermute | solution.py:447
  67.3 49.1 %collective-permute-start.9 = (bf16[96,768]{1,0:T(8,128)(2,1)}, bf16[96,768]{1,0:T(8,128)(2,1)}, u32[]{:S(2)}, u32[]{:S(2)}) collective-permute-start(bf16[96,768]{1,0:T(8,128)(2,1)} %param.20), channel_id=1, source_target_pairs={{0,28},{4,0},{8,4},{12,8},{16,12},{20,16},{24,20},{28,24},{1,29},{... | collective-permute-start | bytes 442376 | tf_op jit(solution)/shard_map/ppermute | solution.py:447
  67.9 46.8 %collective-permute-start.8 = (bf16[96,768]{1,0:T(8,128)(2,1)}, bf16[96,768]{1,0:T(8,128)(2,1)}, u32[]{:S(2)}, u32[]{:S(2)}) collective-permute-start(bf16[96,768]{1,0:T(8,128)(2,1)} %param.20), channel_id=1, source_target_pairs={{0,24},{4,28},{8,0},{12,4},{16,8},{20,12},{24,16},{28,20},{1,25},{... | collective-permute-start | bytes 442376 | tf_op jit(solution)/shard_map/ppermute | solution.py:447
  108.7 15.2 %all-to-all-start = ((bf16[4,192,512]{2,1,0:T(8,128)(2,1)}), bf16[4,192,512]{2,1,0:T(8,128)(2,1)S(1)}, u32[]{:S(2)}, u32[]{:S(2)}) async-start(bf16[4,192,512]{2,1,0:T(8,128)(2,1)} %get-tuple-element.24), calls=%async_computation | async-start | bytes 1572864 | tf_op jit(solution)/shard_map/all_to_all | solution.py:498
  131.5 7.3 %all-to-all-start.3 = ((f32[8,1,128]{2,1,0:T(1,128)}), f32[8,1,128]{2,1,0:T(1,128)}, u32[]{:S(2)}, u32[]{:S(2)}) async-start(f32[8,1,128]{2,1,0:T(1,128)} %bitcast.265), calls=%async_computation.3 | async-start | bytes 8192 | tf_op jit(solution)/shard_map/all_to_all | solution.py:521
  138.7 40.5 %all-to-all-start.2 = ((bf16[8,128,768]{2,1,0:T(8,128)(2,1)}), bf16[8,128,768]{2,1,0:T(8,128)(2,1)}, u32[]{:S(2)}, u32[]{:S(2)}) async-start(bf16[8,128,768]{2,1,0:T(8,128)(2,1)} %bitcast.200), calls=%async_computation.2 | async-start | bytes 3145728 | tf_op jit(solution)/shard_map/all_to_all | solution.py:480
  179.3 41.4 %all-to-all-start.1 = ((bf16[8,128,768]{2,1,0:T(8,128)(2,1)}), bf16[8,128,768]{2,1,0:T(8,128)(2,1)}, u32[]{:S(2)}, u32[]{:S(2)}) async-start(bf16[8,128,768]{2,1,0:T(8,128)(2,1)} %bitcast.199), calls=%async_computation.1 | async-start | bytes 3145728 | tf_op jit(solution)/shard_map/all_to_all | solution.py:480
  267.2 29.0 %collective-permute-start.24 = (bf16[3,1024,768]{2,1,0:T(8,128)(2,1)}, bf16[3,1024,768]{2,1,0:T(8,128)(2,1)}, u32[]{:S(2)}, u32[]{:S(2)}) collective-permute-start(bf16[3,1024,768]{2,1,0:T(8,128)(2,1)} %constant_dynamic-slice_fusion.1), channel_id=1, source_target_pairs={{0,1},{1,0},{2,3},{3,2},{4,5},{5,4},{6,7},{7,6},{8,9},{9,8},{10,11... | collective-permute-start | bytes 14155784 | tf_op jit(solution)/shard_map/ppermute | solution.py:35
  277.1 9.7 %all-to-all-start.6 = ((f32[8,1,128]{2,1,0:T(1,128)}), f32[8,1,128]{2,1,0:T(1,128)S(1)}, u32[]{:S(2)}, u32[]{:S(2)}) async-start(f32[8,1,128]{2,1,0:T(1,128)} %bitcast.45), calls=%async_computation.6 | async-start | bytes 8192 | tf_op jit(solution)/shard_map/all_to_all | solution.py:485
  286.8 40.9 %all-to-all-start.4 = ((bf16[8,128,768]{2,1,0:T(8,128)(2,1)}), bf16[8,128,768]{2,1,0:T(8,128)(2,1)}, u32[]{:S(2)}, u32[]{:S(2)}) async-start(bf16[8,128,768]{2,1,0:T(8,128)(2,1)} %bitcast.198), calls=%async_computation.4 | async-start | bytes 3145728 | tf_op jit(solution)/shard_map/all_to_all | solution.py:485
  303.2 160.8 %collective-permute-start.25 = (bf16[3,1024,768]{2,1,0:T(8,128)(2,1)}, bf16[3,1024,768]{2,1,0:T(8,128)(2,1)}, u32[]{:S(2)}, u32[]{:S(2)}) collective-permute-start(bf16[3,1024,768]{2,1,0:T(8,128)(2,1)} %add_convert_fusion.1), channel_id=1, source_target_pairs={{0,2},{1,3},{2,0},{3,1},{4,6},{5,7},{6,4},{7,5},{8,10},{9,11},{10,... | collective-permute-start | bytes 14155784 | tf_op jit(solution)/shard_map/ppermute | solution.py:35
  348.8 73.4 %all-to-all-start.7 = ((bf16[4,192,512]{2,1,0:T(8,128)(2,1)}), bf16[4,192,512]{2,1,0:T(8,128)(2,1)S(1)}, u32[]{:S(2)}, u32[]{:S(2)}) async-start(bf16[4,192,512]{2,1,0:T(8,128)(2,1)} %bitcast.54), calls=%async_computation.7 | async-start | bytes 1572864 | tf_op jit(solution)/shard_map/all_to_all | solution.py:618
  353.9 65.8 %collective-permute-start.18 = (bf16[768,192]{0,1:T(8,128)(2,1)S(1)}, bf16[768,192]{0,1:T(8,128)(2,1)S(1)}, u32[]{:S(2)}, u32[]{:S(2)}) collective-permute-start(bf16[768,192]{0,1:T(8,128)(2,1)S(1)} %fusion.39), channel_id=1, source_target_pairs={{0,2},{1,3},{2,0},{3,1},{4,6},{5,7},{6,4},{7,5},{8,10},{9,11},{10,... | collective-permute-start | bytes 884744 | tf_op jit(solution)/shard_map/ppermute | solution.py:35
  422.2 37.3 %all-to-all-start.10 = ((f32[8,1,1968]{2,1,0:T(1,128)}), f32[8,1,1968]{2,1,0:T(1,128)S(1)}, u32[]{:S(2)}, u32[]{:S(2)}) async-start(f32[8,1,1968]{2,1,0:T(1,128)} %copy.126), calls=%async_computation.10 | async-start | bytes 131072 | tf_op jit(solution)/shard_map/all_to_all | solution.py:634
  459.4 15.3 %all-to-all-start.9 = ((bf16[8,96,192]{1,2,0:T(8,128)(2,1)}), bf16[8,96,192]{1,2,0:T(8,128)(2,1)S(1)}, u32[]{:S(2)}, u32[]{:S(2)}) async-start(bf16[8,96,192]{1,2,0:T(8,128)(2,1)} %copy.116), calls=%async_computation.9 | async-start | bytes 786432 | tf_op jit(solution)/shard_map/all_to_all | solution.py:650
  471.0 98.6 %collective-permute-start.26 = (bf16[3,1024,768]{2,1,0:T(8,128)(2,1)}, bf16[3,1024,768]{2,1,0:T(8,128)(2,1)}, u32[]{:S(2)}, u32[]{:S(2)}) collective-permute-start(bf16[3,1024,768]{2,1,0:T(8,128)(2,1)} %add_convert_fusion), channel_id=1, source_target_pairs={{0,1},{1,0},{2,3},{3,2},{4,5},{5,4},{6,7},{7,6},{8,9},{9,8},{10,11... | collective-permute-start | bytes 14155784 | tf_op jit(solution)/shard_map/ppermute | solution.py:35
  475.6 27.4 %all-to-all-start.8 = ((bf16[8,96,576]{2,1,0:T(8,128)(2,1)}), bf16[8,96,576]{2,1,0:T(8,128)(2,1)S(1)}, u32[]{:S(2)}, u32[]{:S(2)}) async-start(bf16[8,96,576]{2,1,0:T(8,128)(2,1)} %bitcast.63), calls=%async_computation.8 | async-start | bytes 1966080 | tf_op jit(solution)/shard_map/all_to_all | solution.py:650
  493.9 15.8 %collective-permute-start.11 = (bf16[512,768]{1,0:T(8,128)(2,1)S(1)}, bf16[512,768]{1,0:T(8,128)(2,1)}, u32[]{:S(2)}, u32[]{:S(2)}) collective-permute-start(bf16[512,768]{1,0:T(8,128)(2,1)S(1)} %get-tuple-element.128), channel_id=1, source_target_pairs={{0,1},{1,0},{2,3},{3,2},{4,5},{5,4},{6,7},{7,6},{8,9},{9,8},{10,11... | collective-permute-start | bytes 2359304 | tf_op jit(solution)/shard_map/ppermute | solution.py:35
  502.9 41.1 %collective-permute-start.10 = (bf16[512,768]{1,0:T(8,128)(2,1)}, bf16[512,768]{1,0:T(8,128)(2,1)}, u32[]{:S(2)}, u32[]{:S(2)}) collective-permute-start(bf16[512,768]{1,0:T(8,128)(2,1)} %get-tuple-element.127), channel_id=1, source_target_pairs={{0,1},{1,0},{2,3},{3,2},{4,5},{5,4},{6,7},{7,6},{8,9},{9,8},{10,11... | collective-permute-start | bytes 2359304 | tf_op jit(solution)/shard_map/ppermute | solution.py:35
  502.9 60.1 %all-to-all-start.5 = ((bf16[8,128,768]{2,1,0:T(8,128)(2,1)}), bf16[8,128,768]{2,1,0:T(8,128)(2,1)}, u32[]{:S(2)}, u32[]{:S(2)}) async-start(bf16[8,128,768]{2,1,0:T(8,128)(2,1)} %bitcast.197), calls=%async_computation.5 | async-start | bytes 3145728 | tf_op jit(solution)/shard_map/all_to_all | solution.py:485
  512.2 31.8 %collective-permute-start.12 = (bf16[512,768]{1,0:T(8,128)(2,1)}, bf16[512,768]{1,0:T(8,128)(2,1)}, u32[]{:S(2)}, u32[]{:S(2)}) collective-permute-start(bf16[512,768]{1,0:T(8,128)(2,1)} %fusion.12), channel_id=1, source_target_pairs={{0,2},{1,3},{2,0},{3,1},{4,6},{5,7},{6,4},{7,5},{8,10},{9,11},{10,... | collective-permute-start | bytes 2359304 | tf_op jit(solution)/shard_map/ppermute | solution.py:35
  513.2 19.1 %collective-permute-start.20 = (f32[96,192]{1,0:T(8,128)S(1)}, f32[96,192]{1,0:T(8,128)S(1)}, u32[]{:S(2)}, u32[]{:S(2)}) collective-permute-start(f32[96,192]{1,0:T(8,128)S(1)} %copy.118), channel_id=1, source_target_pairs={{0,2},{1,3},{2,0},{3,1},{4,6},{5,7},{6,4},{7,5},{8,10},{9,11},{10,... | collective-permute-start | bytes 221192 | tf_op jit(solution)/shard_map/ppermute | solution.py:35
  515.9 20.1 %collective-permute-start.19 = (f32[96,192]{1,0:T(8,128)S(1)}, f32[96,192]{1,0:T(8,128)S(1)}, u32[]{:S(2)}, u32[]{:S(2)}) collective-permute-start(f32[96,192]{1,0:T(8,128)S(1)} %copy.118), channel_id=1, source_target_pairs={{0,1},{1,0},{2,3},{3,2},{4,5},{5,4},{6,7},{7,6},{8,9},{9,8},{10,11... | collective-permute-start | bytes 221192 | tf_op jit(solution)/shard_map/ppermute | solution.py:35
  543.4 7.7 %collective-permute-start.14 = (f32[96,576]{1,0:T(8,128)S(1)}, f32[96,576]{1,0:T(8,128)S(1)}, u32[]{:S(2)}, u32[]{:S(2)}) collective-permute-start(f32[96,576]{1,0:T(8,128)S(1)} %convert_reduce_fusion), channel_id=1, source_target_pairs={{0,2},{1,3},{2,0},{3,1},{4,6},{5,7},{6,4},{7,5},{8,10},{9,11},{10,... | collective-permute-start | bytes 663560 | tf_op jit(solution)/shard_map/ppermute | solution.py:35
  543.7 11.5 %collective-permute-start.13 = (f32[96,576]{1,0:T(8,128)S(1)}, f32[96,576]{1,0:T(8,128)S(1)}, u32[]{:S(2)}, u32[]{:S(2)}) collective-permute-start(f32[96,576]{1,0:T(8,128)S(1)} %convert_reduce_fusion), channel_id=1, source_target_pairs={{0,1},{1,0},{2,3},{3,2},{4,5},{5,4},{6,7},{7,6},{8,9},{9,8},{10,11... | collective-permute-start | bytes 663560 | tf_op jit(solution)/shard_map/ppermute | solution.py:35
  (68 other events, 489.9 us)

commit v2 on v1

--- a/solution.py
+++ b/solution.py
@@ -61,10 +61,132 @@
     return held[0]
 
 
-def qkv_kernel(me_ref, h_ref, gain_ref, w_ref, cos_ref, sin_ref, attn_ref, out_ref, wt_ref):
+MESH = pl.DeviceIdType.MESH
+SMALL = 32
+
+
+def greet(peers):
+    barrier = pltpu.get_barrier_semaphore()
+    for peer in peers:
+        pl.semaphore_signal(barrier, inc=1, device_id=peer, device_id_type=MESH)
+    pl.semaphore_wait(barrier, len(peers))
+
+
+def start_kernel(
+    n_seq, n_dp, h_ref, w_ref, again_ref, mgain_ref, vec_ref, mix_ref, router_ref,
+    all_ref, slice_ref, small_ref,
+    small_buf, h_send, h_recv, w_send, w_recv, s_send, s_recv,
+):
+    me, dp = lax.axis_index("seq"), lax.axis_index("dp")
+    shard, width3 = slice_ref.shape[1], slice_ref.shape[2]
+    width = width3 // 3
+    seq_bits = list(bits_high_first(n_seq))
+    greet(
+        [{"seq": me ^ bit} for bit in seq_bits]
+        + [{"dp": lax.rem(dp + k, n_dp)} for k in range(1, n_dp)]
+    )
+
+    def put(place, bit, index):
+        return pltpu.make_async_remote_copy(
+            src_ref=h_ref if place == 0 else all_ref.at[me ^ place],
+            dst_ref=all_ref.at[me ^ place],
+            send_sem=h_send.at[index],
+            recv_sem=h_recv.at[index],
+            device_id={"seq": me ^ bit},
+            device_id_type=MESH,
+        )
+
+    plan, arrival = [], {}
+    order = [(0, bit) for bit in seq_bits]
+    while order:
+        place, bit = order.pop(0)
+        copy = put(place, bit, len(plan))
+        arrival[place ^ bit] = copy
+        plan.append((place, copy))
+        order += [(place ^ bit, low) for low in seq_bits if low < bit]
+    for place, copy in plan:
+        if place == 0:
+            copy.start()
+
+    for j in range(n_seq):
+
+        @pl.when(me == j)
+        def _():
+            for c in range(3):
+                left = c * width * n_seq + j * width
+                slice_ref[dp, :, c * width : (c + 1) * width] = w_ref[:, left : left + width]
+
+    small_buf[dp] = jnp.zeros(small_buf.shape[1:], bf16)
+    small_buf[dp, 0:1, :] = again_ref[...]
+    small_buf[dp, 1:2, :] = mgain_ref[...]
+    small_buf[dp, 2:4, :] = vec_ref[...]
+    small_buf[dp, 4:6, :] = mix_ref[0]
+    small_buf[dp, 6:8, :] = mix_ref[1]
+    small_buf[dp, 8 : 8 + H, :] = router_ref[...].astype(f32).T.astype(bf16)
+    copies = []
+    for k in range(1, n_dp):
+        target = {"dp": lax.rem(dp + k, n_dp)}
+        for ref, send, recv in ((slice_ref, w_send, w_recv), (small_buf, s_send, s_recv)):
+            copy = pltpu.make_async_remote_copy(
+                src_ref=ref.at[dp],
+                dst_ref=ref.at[dp],
+                send_sem=send.at[k],
+                recv_sem=recv.at[k],
+                device_id=target,
+                device_id_type=MESH,
+            )
+            copy.start()
+            copies.append(copy)
+    all_ref[me] = h_ref[...]
+    for place, copy in plan:
+        if place != 0:
+            arrival[place].wait_recv()
+            copy.start()
+    for place in arrival:
+        if not any(p == place for p, _ in plan):
+            arrival[place].wait_recv()
+    for _, copy in plan:
+        copy.wait_send()
+    for copy in copies:
+        copy.wait()
+    small_ref[...] = jnp.concatenate(
+        [small_buf[i].astype(f32) for i in range(n_dp)], axis=1
+    )
+
+
+def start_call(n_seq, n_dp, hidden, w_qkv, attn_gain, moe_gain, vec, mix, router):
+    tok, shard = hidden.shape[0], w_qkv.shape[0]
+    width3 = w_qkv.shape[1] // n_seq
+    vmem = pl.BlockSpec(memory_space=pltpu.VMEM)
+    hops = n_seq - 1
+    dma = pltpu.SemaphoreType.DMA
+    return pl.pallas_call(
+        functools.partial(start_kernel, n_seq, n_dp),
+        out_shape=(
+            jax.ShapeDtypeStruct((n_seq, tok, D), bf16),
+            jax.ShapeDtypeStruct((n_dp, shard, width3), bf16),
+            jax.ShapeDtypeStruct((SMALL, D), f32),
+        ),
+        in_specs=[vmem] * 7,
+        out_specs=[vmem] * 3,
+        scratch_shapes=[
+            pltpu.VMEM((n_dp, SMALL, shard), bf16),
+            dma((hops,)),
+            dma((hops,)),
+            dma((n_dp,)),
+            dma((n_dp,)),
+            dma((n_dp,)),
+            dma((n_dp,)),
+        ],
+        compiler_params=pltpu.CompilerParams(collective_id=0, has_side_effects=True),
+        name="start",
+    )(hidden, w_qkv, attn_gain[None], moe_gain[None], vec, mix, router)
+
+
+def qkv_kernel(h_ref, gain_ref, w_ref, cos_ref, sin_ref, attn_ref, out_ref, wt_ref):
     @pl.when((pl.program_id(0) == 0) & (pl.program_id(1) == 0))
     def _():
-        wt_ref[...] = w_ref[...].T
+        wt_ref[...] = w_ref[...].reshape(D, w_ref.shape[2]).T
 
     x = h_ref[0].astype(f32)
     mean_square = jnp.mean(x * x, axis=-1, keepdims=True)
@@ -82,34 +204,32 @@
     out_ref[2 * rows // 3 :] = y[2 * rows // 3 :].astype(bf16)
 
 
-def qkv_call(me, blocks, gain, w, cos_t, sin_t):
+def qkv_call(blocks, gain, w, cos_t, sin_t):
     parts, tok, _ = blocks.shape
-    seq_len, width = parts * tok, w.shape[1]
+    seq_len, width = parts * tok, w.shape[2]
     per = tok // BLK
     return pl.pallas_call(
         qkv_kernel,
         out_shape=(
             jax.ShapeDtypeStruct((seq_len, D), bf16),
             jax.ShapeDtypeStruct((width, seq_len), bf16),
+            jax.ShapeDtypeStruct((width, D), bf16),
         ),
-        grid_spec=pltpu.PrefetchScalarGridSpec(
-            num_scalar_prefetch=1,
-            grid=(parts, per),
-            in_specs=[
-                pl.BlockSpec((1, BLK, D), lambda b, t, me_ref: (b ^ me_ref[0], t, 0)),
-                pl.BlockSpec((1, D), lambda b, t, me_ref: (0, 0)),
-                pl.BlockSpec((D, width), lambda b, t, me_ref: (0, 0)),
-                pl.BlockSpec((HD // 2, BLK), lambda b, t, me_ref: (0, b * per + t)),
-                pl.BlockSpec((HD // 2, BLK), lambda b, t, me_ref: (0, b * per + t)),
-            ],
-            out_specs=[
-                pl.BlockSpec((BLK, D), lambda b, t, me_ref: (b * per + t, 0)),
-                pl.BlockSpec((width, BLK), lambda b, t, me_ref: (0, b * per + t)),
-            ],
-            scratch_shapes=[pltpu.VMEM((width, D), bf16)],
-        ),
+        grid=(parts, per),
+        in_specs=[
+            pl.BlockSpec((1, BLK, D), lambda b, t: (b, t, 0)),
+            pl.BlockSpec((1, D), lambda b, t: (0, 0)),
+            pl.BlockSpec(w.shape, lambda b, t: (0, 0, 0)),
+            pl.BlockSpec((HD // 2, BLK), lambda b, t: (0, b * per + t)),
+            pl.BlockSpec((HD // 2, BLK), lambda b, t: (0, b * per + t)),
+        ],
+        out_specs=[
+            pl.BlockSpec((BLK, D), lambda b, t: (b * per + t, 0)),
+            pl.BlockSpec((width, BLK), lambda b, t: (0, b * per + t)),
+            pl.BlockSpec((width, D), lambda b, t: (0, 0)),
+        ],
         name="qkv",
-    )(me, blocks, gain, w, cos_t, sin_t)
+    )(blocks, gain, w, cos_t, sin_t)
 
 
 def allowed_block(key_block, query_block, start_row):
@@ -376,6 +496,132 @@
     )(x, g, gate, weights)
 
 
+def tail_kernel(
+    n_seq, n_dp, g_ref, a_ref, wt_ref, h_ref, resid_ref, gain_ref, wq_ref,
+    din_ref, dw_ref, dgain_ref,
+    core_out, core_in, x_out, x_in, part_ref, w_out_buf, w_in, row_buf, row_in,
+    c_send, c_recv, x_send, x_recv, w_send, w_recv, r_send, r_recv,
+):
+    me, dp = lax.axis_index("seq"), lax.axis_index("dp")
+    tok = h_ref.shape[0]
+    shard, width3 = w_in.shape[1], w_in.shape[2]
+    width = width3 // 3
+    bits = list(bits_high_first(n_seq))[::-1]
+    greet(
+        [{"seq": me ^ place} for place in range(1, n_seq)]
+        + [{"dp": lax.rem(dp + k, n_dp)} for k in range(1, n_dp)]
+    )
+
+    def term(place):
+        columns = pl.ds(pl.multiple_of((me ^ place) * tok, tok), tok)
+        return mm(g_ref[:, columns], wt_ref[...], TN)
+
+    def send(src, dst, sems, index, target):
+        copy = pltpu.make_async_remote_copy(
+            src_ref=src, dst_ref=dst, send_sem=sems[0].at[index], recv_sem=sems[1].at[index],
+            device_id=target, device_id_type=MESH,
+        )
+        copy.start()
+        return copy
+
+    pairs = n_seq // 2
+    core_copies = []
+    for i in range(pairs):
+        core_out[i] = term(2 * i + 1).astype(bf16)
+        core_copies.append(
+            send(core_out.at[i], core_in.at[i], (c_send, c_recv), i, {"seq": me ^ 1})
+        )
+    turned = mm(g_ref[...], a_ref[...], NN)
+    w_out_buf[...] = turned.T.astype(bf16).reshape(n_dp, shard, width3)
+    w_in[dp] = w_out_buf[dp]
+    w_copies = [
+        send(
+            w_out_buf.at[lax.rem(dp + k, n_dp)], w_in.at[dp], (w_send, w_recv), k,
+            {"dp": lax.rem(dp + k, n_dp)},
+        )
+        for k in range(1, n_dp)
+    ]
+    x_copies = []
+    for i in range(pairs - 1, -1, -1):
+        part = term(2 * i)
+        core_copies[i].wait_recv()
+        part = part + core_in[i].astype(f32)
+        if i == 0:
+            part_ref[...] = part
+        else:
+            x_out[i - 1] = part.astype(bf16)
+            x_copies.append(
+                send(x_out.at[i - 1], x_in.at[i - 1], (x_send, x_recv), i - 1,
+                     {"seq": me ^ (2 * i)})
+            )
+    for copy in w_copies:
+        copy.wait_recv()
+    rows = jnp.sum(w_in[...].astype(f32), axis=0)
+    row_buf[...] = rows.astype(bf16)
+    row_in[me] = row_buf[...]
+    row_copies = [
+        send(row_buf, row_in.at[me], (r_send, r_recv), place, {"seq": me ^ place})
+        for place in range(1, n_seq)
+    ]
+    for copy in x_copies:
+        copy.wait_recv()
+    grad = part_ref[...]
+    for i in range(pairs - 1):
+        grad = grad + x_in[i].astype(f32)
+    values = h_ref[...].astype(f32)
+    back, _ = norm_back(values, gain_ref[...], grad)
+    din_ref[...] = resid_ref[...] + back
+    for copy in row_copies:
+        copy.wait_recv()
+    for j in range(n_seq):
+        block = row_in[j].astype(f32)
+        for c in range(3):
+            left = c * width * n_seq + j * width
+            dw_ref[:, left : left + width] = block[:, c * width : (c + 1) * width]
+    dgain_ref[...] = jnp.sum(dw_ref[...] * wq_ref[...].astype(f32), axis=1, keepdims=True)
+    for copy in core_copies + w_copies + x_copies + row_copies:
+        copy.wait_send()
+
+
+def tail_call(n_seq, n_dp, grad_qkv, attn_in, w_turned, hidden, grad_resid, gain, w_qkv):
+    tok, shard = hidden.shape[0], w_qkv.shape[0]
+    width3 = grad_qkv.shape[0]
+    pairs = n_seq // 2
+    vmem = pl.BlockSpec(memory_space=pltpu.VMEM)
+    dma = pltpu.SemaphoreType.DMA
+    return pl.pallas_call(
+        functools.partial(tail_kernel, n_seq, n_dp),
+        out_shape=(
+            jax.ShapeDtypeStruct((tok, D), f32),
+            jax.ShapeDtypeStruct(w_qkv.shape, f32),
+            jax.ShapeDtypeStruct((shard, 1), f32),
+        ),
+        in_specs=[vmem] * 7,
+        out_specs=[vmem] * 3,
+        scratch_shapes=[
+            pltpu.VMEM((pairs, tok, D), bf16),
+            pltpu.VMEM((pairs, tok, D), bf16),
+            pltpu.VMEM((pairs - 1, tok, D), bf16),
+            pltpu.VMEM((pairs - 1, tok, D), bf16),
+            pltpu.VMEM((tok, D), f32),
+            pltpu.VMEM((n_dp, shard, width3), bf16),
+            pltpu.VMEM((n_dp, shard, width3), bf16),
+            pltpu.VMEM((shard, width3), bf16),
+            pltpu.VMEM((n_seq, shard, width3), bf16),
+            dma((pairs,)),
+            dma((pairs,)),
+            dma((pairs,)),
+            dma((pairs,)),
+            dma((n_dp,)),
+            dma((n_dp,)),
+            dma((n_seq,)),
+            dma((n_seq,)),
+        ],
+        compiler_params=pltpu.CompilerParams(collective_id=1, has_side_effects=True),
+        name="tail",
+    )(grad_qkv, attn_in, w_turned, hidden, grad_resid, gain, w_qkv)
+
+
 def rope_tables(seq_len):
     freq_index = jnp.arange(HD // 2, dtype=f32)
     inv_freq = jnp.exp(freq_index * (-2.0 * math.log(10000.0) / HD))
@@ -409,7 +655,6 @@
     n_seq, n_dp = lax.axis_size("seq"), lax.axis_size("dp")
     owners = n_dp // E
     me = lax.axis_index("seq")
-    me_arr = me.astype(jnp.int32).reshape(1)
     tok = hidden_in.shape[1]
     seq_len = tok * n_seq
     shard = w_qkv.shape[0]
@@ -423,23 +668,9 @@
     route_rows = routes[0]
     carry_f = w_carry.astype(f32)
 
-    blocks = jnp.stack(gather_relative(hidden, "seq"))
-    w_mine = lax.dynamic_slice_in_dim(
-        w_qkv.reshape(shard, 3, n_seq, width), me, 1, axis=2
-    ).reshape(shard, 3 * width)
-    small = jnp.concatenate(
-        [
-            attn_gain[:, None],
-            moe_gain[:, None],
-            const_vec.T,
-            const_mix.reshape(4, shard).T,
-            w_router,
-        ],
-        axis=1,
-    )
-    first = lax.all_gather(jnp.concatenate([w_mine, small], axis=1), "dp", axis=0, tiled=True)
-    w_slice = first[:, : 3 * width]
-    small_t = first[:, 3 * width :].astype(f32).T
+    blocks, w_slice, small_t = start_call(
+        n_seq, n_dp, hidden, w_qkv, attn_gain, moe_gain, const_vec, const_mix, w_router
+    )
     gain_one, gain_two = small_t[0:1], small_t[1:2]
     vec_f, mix_f, router_t = small_t[2:4], small_t[4:8], small_t[8:20]
     dp_me = lax.axis_index("dp")
@@ -493,7 +724,7 @@
     start = jnp.sum(jnp.where(seg_row[None, :] == doc_ids[:, None], doc_start[:, None], 0), axis=0)
     start_row = start.astype(jnp.int32)[None, :]
     lows = start[::BLK].astype(jnp.int32) // BLK
-    attn_in, qkv = qkv_call(me_arr, blocks, gain_one, w_slice, cos_t, sin_t)
+    attn_in, qkv, w_turned = qkv_call(blocks, gain_one, w_slice, cos_t, sin_t)
     attended, attended_exact, logs = attn_call(lows, qkv, start_row, tok)
     heads_t = lax.all_to_all(attended, "seq", split_axis=0, concat_axis=0, tiled=True).reshape(
         D, tok
@@ -659,22 +890,10 @@
     grad_qkv = attn_back_call(
         lows, qkv, grad_out, attended_exact, logs, start_row, cos_t, sin_t
     )
-    grad_w = lax.dot_general(
-        attn_in, grad_qkv, (((0,), (1,)), ((), ())), preferred_element_type=f32
-    )
-    rows_w = collect_columns(reduce_rows(grad_w.astype(bf16)))
-    d_qkv = (
-        rows_w.reshape(n_seq, shard, 3, width).transpose(1, 2, 0, 3).reshape(shard, 3 * D)
-    )
-    d_attn_gain = jnp.sum(d_qkv * w_qkv.astype(f32), axis=1) / attn_gain.astype(f32)
-
-    grad_in = lax.dot_general(
-        grad_qkv, w_slice, (((0,), (1,)), ((), ())), preferred_element_type=f32
-    ).astype(bf16)
-    grad_in = grad_in.reshape(n_seq, tok, D)[jnp.arange(n_seq) ^ me]
-    grad_attn_in = sum_relative([grad_in[r] for r in range(n_seq)], "seq")
-    grad_first, _ = norm_back(tokens_f, gain_one, grad_attn_in)
-    d_input = grad_resid + grad_first
+    d_input, d_qkv, gain_sum = tail_call(
+        n_seq, n_dp, grad_qkv, attn_in, w_turned, hidden, grad_resid, gain_one, w_qkv
+    )
+    d_attn_gain = gain_sum[:, 0] / attn_gain.astype(f32)
     return (
         block_out[None],
         d_input[None],

time: 598 us -> 560 us (0.936)
  Pallas kernels: 99.8 us -> 182 us
  local copies, waits for them, and re-layouts: 68.6 us -> 34.6 us
  starting transfers between devices: 98.5 us -> 73.9 us
  waiting for transfers between devices: 184 us -> 162 us
  other arithmetic: 64.4 us -> 51 us
  matrix products: 45 us -> 32 us
  blocking collectives: 24.8 us -> 13.8 us
    pallas_call x0 -> x2, Pallas kernels: none -> 82.2 us  [the longest x1 43.3 us: tail_call(): pl.pallas_call(functools.partial(tail_kernel, n_seq, n_dp), out_shape=(ja...]
    all_gather x1 -> x0, blocking collectives: 24.8 us -> none  [per_device(): lax.all_gather(jnp.concatenate([w_mine, small], axis=1), 'dp', axis=0, ti...]
    ppermute x20 -> x11, waiting for transfers between devices: 82.5 us -> 60 us  [swap(): return lax.ppermute(value, axis, [(i, i ^ bit) for i in range(size)])]
    all_to_all x0 -> x1, blocking collectives: none -> 13.8 us  [reduce_rows(): value = lax.all_to_all(value, 'dp', split_axis=0, concat_axis=0, tiled=True)]
    ppermute x20 -> x11, starting transfers between devices: 23.2 us -> 12 us  [swap(): return lax.ppermute(value, axis, [(i, i ^ bit) for i in range(size)])]
    dot_general x2 -> x0, matrix products: 10.7 us -> none  [the longest x1 6.1 us: per_device(): lax.dot_general(grad_qkv, w_slice, (((0,), (1,)), ((), ())), preferred_el...]
    all_to_all x2 -> x0, starting transfers between devices: 9.98 us -> none  [reduce_rows(): value = lax.all_to_all(value, 'dp', split_axis=0, concat_axis=0, tiled=True)]
    dynamic_update_slice x8, local copies, waits for them, and re-layouts: 8.45 us -> 0.13 us  [per_device(): lax.dynamic_update_index_in_dim(out_weight, part, lax.rem(dp_me + n_dp -...]
  transfers between devices with their start and end apart: 38 -> 27, of which waited for: 10 -> 12; matrix products, arithmetic and copies ran while one was open for 25% -> 16% of each run, Pallas kernels for 10% -> 25%
where the time goes in v2:
time: 560 us; the launch traced here: 551 us
  Pallas kernels  182 us (32%)
  waiting for transfers between devices  162 us (29%)
  starting transfers between devices  73.9 us (13%)
  other arithmetic  51 us (9%)
  local copies, waits for them, and re-layouts  34.6 us (6%)
  matrix products  32 us (6%)
  blocking collectives  13.8 us (2%)
    all_to_all x2, waiting for transfers between devices, dispatch(): lax.all_to_all(jnp.repeat(grouped, owners, axis=0), 'dp', split_axis=0, c...  65.4 us
    ppermute x11, waiting for transfers between devices, swap(): return lax.ppermute(value, axis, [(i, i ^ bit) for i in range(size)])  60 us
    pallas_call x1, Pallas kernels, tail_call(): pl.pallas_call(functools.partial(tail_kernel, n_seq, n_dp), out_shape=(ja...  43.3 us
    pallas_call x1, Pallas kernels, expert_call(): pl.pallas_call(expert_kernel, out_shape=(jax.ShapeDtypeStruct((rows, D),...  41.7 us
    pallas_call x1, Pallas kernels, start_call(): pl.pallas_call(functools.partial(start_kernel, n_seq, n_dp), out_shape=(j...  38.9 us
    pallas_call x1, Pallas kernels, attn_back_call(): pl.pallas_call(attn_back_kernel, out_shape=jax.ShapeDtypeStruct((width3,...  25.6 us
    all_to_all x3, waiting for transfers between devices, back_to_source(): return lax.all_to_all(values, 'dp', split_axis=0, concat_axis=0, tiled=True)  25.5 us
    pallas_call x1, Pallas kernels, attn_call(): pl.pallas_call(attn_kernel, out_shape=(jax.ShapeDtypeStruct((seq_len // t...  23.8 us
  transfers between devices with their start and end apart: 27, of which 12 were waited for; matrix products, arithmetic and copies ran while one was open for 16% of the time, Pallas kernels for 25%

profile of v2, /device:TPU:13, one launch (start us, length us, event | category | flops | bytes accessed | tf_op | source)
XLA Modules:
  0.0 551.1 jit_solution(2007968090994753828)
XLA Ops:
  11.1 38.9 %start.1 = (bf16[4,512,768]{2,1,0:T(8,128)(2,1)}, bf16[8,96,576]{2,1,0:T(8,128)(2,1)}, f32[32,768]{1,0:T(8,128)}) custom-call(bf16[512,768]{1,0:T(8,128)(2,1)} %bitcast.147, bf16[96,2304]{1,0:T(8,128)(2,1)} %wq_ref.1, bf16[1,96]{1,0:T(2,128)(2,1)} %bitcast.217, bf16[1,96]{1,0:T(2,128)(2,1)} %bitcast.216, bf16[2,96]{1,0:T(2,128)(2,1)} %vec_ref.1, ...), custom_call_target="tpu_custom_call" | custom-call | tf_op jit(solution)/shard_map/start/pallas_call | solution.py:163
  53.2 8.8 %qkv.1 = (bf16[2048,768]{1,0:T(8,128)(2,1)}, bf16[576,2048]{1,0:T(8,128)(2,1)}, bf16[576,768]{1,0:T(8,128)(2,1)}) custom-call(bf16[4,512,768]{2,1,0:T(8,128)(2,1)} %get-tuple-element.30.h_ref, f32[1,768]{1,0:T(1,128)} %get-tuple-element.142.gain_ref, bf16[8,96,576]{2,1,0:T(8,128)(2,1)} %get-tuple-element.32.w_ref, f32[32,2048]{1,0:T(8,128)} %get-tuple-element.144.cos_ref, ...), custom_call_target="tpu_custom_call" | custom-call | tf_op jit(solution)/shard_map/qkv/pallas_call | solution.py:211
  62.0 23.8 %attend.1 = (bf16[4,192,512]{2,1,0:T(8,128)(2,1)}, f32[192,2048]{1,0:T(8,128)}, f32[3,2048]{1,0:T(4,128)}) custom-call(s32[8]{0:T(128)} %and_select_fusion.lo_ref, bf16[576,2048]{1,0:T(8,128)(2,1)} %get-tuple-element.33.qkv_ref, s32[1,2048]{1,0:T(1,128)} %bitcast.166), custom_call_target="tpu_custom_call" | custom-call | tf_op jit(solution)/shard_map/attend/pallas_call | solution.py:293
  85.7 4.9 all-to-all-start
  91.5 5.3 collective-permute-done.5
  97.5 3.9 all-to-all-done
  106.8 7.5 %all-to-all-start.3 = ((f32[8,1,128]{2,1,0:T(1,128)}), f32[8,1,128]{2,1,0:T(1,128)S(1)}, u32[]{:S(2)}, u32[]{:S(2)}) async-start(f32[8,1,128]{2,1,0:T(1,128)} %bitcast.30), calls=%async_computation.3 | async-start | bytes 8192 | tf_op jit(solution)/shard_map/all_to_all | solution.py:752
  117.5 6.3 %all-to-all-start.2 = ((bf16[8,128,768]{2,1,0:T(8,128)(2,1)}), bf16[8,128,768]{2,1,0:T(8,128)(2,1)}, u32[]{:S(2)}, u32[]{:S(2)}) async-start(bf16[8,128,768]{2,1,0:T(8,128)(2,1)} %bitcast.153), calls=%async_computation.2 | async-start | bytes 3145728 | tf_op jit(solution)/shard_map/all_to_all | solution.py:711
  126.1 32.1 %all-to-all-done.2 = bf16[8,128,768]{2,1,0:T(8,128)(2,1)} async-done(((bf16[8,128,768]{2,1,0:T(8,128)(2,1)}), bf16[8,128,768]{2,1,0:T(8,128)(2,1)}, u32[]{:S(2)}, u32[]{:S(2)}) %all-to-all-start.2) | async-done | bytes 1572896 | tf_op jit(solution)/shard_map/all_to_all | solution.py:711
  158.1 6.7 %all-to-all-start.1 = ((bf16[8,128,768]{2,1,0:T(8,128)(2,1)}), bf16[8,128,768]{2,1,0:T(8,128)(2,1)}, u32[]{:S(2)}, u32[]{:S(2)}) async-start(bf16[8,128,768]{2,1,0:T(8,128)(2,1)} %bitcast.152), calls=%async_computation.1 | async-start | bytes 3145728 | tf_op jit(solution)/shard_map/all_to_all | solution.py:711
  165.8 33.4 %all-to-all-done.1 = bf16[8,128,768]{2,1,0:T(8,128)(2,1)} async-done(((bf16[8,128,768]{2,1,0:T(8,128)(2,1)}), bf16[8,128,768]{2,1,0:T(8,128)(2,1)}, u32[]{:S(2)}, u32[]{:S(2)}) %all-to-all-start.1) | async-done | bytes 1572896 | tf_op jit(solution)/shard_map/all_to_all | solution.py:711
  199.2 41.7 %experts.1 = (bf16[1024,768]{1,0:T(8,128)(2,1)}, bf16[1024,768]{1,0:T(8,128)(2,1)}, f32[1024,1]{1,0:T(8,128)}, bf16[3,2048,768]{2,1,0:T(8,128)(2,1)}) custom-call(bf16[1024,768]{1,0:T(8,128)(2,1)} %bitcast.26.x_ref, bf16[1024,768]{1,0:T(8,128)(2,1)} %bitcast.29.g_ref, f32[1024,1]{1,0:T(8,128)} %copy.65.gate_ref, bf16[3,2048,768]{2,1,0:T(8,128)(2,1)} %w_ref.3), custom_call_target="tpu_custom_call" | custom-call | tf_op jit(solution)/shard_map/experts/pallas_call | solution.py:479
  241.0 4.8 constant_dynamic-slice_fusion
  251.7 6.4 %all-to-all-start.6 = ((f32[8,1,128]{2,1,0:T(1,128)}), f32[8,1,128]{2,1,0:T(1,128)S(1)}, u32[]{:S(2)}, u32[]{:S(2)}) async-start(f32[8,1,128]{2,1,0:T(1,128)} %bitcast.36), calls=%async_computation.6 | async-start | bytes 8192 | tf_op jit(solution)/shard_map/all_to_all | solution.py:716
  261.3 6.5 %all-to-all-start.4 = ((bf16[8,128,768]{2,1,0:T(8,128)(2,1)}), bf16[8,128,768]{2,1,0:T(8,128)(2,1)}, u32[]{:S(2)}, u32[]{:S(2)}) async-start(bf16[8,128,768]{2,1,0:T(8,128)(2,1)} %bitcast.150), calls=%async_computation.4 | async-start | bytes 3145728 | tf_op jit(solution)/shard_map/all_to_all | solution.py:716
  267.9 7.0 %add_convert_fusion.1 = bf16[3,1024,768]{2,1,0:T(8,128)(2,1)} fusion(bf16[3,1024,768]{2,1,0:T(8,128)(2,1)} %collective-permute-done.15, bf16[3,2048,768]{2,1,0:T(8,128)(2,1)} %get-tuple-element.47, s32[]{:T(128)S(6)} %select_n.180), kind=kLoop, calls=%fused_computation.4 | loop fusion | flops 9437184 | bytes 14155780 | tf_op jit(solution)/shard_map/convert_element_type | solution.py:774
  279.8 22.4 %all-to-all-done.4 = bf16[8,128,768]{2,1,0:T(8,128)(2,1)} async-done(((bf16[8,128,768]{2,1,0:T(8,128)(2,1)}), bf16[8,128,768]{2,1,0:T(8,128)(2,1)}, u32[]{:S(2)}, u32[]{:S(2)}) %all-to-all-start.4) | async-done | bytes 1572896 | tf_op jit(solution)/shard_map/all_to_all | solution.py:716
  308.8 6.5 %all-to-all-start.9 = ((f32[8,1,1968]{2,1,0:T(1,128)}), f32[8,1,1968]{2,1,0:T(1,128)S(1)}, u32[]{:S(2)}, u32[]{:S(2)}) async-start(f32[8,1,1968]{2,1,0:T(1,128)} %copy.78), calls=%async_computation.9 | async-start | bytes 131072 | tf_op jit(solution)/shard_map/all_to_all | solution.py:865
  315.3 3.3 convert_bitcast_fusion
  322.3 3.8 gather_fusion
  331.7 45.1 %collective-permute-done.16 = bf16[3,1024,768]{2,1,0:T(8,128)(2,1)} collective-permute-done((bf16[3,1024,768]{2,1,0:T(8,128)(2,1)}, bf16[3,1024,768]{2,1,0:T(8,128)(2,1)}, u32[]{:S(2)}, u32[]{:S(2)}) %collective-permute-start.16) | collective-permute-done | bytes 4718624 | tf_op jit(solution)/shard_map/ppermute | solution.py:35
  376.7 7.0 %add_convert_fusion = bf16[3,1024,768]{2,1,0:T(8,128)(2,1)} fusion(bf16[3,1024,768]{2,1,0:T(8,128)(2,1)} %collective-permute-done.16, bf16[3,1024,768]{2,1,0:T(8,128)(2,1)} %add_convert_fusion.1), kind=kLoop, calls=%fused_computation.3 | loop fusion | flops 9437184 | bytes 14155776 | tf_op jit(solution)/shard_map/convert_element_type | solution.py:781
  386.5 3.5 all-to-all-start.7
  392.6 14.5 %collective-permute-done.9 = bf16[768,192]{0,1:T(8,128)(2,1)S(1)} collective-permute-done((bf16[768,192]{0,1:T(8,128)(2,1)S(1)}, bf16[768,192]{0,1:T(8,128)(2,1)S(1)}, u32[]{:S(2)}, u32[]{:S(2)}) %collective-permute-start.9) | collective-permute-done | bytes 294944 | tf_op jit(solution)/shard_map/ppermute | solution.py:35
  408.8 13.8 %all_to_all.54 = bf16[8,96,192]{1,2,0:T(8,128)(2,1)S(1)} all-to-all(bf16[8,96,192]{1,2,0:T(8,128)(2,1)S(1)} %copy.68), channel_id=1, replica_groups=mesh['dp'=8,'seq'=4] {'dp'}, dimensions={0} | all-to-all | bytes 589824 | tf_op jit(solution)/shard_map/all_to_all | solution.py:881
  422.6 6.9 %all-to-all-start.5 = ((bf16[8,128,768]{2,1,0:T(8,128)(2,1)}), bf16[8,128,768]{2,1,0:T(8,128)(2,1)}, u32[]{:S(2)}, u32[]{:S(2)}) async-start(bf16[8,128,768]{2,1,0:T(8,128)(2,1)} %bitcast.149), calls=%async_computation.5 | async-start | bytes 3145728 | tf_op jit(solution)/shard_map/all_to_all | solution.py:716
  433.6 3.7 collective-permute-start.14
  449.0 25.6 %attend_back.1.g_ref = bf16[576,2048]{1,0:T(8,128)(2,1)} custom-call(s32[8]{0:T(128)} %and_select_fusion.lo_ref, bf16[576,2048]{1,0:T(8,128)(2,1)} %get-tuple-element.33.qkv_ref, bf16[4,192,512]{2,1,0:T(8,128)(2,1)} %copy-done.3, f32[192,2048]{1,0:T(8,128)} %get-tuple-element.40.exact_ref, f32[3,2048]{1,0:T(4,128)} %get-tuple-element.41.log_ref, ...), custom_call_target="tpu_custom_call" | custom-call | tf_op jit(solution)/shard_map/attend_back/pallas_call | solution.py:394
  474.6 43.3 %tail.1 = (f32[512,768]{1,0:T(8,128)}, f32[96,2304]{1,0:T(8,128)}, f32[96,1]{1,0:T(8,128)}) custom-call(bf16[576,2048]{1,0:T(8,128)(2,1)} %attend_back.1.g_ref, bf16[2048,768]{1,0:T(8,128)(2,1)} %get-tuple-element.42.a_ref, bf16[576,768]{1,0:T(8,128)(2,1)} %get-tuple-element.43.wt_ref, bf16[512,768]{1,0:T(8,128)(2,1)} %bitcast.148, ...), custom_call_target="tpu_custom_call" | custom-call | tf_op jit(solution)/shard_map/tail/pallas_call | solution.py:592
  527.6 3.9 fusion.9
  531.5 6.6 %broadcast_select_fusion.1 = (bf16[3,1024,768]{2,1,0:T(8,128)(2,1)S(1)}, bf16[3,1024,768]{2,1,0:T(8,128)(2,1)}) fusion(bf16[3,1024,768]{2,1,0:T(8,128)(2,1)} %add_convert_fusion, bf16[3,1024,768]{2,1,0:T(8,128)(2,1)} %collective-permute-done.17, pred[]{:T(512)S(6)} %eq.164), kind=kLoop, calls=%fused_computation.6 | loop fusion | flops 4718592 | bytes 18874368 | tf_op jit(solution)/shard_map/jit(_where)/select_n | solution.py:784
  538.0 9.9 %maximum_convert_fusion = f32[3,2048,768]{2,1,0:T(8,128)} fusion(bf16[3,1024,768]{2,1,0:T(8,128)(2,1)} %get-tuple-element.136, bf16[3,1024,768]{2,1,0:T(8,128)(2,1)S(1)} %get-tuple-element.135), kind=kLoop, calls=%fused_computation.2 | loop fusion | flops 18874368 | bytes 28311552 | tf_op jit(solution)/shard_map/convert_element_type | solution.py:785
  (218 shorter events, 91.7 us)
Async XLA Ops:
  0.6 104.7 %copy-start = (bf16[12,12]{1,0:T(8,128)(2,1)S(1)}, bf16[12,12]{1,0:T(8,128)(2,1)}, u32[]{:S(2)}) copy-start(bf16[12,12]{1,0:T(8,128)(2,1)} %param.23) | copy-start | bytes 868
  0.7 90.8 %collective-permute-start.4 = (bf16[96,768]{1,0:T(8,128)(2,1)}, bf16[96,768]{1,0:T(8,128)(2,1)S(1)}, u32[]{:S(2)}, u32[]{:S(2)}) collective-permute-start(bf16[96,768]{1,0:T(8,128)(2,1)} %param.20), channel_id=1, source_target_pairs={{0,20},{4,24},{8,28},{12,0},{16,4},{20,8},{24,12},{28,16},{1,21},{... | collective-permute-start | bytes 442376 | tf_op jit(solution)/shard_map/ppermute | solution.py:678
  0.7 90.7 %collective-permute-start.3 = (bf16[96,768]{1,0:T(8,128)(2,1)}, bf16[96,768]{1,0:T(8,128)(2,1)S(1)}, u32[]{:S(2)}, u32[]{:S(2)}) collective-permute-start(bf16[96,768]{1,0:T(8,128)(2,1)} %param.20), channel_id=1, source_target_pairs={{0,16},{4,20},{8,24},{12,28},{16,0},{20,4},{24,8},{28,12},{1,17},{... | collective-permute-start | bytes 442376 | tf_op jit(solution)/shard_map/ppermute | solution.py:678
  3.1 88.2 %collective-permute-start.2 = (bf16[96,768]{1,0:T(8,128)(2,1)}, bf16[96,768]{1,0:T(8,128)(2,1)S(1)}, u32[]{:S(2)}, u32[]{:S(2)}) collective-permute-start(bf16[96,768]{1,0:T(8,128)(2,1)} %param.20), channel_id=1, source_target_pairs={{0,12},{4,16},{8,20},{12,24},{16,28},{20,0},{24,4},{28,8},{1,13},{... | collective-permute-start | bytes 442376 | tf_op jit(solution)/shard_map/ppermute | solution.py:678
  6.3 85.0 %collective-permute-start.1 = (bf16[96,768]{1,0:T(8,128)(2,1)}, bf16[96,768]{1,0:T(8,128)(2,1)S(1)}, u32[]{:S(2)}, u32[]{:S(2)}) collective-permute-start(bf16[96,768]{1,0:T(8,128)(2,1)} %param.20), channel_id=1, source_target_pairs={{0,8},{4,12},{8,16},{12,20},{16,24},{20,28},{24,0},{28,4},{1,9},{5... | collective-permute-start | bytes 442376 | tf_op jit(solution)/shard_map/ppermute | solution.py:678
  6.3 84.9 %collective-permute-start = (bf16[96,768]{1,0:T(8,128)(2,1)}, bf16[96,768]{1,0:T(8,128)(2,1)S(1)}, u32[]{:S(2)}, u32[]{:S(2)}) collective-permute-start(bf16[96,768]{1,0:T(8,128)(2,1)} %param.20), channel_id=1, source_target_pairs={{0,4},{4,8},{8,12},{12,16},{16,20},{20,24},{24,28},{28,0},{1,5},{5... | collective-permute-start | bytes 442376 | tf_op jit(solution)/shard_map/ppermute | solution.py:678
  85.7 15.7 %all-to-all-start = ((bf16[4,192,512]{2,1,0:T(8,128)(2,1)}), bf16[4,192,512]{2,1,0:T(8,128)(2,1)S(1)}, u32[]{:S(2)}, u32[]{:S(2)}) async-start(bf16[4,192,512]{2,1,0:T(8,128)(2,1)} %get-tuple-element.34), calls=%async_computation | async-start | bytes 1572864 | tf_op jit(solution)/shard_map/all_to_all | solution.py:729
  90.6 189.0 %copy-start.23 = (s32[512,1]{0,1:T(1,128)}, s32[512,1]{0,1:T(1,128)S(1)}, u32[]{:S(2)}) copy-start(s32[512,1]{0,1:T(1,128)S(1)} %get-tuple-element.154) | copy-start | bytes 6148
  90.6 189.0 %copy-start.24 = (s32[512,1]{0,1:T(1,128)}, s32[512,1]{0,1:T(1,128)S(1)}, u32[]{:S(2)}) copy-start(s32[512,1]{0,1:T(1,128)S(1)} %get-tuple-element.155) | copy-start | bytes 6148
  91.1 211.1 %copy-start.25 = (s32[512,1]{0,1:T(1,128)}, s32[512,1]{0,1:T(1,128)S(1)}, u32[]{:S(2)}) copy-start(s32[512,1]{0,1:T(1,128)S(1)} %get-tuple-element.152) | copy-start | bytes 6148
  91.1 211.0 %copy-start.27 = (s32[512,1]{0,1:T(1,128)}, s32[512,1]{0,1:T(1,128)S(1)}, u32[]{:S(2)}) copy-start(s32[512,1]{0,1:T(1,128)S(1)} %get-tuple-element.153) | copy-start | bytes 6148
  91.2 6.4 %collective-permute-start.6 = (bf16[96,768]{1,0:T(8,128)(2,1)S(1)}, bf16[96,768]{1,0:T(8,128)(2,1)S(1)}, u32[]{:S(2)}, u32[]{:S(2)}) collective-permute-start(bf16[96,768]{1,0:T(8,128)(2,1)S(1)} %copy-done.15), channel_id=1, source_target_pairs={{0,28},{4,0},{8,4},{12,8},{16,12},{20,16},{24,20},{28,24},{1,29},{... | collective-permute-start | bytes 442376 | tf_op jit(solution)/shard_map/ppermute | solution.py:678
  91.3 5.5 collective-permute-start.5
  106.8 10.6 %all-to-all-start.3 = ((f32[8,1,128]{2,1,0:T(1,128)}), f32[8,1,128]{2,1,0:T(1,128)S(1)}, u32[]{:S(2)}, u32[]{:S(2)}) async-start(f32[8,1,128]{2,1,0:T(1,128)} %bitcast.30), calls=%async_computation.3 | async-start | bytes 8192 | tf_op jit(solution)/shard_map/all_to_all | solution.py:752
  117.5 40.7 %all-to-all-start.2 = ((bf16[8,128,768]{2,1,0:T(8,128)(2,1)}), bf16[8,128,768]{2,1,0:T(8,128)(2,1)}, u32[]{:S(2)}, u32[]{:S(2)}) async-start(bf16[8,128,768]{2,1,0:T(8,128)(2,1)} %bitcast.153), calls=%async_computation.2 | async-start | bytes 3145728 | tf_op jit(solution)/shard_map/all_to_all | solution.py:711
  158.1 41.1 %all-to-all-start.1 = ((bf16[8,128,768]{2,1,0:T(8,128)(2,1)}), bf16[8,128,768]{2,1,0:T(8,128)(2,1)}, u32[]{:S(2)}, u32[]{:S(2)}) async-start(bf16[8,128,768]{2,1,0:T(8,128)(2,1)} %bitcast.152), calls=%async_computation.1 | async-start | bytes 3145728 | tf_op jit(solution)/shard_map/all_to_all | solution.py:711
  245.7 22.1 %collective-permute-start.15 = (bf16[3,1024,768]{2,1,0:T(8,128)(2,1)}, bf16[3,1024,768]{2,1,0:T(8,128)(2,1)}, u32[]{:S(2)}, u32[]{:S(2)}) collective-permute-start(bf16[3,1024,768]{2,1,0:T(8,128)(2,1)} %constant_dynamic-slice_fusion), channel_id=1, source_target_pairs={{0,1},{1,0},{2,3},{3,2},{4,5},{5,4},{6,7},{7,6},{8,9},{9,8},{10,11... | collective-permute-start | bytes 14155784 | tf_op jit(solution)/shard_map/ppermute | solution.py:35
  251.7 9.6 %all-to-all-start.6 = ((f32[8,1,128]{2,1,0:T(1,128)}), f32[8,1,128]{2,1,0:T(1,128)S(1)}, u32[]{:S(2)}, u32[]{:S(2)}) async-start(f32[8,1,128]{2,1,0:T(1,128)} %bitcast.36), calls=%async_computation.6 | async-start | bytes 8192 | tf_op jit(solution)/shard_map/all_to_all | solution.py:716
  261.3 40.9 %all-to-all-start.4 = ((bf16[8,128,768]{2,1,0:T(8,128)(2,1)}), bf16[8,128,768]{2,1,0:T(8,128)(2,1)}, u32[]{:S(2)}, u32[]{:S(2)}) async-start(bf16[8,128,768]{2,1,0:T(8,128)(2,1)} %bitcast.150), calls=%async_computation.4 | async-start | bytes 3145728 | tf_op jit(solution)/shard_map/all_to_all | solution.py:716
  274.9 101.8 %collective-permute-start.16 = (bf16[3,1024,768]{2,1,0:T(8,128)(2,1)}, bf16[3,1024,768]{2,1,0:T(8,128)(2,1)}, u32[]{:S(2)}, u32[]{:S(2)}) collective-permute-start(bf16[3,1024,768]{2,1,0:T(8,128)(2,1)} %add_convert_fusion.1), channel_id=1, source_target_pairs={{0,2},{1,3},{2,0},{3,1},{4,6},{5,7},{6,4},{7,5},{8,10},{9,11},{10,... | collective-permute-start | bytes 14155784 | tf_op jit(solution)/shard_map/ppermute | solution.py:35
  308.8 77.6 %all-to-all-start.9 = ((f32[8,1,1968]{2,1,0:T(1,128)}), f32[8,1,1968]{2,1,0:T(1,128)S(1)}, u32[]{:S(2)}, u32[]{:S(2)}) async-start(f32[8,1,1968]{2,1,0:T(1,128)} %copy.78), calls=%async_computation.9 | async-start | bytes 131072 | tf_op jit(solution)/shard_map/all_to_all | solution.py:865
  328.9 63.7 %collective-permute-start.7 = (bf16[768,192]{0,1:T(8,128)(2,1)}, bf16[768,192]{0,1:T(8,128)(2,1)S(1)}, u32[]{:S(2)}, u32[]{:S(2)}) collective-permute-start(bf16[768,192]{0,1:T(8,128)(2,1)} %get-tuple-element.139), channel_id=1, source_target_pairs={{0,1},{1,0},{2,3},{3,2},{4,5},{5,4},{6,7},{7,6},{8,9},{9,8},{10,11... | collective-permute-start | bytes 884744 | tf_op jit(solution)/shard_map/ppermute | solution.py:35
  329.9 60.0 %collective-permute-start.8 = (bf16[768,192]{0,1:T(8,128)(2,1)}, bf16[768,192]{0,1:T(8,128)(2,1)}, u32[]{:S(2)}, u32[]{:S(2)}) collective-permute-start(bf16[768,192]{0,1:T(8,128)(2,1)} %get-tuple-element.140), channel_id=1, source_target_pairs={{0,1},{1,0},{2,3},{3,2},{4,5},{5,4},{6,7},{7,6},{8,9},{9,8},{10,11... | collective-permute-start | bytes 884744 | tf_op jit(solution)/shard_map/ppermute | solution.py:35
  383.8 147.7 %collective-permute-start.17 = (bf16[3,1024,768]{2,1,0:T(8,128)(2,1)}, bf16[3,1024,768]{2,1,0:T(8,128)(2,1)}, u32[]{:S(2)}, u32[]{:S(2)}) collective-permute-start(bf16[3,1024,768]{2,1,0:T(8,128)(2,1)} %add_convert_fusion), channel_id=1, source_target_pairs={{0,1},{1,0},{2,3},{3,2},{4,5},{5,4},{6,7},{7,6},{8,9},{9,8},{10,11... | collective-permute-start | bytes 14155784 | tf_op jit(solution)/shard_map/ppermute | solution.py:35
  386.5 22.3 %all-to-all-start.7 = ((bf16[4,192,512]{2,1,0:T(8,128)(2,1)}), bf16[4,192,512]{2,1,0:T(8,128)(2,1)S(1)}, u32[]{:S(2)}, u32[]{:S(2)}) async-start(bf16[4,192,512]{2,1,0:T(8,128)(2,1)} %bitcast.45), calls=%async_computation.7 | async-start | bytes 1572864 | tf_op jit(solution)/shard_map/all_to_all | solution.py:849
  391.2 15.9 %collective-permute-start.9 = (bf16[768,192]{0,1:T(8,128)(2,1)S(1)}, bf16[768,192]{0,1:T(8,128)(2,1)S(1)}, u32[]{:S(2)}, u32[]{:S(2)}) collective-permute-start(bf16[768,192]{0,1:T(8,128)(2,1)S(1)} %fusion.30), channel_id=1, source_target_pairs={{0,2},{1,3},{2,0},{3,1},{4,6},{5,7},{6,4},{7,5},{8,10},{9,11},{10,... | collective-permute-start | bytes 884744 | tf_op jit(solution)/shard_map/ppermute | solution.py:35
  422.6 102.5 %all-to-all-start.5 = ((bf16[8,128,768]{2,1,0:T(8,128)(2,1)}), bf16[8,128,768]{2,1,0:T(8,128)(2,1)}, u32[]{:S(2)}, u32[]{:S(2)}) async-start(bf16[8,128,768]{2,1,0:T(8,128)(2,1)} %bitcast.149), calls=%async_computation.5 | async-start | bytes 3145728 | tf_op jit(solution)/shard_map/all_to_all | solution.py:716
  430.1 2.7 collective-permute-start.13
  433.6 5.2 collective-permute-start.14
  447.2 71.8 %collective-permute-start.11 = (f32[96,192]{1,0:T(8,128)S(1)}, f32[96,192]{1,0:T(8,128)S(1)}, u32[]{:S(2)}, u32[]{:S(2)}) collective-permute-start(f32[96,192]{1,0:T(8,128)S(1)} %copy.70), channel_id=1, source_target_pairs={{0,2},{1,3},{2,0},{3,1},{4,6},{5,7},{6,4},{7,5},{8,10},{9,11},{10,... | collective-permute-start | bytes 221192 | tf_op jit(solution)/shard_map/ppermute | solution.py:35
  518.9 1.4 collective-permute-start.10
  519.0 1.4 collective-permute-start.12
  (33 other events, 486.7 us)

commit v3 on v2

v3 whole, which is shorter than its diff:
```python
import functools
import math

import jax
import jax.numpy as jnp
from jax import lax
from jax.experimental import pallas as pl
from jax.experimental.pallas import tpu as pltpu
from jax.sharding import PartitionSpec as P

D = 768
H = 12
HD = 64
E = 8
CAP = 128
BLK = 256
N_CROSS = 1

exact_prec = lax.Precision.HIGHEST
neg_large = -1e30
score_scale = 0.125 * math.log2(math.e)
f32 = jnp.float32
bf16 = jnp.bfloat16

NN = (((1,), (0,)), ((), ()))
NT = (((1,), (1,)), ((), ()))
TN = (((0,), (0,)), ((), ()))


def mm(a, b, dims):
    return lax.dot_general(a, b, dims, preferred_element_type=f32)


def swap(value, axis, bit):
    size = lax.axis_size(axis)
    return lax.ppermute(value, axis, [(i, i ^ bit) for i in range(size)])


def bits_high_first(size):
    bit = size // 2
    while bit >= 1:
        yield bit
        bit //= 2


MESH = pl.DeviceIdType.MESH
SMALL = 32


def greet(peers):
    barrier = pltpu.get_barrier_semaphore()
    for peer in peers:
        pl.semaphore_signal(barrier, inc=1, device_id=peer, device_id_type=MESH)
    pl.semaphore_wait(barrier, len(peers))


def one_hot(condition):
    return jnp.where(condition, 1.0, 0.0).astype(bf16)


def picks_of(slot_ref):
    tok = slot_ref.shape[0]
    slots = lax.broadcasted_iota(jnp.int32, (tok, E * CAP), 1)
    return [slot_ref[:, k : k + 1] == slots for k in range(2)]


def make_slots(route_ref, cot_ref, slot_ref, g_ref):
    tok = route_ref.shape[0]
    ids = lax.broadcasted_iota(jnp.int32, (tok, E), 1)
    named = [route_ref[:, k : k + 1] == ids for k in range(2)]
    earlier = lax.broadcasted_iota(jnp.int32, (tok, tok), 1) < lax.broadcasted_iota(
        jnp.int32, (tok, tok), 0
    )
    ranks = mm(one_hot(earlier), one_hot(named[0] | named[1]), NN)
    for k in range(2):
        route = route_ref[:, k : k + 1]
        rank = jnp.sum(jnp.where(named[k], ranks, 0.0), axis=1, keepdims=True)
        slot_ref[:, k : k + 1] = jnp.where(
            route < E, route * CAP + rank.astype(jnp.int32), E * CAP
        )
    picks = picks_of(slot_ref)
    rows = mm(one_hot(picks[0] | picks[1]), cot_ref[...], TN)
    g_ref[...] = rows.astype(bf16).reshape(g_ref.shape)


def start_kernel(
    n_seq, n_dp, h_ref, w_ref, again_ref, mgain_ref, vec_ref, mix_ref, router_ref,
    route_ref, cot_ref,
    all_ref, slice_ref, small_ref, slot_ref, *refs,
):
    g_refs, refs = refs[:n_dp], refs[n_dp:]
    g_buf, small_buf, h_send, h_recv, w_send, w_recv, s_send, s_recv = refs
    owners = n_dp // E
    me, dp = lax.axis_index("seq"), lax.axis_index("dp")
    shard, width3 = slice_ref.shape[1], slice_ref.shape[2]
    width = width3 // 3
    seq_bits = list(bits_high_first(n_seq))
    greet(
        [{"seq": me ^ bit} for bit in seq_bits]
        + [{"dp": lax.rem(dp + k, n_dp)} for k in range(1, n_dp)]
    )

    def put(place, bit, index):
        return pltpu.make_async_remote_copy(
            src_ref=h_ref if place == 0 else all_ref.at[me ^ place],
            dst_ref=all_ref.at[me ^ place],
            send_sem=h_send.at[index],
            recv_sem=h_recv.at[index],
            device_id={"seq": me ^ bit},
            device_id_type=MESH,
        )

    plan, arrival = [], {}
    order = [(0, bit) for bit in seq_bits]
    while order:
        place, bit = order.pop(0)
        copy = put(place, bit, len(plan))
        arrival[place ^ bit] = copy
        plan.append((place, copy))
        order += [(place ^ bit, low) for low in seq_bits if low < bit]
    for place, copy in plan:
        if place == 0:
            copy.start()

    for j in range(n_seq):

        @pl.when(me == j)
        def _():
            for c in range(3):
                left = c * width * n_seq + j * width
                slice_ref[dp, :, c * width : (c + 1) * width] = w_ref[:, left : left + width]

    small_buf[dp] = jnp.zeros(small_buf.shape[1:], bf16)
    small_buf[dp, 0:1, :] = again_ref[...]
    small_buf[dp, 1:2, :] = mgain_ref[...]
    small_buf[dp, 2:4, :] = vec_ref[...]
    small_buf[dp, 4:6, :] = mix_ref[0]
    small_buf[dp, 6:8, :] = mix_ref[1]
    small_buf[dp, 8 : 8 + H, :] = router_ref[...].astype(f32).T.astype(bf16)
    copies = []
    for k in range(1, n_dp):
        target = {"dp": lax.rem(dp + k, n_dp)}
        for ref, send, recv in ((slice_ref, w_send, w_recv), (small_buf, s_send, s_recv)):
            copy = pltpu.make_async_remote_copy(
                src_ref=ref.at[dp],
                dst_ref=ref.at[dp],
                send_sem=send.at[k],
                recv_sem=recv.at[k],
                device_id=target,
                device_id_type=MESH,
            )
            copy.start()
            copies.append(copy)
    all_ref[me] = h_ref[...]
    make_slots(route_ref, cot_ref, slot_ref, g_buf)
    for k in range(n_dp):
        g_refs[k][...] = g_buf[(dp ^ k) // owners]
    for place, copy in plan:
        if place != 0:
            arrival[place].wait_recv()
            copy.start()
    for place in arrival:
        if not any(p == place for p, _ in plan):
            arrival[place].wait_recv()
    for _, copy in plan:
        copy.wait_send()
    for copy in copies:
        copy.wait()
    small_ref[...] = jnp.concatenate(
        [small_buf[i].astype(f32) for i in range(n_dp)], axis=1
    )


def start_call(
    n_seq, n_dp, hidden, w_qkv, attn_gain, moe_gain, vec, mix, router, routes, cotangent
):
    tok, shard = hidden.shape[0], w_qkv.shape[0]
    width3 = w_qkv.shape[1] // n_seq
    vmem = pl.BlockSpec(memory_space=pltpu.VMEM)
    hops = n_seq - 1
    dma = pltpu.SemaphoreType.DMA
    return pl.pallas_call(
        functools.partial(start_kernel, n_seq, n_dp),
        out_shape=(
            jax.ShapeDtypeStruct((n_seq, tok, D), bf16),
            jax.ShapeDtypeStruct((n_dp, shard, width3), bf16),
            jax.ShapeDtypeStruct((SMALL, D), f32),
            jax.ShapeDtypeStruct(routes.shape, jnp.int32),
        )
        + (jax.ShapeDtypeStruct((CAP, D), bf16),) * n_dp,
        in_specs=[vmem] * 9,
        out_specs=[vmem] * (4 + n_dp),
        scratch_shapes=[
            pltpu.VMEM((E, CAP, D), bf16),
            pltpu.VMEM((n_dp, SMALL, shard), bf16),
            dma((hops,)),
            dma((hops,)),
            dma((n_dp,)),
            dma((n_dp,)),
            dma((n_dp,)),
            dma((n_dp,)),
        ],
        compiler_params=pltpu.CompilerParams(collective_id=0, has_side_effects=True),
        name="start",
    )(hidden, w_qkv, attn_gain[None], moe_gain[None], vec, mix, router, routes, cotangent)


def qkv_kernel(h_ref, gain_ref, w_ref, cos_ref, sin_ref, attn_ref, out_ref, wt_ref):
    @pl.when((pl.program_id(0) == 0) & (pl.program_id(1) == 0))
    def _():
        wt_ref[...] = w_ref[...].reshape(D, w_ref.shape[2]).T

    x = h_ref[0].astype(f32)
    mean_square = jnp.mean(x * x, axis=-1, keepdims=True)
    attn = (x * lax.rsqrt(mean_square + 1e-06) * gain_ref[...]).astype(bf16)
    attn_ref[...] = attn
    y = mm(wt_ref[...], attn, NT)
    cos, sin = cos_ref[...], sin_ref[...]
    rows = y.shape[0]
    half = HD // 2
    for head in range(2 * rows // (3 * HD)):
        a = y[head * HD : head * HD + half]
        b = y[head * HD + half : (head + 1) * HD]
        out_ref[head * HD : head * HD + half] = (a * cos - b * sin).astype(bf16)
        out_ref[head * HD + half : (head + 1) * HD] = (a * sin + b * cos).astype(bf16)
    out_ref[2 * rows // 3 :] = y[2 * rows // 3 :].astype(bf16)


def qkv_call(blocks, gain, w, cos_t, sin_t):
    parts, tok, _ = blocks.shape
    seq_len, width = parts * tok, w.shape[2]
    per = tok // BLK
    return pl.pallas_call(
        qkv_kernel,
        out_shape=(
            jax.ShapeDtypeStruct((seq_len, D), bf16),
            jax.ShapeDtypeStruct((width, seq_len), bf16),
            jax.ShapeDtypeStruct((width, D), bf16),
        ),
        grid=(parts, per),
        in_specs=[
            pl.BlockSpec((1, BLK, D), lambda b, t: (b, t, 0)),
            pl.BlockSpec((1, D), lambda b, t: (0, 0)),
            pl.BlockSpec(w.shape, lambda b, t: (0, 0, 0)),
            pl.BlockSpec((HD // 2, BLK), lambda b, t: (0, b * per + t)),
            pl.BlockSpec((HD // 2, BLK), lambda b, t: (0, b * per + t)),
        ],
        out_specs=[
            pl.BlockSpec((BLK, D), lambda b, t: (b * per + t, 0)),
            pl.BlockSpec((width, BLK), lambda b, t: (0, b * per + t)),
            pl.BlockSpec((width, D), lambda b, t: (0, 0)),
        ],
        name="qkv",
    )(blocks, gain, w, cos_t, sin_t)


def allowed_block(key_block, query_block, start_row):
    key_pos = key_block * BLK + lax.broadcasted_iota(jnp.int32, (BLK, BLK), 0)
    query_pos = query_block * BLK + lax.broadcasted_iota(jnp.int32, (BLK, BLK), 1)
    return (key_pos >= start_row) & (key_pos <= query_pos)


def attn_kernel(lo_ref, qkv_ref, start_ref, out_ref, exact_ref, log_ref, keys_ref):
    heads, seq_len, _ = keys_ref.shape
    width = heads * HD
    qb = pl.program_id(0)

    @pl.when(qb == 0)
    def _():
        for h in range(heads):
            keys_ref[h] = qkv_ref[width + h * HD : width + (h + 1) * HD, :].T

    here = pl.ds(pl.multiple_of(qb * BLK, BLK), BLK)
    start_row = start_ref[...]

    def step(kb, carry):
        there = pl.ds(pl.multiple_of(kb * BLK, BLK), BLK)
        allowed = allowed_block(kb, qb, start_row)
        new = []
        for h in range(heads):
            top, total, acc = carry[h]
            scores = mm(keys_ref[h, there, :], qkv_ref[h * HD : (h + 1) * HD, here], NN)
            scores = jnp.where(allowed, scores * score_scale, neg_large)
            new_top = jnp.maximum(top, jnp.max(scores, axis=0, keepdims=True))
            fade = jnp.exp2(top - new_top)
            weights = jnp.exp2(scores - new_top)
            total = total * fade + jnp.sum(weights, axis=0, keepdims=True)
            values = qkv_ref[2 * width + h * HD : 2 * width + (h + 1) * HD, there]
            acc = acc * fade + mm(values, weights.astype(bf16), NN)
            new.append((new_top, total, acc))
        return tuple(new)

    first = tuple(
        (
            jnp.full((1, BLK), neg_large, f32),
            jnp.zeros((1, BLK), f32),
            jnp.zeros((HD, BLK), f32),
        )
        for _ in range(heads)
    )
    done = lax.fori_loop(lo_ref[qb], qb + 1, step, first)
    for h in range(heads):
        top, total, acc = done[h]
        attended = acc / total
        exact_ref[h * HD : (h + 1) * HD, :] = attended
        out_ref[0, h * HD : (h + 1) * HD, :] = attended.astype(bf16)
        log_ref[h : h + 1, :] = top + jnp.log2(total)


def attn_call(lows, qkv, start_row, tok):
    width3, seq_len = qkv.shape
    width = width3 // 3
    heads = width // HD
    per = tok // BLK
    return pl.pallas_call(
        attn_kernel,
        out_shape=(
            jax.ShapeDtypeStruct((seq_len // tok, width, tok), bf16),
            jax.ShapeDtypeStruct((width, seq_len), f32),
            jax.ShapeDtypeStruct((heads, seq_len), f32),
        ),
        grid_spec=pltpu.PrefetchScalarGridSpec(
            num_scalar_prefetch=1,
            grid=(seq_len // BLK,),
            in_specs=[
                pl.BlockSpec((width3, seq_len), lambda i, lo: (0, 0)),
                pl.BlockSpec((1, BLK), lambda i, lo: (0, i)),
            ],
            out_specs=[
                pl.BlockSpec((1, width, BLK), lambda i, lo: (i // per, 0, i % per)),
                pl.BlockSpec((width, BLK), lambda i, lo: (0, i)),
                pl.BlockSpec((heads, BLK), lambda i, lo: (0, i)),
            ],
            scratch_shapes=[pltpu.VMEM((heads, seq_len, HD), bf16)],
        ),
        name="attend",
    )(lows, qkv, start_row)


def attn_back_kernel(
    lo_ref, qkv_ref, go_ref, exact_ref, log_ref, start_ref, cos_ref, sin_ref, out_ref,
    keys_ref, values_ref, dk_ref, dv_ref,
):
    heads, seq_len, _ = keys_ref.shape
    width = heads * HD
    half = HD // 2
    qb = pl.program_id(0)

    @pl.when(qb == 0)
    def _():
        for h in range(heads):
            keys_ref[h] = qkv_ref[width + h * HD : width + (h + 1) * HD, :].T
            values_ref[h] = qkv_ref[2 * width + h * HD : 2 * width + (h + 1) * HD, :].T
        dk_ref[...] = jnp.zeros_like(dk_ref)
        dv_ref[...] = jnp.zeros_like(dv_ref)

    here = pl.ds(pl.multiple_of(qb * BLK, BLK), BLK)
    start_row = start_ref[...]
    grad = go_ref[0]
    deltas = [
        jnp.sum(
            exact_ref[h * HD : (h + 1) * HD, :] * grad[h * HD : (h + 1) * HD].astype(f32),
            axis=0,
            keepdims=True,
        )
        for h in range(heads)
    ]

    def step(kb, carry):
        there = pl.ds(pl.multiple_of(kb * BLK, BLK), BLK)
        allowed = allowed_block(kb, qb, start_row)
        new = []
        for h in range(heads):
            rows = slice(h * HD, (h + 1) * HD)
            queries = qkv_ref[rows, here]
            scores = mm(keys_ref[h, there, :], queries, NN)
            scores = jnp.where(allowed, scores * score_scale, neg_large)
            probs = jnp.exp2(scores - log_ref[h : h + 1, :])
            grad_probs = mm(values_ref[h, there, :], grad[rows], NN)
            grad_scores = (probs * (grad_probs - deltas[h])).astype(bf16)
            dv_ref[rows, there] += mm(grad[rows], probs.astype(bf16), NT)
            dk_ref[rows, there] += mm(queries, grad_scores, NT)
            keys = qkv_ref[width + h * HD : width + (h + 1) * HD, there]
            new.append(carry[h] + mm(keys, grad_scores, NN))
        return tuple(new)

    grads = lax.fori_loop(
        lo_ref[qb], qb + 1, step, tuple(jnp.zeros((HD, BLK), f32) for _ in range(heads))
    )

    def turn_back(value, cos, sin):
        value = value.astype(bf16).astype(f32)
        a, b = value[:half], value[half:]
        return (a * cos + b * sin).astype(bf16), (b * cos - a * sin).astype(bf16)

    for h in range(heads):
        a, b = turn_back(grads[h] * 0.125, cos_ref[:, here], sin_ref[:, here])
        out_ref[h * HD : h * HD + half, here] = a
        out_ref[h * HD + half : (h + 1) * HD, here] = b

    @pl.when(qb == pl.num_programs(0) - 1)
    def _():
        cos, sin = cos_ref[...], sin_ref[...]
        for h in range(heads):
            a, b = turn_back(dk_ref[h * HD : (h + 1) * HD, :] * 0.125, cos, sin)
            out_ref[width + h * HD : width + h * HD + half, :] = a
            out_ref[width + h * HD + half : width + (h + 1) * HD, :] = b
        out_ref[2 * width :, :] = dv_ref[...].astype(bf16)


def attn_back_call(lows, qkv, grad_out, exact, logs, start_row, cos_t, sin_t):
    width3, seq_len = qkv.shape
    width = width3 // 3
    heads = width // HD
    per = grad_out.shape[2] // BLK
    return pl.pallas_call(
        attn_back_kernel,
        out_shape=jax.ShapeDtypeStruct((width3, seq_len), bf16),
        grid_spec=pltpu.PrefetchScalarGridSpec(
            num_scalar_prefetch=1,
            grid=(seq_len // BLK,),
            in_specs=[
                pl.BlockSpec((width3, seq_len), lambda i, lo: (0, 0)),
                pl.BlockSpec((1, width, BLK), lambda i, lo: (i // per, 0, i % per)),
                pl.BlockSpec((width, BLK), lambda i, lo: (0, i)),
                pl.BlockSpec((heads, BLK), lambda i, lo: (0, i)),
                pl.BlockSpec((1, BLK), lambda i, lo: (0, i)),
                pl.BlockSpec((HD // 2, seq_len), lambda i, lo: (0, 0)),
                pl.BlockSpec((HD // 2, seq_len), lambda i, lo: (0, 0)),
            ],
            out_specs=pl.BlockSpec((width3, seq_len), lambda i, lo: (0, 0)),
            scratch_shapes=[
                pltpu.VMEM((heads, seq_len, HD), bf16),
                pltpu.VMEM((heads, seq_len, HD), bf16),
                pltpu.VMEM((width, seq_len), f32),
                pltpu.VMEM((width, seq_len), f32),
            ],
        ),
        name="attend_back",
    )(lows, qkv, grad_out, exact, logs, start_row, cos_t, sin_t)


PAIR = 2 * CAP
TILE = 512
UNITS = 256


def moe_kernel(n_dp, n_cross, x_ref, gate_ref, w_hbm, *refs):
    g_refs, refs = refs[:n_dp], refs[n_dp:]
    piece_ref, dots_ref, refs = refs[0], refs[1], refs[2:]
    out_refs, refs = refs[:n_dp], refs[n_dp:]
    units = w_hbm.shape[1]
    tiles = units // UNITS // 2
    sum_refs, refs = refs[:tiles], refs[tiles:]
    far_refs, refs = refs[:n_cross], refs[n_cross:]
    (
        w_ref, x_in, gate_in, gs_ref, hid_ref, gg_ref, gu_ref, oacc_ref, pacc_ref, piece_out,
        dot_out, dw_out, dw_in, w_sem, x_send, x_recv, t_send, t_recv, p_send, p_recv,
        d_send, d_recv, c_send, c_recv, f_send, f_recv,
    ) = refs
    me, dp = lax.axis_index("seq"), lax.axis_index("dp")
    owners = n_dp // E
    pairs = n_dp // 2
    order = [i ^ (i >> 1) for i in range(pairs)]
    greet([{"dp": dp ^ k} for k in range(1, n_dp)] + [{"seq": me ^ 1}, {"seq": me ^ 2}])
    loads = [pltpu.make_async_copy(w_hbm.at[j], w_ref.at[j], w_sem.at[j]) for j in range(3)]
    x_copies, gate_copies = {}, {}
    for p in order:
        for k in (2 * p, 2 * p + 1):
            mine = (dp ^ k) // owners
            if k:
                target = {"dp": dp ^ k}
                gate_copies[k] = remote(
                    gate_ref.at[mine], gate_in.at[k], (t_send, t_recv), k, target
                )
                x_copies[k] = remote(x_ref.at[mine], x_in.at[k], (x_send, x_recv), k, target)
    for load in loads:
        load.start()
    x_in[0] = x_ref[dp // owners]
    gate_in[0] = gate_ref[dp // owners]
    piece_copies, dot_copies = {}, {}
    for count, p in enumerate(order):
        rows = slice(p * PAIR, (p + 1) * PAIR)
        for k in (2 * p, 2 * p + 1):
            if k:
                x_copies[k].wait_recv()
                gate_copies[k].wait_recv()
            column = jnp.broadcast_to(gate_in[k], (CAP, CAP)).T[:, 0:1]
            gs_ref[k * CAP : (k + 1) * CAP] = (g_refs[k][...].astype(f32) * column).astype(bf16)
        if count == 0:
            for load in loads:
                load.wait()
        oacc_ref[...] = jnp.zeros_like(oacc_ref)
        pacc_ref[...] = jnp.zeros_like(pacc_ref)

        @pl.loop(0, units // TILE)
        def _(t):
            part = pl.ds(pl.multiple_of(t * TILE, TILE), TILE)
            x = x_in[2 * p : 2 * p + 2].reshape(PAIR, D)
            gate_pre = mm(x, w_ref[0, part], NT)
            up_pre = mm(x, w_ref[1, part], NT)
            sig = 1.0 / (1.0 + jnp.exp(-gate_pre))
            silu = gate_pre * sig
            hidden = (silu * up_pre).astype(bf16)
            hid_ref[rows, part] = hidden
            oacc_ref[...] += mm(hidden, w_ref[2, part], NN)
            grad_hidden = mm(gs_ref[rows], w_ref[2, part], NT)
            grad_gate = (grad_hidden * up_pre * sig * (1.0 + gate_pre * (1.0 - sig))).astype(bf16)
            grad_up = (grad_hidden * silu).astype(bf16)
            gg_ref[rows, part] = grad_gate
            gu_ref[rows, part] = grad_up
            pacc_ref[...] += mm(grad_gate, w_ref[0, part], NN) + mm(grad_up, w_ref[1, part], NN)

        for k in (2 * p, 2 * p + 1):
            half = slice((k % 2) * CAP, (k % 2 + 1) * CAP)
            out = oacc_ref[half].astype(bf16)
            out_refs[k][...] = out
            product = out.astype(f32) * g_refs[k][...].astype(f32)
            dot_out[k] = lax.dot_general(
                jnp.ones((8, D), f32), product, NT, precision=exact_prec,
                preferred_element_type=f32,
            )[0:1]
            piece_out[k] = pacc_ref[half].astype(bf16)
            if k:
                target = {"dp": dp ^ k}
                dot_copies[k] = remote(
                    dot_out.at[k], dots_ref.at[dp], (d_send, d_recv), k, target
                )
                piece_copies[k] = remote(
                    piece_out.at[k], piece_ref.at[dp], (p_send, p_recv), k, target
                )
            else:
                dots_ref[dp] = dot_out[k]
                piece_ref[dp] = piece_out[k]
    core = me & 1
    x_all = x_in[...].reshape(n_dp * CAP, D)

    def weight_grad(half, t, ref):
        part = pl.ds(pl.multiple_of((half * tiles + t) * UNITS, UNITS), UNITS)
        ref[0] = mm(gg_ref[:, part], x_all, TN).astype(ref.dtype)
        ref[1] = mm(gu_ref[:, part], x_all, TN).astype(ref.dtype)
        ref[2] = mm(hid_ref[:, part], gs_ref[...], TN).astype(ref.dtype)

    core_copies = []
    for t in range(tiles):
        weight_grad(1 - core, t, dw_out.at[t])
        core_copies.append(
            remote(dw_out.at[t], dw_in.at[t], (c_send, c_recv), t, {"seq": me ^ 1})
        )
    far_copies = []
    for t in range(tiles):
        weight_grad(core, t, sum_refs[t])
        core_copies[t].wait_recv()
        sum_refs[t][...] = (sum_refs[t][...].astype(f32) + dw_in[t].astype(f32)).astype(bf16)
        if t < n_cross:
            far_copies.append(
                remote(sum_refs[t], far_refs[t], (f_send, f_recv), t, {"seq": me ^ 2})
            )
    for k in range(1, n_dp):
        piece_copies[k].wait_recv()
        dot_copies[k].wait_recv()
    for copy in far_copies:
        copy.wait_recv()
    for copies in (x_copies, gate_copies, piece_copies, dot_copies):
        for copy in copies.values():
            copy.wait_send()
    for copy in core_copies + far_copies:
        copy.wait_send()


def moe_call(n_dp, n_cross, x_slots, gate_slots, weights, grads):
    units = weights.shape[1]
    rows = n_dp * CAP
    tiles = units // UNITS // 2
    part = (3, UNITS, D)
    vmem = pl.BlockSpec(memory_space=pltpu.VMEM)
    dma = pltpu.SemaphoreType.DMA
    outs = pl.pallas_call(
        functools.partial(moe_kernel, n_dp, n_cross),
        out_shape=(
            jax.ShapeDtypeStruct((n_dp, CAP, D), bf16),
            jax.ShapeDtypeStruct((n_dp, 1, CAP), f32),
        )
        + (jax.ShapeDtypeStruct((CAP, D), bf16),) * n_dp
        + (jax.ShapeDtypeStruct(part, bf16),) * (tiles + n_cross),
        in_specs=[vmem, vmem, pl.BlockSpec(memory_space=pl.ANY)] + [vmem] * n_dp,
        out_specs=[vmem] * (2 + n_dp + tiles + n_cross),
        scratch_shapes=[
            pltpu.VMEM(weights.shape, bf16),
            pltpu.VMEM((n_dp, CAP, D), bf16),
            pltpu.VMEM((n_dp, 1, CAP), f32),
            pltpu.VMEM((rows, D), bf16),
            pltpu.VMEM((rows, units), bf16),
            pltpu.VMEM((rows, units), bf16),
            pltpu.VMEM((rows, units), bf16),
            pltpu.VMEM((PAIR, D), f32),
            pltpu.VMEM((PAIR, D), f32),
            pltpu.VMEM((n_dp, CAP, D), bf16),
            pltpu.VMEM((n_dp, 1, CAP), f32),
            pltpu.VMEM((tiles, *part), bf16),
            pltpu.VMEM((tiles, *part), bf16),
            dma((3,)),
        ]
        + [dma((n_dp,))] * 8
        + [dma((tiles,))] * 2
        + [dma((max(n_cross, 1),))] * 2,
        compiler_params=pltpu.CompilerParams(
            collective_id=4, has_side_effects=True, vmem_limit_bytes=67043328
        ),
        name="experts",
    )(x_slots, gate_slots, weights, *grads)
    piece, dots, outs = outs[0], outs[1], outs[2:]
    return piece, dots, outs[:n_dp], outs[n_dp : n_dp + tiles], outs[n_dp + tiles :]


def remote(src, dst, sems, index, target):
    copy = pltpu.make_async_remote_copy(
        src_ref=src,
        dst_ref=dst,
        send_sem=sems[0].at[index],
        recv_sem=sems[1].at[index],
        device_id=target,
        device_id_type=MESH,
    )
    copy.start()
    return copy


def fill_rows(full_ref, part_refs, dp):
    for k, part in enumerate(part_refs):
        full_ref[dp ^ k] = part[...]


def mid_kernel(n_seq, n_dp, *refs):
    (att_ref, h_ref, prev_ref, carry_ref, small_ref, slot_ref, route_ref), refs = refs[:7], refs[7:]
    parts, refs = refs[:n_dp], refs[n_dp:]
    heads_ref, mid_ref, gate_ref, clog_ref, x_ref, gs_ref, wfull_ref = refs[:7]
    sems = refs[7:]
    me, dp = lax.axis_index("seq"), lax.axis_index("dp")
    tok = h_ref.shape[0]
    greet([{"seq": me ^ place} for place in range(1, n_seq)])
    copies = [
        remote(att_ref.at[me ^ place], heads_ref.at[me], sems, place, {"seq": me ^ place})
        for place in range(1, n_seq)
    ]
    heads_ref[me] = att_ref[me]
    fill_rows(wfull_ref, parts, dp)
    picks = picks_of(slot_ref)
    pick_any = one_hot(picks[0] | picks[1])
    carried = jnp.dot(prev_ref[...], carry_ref[...], precision=exact_prec)
    for copy in copies:
        copy.wait_recv()
    attn_out = mm(heads_ref[...].reshape(D, tok), wfull_ref[...].reshape(D, D), TN)
    resid = h_ref[...].astype(f32) + attn_out
    mid_ref[...] = resid
    rate = lax.rsqrt(jnp.mean(resid * resid, axis=-1, keepdims=True) + 1e-06)
    normed = resid * rate * small_ref[1:2]
    low = normed.astype(bf16)
    x_ref[...] = mm(pick_any, low, TN).astype(bf16).reshape(x_ref.shape)
    logits = mm(low, small_ref[8 : 8 + H].astype(bf16), NT) + carried
    ids = lax.broadcasted_iota(jnp.int32, (tok, H), 1)
    chosen = [
        jnp.sum(jnp.where(route_ref[:, k : k + 1] == ids, logits, 0.0), axis=1, keepdims=True)
        for k in range(2)
    ]
    top = jnp.maximum(chosen[0], chosen[1])
    exps = [jnp.exp(c - top) for c in chosen]
    total = exps[0] + exps[1]
    gates = [e / total for e in exps]
    gate_ref[:, 0:1] = gates[0]
    gate_ref[:, 1:2] = gates[1]
    clog_ref[...] = lax.dot_general(
        normed, small_ref[4:8], NT, precision=exact_prec, preferred_element_type=f32
    )
    slot_gates = jnp.sum(
        jnp.where(picks[0], gates[0], 0.0) + jnp.where(picks[1], gates[1], 0.0),
        axis=0,
        keepdims=True,
    )
    for e in range(E):
        gs_ref[e] = slot_gates[:, e * CAP : (e + 1) * CAP]
    for copy in copies:
        copy.wait_send()


def mid_call(n_seq, n_dp, attended, hidden, prev, carry, small, slot_of, routes, parts):
    tok, width = hidden.shape[0], attended.shape[1]
    shard = parts[0].shape[0]
    vmem = pl.BlockSpec(memory_space=pltpu.VMEM)
    dma = pltpu.SemaphoreType.DMA
    return pl.pallas_call(
        functools.partial(mid_kernel, n_seq, n_dp),
        out_shape=(
            jax.ShapeDtypeStruct((n_seq, width, tok), bf16),
            jax.ShapeDtypeStruct((tok, D), f32),
            jax.ShapeDtypeStruct((tok, 2), f32),
            jax.ShapeDtypeStruct((tok, 4), f32),
            jax.ShapeDtypeStruct((E, CAP, D), bf16),
            jax.ShapeDtypeStruct((E, 1, CAP), f32),
            jax.ShapeDtypeStruct((n_dp, shard, D), bf16),
        ),
        in_specs=[vmem] * (7 + n_dp),
        out_specs=[vmem] * 7,
        scratch_shapes=[dma((n_seq,)), dma((n_seq,))],
        compiler_params=pltpu.CompilerParams(collective_id=2, has_side_effects=True),
        name="mid",
    )(attended, hidden, prev, carry, small, slot_of, routes, *parts)


LINES = 40


def mid_back_kernel(
    n_seq, n_dp, piece_ref, dots_ref, cot_ref, mid_ref, gate_ref, clog_ref, slot_ref, route_ref,
    small_ref, heads_ref, w_ref, prev_ref, carry_ref,
    resid_ref, go_ref, base_ref, dprev_ref, pack_ref, own_ref, cross_ref,
    gh_ref, wo_ref, wo_in, a_send, a_recv, c_send, c_recv,
):
    me = lax.axis_index("seq")
    tok = cot_ref.shape[0]
    width = heads_ref.shape[1]
    owners = n_dp // E
    pairs = n_seq // 2
    greet([{"seq": me ^ place} for place in range(1, n_seq)])
    cot = cot_ref[...]
    grad_top = cot.astype(f32)
    resid_mid = mid_ref[...]
    gain = small_ref[1:2]
    vec, mix = small_ref[2:4], small_ref[4:8]
    rate = lax.rsqrt(jnp.mean(resid_mid * resid_mid, axis=-1, keepdims=True) + 1e-06)
    normed = resid_mid * rate * gain
    picks = picks_of(slot_ref)
    gates = [gate_ref[:, k : k + 1] for k in range(2)]
    routes = [route_ref[:, k : k + 1] for k in range(2)]
    normed_dot = jnp.sum(grad_top * normed, axis=1, keepdims=True)
    vec_dot = mm(cot, vec.astype(bf16), NT)
    alphas, const_dot = [], []
    for j in range(2):
        pair = [clog_ref[:, 2 * j + c : 2 * j + c + 1] for c in range(2)]
        top = jnp.maximum(pair[0], pair[1])
        exps = [jnp.exp(p - top) for p in pair]
        total = exps[0] + exps[1]
        alphas.append([e / total for e in exps])
        const_dot.append(alphas[j][0] * normed_dot + alphas[j][1] * vec_dot[:, j : j + 1])
    slot_dots = jnp.concatenate(
        [sum(dots_ref[e * owners + o] for o in range(owners)) for e in range(E)], axis=1
    )
    out_dots = []
    for k in range(2):
        value = jnp.sum(jnp.where(picks[k], slot_dots, 0.0), axis=1, keepdims=True)
        value = value + jnp.where(routes[k] == E + 1, normed_dot, 0.0)
        for j in range(2):
            value = value + jnp.where(routes[k] == E + 2 + j, const_dot[j], 0.0)
        out_dots.append(value)
    mean_dot = gates[0] * out_dots[0] + gates[1] * out_dots[1]
    ids = lax.broadcasted_iota(jnp.int32, (tok, H), 1)
    grad_logits = sum(
        jnp.where(routes[k] == ids, gates[k] * (out_dots[k] - mean_dot), 0.0) for k in range(2)
    )

    def gate_of(expert):
        return sum(jnp.where(routes[k] == expert, gates[k], 0.0) for k in range(2))

    const_gate = [gate_of(E + 2 + j) for j in range(2)]
    normed_gate = gate_of(E + 1) + sum(const_gate[j] * alphas[j][0] for j in range(2))
    vec_gate = [const_gate[j] * alphas[j][1] for j in range(2)]
    mix_grads = []
    for j in range(2):
        terms = [normed_dot, vec_dot[:, j : j + 1]]
        for c in range(2):
            mix_grads.append(const_gate[j] * alphas[j][c] * (terms[c] - const_dot[j]))
    mix_grads = jnp.concatenate(mix_grads, axis=1)
    pick_any = one_hot(picks[0] | picks[1])
    grad_normed = grad_top * normed_gate
    grad_normed = grad_normed + jnp.dot(
        jnp.concatenate([grad_logits, mix_grads], axis=1),
        jnp.concatenate([small_ref[8 : 8 + H], mix], axis=0),
        precision=exact_prec,
        preferred_element_type=f32,
    )
    pieces = piece_ref[...].reshape(E, owners, CAP, D)
    for o in range(owners):
        grad_normed = grad_normed + mm(pick_any, pieces[:, o].reshape(E * CAP, D), NN)
    back, _ = norm_back(resid_mid, gain, grad_normed)
    grad_resid = grad_top + back
    resid_ref[...] = grad_resid
    grad_attn = grad_resid.astype(bf16)
    gh_ref[...] = mm(w_ref[...].reshape(D, D), grad_attn, NT).astype(bf16).reshape(gh_ref.shape)
    copies = [
        remote(gh_ref.at[me ^ place], go_ref.at[me], (a_send, a_recv), place, {"seq": me ^ place})
        for place in range(1, n_seq)
    ]
    go_ref[me] = gh_ref[me]
    grad_w = mm(heads_ref[...].reshape(D, tok), grad_attn, NN)
    for j in range(n_seq):
        wo_ref[j] = grad_w[:, j * width : (j + 1) * width].astype(bf16)
    core_copies = [
        remote(wo_ref.at[me ^ (2 * i + 1)], wo_in.at[i], (c_send, c_recv), i, {"seq": me ^ 1})
        for i in range(pairs)
    ]
    base = resid_mid + normed * normed_gate
    for j in range(2):
        base = base + vec_gate[j] * vec[j : j + 1]
    base_ref[...] = base
    dprev_ref[...] = lax.dot_general(
        grad_logits, carry_ref[...], NT, precision=exact_prec, preferred_element_type=f32
    )

    def rows_of(left, right):
        return lax.dot_general(left, right, TN, precision=exact_prec, preferred_element_type=f32)

    packed = jnp.concatenate(
        [
            rows_of(grad_logits, normed.astype(bf16).astype(f32)),
            rows_of(mix_grads, normed),
            rows_of(jnp.concatenate(vec_gate, axis=1), grad_top),
            jnp.sum(grad_normed * resid_mid * rate, axis=0, keepdims=True),
        ],
        axis=0,
    )
    carry_grad = rows_of(prev_ref[...], grad_logits)
    lines, shard = packed.shape[0], D // n_dp
    for i in range(n_dp):
        pack_ref[i] = jnp.zeros(pack_ref.shape[1:], f32)
        pack_ref[i, 0:lines, :] = packed[:, i * shard : (i + 1) * shard]
        pack_ref[i, 24 : 24 + H, 0:H] = carry_grad
    for i in range(pairs):
        core_copies[i].wait_recv()
        summed = wo_ref[me ^ (2 * i)].astype(f32) + wo_in[i].astype(f32)
        if i == 0:
            own_ref[...] = summed
        else:
            cross_ref[i - 1] = summed.astype(bf16)
    for copy in copies:
        copy.wait()
    for copy in core_copies:
        copy.wait_send()


def mid_back_call(
    n_seq, n_dp, piece, dots, cot, mid, gates, clog, slot_of, routes, small, heads, w, prev, carry
):
    tok, width = cot.shape[0], heads.shape[1]
    pairs = n_seq // 2
    vmem = pl.BlockSpec(memory_space=pltpu.VMEM)
    dma = pltpu.SemaphoreType.DMA
    return pl.pallas_call(
        functools.partial(mid_back_kernel, n_seq, n_dp),
        out_shape=(
            jax.ShapeDtypeStruct((tok, D), f32),
            jax.ShapeDtypeStruct((n_seq, width, tok), bf16),
            jax.ShapeDtypeStruct((tok, D), f32),
            jax.ShapeDtypeStruct((tok, H), f32),
            jax.ShapeDtypeStruct((n_dp, LINES, D // n_dp), f32),
            jax.ShapeDtypeStruct((D, width), f32),
            jax.ShapeDtypeStruct((pairs - 1, D, width), bf16),
        ),
        in_specs=[vmem] * 13,
        out_specs=[vmem] * 7,
        scratch_shapes=[
            pltpu.VMEM((n_seq, width, tok), bf16),
            pltpu.VMEM((n_seq, D, width), bf16),
            pltpu.VMEM((pairs, D, width), bf16),
            dma((n_seq,)),
            dma((n_seq,)),
            dma((pairs,)),
            dma((pairs,)),
        ],
        compiler_params=pltpu.CompilerParams(collective_id=3, has_side_effects=True),
        name="mid_back",
    )(piece, dots, cot, mid, gates, clog, slot_of, routes, small, heads, w, prev, carry)


def tail_kernel(
    n_seq, n_dp, g_ref, a_ref, wt_ref, h_ref, resid_ref, gain_ref, wq_ref,
    own_ref, cross_ref, pack_ref, gate_ref, slot_ref, base_ref, *refs,
):
    out_parts, refs = refs[:n_dp], refs[n_dp:]
    tail_body(n_seq, n_dp, g_ref, a_ref, wt_ref, h_ref, resid_ref, gain_ref, wq_ref,
              own_ref, cross_ref, pack_ref, gate_ref, slot_ref, base_ref, out_parts, *refs)


def tail_body(
    n_seq, n_dp, g_ref, a_ref, wt_ref, h_ref, resid_ref, gain_ref, wq_ref,
    own_ref, cross_ref, pack_ref, gate_ref, slot_ref, base_ref, out_parts,
    din_ref, dw_ref, dgain_ref, dwo_ref, line_ref, block_ref,
    core_out, core_in, x_out, x_in, part_ref, w_out_buf, w_in, row_buf, row_in,
    cross_in, wo_buf, wo_in, pack_in, line_buf, line_in, rows_ref,
    c_send, c_recv, x_send, x_recv, w_send, w_recv, r_send, r_recv,
    o_send, o_recv, p_send, p_recv, q_send, q_recv, l_send, l_recv,
):
    me, dp = lax.axis_index("seq"), lax.axis_index("dp")
    tok = h_ref.shape[0]
    shard, width3 = w_in.shape[1], w_in.shape[2]
    width = width3 // 3
    owners = n_dp // E
    others = range(1, n_dp)
    greet(
        [{"seq": me ^ place} for place in range(1, n_seq)]
        + [{"dp": lax.rem(dp + k, n_dp)} for k in others]
    )

    def there(k):
        return lax.rem(dp + k, n_dp)

    def term(place):
        columns = pl.ds(pl.multiple_of((me ^ place) * tok, tok), tok)
        return mm(g_ref[:, columns], wt_ref[...], TN)

    pairs = n_seq // 2
    cross_copies = [
        remote(cross_ref.at[i - 1], cross_in.at[i - 1], (o_send, o_recv), i - 1,
               {"seq": me ^ (2 * i)})
        for i in range(1, pairs)
    ]
    pack_copies = [
        remote(pack_ref.at[there(k)], pack_in.at[dp], (p_send, p_recv), k, {"dp": there(k)})
        for k in others
    ]
    pack_in[dp] = pack_ref[dp]
    core_copies = []
    for i in range(pairs):
        core_out[i] = term(2 * i + 1).astype(bf16)
        core_copies.append(
            remote(core_out.at[i], core_in.at[i], (c_send, c_recv), i, {"seq": me ^ 1})
        )
    turned = mm(g_ref[...], a_ref[...], NN)
    w_out_buf[...] = turned.T.astype(bf16).reshape(n_dp, shard, width3)
    w_in[dp] = w_out_buf[dp]
    w_copies = [
        remote(w_out_buf.at[there(k)], w_in.at[dp], (w_send, w_recv), k, {"dp": there(k)})
        for k in others
    ]
    x_copies = []
    for i in range(pairs - 1, -1, -1):
        part = term(2 * i)
        core_copies[i].wait_recv()
        part = part + core_in[i].astype(f32)
        if i == 0:
            part_ref[...] = part
        else:
            x_out[i - 1] = part.astype(bf16)
            x_copies.append(
                remote(x_out.at[i - 1], x_in.at[i - 1], (x_send, x_recv), i - 1,
                       {"seq": me ^ (2 * i)})
            )
    own = own_ref[...]
    for i in range(pairs - 1):
        cross_copies[i].wait_recv()
        own = own + cross_in[i].astype(f32)
    wo_buf[...] = own.astype(bf16).reshape(n_dp, shard, width)
    wo_in[dp] = wo_buf[dp]
    wo_copies = [
        remote(wo_buf.at[there(k)], wo_in.at[dp], (q_send, q_recv), k, {"dp": there(k)})
        for k in others
    ]
    picks = picks_of(slot_ref)
    fill_rows(rows_ref, out_parts, dp)
    rows = rows_ref[...].reshape(E, owners, CAP, D)
    block = base_ref[...]
    for k in range(2):
        hot = one_hot(picks[k])
        picked = sum(mm(hot, rows[:, o].reshape(E * CAP, D), NN) for o in range(owners))
        block = block + gate_ref[:, k : k + 1] * picked
    block_ref[...] = block.astype(bf16)

    for copy in pack_copies:
        copy.wait_recv()
    line_buf[...] = jnp.sum(pack_in[...], axis=0)
    line_in[me] = line_buf[...]
    line_copies = [
        remote(line_buf, line_in.at[me], (l_send, l_recv), place, {"seq": me ^ place})
        for place in range(1, n_seq)
    ]
    for copy in w_copies + wo_copies:
        copy.wait_recv()
    row_buf[:, :width3] = jnp.sum(w_in[...].astype(f32), axis=0).astype(bf16)
    row_buf[:, width3:] = jnp.sum(wo_in[...].astype(f32), axis=0).astype(bf16)
    row_in[me] = row_buf[...]
    row_copies = [
        remote(row_buf, row_in.at[me], (r_send, r_recv), place, {"seq": me ^ place})
        for place in range(1, n_seq)
    ]
    for copy in x_copies:
        copy.wait_recv()
    grad = part_ref[...]
    for i in range(pairs - 1):
        grad = grad + x_in[i].astype(f32)
    values = h_ref[...].astype(f32)
    back, _ = norm_back(values, gain_ref[...], grad)
    din_ref[...] = resid_ref[...] + back
    for copy in line_copies:
        copy.wait_recv()
    line_ref[...] = jnp.sum(line_in[...], axis=0)
    for copy in row_copies:
        copy.wait_recv()
    for j in range(n_seq):
        block = row_in[j].astype(f32)
        for c in range(3):
            left = c * width * n_seq + j * width
            dw_ref[:, left : left + width] = block[:, c * width : (c + 1) * width]
        dwo_ref[:, j * width : (j + 1) * width] = block[:, width3:]
    dgain_ref[...] = jnp.sum(dw_ref[...] * wq_ref[...].astype(f32), axis=1, keepdims=True)
    for copy in (
        core_copies + w_copies + x_copies + row_copies + wo_copies + pack_copies
        + line_copies + cross_copies
    ):
        copy.wait_send()


def tail_call(
    n_seq, n_dp, grad_qkv, attn_in, w_turned, hidden, grad_resid, gain, w_qkv,
    own, cross, pack, gates, slot_of, base, out_parts,
):
    tok, shard = hidden.shape[0], w_qkv.shape[0]
    width3 = grad_qkv.shape[0]
    width = width3 // 3
    pairs = n_seq // 2
    vmem = pl.BlockSpec(memory_space=pltpu.VMEM)
    dma = pltpu.SemaphoreType.DMA
    return pl.pallas_call(
        functools.partial(tail_kernel, n_seq, n_dp),
        out_shape=(
            jax.ShapeDtypeStruct((tok, D), f32),
            jax.ShapeDtypeStruct(w_qkv.shape, f32),
            jax.ShapeDtypeStruct((shard, 1), f32),
            jax.ShapeDtypeStruct((shard, D), f32),
            jax.ShapeDtypeStruct((LINES, shard), f32),
            jax.ShapeDtypeStruct((tok, D), bf16),
        ),
        in_specs=[vmem] * (13 + n_dp),
        out_specs=[vmem] * 6,
        scratch_shapes=[
            pltpu.VMEM((pairs, tok, D), bf16),
            pltpu.VMEM((pairs, tok, D), bf16),
            pltpu.VMEM((pairs - 1, tok, D), bf16),
            pltpu.VMEM((pairs - 1, tok, D), bf16),
            pltpu.VMEM((tok, D), f32),
            pltpu.VMEM((n_dp, shard, width3), bf16),
            pltpu.VMEM((n_dp, shard, width3), bf16),
            pltpu.VMEM((shard, width3 + width), bf16),
            pltpu.VMEM((n_seq, shard, width3 + width), bf16),
            pltpu.VMEM((pairs - 1, D, width), bf16),
            pltpu.VMEM((n_dp, shard, width), bf16),
            pltpu.VMEM((n_dp, shard, width), bf16),
            pltpu.VMEM((n_dp, LINES, shard), f32),
            pltpu.VMEM((LINES, shard), f32),
            pltpu.VMEM((n_seq, LINES, shard), f32),
            pltpu.VMEM((n_dp, CAP, D), bf16),
        ]
        + [dma((pairs,))] * 4
        + [dma((n_dp,))] * 2
        + [dma((n_seq,))] * 2
        + [dma((pairs,))] * 2
        + [dma((n_dp,))] * 4
        + [dma((n_seq,))] * 2,
        compiler_params=pltpu.CompilerParams(collective_id=1, has_side_effects=True),
        name="tail",
    )(
        grad_qkv, attn_in, w_turned, hidden, grad_resid, gain, w_qkv,
        own, cross, pack, gates, slot_of, base, *out_parts,
    )


def rope_tables(seq_len):
    freq_index = jnp.arange(HD // 2, dtype=f32)
    inv_freq = jnp.exp(freq_index * (-2.0 * math.log(10000.0) / HD))
    angles = jnp.arange(seq_len, dtype=jnp.int32).astype(f32)[None, :] * inv_freq[:, None]
    return jnp.cos(angles), jnp.sin(angles)


def norm_back(values, gain, grad):
    rate = lax.rsqrt(jnp.mean(values * values, axis=-1, keepdims=True) + 1e-06)
    scaled = gain * grad
    inner = jnp.mean(values * scaled, axis=-1, keepdims=True)
    return rate * scaled - values * (rate * rate * rate) * inner, rate


def per_device(
    hidden_in,
    prev_logits,
    segments,
    routes,
    attn_gain,
    w_qkv,
    w_out,
    moe_gain,
    w_router,
    w_carry,
    const_vec,
    const_mix,
    experts,
    cotangent,
):
    n_seq, n_dp = lax.axis_size("seq"), lax.axis_size("dp")
    me = lax.axis_index("seq")
    tok = hidden_in.shape[1]
    seq_len = tok * n_seq
    hidden = hidden_in[0]
    grad_low = cotangent[0]
    prev_rows = prev_logits[0]
    route_rows = routes[0]
    carry_f = w_carry.astype(f32)

    blocks, w_slice, small, slot_of, *grad_slots = start_call(
        n_seq, n_dp, hidden, w_qkv, attn_gain, moe_gain, const_vec, const_mix, w_router,
        route_rows, grad_low,
    )
    gain_one = small[0:1]
    w_out_parts = [w_out] + [swap(w_out, "dp", k) for k in range(1, n_dp)]

    def swap_all(parts):
        return [parts[0]] + [swap(parts[k], "dp", k) for k in range(1, n_dp)]

    arrived_grad = swap_all(grad_slots)

    cos_t, sin_t = rope_tables(seq_len)
    seg_row = segments[0]
    doc_ids = jnp.arange(16, dtype=jnp.int32)
    doc_start = jnp.sum((seg_row[None, :] < doc_ids[:, None]).astype(jnp.int32), axis=1)
    start = jnp.sum(jnp.where(seg_row[None, :] == doc_ids[:, None], doc_start[:, None], 0), axis=0)
    start_row = start.astype(jnp.int32)[None, :]
    lows = start[::BLK].astype(jnp.int32) // BLK
    attn_in, qkv, w_turned = qkv_call(blocks, gain_one, w_slice, cos_t, sin_t)
    attended, attended_exact, logs = attn_call(lows, qkv, start_row, tok)

    heads_t, resid_mid, gates, const_logits, x_slots, gate_slots, out_weight = mid_call(
        n_seq, n_dp, attended, hidden, prev_rows, carry_f, small, slot_of, route_rows, w_out_parts
    )
    n_cross = min(N_CROSS, experts.shape[1] // UNITS // 2 - 1)
    back_piece, back_dots, partial, sums, far = moe_call(
        n_dp, n_cross, x_slots, gate_slots, experts, arrived_grad
    )
    back_out = swap_all(partial)
    far = list(far) + [swap(part, "seq", 2) for part in sums[n_cross:]]

    grad_resid, grad_out, base, d_prev, pack, own, cross = mid_back_call(
        n_seq, n_dp, back_piece, back_dots, grad_low, resid_mid, gates, const_logits, slot_of,
        route_rows, small, heads_t, out_weight, prev_rows, carry_f,
    )
    grad_qkv = attn_back_call(
        lows, qkv, grad_out, attended_exact, logs, start_row, cos_t, sin_t
    )
    d_input, d_qkv, gain_sum, d_out, lines, block_out = tail_call(
        n_seq, n_dp, grad_qkv, attn_in, w_turned, hidden, grad_resid, gain_one, w_qkv,
        own, cross, pack, gates, slot_of, base, back_out,
    )
    mine, d_input = lax.optimization_barrier((list(zip(sums, far)), d_input))
    mine = jnp.concatenate(
        [(a.astype(f32) + b.astype(f32)).astype(bf16) for a, b in mine], axis=1
    )
    other = swap(mine, "seq", 1)
    core = me & 1
    d_experts = jnp.concatenate(
        [jnp.where(core == 0, mine, other), jnp.where(core == 0, other, mine)], axis=1
    ).astype(f32)
    return (
        block_out[None],
        d_input[None],
        d_prev[None],
        gain_sum[:, 0] / attn_gain.astype(f32),
        d_qkv,
        d_out,
        lines[H + 6],
        lines[:H].T,
        lines[24 : 24 + H, :H],
        lines[H + 4 : H + 6],
        lines[H : H + 4].reshape(2, 2, -1),
        d_experts,
    )


def solution(mesh):
    return jax.shard_map(
        per_device,
        mesh=mesh,
        in_specs=(
            P("dp", "seq", None),
            P("dp", "seq", None),
            P("dp", None),
            P("dp", "seq", None),
            P("dp"),
            P("dp", None),
            P("dp", None),
            P("dp"),
            P("dp", None),
            P(),
            P(None, "dp"),
            P(None, None, "dp"),
            P(None, "dp", None),
            P("dp", "seq", None),
        ),
        out_specs=(
            P("dp", "seq", None),
            P("dp", "seq", None),
            P("dp", "seq", None),
            P("dp"),
            P("dp", None),
            P("dp", None),
            P("dp"),
            P("dp", None),
            P(),
            P(None, "dp"),
            P(None, None, "dp"),
            P(None, "dp", None),
        ),
        check_vma=False,
    )
```

time: 560 us -> 426 us (0.76)
  waiting for transfers between devices: 162 us -> 12.9 us
  Pallas kernels: 182 us -> 320 us
  starting transfers between devices: 73.9 us -> 39.6 us
  matrix products: 32 us -> 0 us
  other arithmetic: 51 us -> 24.7 us
  blocking collectives: 13.8 us -> 0 us
  local copies, waits for them, and re-layouts: 34.6 us -> 23.6 us
    pallas_call x1 -> x3, Pallas kernels: 41.7 us -> 167 us  [the longest x1 88.7 us: moe_call(): pl.pallas_call(functools.partial(moe_kernel, n_dp, n_cross), out_shape=(j...]
    all_to_all x9 -> x0, waiting for transfers between devices: 95.7 us -> none  [the longest x2 65.4 us: dispatch(): lax.all_to_all(jnp.repeat(grouped, owners, axis=0), 'dp', split_axis=0, c...]
    all_to_all x9 -> x0, starting transfers between devices: 55 us -> none  [the longest x3 19.8 us: back_to_source(): return lax.all_to_all(values, 'dp', split_axis=0, concat_axis=0, tiled=True)]
    ppermute x11 -> x25, waiting for transfers between devices: 60 us -> 12.9 us  [swap(): return lax.ppermute(value, axis, [(i, i ^ bit) for i in range(size)])]
    dot_general x20 -> x0, matrix products: 32 us -> none  [the longest x10 20.9 us: mm(): return lax.dot_general(a, b, dims, preferred_element_type=f32)]
    ppermute x11 -> x25, starting transfers between devices: 12 us -> 39.6 us  [swap(): return lax.ppermute(value, axis, [(i, i ^ bit) for i in range(size)])]
    pallas_call x1, Pallas kernels: 43.3 us -> 59.8 us  [tail_call(): pl.pallas_call(functools.partial(tail_kernel, n_seq, n_dp), out_shape=(ja...]
    all_to_all x1 -> x0, blocking collectives: 13.8 us -> none  [reduce_rows(): value = lax.all_to_all(value, 'dp', split_axis=0, concat_axis=0, tiled=True)]
  transfers between devices with their start and end apart: 27 -> 25, of which waited for: 12 -> 2; matrix products, arithmetic and copies ran while one was open for 16% -> 4% of each run, Pallas kernels for 25% -> 55%
where the time goes in v3:
time: 426 us; the launch traced here: 422 us
  Pallas kernels  320 us (75%)
  starting transfers between devices  39.6 us (9%)
  other arithmetic  24.7 us (6%)
  local copies, waits for them, and re-layouts  23.6 us (6%)
  waiting for transfers between devices  12.9 us (3%)
    pallas_call x1, Pallas kernels, moe_call(): pl.pallas_call(functools.partial(moe_kernel, n_dp, n_cross), out_shape=(j...  88.7 us
    pallas_call x1, Pallas kernels, tail_call(): pl.pallas_call(functools.partial(tail_kernel, n_seq, n_dp), out_shape=(ja...  59.8 us
    pallas_call x1, Pallas kernels, mid_back_call(): pl.pallas_call(functools.partial(mid_back_kernel, n_seq, n_dp), out_shape...  54.7 us
    ppermute x25, starting transfers between devices, swap(): return lax.ppermute(value, axis, [(i, i ^ bit) for i in range(size)])  39.6 us
    pallas_call x1, Pallas kernels, start_call(): pl.pallas_call(functools.partial(start_kernel, n_seq, n_dp), out_shape=(j...  34.8 us
    pallas_call x1, Pallas kernels, attn_back_call(): pl.pallas_call(attn_back_kernel, out_shape=jax.ShapeDtypeStruct((width3,...  25.7 us
    pallas_call x1, Pallas kernels, attn_call(): pl.pallas_call(attn_kernel, out_shape=(jax.ShapeDtypeStruct((seq_len // t...  23.6 us
    pallas_call x1, Pallas kernels, mid_call(): pl.pallas_call(functools.partial(mid_kernel, n_seq, n_dp), out_shape=(jax...  23.2 us
  transfers between devices with their start and end apart: 25, of which 2 were waited for; matrix products, arithmetic and copies ran while one was open for 4% of the time, Pallas kernels for 55%

profile of v3, /device:TPU:13, one launch (start us, length us, event | category | flops | bytes accessed | tf_op | source)
XLA Modules:
  0.0 421.7 jit_solution(11665409045113140781)
XLA Ops:
  0.7 1.4 collective-permute-start.5
  3.1 1.3 collective-permute-start.3
  4.4 3.2 collective-permute-start.2
  7.5 1.8 multiply_sine_fusion
  9.3 1.4 copy.35.router_ref
  10.7 1.5 copy.34
  12.3 34.8 %start.1 = (bf16[4,512,768]{2,1,0:T(8,128)(2,1)}, bf16[8,96,576]{2,1,0:T(8,128)(2,1)}, f32[32,768]{1,0:T(8,128)}, s32[512,2]{1,0:T(8,128)}, bf16[128,768]{1,0:T(...) custom-call(bf16[512,768]{1,0:T(8,128)(2,1)} %bitcast.16, ...), custom_call_target="tpu_custom_call" | custom-call | tf_op jit(solution)/shard_map/start/pallas_call | solution.py:182
  48.8 2.9 collective-permute-start.8
  53.5 1.4 slice.22.gain_ref
  54.9 9.0 %qkv.1 = (bf16[2048,768]{1,0:T(8,128)(2,1)}, bf16[576,2048]{1,0:T(8,128)(2,1)}, bf16[576,768]{1,0:T(8,128)(2,1)}) custom-call(bf16[4,512,768]{2,1,0:T(8,128)(2,1)} %get-tuple-element.74.h_ref, f32[1,768]{1,0:T(1,128)} %slice.22.gain_ref, bf16[8,96,576]{2,1,0:T(8,128)(2,1)} %get-tuple-element.76.w_ref, f32[32,2048]{1,0:T(8,128)} %get-tuple-element.175.cos_ref, ...), custom_call_target="tpu_custom_call" | custom-call | tf_op jit(solution)/shard_map/qkv/pallas_call | solution.py:233
  65.2 2.4 collective-permute-start.11
  68.0 2.1 collective-permute-start.13
  70.6 23.6 %attend.1 = (bf16[4,192,512]{2,1,0:T(8,128)(2,1)}, f32[192,2048]{1,0:T(8,128)}, f32[3,2048]{1,0:T(4,128)}) custom-call(s32[8]{0:T(128)} %and_select_fusion.lo_ref, bf16[576,2048]{1,0:T(8,128)(2,1)} %get-tuple-element.77.qkv_ref, s32[1,2048]{1,0:T(1,128)} %bitcast.29), custom_call_target="tpu_custom_call" | custom-call | tf_op jit(solution)/shard_map/attend/pallas_call | solution.py:315
  94.3 23.2 %mid.1 = (bf16[4,192,512]{2,1,0:T(8,128)(2,1)}, f32[512,768]{1,0:T(8,128)}, f32[512,2]{1,0:T(8,128)}, f32[512,4]{1,0:T(8,128)}, bf16[8,128,768]{2,1,0:T(8,128)(2...) custom-call(bf16[4,192,512]{2,1,0:T(8,128)(2,1)} %get-tuple-element.78.refs_0_, bf16[512,768]{1,0:T(8,128)(2,1)} %bitcast.17, ...), custom_call_target="tpu_custom_call" | custom-call | tf_op jit(solution)/shard_map/mid/pallas_call | solution.py:691
  121.0 88.7 %experts.1 = (bf16[8,128,768]{2,1,0:T(8,128)(2,1)}, f32[8,1,128]{2,1,0:T(1,128)}, bf16[128,768]{1,0:T(8,128)(2,1)}, bf16[128,768]{1,0:T(8,128)(2,1)}, bf16[128,7...) custom-call(bf16[8,128,768]{2,1,0:T(8,128)(2,1)} %get-tuple-element., ...), custom_call_target="tpu_custom_call" | custom-call | tf_op jit(solution)/shard_map/experts/pallas_call | solution.py:578
  209.8 1.5 collective-permute-start.22
  212.1 4.2 collective-permute-start.15
  216.3 4.7 %collective-permute-start.16 = (bf16[128,768]{1,0:T(8,128)(2,1)}, bf16[128,768]{1,0:T(8,128)(2,1)}, u32[]{:S(2)}, u32[]{:S(2)}) collective-permute-start(bf16[128,768]{1,0:T(8,128)(2,1)} %get-tuple-element.110), channel_id=1, source_target_pairs={{0,12},{4,8},{8,4},{12,0},{16,28},{20,24},{24,20},{28,16},{1,13},{... | collective-permute-start | bytes 589832 | tf_op jit(solution)/shard_map/ppermute | solution.py:36
  221.0 3.6 collective-permute-start.17
  225.9 7.1 %collective-permute-start.18 = (bf16[128,768]{1,0:T(8,128)(2,1)}, bf16[128,768]{1,0:T(8,128)(2,1)}, u32[]{:S(2)}, u32[]{:S(2)}) collective-permute-start(bf16[128,768]{1,0:T(8,128)(2,1)} %get-tuple-element.112), channel_id=1, source_target_pairs={{0,20},{4,16},{8,28},{12,24},{16,4},{20,0},{24,12},{28,8},{1,21},{... | collective-permute-start | bytes 589832 | tf_op jit(solution)/shard_map/ppermute | solution.py:36
  233.0 11.6 %collective-permute-done.18.refs_5_ = bf16[128,768]{1,0:T(8,128)(2,1)} collective-permute-done((bf16[128,768]{1,0:T(8,128)(2,1)}, bf16[128,768]{1,0:T(8,128)(2,1)}, u32[]{:S(2)}, u32[]{:S(2)}) %collective-permute-start.18) | collective-permute-done | bytes 196640 | tf_op jit(solution)/shard_map/ppermute | solution.py:36
  244.5 54.7 %mid_back.1 = (f32[512,768]{1,0:T(8,128)}, bf16[4,192,512]{2,1,0:T(8,128)(2,1)}, f32[512,768]{1,0:T(8,128)}, f32[512,12]{1,0:T(8,128)}, f32[8,40,96]{2,1,0:T(8,1...) custom-call(bf16[8,128,768]{2,1,0:T(8,128)(2,1)} %get-tuple-element.90.piece_ref, ...), custom_call_target="tpu_custom_call" | custom-call | tf_op jit(solution)/shard_map/mid_back/pallas_call | solution.py:847
  299.2 25.7 %attend_back.1.g_ref = bf16[576,2048]{1,0:T(8,128)(2,1)} custom-call(s32[8]{0:T(128)} %and_select_fusion.lo_ref, bf16[576,2048]{1,0:T(8,128)(2,1)} %get-tuple-element.77.qkv_ref, bf16[4,192,512]{2,1,0:T(8,128)(2,1)} %get-tuple-element.97.go_ref, f32[192,2048]{1,0:T(8,128)} %get-tuple-element.98.exact_ref, f32[3,2048]{1,0:T(4,128)} %get-tuple-element.99.log_ref, ...), custom_call_target="tpu_custom_call" | custom-call | tf_op jit(solution)/shard_map/attend_back/pallas_call | solution.py:416
  325.7 59.8 %tail.1 = (f32[512,768]{1,0:T(8,128)}, f32[96,2304]{1,0:T(8,128)}, f32[96,1]{1,0:T(8,128)}, f32[96,768]{1,0:T(8,128)}, f32[40,96]{1,0:T(8,128)}, /*index=5*/bf16[512,768]{1,0:T(8,128)(2,1)}) custom-call(bf16[576,2048]{1,0:T(8,128)(2,1)} %attend_back.1.g_ref, bf16[2048,768]{1,0:T(8,128)(2,1)} %get-tuple-element.100.a_ref, ...), custom_call_target="tpu_custom_call" | custom-call | tf_op jit(solution)/shard_map/tail/pallas_call | solution.py:1021
  387.0 2.7 add_convert_fusion.2
  390.0 1.8 add_convert_fusion
  391.9 2.7 pad_maximum_fusion
  394.8 1.7 copy.37
  398.9 1.3 slice.25
  402.9 1.3 slice_bitcast_fusion
  404.2 4.1 broadcast_select_fusion.1
  408.3 8.7 %maximum_convert_fusion = f32[3,2048,768]{2,1,0:T(8,128)} fusion(bf16[3,1024,768]{2,1,0:T(8,128)(2,1)S(1)} %get-tuple-element.173, bf16[3,1024,768]{2,1,0:T(8,128)(2,1)S(1)} %get-tuple-element.172), kind=kLoop, calls=%fused_computation | loop fusion | flops 18874368 | bytes 28311552 | tf_op jit(solution)/shard_map/convert_element_type | solution.py:1156
  (131 shorter events, 24.3 us)
Async XLA Ops:
  0.6 46.5 %copy-start.20 = (bf16[96,768]{1,0:T(8,128)(2,1)S(1)}, bf16[96,768]{1,0:T(8,128)(2,1)}, u32[]{:S(2)}) copy-start(bf16[96,768]{1,0:T(8,128)(2,1)} %refs_7_.1) | copy-start | bytes 442372
  0.7 51.0 %copy-start.29 = (s32[1,2048]{1,0:T(1,128)S(1)}, s32[1,2048]{1,0:T(1,128)}, u32[]{:S(2)}) copy-start(s32[1,2048]{1,0:T(1,128)} %param.16) | copy-start | bytes 24580
  0.7 51.4 %copy-start.31 = (bf16[12,12]{1,0:T(8,128)(2,1)S(1)}, bf16[12,12]{1,0:T(8,128)(2,1)}, u32[]{:S(2)}) copy-start(bf16[12,12]{1,0:T(8,128)(2,1)} %param.23) | copy-start | bytes 868
  0.7 52.0 %copy-start.30 = (f32[1,512,12]{1,0,2:T(1,128)S(1)}, f32[1,512,12]{1,0,2:T(1,128)}, u32[]{:S(2)}) copy-start(f32[1,512,12]{1,0,2:T(1,128)} %param.15) | copy-start | bytes 73732
  0.7 46.4 %collective-permute-start.5 = (bf16[96,768]{1,0:T(8,128)(2,1)}, bf16[96,768]{1,0:T(8,128)(2,1)S(1)}, u32[]{:S(2)}, u32[]{:S(2)}) collective-permute-start(bf16[96,768]{1,0:T(8,128)(2,1)} %refs_7_.1), channel_id=1, source_target_pairs={{0,24},{4,28},{8,16},{12,20},{16,8},{20,12},{24,0},{28,4},{1,25},{... | collective-permute-start | bytes 442376 | tf_op jit(solution)/shard_map/ppermute | solution.py:36
  2.0 45.2 %collective-permute-start.4 = (bf16[96,768]{1,0:T(8,128)(2,1)}, bf16[96,768]{1,0:T(8,128)(2,1)S(1)}, u32[]{:S(2)}, u32[]{:S(2)}) collective-permute-start(bf16[96,768]{1,0:T(8,128)(2,1)} %refs_7_.1), channel_id=1, source_target_pairs={{0,20},{4,16},{8,28},{12,24},{16,4},{20,0},{24,12},{28,8},{1,21},{... | collective-permute-start | bytes 442376 | tf_op jit(solution)/shard_map/ppermute | solution.py:36
  3.1 44.6 %collective-permute-start.3 = (bf16[96,768]{1,0:T(8,128)(2,1)}, bf16[96,768]{1,0:T(8,128)(2,1)S(1)}, u32[]{:S(2)}, u32[]{:S(2)}) collective-permute-start(bf16[96,768]{1,0:T(8,128)(2,1)} %refs_7_.1), channel_id=1, source_target_pairs={{0,16},{4,20},{8,24},{12,28},{16,0},{20,4},{24,8},{28,12},{1,17},{... | collective-permute-start | bytes 442376 | tf_op jit(solution)/shard_map/ppermute | solution.py:36
  4.4 44.4 %collective-permute-start.2 = (bf16[96,768]{1,0:T(8,128)(2,1)}, bf16[96,768]{1,0:T(8,128)(2,1)S(1)}, u32[]{:S(2)}, u32[]{:S(2)}) collective-permute-start(bf16[96,768]{1,0:T(8,128)(2,1)} %refs_7_.1), channel_id=1, source_target_pairs={{0,12},{4,8},{8,4},{12,0},{16,28},{20,24},{24,20},{28,16},{1,13},{... | collective-permute-start | bytes 442376 | tf_op jit(solution)/shard_map/ppermute | solution.py:36
  7.5 56.4 %collective-permute-start.1 = (bf16[96,768]{1,0:T(8,128)(2,1)}, bf16[96,768]{1,0:T(8,128)(2,1)S(1)}, u32[]{:S(2)}, u32[]{:S(2)}) collective-permute-start(bf16[96,768]{1,0:T(8,128)(2,1)} %refs_7_.1), channel_id=1, source_target_pairs={{0,8},{4,12},{8,0},{12,4},{16,24},{20,28},{24,16},{28,20},{1,9},{5... | collective-permute-start | bytes 442376 | tf_op jit(solution)/shard_map/ppermute | solution.py:36
  47.1 18.0 %collective-permute-start = (bf16[96,768]{1,0:T(8,128)(2,1)S(1)}, bf16[96,768]{1,0:T(8,128)(2,1)S(1)}, u32[]{:S(2)}, u32[]{:S(2)}) collective-permute-start(bf16[96,768]{1,0:T(8,128)(2,1)S(1)} %copy-done.20), channel_id=1, source_target_pairs={{0,4},{4,0},{8,12},{12,8},{16,20},{20,16},{24,28},{28,24},{1,5},{5... | collective-permute-start | bytes 442376 | tf_op jit(solution)/shard_map/ppermute | solution.py:36
  47.2 18.0 %collective-permute-start.6 = (bf16[96,768]{1,0:T(8,128)(2,1)S(1)}, bf16[96,768]{1,0:T(8,128)(2,1)S(1)}, u32[]{:S(2)}, u32[]{:S(2)}) collective-permute-start(bf16[96,768]{1,0:T(8,128)(2,1)S(1)} %copy-done.20), channel_id=1, source_target_pairs={{0,28},{4,24},{8,20},{12,16},{16,12},{20,8},{24,4},{28,0},{1,29},{... | collective-permute-start | bytes 442376 | tf_op jit(solution)/shard_map/ppermute | solution.py:36
  47.6 20.0 %collective-permute-start.7 = (bf16[128,768]{1,0:T(8,128)(2,1)}, bf16[128,768]{1,0:T(8,128)(2,1)S(1)}, u32[]{:S(2)}, u32[]{:S(2)}) collective-permute-start(bf16[128,768]{1,0:T(8,128)(2,1)} %get-tuple-element.83), channel_id=1, source_target_pairs={{0,4},{4,0},{8,12},{12,8},{16,20},{20,16},{24,28},{28,24},{1,5},{5... | collective-permute-start | bytes 589832 | tf_op jit(solution)/shard_map/ppermute | solution.py:36
  48.8 19.3 %collective-permute-start.8 = (bf16[128,768]{1,0:T(8,128)(2,1)}, bf16[128,768]{1,0:T(8,128)(2,1)S(1)}, u32[]{:S(2)}, u32[]{:S(2)}) collective-permute-start(bf16[128,768]{1,0:T(8,128)(2,1)} %get-tuple-element.84), channel_id=1, source_target_pairs={{0,8},{4,12},{8,0},{12,4},{16,24},{20,28},{24,16},{28,20},{1,9},{5... | collective-permute-start | bytes 589832 | tf_op jit(solution)/shard_map/ppermute | solution.py:36
  64.0 53.6 %collective-permute-start.9 = (bf16[128,768]{1,0:T(8,128)(2,1)S(1)}, bf16[128,768]{1,0:T(8,128)(2,1)S(1)}, u32[]{:S(2)}, u32[]{:S(2)}) collective-permute-start(bf16[128,768]{1,0:T(8,128)(2,1)S(1)} %copy-done.37), channel_id=1, source_target_pairs={{0,12},{4,8},{8,4},{12,0},{16,28},{20,24},{24,20},{28,16},{1,13},{... | collective-permute-start | bytes 589832 | tf_op jit(solution)/shard_map/ppermute | solution.py:36
  65.1 53.1 %collective-permute-start.10 = (bf16[128,768]{1,0:T(8,128)(2,1)S(1)}, bf16[128,768]{1,0:T(8,128)(2,1)S(1)}, u32[]{:S(2)}, u32[]{:S(2)}) collective-permute-start(bf16[128,768]{1,0:T(8,128)(2,1)S(1)} %copy-done.36), channel_id=1, source_target_pairs={{0,16},{4,20},{8,24},{12,28},{16,0},{20,4},{24,8},{28,12},{1,17},{... | collective-permute-start | bytes 589832 | tf_op jit(solution)/shard_map/ppermute | solution.py:36
  65.2 53.7 %collective-permute-start.11 = (bf16[128,768]{1,0:T(8,128)(2,1)S(1)}, bf16[128,768]{1,0:T(8,128)(2,1)S(1)}, u32[]{:S(2)}, u32[]{:S(2)}) collective-permute-start(bf16[128,768]{1,0:T(8,128)(2,1)S(1)} %copy-done.35), channel_id=1, source_target_pairs={{0,20},{4,16},{8,28},{12,24},{16,4},{20,0},{24,12},{28,8},{1,21},{... | collective-permute-start | bytes 589832 | tf_op jit(solution)/shard_map/ppermute | solution.py:36
  67.7 49.9 %copy-start.13 = (bf16[128,768]{1,0:T(8,128)(2,1)}, bf16[128,768]{1,0:T(8,128)(2,1)S(1)}, u32[]{:S(2)}) copy-start(bf16[128,768]{1,0:T(8,128)(2,1)S(1)} %collective-permute-done.7.refs_1_) | copy-start | bytes 589828
  67.7 52.0 %collective-permute-start.12 = (bf16[128,768]{1,0:T(8,128)(2,1)S(1)}, bf16[128,768]{1,0:T(8,128)(2,1)S(1)}, u32[]{:S(2)}, u32[]{:S(2)}) collective-permute-start(bf16[128,768]{1,0:T(8,128)(2,1)S(1)} %copy-done.34), channel_id=1, source_target_pairs={{0,24},{4,28},{8,16},{12,20},{16,8},{20,12},{24,0},{28,4},{1,25},{... | collective-permute-start | bytes 589832 | tf_op jit(solution)/shard_map/ppermute | solution.py:36
  68.0 49.5 %copy-start.14 = (bf16[128,768]{1,0:T(8,128)(2,1)}, bf16[128,768]{1,0:T(8,128)(2,1)S(1)}, u32[]{:S(2)}) copy-start(bf16[128,768]{1,0:T(8,128)(2,1)S(1)} %collective-permute-done.8.refs_2_) | copy-start | bytes 589828
  68.0 52.3 %collective-permute-start.13 = (bf16[128,768]{1,0:T(8,128)(2,1)S(1)}, bf16[128,768]{1,0:T(8,128)(2,1)S(1)}, u32[]{:S(2)}, u32[]{:S(2)}) collective-permute-start(bf16[128,768]{1,0:T(8,128)(2,1)S(1)} %copy-done.33), channel_id=1, source_target_pairs={{0,28},{4,24},{8,20},{12,16},{16,12},{20,8},{24,4},{28,0},{1,29},{... | collective-permute-start | bytes 589832 | tf_op jit(solution)/shard_map/ppermute | solution.py:36
  209.7 175.8 %collective-permute-start.21 = (bf16[3,256,768]{2,1,0:T(8,128)(2,1)}, bf16[3,256,768]{2,1,0:T(8,128)(2,1)S(1)}, u32[]{:S(2)}, u32[]{:S(2)}) collective-permute-start(bf16[3,256,768]{2,1,0:T(8,128)(2,1)} %get-tuple-element.130), channel_id=1, source_target_pairs={{0,2},{1,3},{2,0},{3,1},{4,6},{5,7},{6,4},{7,5},{8,10},{9,11},{10,... | collective-permute-start | bytes 3538952 | tf_op jit(solution)/shard_map/ppermute | solution.py:36
  209.8 175.8 %collective-permute-start.22 = (bf16[3,256,768]{2,1,0:T(8,128)(2,1)}, bf16[3,256,768]{2,1,0:T(8,128)(2,1)S(1)}, u32[]{:S(2)}, u32[]{:S(2)}) collective-permute-start(bf16[3,256,768]{2,1,0:T(8,128)(2,1)} %get-tuple-element.132), channel_id=1, source_target_pairs={{0,2},{1,3},{2,0},{3,1},{4,6},{5,7},{6,4},{7,5},{8,10},{9,11},{10,... | collective-permute-start | bytes 3538952 | tf_op jit(solution)/shard_map/ppermute | solution.py:36
  211.3 174.4 %collective-permute-start.23 = (bf16[3,256,768]{2,1,0:T(8,128)(2,1)}, bf16[3,256,768]{2,1,0:T(8,128)(2,1)}, u32[]{:S(2)}, u32[]{:S(2)}) collective-permute-start(bf16[3,256,768]{2,1,0:T(8,128)(2,1)} %get-tuple-element.134), channel_id=1, source_target_pairs={{0,2},{1,3},{2,0},{3,1},{4,6},{5,7},{6,4},{7,5},{8,10},{9,11},{10,... | collective-permute-start | bytes 3538952 | tf_op jit(solution)/shard_map/ppermute | solution.py:36
  211.3 4.9 %collective-permute-start.14 = (bf16[128,768]{1,0:T(8,128)(2,1)}, bf16[128,768]{1,0:T(8,128)(2,1)}, u32[]{:S(2)}, u32[]{:S(2)}) collective-permute-start(bf16[128,768]{1,0:T(8,128)(2,1)} %get-tuple-element.108), channel_id=1, source_target_pairs={{0,4},{4,0},{8,12},{12,8},{16,20},{20,16},{24,28},{28,24},{1,5},{5... | collective-permute-start | bytes 589832 | tf_op jit(solution)/shard_map/ppermute | solution.py:36
  212.1 8.9 %collective-permute-start.15 = (bf16[128,768]{1,0:T(8,128)(2,1)}, bf16[128,768]{1,0:T(8,128)(2,1)}, u32[]{:S(2)}, u32[]{:S(2)}) collective-permute-start(bf16[128,768]{1,0:T(8,128)(2,1)} %get-tuple-element.109), channel_id=1, source_target_pairs={{0,8},{4,12},{8,0},{12,4},{16,24},{20,28},{24,16},{28,20},{1,9},{5... | collective-permute-start | bytes 589832 | tf_op jit(solution)/shard_map/ppermute | solution.py:36
  216.3 9.6 %collective-permute-start.16 = (bf16[128,768]{1,0:T(8,128)(2,1)}, bf16[128,768]{1,0:T(8,128)(2,1)}, u32[]{:S(2)}, u32[]{:S(2)}) collective-permute-start(bf16[128,768]{1,0:T(8,128)(2,1)} %get-tuple-element.110), channel_id=1, source_target_pairs={{0,12},{4,8},{8,4},{12,0},{16,28},{20,24},{24,20},{28,16},{1,13},{... | collective-permute-start | bytes 589832 | tf_op jit(solution)/shard_map/ppermute | solution.py:36
  221.0 11.9 %collective-permute-start.17 = (bf16[128,768]{1,0:T(8,128)(2,1)}, bf16[128,768]{1,0:T(8,128)(2,1)}, u32[]{:S(2)}, u32[]{:S(2)}) collective-permute-start(bf16[128,768]{1,0:T(8,128)(2,1)} %get-tuple-element.111), channel_id=1, source_target_pairs={{0,16},{4,20},{8,24},{12,28},{16,0},{20,4},{24,8},{28,12},{1,17},{... | collective-permute-start | bytes 589832 | tf_op jit(solution)/shard_map/ppermute | solution.py:36
  225.9 18.7 %collective-permute-start.18 = (bf16[128,768]{1,0:T(8,128)(2,1)}, bf16[128,768]{1,0:T(8,128)(2,1)}, u32[]{:S(2)}, u32[]{:S(2)}) collective-permute-start(bf16[128,768]{1,0:T(8,128)(2,1)} %get-tuple-element.112), channel_id=1, source_target_pairs={{0,20},{4,16},{8,28},{12,24},{16,4},{20,0},{24,12},{28,8},{1,21},{... | collective-permute-start | bytes 589832 | tf_op jit(solution)/shard_map/ppermute | solution.py:36
  232.9 92.0 %collective-permute-start.19 = (bf16[128,768]{1,0:T(8,128)(2,1)}, bf16[128,768]{1,0:T(8,128)(2,1)S(1)}, u32[]{:S(2)}, u32[]{:S(2)}) collective-permute-start(bf16[128,768]{1,0:T(8,128)(2,1)} %get-tuple-element.113), channel_id=1, source_target_pairs={{0,24},{4,28},{8,16},{12,20},{16,8},{20,12},{24,0},{28,4},{1,25},{... | collective-permute-start | bytes 589832 | tf_op jit(solution)/shard_map/ppermute | solution.py:36
  244.5 80.5 %collective-permute-start.20 = (bf16[128,768]{1,0:T(8,128)(2,1)}, bf16[128,768]{1,0:T(8,128)(2,1)S(1)}, u32[]{:S(2)}, u32[]{:S(2)}) collective-permute-start(bf16[128,768]{1,0:T(8,128)(2,1)} %get-tuple-element.114), channel_id=1, source_target_pairs={{0,28},{4,24},{8,20},{12,16},{16,12},{20,8},{24,4},{28,0},{1,29},{... | collective-permute-start | bytes 589832 | tf_op jit(solution)/shard_map/ppermute | solution.py:36
  325.7 61.3 %copy-start.4 = (bf16[3,256,768]{2,1,0:T(8,128)(2,1)S(1)}, bf16[3,256,768]{2,1,0:T(8,128)(2,1)}, u32[]{:S(2)}) copy-start(bf16[3,256,768]{2,1,0:T(8,128)(2,1)} %get-tuple-element.128) | copy-start | bytes 3538948
  394.6 9.5 %collective-permute-start.24 = (bf16[3,1024,768]{2,1,0:T(8,128)(2,1)}, bf16[3,1024,768]{2,1,0:T(8,128)(2,1)}, u32[]{:S(2)}, u32[]{:S(2)}) collective-permute-start(bf16[3,1024,768]{2,1,0:T(8,128)(2,1)} %pad_maximum_fusion), channel_id=1, source_target_pairs={{0,1},{1,0},{2,3},{3,2},{4,5},{5,4},{6,7},{7,6},{8,9},{9,8},{10,11... | collective-permute-start | bytes 14155784 | tf_op jit(solution)/shard_map/ppermute | solution.py:36
  (31 other events, 270.9 us)

commit v4 on v3

v4 whole, which is shorter than its diff:
```python
import functools
import math

import jax
import jax.numpy as jnp
from jax import lax
from jax.experimental import pallas as pl
from jax.experimental.pallas import tpu as pltpu
from jax.sharding import PartitionSpec as P

D = 768
H = 12
HD = 64
E = 8
CAP = 128
BLK = 256
PAIR = 2 * CAP
TILE = 1024
UNITS = 256
SMALL = 32
LINES = 40

exact_prec = lax.Precision.HIGHEST
neg_large = -1e30
score_scale = 0.125 * math.log2(math.e)
f32 = jnp.float32
bf16 = jnp.bfloat16

NN = (((1,), (0,)), ((), ()))
NT = (((1,), (1,)), ((), ()))
TN = (((0,), (0,)), ((), ()))


MESH = pl.DeviceIdType.MESH
VMEM = pl.BlockSpec(memory_space=pltpu.VMEM)
HBM = pl.BlockSpec(memory_space=pl.ANY)
DMA = pltpu.SemaphoreType.DMA


def mm(a, b, dims):
    return lax.dot_general(a, b, dims, preferred_element_type=f32)


def swap(value, axis, bit):
    size = lax.axis_size(axis)
    return lax.ppermute(value, axis, [(i, i ^ bit) for i in range(size)])


def bits_high_first(size):
    bit = size // 2
    while bit >= 1:
        yield bit
        bit //= 2


def greet(peers):
    barrier = pltpu.get_barrier_semaphore()
    for peer in peers:
        pl.semaphore_signal(barrier, inc=1, device_id=peer, device_id_type=MESH)
    pl.semaphore_wait(barrier, len(peers))


def remote_later(src, dst, sems, index, target):
    return pltpu.make_async_remote_copy(
        src_ref=src,
        dst_ref=dst,
        send_sem=sems[0].at[index],
        recv_sem=sems[1].at[index],
        device_id=target,
        device_id_type=MESH,
    )


def remote(src, dst, sems, index, target):
    copy = remote_later(src, dst, sems, index, target)
    copy.start()
    return copy


def one_hot(condition):
    return jnp.where(condition, 1.0, 0.0).astype(bf16)


def picks_of(slot_ref):
    slots = lax.broadcasted_iota(jnp.int32, (E * CAP, slot_ref.shape[1]), 0)
    return [one_hot(slots == slot_ref[k : k + 1, :]) for k in range(2)]


def split(rows):
    high = rows.astype(bf16)
    rest = rows - high.astype(f32)
    middle = rest.astype(bf16)
    low = (rest - middle.astype(f32)).astype(bf16)
    return jnp.concatenate([high, middle, low], axis=0)


def unsplit(rows):
    third = rows.shape[0] // 3
    return rows[:third] + rows[third : 2 * third] + rows[2 * third :]


def column_to_row(column):
    return jnp.broadcast_to(column, (column.shape[0], 128)).T[0:1]


def norm_back(values, gain, grad):
    rate = lax.rsqrt(jnp.mean(values * values, axis=-1, keepdims=True) + 1e-06)
    scaled = gain * grad
    inner = jnp.mean(values * scaled, axis=-1, keepdims=True)
    return rate * scaled - values * (rate * rate * rate) * inner


def make_slots(route_ref, cot_ref, slot_ref, g_ref):
    tok = route_ref.shape[1]
    ids = lax.broadcasted_iota(jnp.int32, (E, tok), 0)
    named = [route_ref[k : k + 1, :] == ids for k in range(2)]
    earlier = lax.broadcasted_iota(jnp.int32, (tok, tok), 0) < lax.broadcasted_iota(
        jnp.int32, (tok, tok), 1
    )
    ranks = mm(one_hot(named[0] | named[1]), one_hot(earlier), NN)
    for k in range(2):
        route = route_ref[k : k + 1, :]
        rank = jnp.sum(jnp.where(named[k], ranks, 0.0), axis=0, keepdims=True)
        slot_ref[k : k + 1, :] = jnp.where(
            route < E, route * CAP + rank.astype(jnp.int32), E * CAP
        )
    picks = picks_of(slot_ref)
    g_ref[...] = mm(picks[0] + picks[1], cot_ref[...], NN).astype(bf16).reshape(g_ref.shape)


def start_kernel(
    n_seq, n_dp, h_ref, w_ref, again_ref, mgain_ref, vec_ref, mix_ref, router_ref,
    route_ref, cot_ref, cos_ref, sin_ref, wo_ref,
    attn_ref, qkv_ref, wt_ref, small_ref, slot_ref, g_ref, wo_all,
    all_ref, slice_ref, small_buf, h_send, h_recv, w_send, w_recv, s_send, s_recv,
    o_send, o_recv, c_send, c_recv,
):
    me, dp = lax.axis_index("seq"), lax.axis_index("dp")
    tok = h_ref.shape[0]
    width = slice_ref.shape[2] // 3
    seq_bits = list(bits_high_first(n_seq))
    greet(
        [{"seq": me ^ bit} for bit in seq_bits]
        + [{"dp": lax.rem(dp + k, n_dp)} for k in range(1, n_dp)]
    )

    plan, arrival = [], {}
    order = [(0, bit) for bit in seq_bits]
    while order:
        place, bit = order.pop(0)
        copy = remote_later(
            h_ref if place == 0 else all_ref.at[me ^ place],
            all_ref.at[me ^ place],
            (h_send, h_recv),
            len(plan),
            {"seq": me ^ bit},
        )
        arrival[place ^ bit] = copy
        plan.append((place, copy))
        order += [(place ^ bit, low) for low in seq_bits if low < bit]
    for place, copy in plan:
        if place == 0:
            copy.start()

    for j in range(n_seq):

        @pl.when(me == j)
        def _():
            for c in range(3):
                left = c * width * n_seq + j * width
                slice_ref[dp, :, c * width : (c + 1) * width] = w_ref[:, left : left + width]

    small_buf[dp] = jnp.zeros(small_buf.shape[1:], bf16)
    small_buf[dp, 0:1, :] = again_ref[...]
    small_buf[dp, 1:2, :] = mgain_ref[...]
    small_buf[dp, 2:4, :] = vec_ref[...]
    small_buf[dp, 4:6, :] = mix_ref[0]
    small_buf[dp, 6:8, :] = mix_ref[1]
    small_buf[dp, 8 : 8 + H, :] = router_ref[...]
    small_copies, w_copies = [], []
    for k in range(1, n_dp):
        target = {"dp": lax.rem(dp + k, n_dp)}
        small_copies.append(
            remote(small_buf.at[dp], small_buf.at[dp], (s_send, s_recv), k, target)
        )
        w_copies.append(remote(slice_ref.at[dp], slice_ref.at[dp], (w_send, w_recv), k, target))
    cols = pl.ds(pl.multiple_of((me & 1) * (D // 2), D // 2), D // 2)
    wo_copies = [
        remote(
            wo_ref.at[:, cols], wo_all.at[dp, :, cols], (o_send, o_recv), k,
            {"dp": lax.rem(dp + k, n_dp)},
        )
        for k in range(1, n_dp)
    ]
    make_slots(route_ref, cot_ref, slot_ref, g_ref)
    for copy in small_copies:
        copy.wait()
    small_ref[...] = jnp.concatenate([small_buf[i].astype(f32) for i in range(n_dp)], axis=1)

    def normalize(block, ref):
        x = ref.astype(f32)
        mean_square = jnp.mean(x * x, axis=-1, keepdims=True)
        rows = pl.ds(pl.multiple_of(block * tok, tok), tok)
        attn_ref[rows, :] = (x * lax.rsqrt(mean_square + 1e-06) * small_ref[0:1]).astype(bf16)

    normalize(me, h_ref[...])
    for place in arrival:
        arrival[place].wait_recv()
        for source, copy in plan:
            if source == place:
                copy.start()
        normalize(me ^ place, all_ref[me ^ place])
    for copy in w_copies:
        copy.wait()
    wt_ref[...] = slice_ref[...].reshape(D, 3 * width).T
    half = HD // 2

    @pl.loop(0, attn_ref.shape[0] // BLK)
    def _(i):
        rows = pl.ds(pl.multiple_of(i * BLK, BLK), BLK)
        y = mm(wt_ref[...], attn_ref[rows, :], NT)
        cos, sin = cos_ref[:, rows], sin_ref[:, rows]
        for head in range(2 * width // HD):
            low, middle, high = head * HD, head * HD + half, (head + 1) * HD
            a, b = y[low:middle], y[middle:high]
            qkv_ref[low:middle, rows] = (a * cos - b * sin).astype(bf16)
            qkv_ref[middle:high, rows] = (a * sin + b * cos).astype(bf16)
        qkv_ref[2 * width :, rows] = y[2 * width :].astype(bf16)

    for copy in wo_copies:
        copy.wait()
    wo_all[dp, :, cols] = wo_ref[:, cols]
    trade = remote(
        wo_all.at[:, :, cols], wo_all.at[:, :, cols], (c_send, c_recv), 0, {"seq": me ^ 1}
    )
    for _, copy in plan:
        copy.wait_send()
    trade.wait()


def start_call(
    n_seq, n_dp, hidden, w_qkv, attn_gain, moe_gain, vec, mix, router, routes, cotangent, cos, sin,
    w_out,
):
    tok, shard = hidden.shape[0], w_qkv.shape[0]
    width3 = w_qkv.shape[1] // n_seq
    hops = n_seq - 1
    return pl.pallas_call(
        functools.partial(start_kernel, n_seq, n_dp),
        out_shape=(
            jax.ShapeDtypeStruct((n_seq * tok, D), bf16),
            jax.ShapeDtypeStruct((width3, n_seq * tok), bf16),
            jax.ShapeDtypeStruct((width3, D), bf16),
            jax.ShapeDtypeStruct((SMALL, D), f32),
            jax.ShapeDtypeStruct(routes.shape, jnp.int32),
            jax.ShapeDtypeStruct((E, CAP, D), bf16),
            jax.ShapeDtypeStruct((n_dp, shard, D), bf16),
        ),
        in_specs=[VMEM] * 12,
        out_specs=[VMEM] * 7,
        scratch_shapes=[
            pltpu.VMEM((n_seq, tok, D), bf16),
            pltpu.VMEM((n_dp, shard, width3), bf16),
            pltpu.VMEM((n_dp, SMALL, shard), bf16),
            DMA((hops,)),
            DMA((hops,)),
            DMA((n_dp,)),
            DMA((n_dp,)),
            DMA((n_dp,)),
            DMA((n_dp,)),
            DMA((n_dp,)),
            DMA((n_dp,)),
            DMA((1,)),
            DMA((1,)),
        ],
        compiler_params=pltpu.CompilerParams(collective_id=0, has_side_effects=True),
        name="start",
    )(
        hidden, w_qkv, attn_gain[None], moe_gain[None], vec, mix, router, routes, cotangent,
        cos, sin, w_out,
    )


def allowed_block(key_block, query_block, start_row):
    key_pos = key_block * BLK + lax.broadcasted_iota(jnp.int32, (BLK, BLK), 0)
    query_pos = query_block * BLK + lax.broadcasted_iota(jnp.int32, (BLK, BLK), 1)
    return (key_pos >= start_row) & (key_pos <= query_pos)


def attn_kernel(lo_ref, qkv_ref, start_ref, out_ref, exact_ref, log_ref, keys_ref):
    heads, seq_len, _ = keys_ref.shape
    width = heads * HD
    qb = pl.program_id(0)

    @pl.when(qb == 0)
    def _():
        for h in range(heads):
            keys_ref[h] = qkv_ref[width + h * HD : width + (h + 1) * HD, :].T

    here = pl.ds(pl.multiple_of(qb * BLK, BLK), BLK)
    start_row = start_ref[...]

    def step(kb, carry):
        there = pl.ds(pl.multiple_of(kb * BLK, BLK), BLK)
        allowed = allowed_block(kb, qb, start_row)
        new = []
        for h in range(heads):
            top, total, acc = carry[h]
            scores = mm(keys_ref[h, there, :], qkv_ref[h * HD : (h + 1) * HD, here], NN)
            scores = jnp.where(allowed, scores * score_scale, neg_large)
            new_top = jnp.maximum(top, jnp.max(scores, axis=0, keepdims=True))
            fade = jnp.exp2(top - new_top)
            weights = jnp.exp2(scores - new_top)
            total = total * fade + jnp.sum(weights, axis=0, keepdims=True)
            values = qkv_ref[2 * width + h * HD : 2 * width + (h + 1) * HD, there]
            acc = acc * fade + mm(values, weights.astype(bf16), NN)
            new.append((new_top, total, acc))
        return tuple(new)

    first = tuple(
        (
            jnp.full((1, BLK), neg_large, f32),
            jnp.zeros((1, BLK), f32),
            jnp.zeros((HD, BLK), f32),
        )
        for _ in range(heads)
    )
    done = lax.fori_loop(lo_ref[qb], qb + 1, step, first)
    for h in range(heads):
        top, total, acc = done[h]
        attended = acc / total
        exact_ref[h * HD : (h + 1) * HD, :] = attended
        out_ref[0, h * HD : (h + 1) * HD, :] = attended.astype(bf16)
        log_ref[h : h + 1, :] = top + jnp.log2(total)


def attn_call(lows, qkv, start_row, tok):
    width3, seq_len = qkv.shape
    width = width3 // 3
    heads = width // HD
    per = tok // BLK
    return pl.pallas_call(
        attn_kernel,
        out_shape=(
            jax.ShapeDtypeStruct((seq_len // tok, width, tok), bf16),
            jax.ShapeDtypeStruct((width, seq_len), f32),
            jax.ShapeDtypeStruct((heads, seq_len), f32),
        ),
        grid_spec=pltpu.PrefetchScalarGridSpec(
            num_scalar_prefetch=1,
            grid=(seq_len // BLK,),
            in_specs=[
                pl.BlockSpec((width3, seq_len), lambda i, lo: (0, 0)),
                pl.BlockSpec((1, BLK), lambda i, lo: (0, i)),
            ],
            out_specs=[
                pl.BlockSpec((1, width, BLK), lambda i, lo: (i // per, 0, i % per)),
                pl.BlockSpec((width, BLK), lambda i, lo: (0, i)),
                pl.BlockSpec((heads, BLK), lambda i, lo: (0, i)),
            ],
            scratch_shapes=[pltpu.VMEM((heads, seq_len, HD), bf16)],
        ),
        cost_estimate=pl.CostEstimate(
            flops=16_000_000_000, transcendentals=0, bytes_accessed=16_000_000
        ),
        name="attend",
    )(lows, qkv, start_row)


def attn_back_kernel(
    lo_ref, qkv_ref, go_ref, exact_ref, log_ref, start_ref, cos_ref, sin_ref, out_ref,
    keys_ref, values_ref, dk_ref, dv_ref,
):
    heads, seq_len, _ = keys_ref.shape
    width = heads * HD
    half = HD // 2
    qb = pl.program_id(0)

    @pl.when(qb == 0)
    def _():
        for h in range(heads):
            keys_ref[h] = qkv_ref[width + h * HD : width + (h + 1) * HD, :].T
            values_ref[h] = qkv_ref[2 * width + h * HD : 2 * width + (h + 1) * HD, :].T
        dk_ref[...] = jnp.zeros_like(dk_ref)
        dv_ref[...] = jnp.zeros_like(dv_ref)

    here = pl.ds(pl.multiple_of(qb * BLK, BLK), BLK)
    start_row = start_ref[...]
    grad = go_ref[0]
    deltas = [
        jnp.sum(
            exact_ref[h * HD : (h + 1) * HD, :] * grad[h * HD : (h + 1) * HD].astype(f32),
            axis=0,
            keepdims=True,
        )
        for h in range(heads)
    ]

    def step(kb, carry):
        there = pl.ds(pl.multiple_of(kb * BLK, BLK), BLK)
        allowed = allowed_block(kb, qb, start_row)
        new = []
        for h in range(heads):
            rows = slice(h * HD, (h + 1) * HD)
            queries = qkv_ref[rows, here]
            scores = mm(keys_ref[h, there, :], queries, NN)
            scores = jnp.where(allowed, scores * score_scale, neg_large)
            probs = jnp.exp2(scores - log_ref[h : h + 1, :])
            grad_probs = mm(values_ref[h, there, :], grad[rows], NN)
            grad_scores = (probs * (grad_probs - deltas[h])).astype(bf16)
            dv_ref[rows, there] += mm(grad[rows], probs.astype(bf16), NT)
            dk_ref[rows, there] += mm(queries, grad_scores, NT)
            keys = qkv_ref[width + h * HD : width + (h + 1) * HD, there]
            new.append(carry[h] + mm(keys, grad_scores, NN))
        return tuple(new)

    grads = lax.fori_loop(
        lo_ref[qb], qb + 1, step, tuple(jnp.zeros((HD, BLK), f32) for _ in range(heads))
    )

    def turn_back(value, cos, sin):
        value = value.astype(bf16).astype(f32)
        a, b = value[:half], value[half:]
        return (a * cos + b * sin).astype(bf16), (b * cos - a * sin).astype(bf16)

    for h in range(heads):
        a, b = turn_back(grads[h] * 0.125, cos_ref[:, here], sin_ref[:, here])
        out_ref[h * HD : h * HD + half, here] = a
        out_ref[h * HD + half : (h + 1) * HD, here] = b

    @pl.when(qb == pl.num_programs(0) - 1)
    def _():
        cos, sin = cos_ref[...], sin_ref[...]
        for h in range(heads):
            a, b = turn_back(dk_ref[h * HD : (h + 1) * HD, :] * 0.125, cos, sin)
            out_ref[width + h * HD : width + h * HD + half, :] = a
            out_ref[width + h * HD + half : width + (h + 1) * HD, :] = b
        out_ref[2 * width :, :] = dv_ref[...].astype(bf16)


def attn_back_call(lows, qkv, grad_out, exact, logs, start_row, cos_t, sin_t):
    width3, seq_len = qkv.shape
    width = width3 // 3
    heads = width // HD
    per = grad_out.shape[2] // BLK
    return pl.pallas_call(
        attn_back_kernel,
        out_shape=jax.ShapeDtypeStruct((width3, seq_len), bf16),
        grid_spec=pltpu.PrefetchScalarGridSpec(
            num_scalar_prefetch=1,
            grid=(seq_len // BLK,),
            in_specs=[
                pl.BlockSpec((width3, seq_len), lambda i, lo: (0, 0)),
                pl.BlockSpec((1, width, BLK), lambda i, lo: (i // per, 0, i % per)),
                pl.BlockSpec((width, BLK), lambda i, lo: (0, i)),
                pl.BlockSpec((heads, BLK), lambda i, lo: (0, i)),
                pl.BlockSpec((1, BLK), lambda i, lo: (0, i)),
                pl.BlockSpec((HD // 2, seq_len), lambda i, lo: (0, 0)),
                pl.BlockSpec((HD // 2, seq_len), lambda i, lo: (0, 0)),
            ],
            out_specs=pl.BlockSpec((width3, seq_len), lambda i, lo: (0, 0)),
            scratch_shapes=[
                pltpu.VMEM((heads, seq_len, HD), bf16),
                pltpu.VMEM((heads, seq_len, HD), bf16),
                pltpu.VMEM((width, seq_len), f32),
                pltpu.VMEM((width, seq_len), f32),
            ],
        ),
        cost_estimate=pl.CostEstimate(
            flops=16_000_000_000, transcendentals=0, bytes_accessed=16_000_000
        ),
        name="attend_back",
    )(lows, qkv, grad_out, exact, logs, start_row, cos_t, sin_t)


def moe_kernel(n_dp, n_cross, x_ref, gate_ref, w_hbm, g_ref, *refs):
    piece_ref, dots_ref, out_ref, refs = refs[0], refs[1], refs[2], refs[3:]
    units = w_hbm.shape[1]
    tile = min(TILE, units)
    tiles = units // UNITS // 2
    sum_hbm, refs = refs[:tiles], refs[tiles:]
    far_refs, refs = refs[:n_cross], refs[n_cross:]
    (
        w_ref, x_in, gate_in, gs_ref, hid_ref, gg_ref, gu_ref, piece_out,
        dot_out, dw_out, dw_in, dw_keep, w_sem, x_send, x_recv, t_send, t_recv, p_send, p_recv,
        d_send, d_recv, c_send, c_recv, f_send, f_recv, keep_sem,
    ) = refs
    me, dp = lax.axis_index("seq"), lax.axis_index("dp")
    owners = n_dp // E
    pairs = n_dp // 2
    greet([{"dp": dp ^ k} for k in range(1, n_dp)] + [{"seq": me ^ 1}, {"seq": me ^ 2}])

    def x_copy(k):
        return remote_later(
            x_ref.at[(dp ^ k) // owners], x_in.at[k], (x_send, x_recv), k, {"dp": dp ^ k}
        )

    def gate_copy(k):
        return remote_later(
            gate_ref.at[(dp ^ k) // owners], gate_in.at[k], (t_send, t_recv), k, {"dp": dp ^ k}
        )

    def piece_copy(k):
        return remote_later(
            piece_out.at[k], piece_ref.at[dp], (p_send, p_recv), k, {"dp": dp ^ k}
        )

    def dot_copy(k):
        return remote_later(dot_out.at[k], dots_ref.at[dp], (d_send, d_recv), k, {"dp": dp ^ k})

    def core_copy(t):
        return remote_later(dw_out.at[t], dw_in.at[t], (c_send, c_recv), t, {"seq": me ^ 1})

    def far_copy(t):
        return remote_later(dw_keep.at[t], far_refs[t], (f_send, f_recv), t, {"seq": me ^ 2})

    for p in [0, pairs - 1, *range(1, pairs - 1)]:
        for k in (2 * p, 2 * p + 1):
            if k:
                gate_copy(k).start()
                x_copy(k).start()
    loads = [pltpu.make_async_copy(w_hbm.at[j], w_ref.at[j], w_sem.at[j]) for j in range(3)]
    loads.append(pltpu.make_async_copy(x_ref.at[dp // owners], x_in.at[0], w_sem.at[3]))
    for load in loads:
        load.start()
    gate_in[0] = gate_ref[dp // owners]
    for load in loads:
        load.wait()

    @pl.loop(0, pairs)
    def _(i):
        p = jnp.where(i == 0, 0, 1 + lax.rem(i + pairs - 3, pairs - 1))
        rows = pl.ds(pl.multiple_of(p * PAIR, PAIR), PAIR)

        def arrive(k):
            x_copy(k).wait_recv()
            gate_copy(k).wait_recv()

        @pl.when(p > 0)
        def _():
            arrive(2 * p)

        arrive(2 * p + 1)
        for side in range(2):
            k = 2 * p + side
            column = jnp.broadcast_to(gate_in[k], (CAP, CAP)).T[:, 0:1]
            here = pl.ds(pl.multiple_of(k * CAP, CAP), CAP)
            gs_ref[here] = (g_ref[dp ^ k].astype(f32) * column).astype(bf16)

        @pl.loop(0, units // tile)
        def _(t):
            part = pl.ds(pl.multiple_of(t * tile, tile), tile)
            x = x_in[pl.ds(2 * p, 2)].reshape(PAIR, D)
            gate_pre = mm(x, w_ref[0, part], NT)
            up_pre = mm(x, w_ref[1, part], NT)
            grad_hidden = mm(gs_ref[rows], w_ref[2, part], NT)
            sig = 1.0 / (1.0 + jnp.exp(-gate_pre))
            silu = gate_pre * sig
            hid_ref[rows, part] = (silu * up_pre).astype(bf16)
            gu_ref[rows, part] = (grad_hidden * silu).astype(bf16)
            gg_ref[rows, part] = (
                grad_hidden * up_pre * sig * (1.0 + gate_pre * (1.0 - sig))
            ).astype(bf16)

        pieces = mm(gg_ref[rows], w_ref[0], NN) + mm(gu_ref[rows], w_ref[1], NN)
        piece_out[pl.ds(2 * p, 2)] = pieces.astype(bf16).reshape(2, CAP, D)
        piece_copy(2 * p + 1).start()

        @pl.when(p > 0)
        def _():
            piece_copy(2 * p).start()

        outs = mm(hid_ref[rows], w_ref[2], NN)
        for side in range(2):
            k = 2 * p + side
            out = outs[side * CAP : (side + 1) * CAP].astype(bf16)
            out_ref[dp ^ k] = out
            product = out.astype(f32) * g_ref[dp ^ k].astype(f32)
            dot_out[k] = column_to_row(jnp.sum(product, axis=1, keepdims=True))
        dot_copy(2 * p + 1).start()

        @pl.when(p > 0)
        def _():
            dot_copy(2 * p).start()

    piece_ref[dp] = piece_out[0]
    dots_ref[dp] = dot_out[0]
    core = me & 1

    def weight_grad(half, t, ref):
        part = pl.ds(pl.multiple_of((half * tiles + t) * UNITS, UNITS), UNITS)
        x_all = x_in[...].reshape(n_dp * CAP, D)
        ref[0] = mm(gg_ref[:, part], x_all, TN).astype(ref.dtype)
        ref[1] = mm(gu_ref[:, part], x_all, TN).astype(ref.dtype)
        ref[2] = mm(hid_ref[:, part], gs_ref[...], TN).astype(ref.dtype)

    @pl.loop(0, tiles)
    def _(t):
        weight_grad(1 - core, t, dw_out.at[t])
        core_copy(t).start()
        weight_grad(core, t, dw_keep.at[t])
        core_copy(t).wait_recv()
        dw_keep[t] = (dw_keep[t].astype(f32) + dw_in[t].astype(f32)).astype(bf16)
        for c in range(n_cross):

            @pl.when(t == c)
            def _():
                far_copy(c).start()

    keeps = [
        pltpu.make_async_copy(dw_keep.at[t], sum_hbm[t], keep_sem.at[t]) for t in range(tiles)
    ]
    for keep in keeps:
        keep.start()
    for k in range(1, n_dp):
        piece_copy(k).wait()
        dot_copy(k).wait()
        x_copy(k).wait_send()
        gate_copy(k).wait_send()
    for t in range(n_cross):
        far_copy(t).wait()
    for t in range(tiles):
        core_copy(t).wait_send()
    for keep in keeps:
        keep.wait()


def moe_call(n_dp, n_cross, x_slots, gate_slots, weights, grads):
    units = weights.shape[1]
    rows = n_dp * CAP
    tiles = units // UNITS // 2
    part = (3, UNITS, D)
    outs = pl.pallas_call(
        functools.partial(moe_kernel, n_dp, n_cross),
        out_shape=(
            jax.ShapeDtypeStruct((n_dp, CAP, D), bf16),
            jax.ShapeDtypeStruct((n_dp, 1, CAP), f32),
            jax.ShapeDtypeStruct((n_dp, CAP, D), bf16),
        )
        + (jax.ShapeDtypeStruct(part, bf16),) * (tiles + n_cross),
        in_specs=[HBM, VMEM, HBM, VMEM],
        out_specs=[VMEM] * 3 + [HBM] * tiles + [VMEM] * n_cross,
        scratch_shapes=[
            pltpu.VMEM(weights.shape, bf16),
            pltpu.VMEM((n_dp, CAP, D), bf16),
            pltpu.VMEM((n_dp, 1, CAP), f32),
            pltpu.VMEM((rows, D), bf16),
            pltpu.VMEM((rows, units), bf16),
            pltpu.VMEM((rows, units), bf16),
            pltpu.VMEM((rows, units), bf16),
            pltpu.VMEM((n_dp, CAP, D), bf16),
            pltpu.VMEM((n_dp, 1, CAP), f32),
            pltpu.VMEM((tiles, *part), bf16),
            pltpu.VMEM((tiles, *part), bf16),
            pltpu.VMEM((tiles, *part), bf16),
            DMA((4,)),
        ]
        + [DMA((n_dp,))] * 8
        + [DMA((tiles,))] * 2
        + [DMA((max(n_cross, 1),))] * 2
        + [DMA((tiles,))],
        compiler_params=pltpu.CompilerParams(
            collective_id=4, has_side_effects=True, vmem_limit_bytes=67043328
        ),
        name="experts",
    )(x_slots, gate_slots, weights, grads)
    return outs[0], outs[1], outs[2], outs[3 : 3 + tiles], outs[3 + tiles :]


def mid_kernel(
    n_seq, att_ref, h_ref, prev_ref, carry_ref, small_ref, slot_ref, route_ref, w_ref,
    heads_ref, mid_ref, gate_ref, x_ref, gs_ref, send_sem, recv_sem,
):
    me = lax.axis_index("seq")
    tok = h_ref.shape[0]
    greet([{"seq": me ^ place} for place in range(1, n_seq)])
    copies = [
        remote(
            att_ref.at[me ^ place], heads_ref.at[me], (send_sem, recv_sem), place,
            {"seq": me ^ place},
        )
        for place in range(1, n_seq)
    ]
    heads_ref[me] = att_ref[me]
    picks = picks_of(slot_ref)
    pick_any = picks[0] + picks[1]
    carried = lax.dot_general(
        carry_ref[...].astype(f32), prev_ref[:, 0, :], TN, precision=exact_prec,
        preferred_element_type=f32,
    )
    for copy in copies:
        copy.wait_recv()
    attn_out = mm(heads_ref[...].reshape(D, tok), w_ref[...].reshape(D, D), TN)
    resid = h_ref[...].astype(f32) + attn_out
    mid_ref[...] = resid
    rate = lax.rsqrt(jnp.mean(resid * resid, axis=-1, keepdims=True) + 1e-06)
    normed = resid * rate * small_ref[1:2]
    low = normed.astype(bf16)
    x_ref[...] = mm(pick_any, low, NN).astype(bf16).reshape(x_ref.shape)
    heads_rows = small_ref[4 : 8 + H].astype(bf16)
    products = mm(heads_rows, low, NT)
    rest = mm(heads_rows, (normed - low.astype(f32)).astype(bf16), NT)
    logits = products[4:] + carried
    ids = lax.broadcasted_iota(jnp.int32, (H, tok), 0)
    chosen = [
        jnp.sum(jnp.where(route_ref[k : k + 1, :] == ids, logits, 0.0), axis=0, keepdims=True)
        for k in range(2)
    ]
    top = jnp.maximum(chosen[0], chosen[1])
    exps = [jnp.exp(c - top) for c in chosen]
    total = exps[0] + exps[1]
    gates = [e / total for e in exps]
    gate_ref[...] = jnp.concatenate(
        [gates[0], gates[1], products[:4] + rest[:4], jnp.zeros((2, tok), f32)], axis=0
    )
    slot_gates = sum(unsplit(mm(split(gates[k]), picks[k], NT)) for k in range(2))
    for e in range(E):
        gs_ref[e] = slot_gates[:, e * CAP : (e + 1) * CAP]
    for copy in copies:
        copy.wait_send()


def mid_call(n_seq, attended, hidden, prev, carry, small, slot_of, routes, w_out):
    tok, width = hidden.shape[0], attended.shape[1]
    return pl.pallas_call(
        functools.partial(mid_kernel, n_seq),
        out_shape=(
            jax.ShapeDtypeStruct((n_seq, width, tok), bf16),
            jax.ShapeDtypeStruct((tok, D), f32),
            jax.ShapeDtypeStruct((8, tok), f32),
            jax.ShapeDtypeStruct((E, CAP, D), bf16),
            jax.ShapeDtypeStruct((E, 1, CAP), f32),
        ),
        in_specs=[VMEM] * 8,
        out_specs=[VMEM] * 5,
        scratch_shapes=[DMA((n_seq,)), DMA((n_seq,))],
        compiler_params=pltpu.CompilerParams(collective_id=2, has_side_effects=True),
        name="mid",
    )(attended, hidden, prev, carry, small, slot_of, routes, w_out)


def mid_back_kernel(
    n_seq, n_dp, piece_ref, dots_ref, cot_ref, mid_ref, gate_ref, slot_ref, route_ref,
    small_ref, heads_ref, w_ref, prev_ref, carry_ref,
    resid_ref, go_ref, base_ref, dprev_ref, pack_ref, wo_sum_ref,
    gh_ref, wo_ref, wo_in, a_send, a_recv, c_send, c_recv,
):
    me = lax.axis_index("seq")
    tok = cot_ref.shape[0]
    width = heads_ref.shape[1]
    owners = n_dp // E
    pairs = n_seq // 2
    greet([{"seq": me ^ place} for place in range(1, n_seq)])
    cot = cot_ref[...]
    grad_top = cot.astype(f32)
    resid_mid = mid_ref[...]
    gain = small_ref[1:2]
    rate = lax.rsqrt(jnp.mean(resid_mid * resid_mid, axis=-1, keepdims=True) + 1e-06)
    normed = resid_mid * rate * gain
    low = normed.astype(bf16)
    picks = picks_of(slot_ref)
    gates = [gate_ref[k : k + 1, :] for k in range(2)]
    routes = [route_ref[k : k + 1, :] for k in range(2)]
    normed_dot = column_to_row(jnp.sum(grad_top * normed, axis=1, keepdims=True))
    vecs = small_ref[2:4].astype(bf16)
    vec_dot = mm(vecs, cot, NT)
    alphas, const_dot = [], []
    for j in range(2):
        pair = [gate_ref[2 + 2 * j + c : 3 + 2 * j + c, :] for c in range(2)]
        top = jnp.maximum(pair[0], pair[1])
        exps = [jnp.exp(p - top) for p in pair]
        total = exps[0] + exps[1]
        alphas.append([e / total for e in exps])
        const_dot.append(alphas[j][0] * normed_dot + alphas[j][1] * vec_dot[j : j + 1])
    slot_dots = split(
        jnp.concatenate(
            [sum(dots_ref[e * owners + o] for o in range(owners)) for e in range(E)], axis=1
        )
    )
    out_dots = []
    for k in range(2):
        value = unsplit(mm(slot_dots, picks[k], NN))
        value = value + jnp.where(routes[k] == E + 1, normed_dot, 0.0)
        for j in range(2):
            value = value + jnp.where(routes[k] == E + 2 + j, const_dot[j], 0.0)
        out_dots.append(value)
    mean_dot = gates[0] * out_dots[0] + gates[1] * out_dots[1]
    ids = lax.broadcasted_iota(jnp.int32, (H, tok), 0)
    grad_logits = sum(
        jnp.where(routes[k] == ids, gates[k] * (out_dots[k] - mean_dot), 0.0) for k in range(2)
    )

    def gate_of(expert):
        return sum(jnp.where(routes[k] == expert, gates[k], 0.0) for k in range(2))

    const_gate = [gate_of(E + 2 + j) for j in range(2)]
    normed_gate = gate_of(E + 1) + sum(const_gate[j] * alphas[j][0] for j in range(2))
    vec_gate = split(jnp.concatenate([const_gate[j] * alphas[j][1] for j in range(2)], axis=0))
    mix_grads = []
    for j in range(2):
        terms = [normed_dot, vec_dot[j : j + 1]]
        for c in range(2):
            mix_grads.append(const_gate[j] * alphas[j][c] * (terms[c] - const_dot[j]))
    token_rows = split(jnp.concatenate(mix_grads + [grad_logits], axis=0))
    normed_column = jnp.broadcast_to(normed_gate, (8, tok)).T[:, 0:1]
    heads_rows = small_ref[4 : 8 + H].astype(bf16)
    pick_any = picks[0] + picks[1]
    grad_normed = grad_top * normed_column
    grad_normed = grad_normed + mm(
        token_rows, jnp.concatenate([heads_rows] * 3, axis=0), TN
    )
    pieces = piece_ref[...].reshape(E, owners, CAP, D)
    for o in range(owners):
        grad_normed = grad_normed + mm(pick_any, pieces[:, o].reshape(E * CAP, D), TN)
    grad_resid = grad_top + norm_back(resid_mid, gain, grad_normed)
    resid_ref[...] = grad_resid
    grad_attn = grad_resid.astype(bf16)
    gh_ref[...] = mm(w_ref[...].reshape(D, D), grad_attn, NT).astype(bf16).reshape(gh_ref.shape)
    copies = [
        remote(gh_ref.at[me ^ place], go_ref.at[me], (a_send, a_recv), place, {"seq": me ^ place})
        for place in range(1, n_seq)
    ]
    go_ref[me] = gh_ref[me]
    grad_w = mm(heads_ref[...].reshape(D, tok), grad_attn, NN)
    for j in range(n_seq):
        wo_ref[j] = grad_w[:, j * width : (j + 1) * width].astype(bf16)
    core_copies = [
        remote(wo_ref.at[me ^ (2 * i + 1)], wo_in.at[i], (c_send, c_recv), i, {"seq": me ^ 1})
        for i in range(pairs)
    ]
    base_ref[...] = (
        resid_mid
        + normed * normed_column
        + mm(vec_gate, jnp.concatenate([vecs] * 3, axis=0), TN)
    )
    dprev_ref[:, 0, :] = lax.dot_general(
        carry_ref[...].astype(f32), grad_logits, NN, precision=exact_prec,
        preferred_element_type=f32,
    )
    rest = (normed - low.astype(f32)).astype(bf16)
    row_sums = unsplit(mm(token_rows, low, NN))
    mix_sums = row_sums[:4] + unsplit(mm(token_rows, rest, NN))[:4]
    vec_sums = unsplit(mm(vec_gate, cot, NN))
    gain_sum = jnp.sum(grad_normed * resid_mid * rate, axis=0, keepdims=True)
    carry_grad = lax.dot_general(
        prev_ref[:, 0, :], grad_logits, NT, precision=exact_prec, preferred_element_type=f32
    )
    packed = jnp.concatenate([mix_sums, row_sums[4:], vec_sums, gain_sum], axis=0)
    lines, shard = packed.shape[0], D // n_dp
    for i in range(n_dp):
        pack_ref[i] = jnp.zeros(pack_ref.shape[1:], f32)
        pack_ref[i, 0:lines, :] = packed[:, i * shard : (i + 1) * shard]
        pack_ref[i, 24 : 24 + H, 0:H] = carry_grad
    for i in range(pairs):
        core_copies[i].wait_recv()
        wo_sum_ref[i] = (
            wo_ref[me ^ (2 * i)].astype(f32) + wo_in[i].astype(f32)
        ).astype(bf16)
    for copy in copies:
        copy.wait()
    for copy in core_copies:
        copy.wait_send()


def mid_back_call(
    n_seq, n_dp, piece, dots, cot, mid, gates, slot_of, routes, small, heads, w, prev, carry
):
    tok, width = cot.shape[0], heads.shape[1]
    pairs = n_seq // 2
    return pl.pallas_call(
        functools.partial(mid_back_kernel, n_seq, n_dp),
        out_shape=(
            jax.ShapeDtypeStruct((tok, D), f32),
            jax.ShapeDtypeStruct((n_seq, width, tok), bf16),
            jax.ShapeDtypeStruct((tok, D), f32),
            jax.ShapeDtypeStruct((H, 1, tok), f32),
            jax.ShapeDtypeStruct((n_dp, LINES, D // n_dp), f32),
            jax.ShapeDtypeStruct((pairs, D, width), bf16),
        ),
        in_specs=[VMEM] * 12,
        out_specs=[VMEM] * 6,
        scratch_shapes=[
            pltpu.VMEM((n_seq, width, tok), bf16),
            pltpu.VMEM((n_seq, D, width), bf16),
            pltpu.VMEM((pairs, D, width), bf16),
            DMA((n_seq,)),
            DMA((n_seq,)),
            DMA((pairs,)),
            DMA((pairs,)),
        ],
        compiler_params=pltpu.CompilerParams(collective_id=3, has_side_effects=True),
        name="mid_back",
    )(piece, dots, cot, mid, gates, slot_of, routes, small, heads, w, prev, carry)


def tail_kernel(
    n_seq, n_dp, tiles, g_ref, wt_ref, wo_ref, pack_ref, gate_ref, slot_ref, gain_ref,
    a_hbm, h_hbm, resid_hbm, base_hbm, out_hbm, *refs,
):
    sum_hbm, refs = refs[:tiles], refs[tiles:]
    n_far = tiles - 1
    far_hbm, refs = refs[:n_far], refs[n_far:]
    din_ref, row_in, line_ref, block_ref, both_ref, refs = *refs[:5], refs[5:]
    (
        a_ref, h_ref, resid_ref, base_ref, rows_ref, far_ref, sum_ref, fin_ref,
        core_out, core_in, x_out, x_in, part_ref, w_out_buf, w_in, wo_buf, wo_in, wo_x, wo_far,
        row_buf, pack_in, line_buf, line_in, load_sem, c_sems, x_sems, w_sems, r_sems, o_sems,
        p_sems, q_sems, l_sems, t_sems, f_sems, keep_sem,
    ) = refs
    me, dp = lax.axis_index("seq"), lax.axis_index("dp")
    tok = h_ref.shape[0]
    shard, width3 = w_in.shape[1], w_in.shape[2]
    width = width3 // 3
    owners = n_dp // E
    pairs = n_seq // 2
    others = range(1, n_dp)

    def both(sems):
        return sems.at[0], sems.at[1]

    c_sems, x_sems, w_sems, r_sems, o_sems, p_sems, q_sems, l_sems, t_sems, f_sems = (
        both(sems)
        for sems in (
            c_sems, x_sems, w_sems, r_sems, o_sems, p_sems, q_sems, l_sems, t_sems, f_sems
        )
    )

    loads = []
    for src, dst in [
        (a_hbm, a_ref), (out_hbm, rows_ref), (base_hbm, base_ref), (h_hbm, h_ref),
        (resid_hbm, resid_ref),
    ] + [(far_hbm[t], far_ref.at[t]) for t in range(n_far)] + [
        (sum_hbm[t], sum_ref.at[t]) for t in range(n_far)
    ]:
        load = pltpu.make_async_copy(src, dst, load_sem.at[len(loads)])
        load.start()
        loads.append(load)
    greet(
        [{"seq": me ^ place} for place in range(1, n_seq)]
        + [{"dp": lax.rem(dp + k, n_dp)} for k in others]
    )

    def there(k):
        return lax.rem(dp + k, n_dp)

    def term(place):
        columns = pl.ds(pl.multiple_of((me ^ place) * tok, tok), tok)
        return mm(g_ref[:, columns], wt_ref[...], TN)

    last, cut = sum_hbm[tiles - 1], UNITS // 2
    tile_copies = []

    def send_part(i):
        part = pl.ds(i * cut, cut)
        tile_copies.append(
            remote(last.at[:, part], far_ref.at[tiles - 1, :, part], t_sems, i, {"seq": me ^ 2})
        )

    send_part(0)
    last_load = pltpu.make_async_copy(last, sum_ref.at[tiles - 1], load_sem.at[len(loads)])
    last_load.start()
    pack_copies = [
        remote(pack_ref.at[there(k)], pack_in.at[dp], p_sems, k, {"dp": there(k)}) for k in others
    ]
    pack_in[dp] = pack_ref[dp]
    for i in range(pairs):
        wo_buf[:, :, i * width : (i + 1) * width] = wo_ref[i].reshape(n_dp, shard, width)
    wo_in[dp] = wo_buf[dp]
    wo_copies = [
        remote(wo_buf.at[there(k)], wo_in.at[dp], q_sems, k, {"dp": there(k)}) for k in others
    ]
    core_copies = []
    for i in range(pairs - 1, -1, -1):
        core_out[i] = term(2 * i + 1).astype(bf16)
        core_copies.insert(0, remote(core_out.at[i], core_in.at[i], c_sems, i, {"seq": me ^ 1}))
    x_copies = []
    for i in range(pairs - 1, 0, -1):
        part = term(2 * i)
        core_copies[i].wait_recv()
        x_out[i - 1] = (part + core_in[i].astype(f32)).astype(bf16)
        x_copies.append(
            remote(x_out.at[i - 1], x_in.at[i - 1], x_sems, i - 1, {"seq": me ^ (2 * i)})
        )
    send_part(1)
    loads[0].wait()
    turned = mm(g_ref[...], a_ref[...], NN)
    w_out_buf[...] = turned.T.astype(bf16).reshape(n_dp, shard, width3)
    w_in[dp] = w_out_buf[dp]
    w_copies = [
        remote(w_out_buf.at[there(k)], w_in.at[dp], w_sems, k, {"dp": there(k)}) for k in others
    ]
    part = term(0)
    core_copies[0].wait_recv()
    part_ref[...] = part + core_in[0].astype(f32)

    for copy in pack_copies:
        copy.wait_recv()
    line_buf[...] = jnp.sum(pack_in[...], axis=0)
    line_in[me] = line_buf[...]
    line_copies = [
        remote(line_buf, line_in.at[me], l_sems, place, {"seq": me ^ place})
        for place in range(1, n_seq)
    ]

    fin_copies, keeps = [], []

    def finish(t):
        fin_ref[t] = (sum_ref[t].astype(f32) + far_ref[t].astype(f32)).astype(bf16)
        fin_copies.append(remote(fin_ref.at[t], both_ref.at[1, t], f_sems, t, {"seq": me ^ 1}))
        keep = pltpu.make_async_copy(fin_ref.at[t], both_ref.at[0, t], keep_sem.at[t])
        keep.start()
        keeps.append(keep)

    for t in range(n_far):
        loads[5 + t].wait()
        loads[5 + n_far + t].wait()
        finish(t)

    for copy in wo_copies:
        copy.wait_recv()
    wo_total = jnp.sum(wo_in[...].astype(f32), axis=0)
    wo_cross = []
    for i in range(1, pairs):
        wo_x[i - 1] = wo_total[:, i * width : (i + 1) * width].astype(bf16)
        wo_cross.append(
            remote(wo_x.at[i - 1], wo_far.at[i - 1], o_sems, i - 1, {"seq": me ^ (2 * i)})
        )

    loads[1].wait()
    loads[2].wait()
    picks = picks_of(slot_ref)
    rows = rows_ref[...].reshape(E, owners, CAP, D)
    columns = gate_ref[...].T
    block = base_ref[...]
    for k in range(2):
        picked = sum(
            mm(picks[k], rows[:, o].reshape(E * CAP, D), TN) for o in range(owners)
        )
        block = block + columns[:, k : k + 1] * picked
    block_ref[...] = block.astype(bf16)

    for copy in x_copies:
        copy.wait_recv()
    grad = part_ref[...]
    for i in range(pairs - 1):
        grad = grad + x_in[i].astype(f32)
    loads[3].wait()
    loads[4].wait()
    din_ref[...] = resid_ref[...] + norm_back(h_ref[...].astype(f32), gain_ref[0:1], grad)

    for copy in w_copies + wo_cross:
        copy.wait_recv()
    row_buf[:, :width3] = jnp.sum(w_in[...].astype(f32), axis=0).astype(bf16)
    wo_mine = wo_total[:, :width]
    for i in range(pairs - 1):
        wo_mine = wo_mine + wo_far[i].astype(f32)
    row_buf[:, width3:] = wo_mine.astype(bf16)
    row_in[me] = row_buf[...]
    row_copies = [
        remote(row_buf, row_in.at[me], r_sems, place, {"seq": me ^ place})
        for place in range(1, n_seq)
    ]
    for copy in line_copies:
        copy.wait_recv()
    line_ref[...] = jnp.sum(line_in[...], axis=0)
    last_load.wait()
    for copy in tile_copies:
        copy.wait_recv()
    finish(tiles - 1)
    for copy in row_copies + fin_copies:
        copy.wait_recv()
    for copy in (
        core_copies + w_copies + x_copies + row_copies + wo_copies + pack_copies
        + line_copies + wo_cross + tile_copies + fin_copies
    ):
        copy.wait_send()
    for keep in keeps:
        keep.wait()


def tail_call(
    n_seq, n_dp, grad_qkv, w_turned, wo_sum, pack, gates, slot_of, small,
    attn_in, hidden, grad_resid, base, back_out, sums, far,
):
    tok = hidden.shape[0]
    shard, width3 = D // n_dp, grad_qkv.shape[0]
    width = width3 // 3
    pairs = n_seq // 2
    tiles = len(sums)
    part = sums[0].shape
    return pl.pallas_call(
        functools.partial(tail_kernel, n_seq, n_dp, tiles),
        out_shape=(
            jax.ShapeDtypeStruct((tok, D), f32),
            jax.ShapeDtypeStruct((n_seq, shard, width3 + width), bf16),
            jax.ShapeDtypeStruct((LINES, shard), f32),
            jax.ShapeDtypeStruct((tok, D), bf16),
            jax.ShapeDtypeStruct((2, tiles, *part), bf16),
        ),
        in_specs=[VMEM] * 7 + [HBM] * (5 + tiles + len(far)),
        out_specs=[VMEM] * 4 + [HBM],
        scratch_shapes=[
            pltpu.VMEM((n_seq * tok, D), bf16),
            pltpu.VMEM((tok, D), bf16),
            pltpu.VMEM((tok, D), f32),
            pltpu.VMEM((tok, D), f32),
            pltpu.VMEM((n_dp, CAP, D), bf16),
            pltpu.VMEM((tiles, *part), bf16),
            pltpu.VMEM((tiles, *part), bf16),
            pltpu.VMEM((tiles, *part), bf16),
            pltpu.VMEM((pairs, tok, D), bf16),
            pltpu.VMEM((pairs, tok, D), bf16),
            pltpu.VMEM((pairs - 1, tok, D), bf16),
            pltpu.VMEM((pairs - 1, tok, D), bf16),
            pltpu.VMEM((tok, D), f32),
            pltpu.VMEM((n_dp, shard, width3), bf16),
            pltpu.VMEM((n_dp, shard, width3), bf16),
            pltpu.VMEM((n_dp, shard, pairs * width), bf16),
            pltpu.VMEM((n_dp, shard, pairs * width), bf16),
            pltpu.VMEM((pairs - 1, shard, width), bf16),
            pltpu.VMEM((pairs - 1, shard, width), bf16),
            pltpu.VMEM((shard, width3 + width), bf16),
            pltpu.VMEM((n_dp, LINES, shard), f32),
            pltpu.VMEM((LINES, shard), f32),
            pltpu.VMEM((n_seq, LINES, shard), f32),
            DMA((4 + 2 * tiles,)),
            DMA((2, pairs)),
            DMA((2, pairs)),
            DMA((2, n_dp)),
            DMA((2, n_seq)),
            DMA((2, pairs)),
            DMA((2, n_dp)),
            DMA((2, n_dp)),
            DMA((2, n_seq)),
            DMA((2, 2)),
            DMA((2, tiles)),
            DMA((tiles,)),
        ],
        compiler_params=pltpu.CompilerParams(
            collective_id=1, has_side_effects=True, vmem_limit_bytes=67043328
        ),
        name="tail",
    )(
        grad_qkv, w_turned, wo_sum, pack, gates, slot_of, small,
        attn_in, hidden, grad_resid, base, back_out, *sums, *far,
    )


def finish_kernel(
    n_seq, me_ref, both_ref, row_ref, line_ref, wq_ref, gain_ref,
    de_ref, dw_ref, dwo_ref, again_ref, mgain_ref, router_ref, carry_ref, vec_ref, mix_ref,
):
    de_ref[...] = both_ref[0, 0].astype(f32)

    @pl.when(pl.program_id(0) == 0)
    def _():
        width = row_ref.shape[2] // 4
        for j in range(n_seq):
            block = row_ref[j].astype(f32)
            for c in range(3):
                left = c * width * n_seq + j * width
                dw_ref[:, left : left + width] = block[:, c * width : (c + 1) * width]
            dwo_ref[:, j * width : (j + 1) * width] = block[:, 3 * width :]
        sums = jnp.sum(dw_ref[...] * wq_ref[...].astype(f32), axis=1, keepdims=True)
        again_ref[...] = column_to_row(sums) / gain_ref[...].astype(f32)
        mix_ref[0] = line_ref[0:2]
        mix_ref[1] = line_ref[2:4]
        router_ref[...] = line_ref[4 : 4 + H]
        vec_ref[...] = line_ref[4 + H : 6 + H]
        mgain_ref[...] = line_ref[6 + H : 7 + H]
        carry_ref[...] = line_ref[24 : 24 + H, 0:H]


def finish_call(n_seq, me, both, row_in, lines, w_qkv, attn_gain):
    shard = w_qkv.shape[0]
    _, tiles, three, step, _ = both.shape
    units = 2 * tiles * step

    def whole(shape):
        return pl.BlockSpec(shape, lambda i, me_ref: (0,) * len(shape))

    shapes = [(shard, 3 * D), (shard, D), (1, shard), (1, shard), (H, shard), (H, H), (2, shard),
              (2, 2, shard)]
    return pl.pallas_call(
        functools.partial(finish_kernel, n_seq),
        out_shape=[jax.ShapeDtypeStruct((three, units, D), f32)]
        + [jax.ShapeDtypeStruct(shape, f32) for shape in shapes],
        grid_spec=pltpu.PrefetchScalarGridSpec(
            num_scalar_prefetch=1,
            grid=(2 * tiles,),
            in_specs=[
                pl.BlockSpec(
                    (1, 1, three, step, D),
                    lambda i, me_ref: ((i // tiles) ^ (me_ref[0] & 1), i % tiles, 0, 0, 0),
                ),
                whole(row_in.shape),
                whole(lines.shape),
                whole(w_qkv.shape),
                whole((1, shard)),
            ],
            out_specs=[pl.BlockSpec((three, step, D), lambda i, me_ref: (0, i, 0))]
            + [whole(shape) for shape in shapes],
        ),
        name="finish",
    )(me, both, row_in, lines, w_qkv, attn_gain[None])


def rope_tables(seq_len):
    freq_index = jnp.arange(HD // 2, dtype=f32)
    inv_freq = jnp.exp(freq_index * (-2.0 * math.log(10000.0) / HD))
    angles = jnp.arange(seq_len, dtype=jnp.int32).astype(f32)[None, :] * inv_freq[:, None]
    return jnp.cos(angles), jnp.sin(angles)


def per_device(
    hidden_in,
    prev_logits,
    segments,
    routes,
    attn_gain,
    w_qkv,
    w_out,
    moe_gain,
    w_router,
    w_carry,
    const_vec,
    const_mix,
    experts,
    cotangent,
):
    n_seq, n_dp = lax.axis_size("seq"), lax.axis_size("dp")
    owners = n_dp // E
    me = lax.axis_index("seq")
    tok = hidden_in.shape[1]
    hidden, cot = hidden_in[0], cotangent[0]
    prev_t = jnp.transpose(prev_logits, (2, 0, 1))
    routes_t = routes[0].T

    def to_owners(values):
        return lax.all_to_all(
            jnp.repeat(values, owners, axis=0), "dp", split_axis=0, concat_axis=0, tiled=True
        )

    def to_sources(values):
        return lax.all_to_all(values, "dp", split_axis=0, concat_axis=0, tiled=True)

    cos_t, sin_t = rope_tables(tok * n_seq)
    attn_in, qkv, w_turned, small, slot_of, grad_slots, out_weight = start_call(
        n_seq, n_dp, hidden, w_qkv, attn_gain, moe_gain, const_vec, const_mix, w_router.T,
        routes_t, cot, cos_t, sin_t, w_out,
    )
    arrived_grad = to_owners(grad_slots)

    seg_row = segments[0]
    doc_ids = jnp.arange(16, dtype=jnp.int32)
    doc_start = jnp.sum((seg_row[None, :] < doc_ids[:, None]).astype(jnp.int32), axis=1)
    start = jnp.sum(jnp.where(seg_row[None, :] == doc_ids[:, None], doc_start[:, None], 0), axis=0)
    start_row = start.astype(jnp.int32)[None, :]
    lows = start[::BLK].astype(jnp.int32) // BLK
    attended, attended_exact, logs = attn_call(lows, qkv, start_row, tok)

    heads_t, resid_mid, gates, x_slots, gate_slots = mid_call(
        n_seq, attended, hidden, prev_t, w_carry, small, slot_of, routes_t, out_weight
    )
    tiles = experts.shape[1] // UNITS // 2
    n_cross = 1 if tiles > 1 else 0
    piece, dots, partial, sums, far = moe_call(
        n_dp, n_cross, x_slots, gate_slots, experts, arrived_grad
    )
    far = list(far) + [swap(part, "seq", 2) for part in sums[n_cross : min(2, tiles - 1)]]
    back_out = to_sources(partial)

    grad_resid, grad_out, base, d_prev, pack, wo_sum = mid_back_call(
        n_seq, n_dp, piece, dots, cot, resid_mid, gates, slot_of, routes_t, small, heads_t,
        out_weight, prev_t, w_carry,
    )
    later, grad_out = lax.optimization_barrier((list(sums[2 : tiles - 1]), grad_out))
    far += [swap(part, "seq", 2) for part in later]
    grad_qkv = attn_back_call(
        lows, qkv, grad_out, attended_exact, logs, start_row, cos_t, sin_t
    )
    d_input, row_in, lines, block_out, both = tail_call(
        n_seq, n_dp, grad_qkv, w_turned, wo_sum, pack, gates, slot_of, small,
        attn_in, hidden, grad_resid, base, back_out, sums, far,
    )
    d_experts, d_qkv, d_out, again, mgain, router, carry, vec, mix = finish_call(
        n_seq, me.astype(jnp.int32).reshape(1), both, row_in, lines, w_qkv, attn_gain
    )
    return (
        block_out[None],
        d_input[None],
        jnp.transpose(d_prev, (1, 2, 0)),
        again[0],
        d_qkv,
        d_out,
        mgain[0],
        router.T,
        carry,
        vec,
        mix,
        d_experts,
    )


def solution(mesh):
    return jax.shard_map(
        per_device,
        mesh=mesh,
        in_specs=(
            P("dp", "seq", None),
            P("dp", "seq", None),
            P("dp", None),
            P("dp", "seq", None),
            P("dp"),
            P("dp", None),
            P("dp", None),
            P("dp"),
            P("dp", None),
            P(),
            P(None, "dp"),
            P(None, None, "dp"),
            P(None, "dp", None),
            P("dp", "seq", None),
        ),
        out_specs=(
            P("dp", "seq", None),
            P("dp", "seq", None),
            P("dp", "seq", None),
            P("dp"),
            P("dp", None),
            P("dp", None),
            P("dp"),
            P("dp", None),
            P(),
            P(None, "dp"),
            P(None, None, "dp"),
            P(None, "dp", None),
        ),
        check_vma=False,
    )
```

time: 426 us -> 353 us (0.83)
  starting transfers between devices: 39.6 us -> 11.4 us
  other arithmetic: 24.7 us -> 2.58 us
  local copies, waits for them, and re-layouts: 23.6 us -> 3.55 us
  Pallas kernels: 320 us -> 302 us
  waiting for transfers between devices: 12.9 us -> 29.7 us
    ppermute x25 -> x2, starting transfers between devices: 39.6 us -> 1.55 us  [swap(): return lax.ppermute(value, axis, [(i, i ^ bit) for i in range(size)])]
    pallas_call x1, Pallas kernels: 54.7 us -> 20.9 us  [mid_back_call(): pl.pallas_call(functools.partial(mid_back_kernel, n_seq, n_dp), out_shape...]
    ppermute x25 -> x2, waiting for transfers between devices: 12.9 us -> 29.7 us  [swap(): return lax.ppermute(value, axis, [(i, i ^ bit) for i in range(size)])]
    convert_element_type x4 -> x0, other arithmetic: 13.8 us -> none  [the longest x1 8.72 us: per_device(): d_experts = jnp.concatenate([jnp.where(core == 0, mine, other), jnp.where...]
    pallas_call x1, Pallas kernels: 34.8 us -> 47.7 us  [start_call(): pl.pallas_call(functools.partial(start_kernel, n_seq, n_dp), out_shape=(j...]
    unnamed x84 -> x19, local copies, waits for them, and re-layouts: 15.8 us -> 3.46 us
    pallas_call x1, Pallas kernels: 88.7 us -> 100 us  [moe_call(): pl.pallas_call(functools.partial(moe_kernel, n_dp, n_cross), out_shape=(j...]
    all_to_all x0 -> x2, starting transfers between devices: none -> 9.86 us  [the longest x1 5.36 us: to_owners(): lax.all_to_all(jnp.repeat(values, owners, axis=0), 'dp', split_axis=0, co...]
  transfers between devices with their start and end apart: 25 -> 4, of which waited for: 2 -> 2; matrix products, arithmetic and copies ran while one was open for 4% -> 0% of each run, Pallas kernels for 55% -> 23%
where the time goes in v4:
time: 353 us; the launch traced here: 350 us
  Pallas kernels  302 us (86%)
  waiting for transfers between devices  29.7 us (8%)
  starting transfers between devices  11.4 us (3%)
  local copies, waits for them, and re-layouts  3.55 us (1%)
    pallas_call x1, Pallas kernels, moe_call(): pl.pallas_call(functools.partial(moe_kernel, n_dp, n_cross), out_shape=(j...  100 us
    pallas_call x1, Pallas kernels, tail_call(): pl.pallas_call(functools.partial(tail_kernel, n_seq, n_dp, tiles), out_sh...  60 us
    pallas_call x1, Pallas kernels, start_call(): pl.pallas_call(functools.partial(start_kernel, n_seq, n_dp), out_shape=(j...  47.7 us
    ppermute x2, waiting for transfers between devices, swap(): return lax.ppermute(value, axis, [(i, i ^ bit) for i in range(size)])  29.7 us
    pallas_call x1, Pallas kernels, attn_back_call(): pl.pallas_call(attn_back_kernel, out_shape=jax.ShapeDtypeStruct((width3,...  21.9 us
    pallas_call x1, Pallas kernels, mid_back_call(): pl.pallas_call(functools.partial(mid_back_kernel, n_seq, n_dp), out_shape...  20.9 us
    pallas_call x1, Pallas kernels, attn_call(): pl.pallas_call(attn_kernel, out_shape=(jax.ShapeDtypeStruct((seq_len // t...  19.9 us
    pallas_call x1, Pallas kernels, mid_call(): pl.pallas_call(functools.partial(mid_kernel, n_seq), out_shape=(jax.Shape...  18.4 us
  transfers between devices with their start and end apart: 4, of which 2 were waited for; matrix products, arithmetic and copies ran while one was open for 0% of the time, Pallas kernels for 23%

profile of v4, /device:TPU:13, one launch (start us, length us, event | category | flops | bytes accessed | tf_op | source)
XLA Modules:
  0.0 349.7 jit_solution(10228576975084305231)
XLA Ops:
  0.7 1.8 multiply_sine_fusion
  2.5 47.7 %start.1 = (bf16[2048,768]{1,0:T(8,128)(2,1)}, bf16[576,2048]{1,0:T(8,128)(2,1)}, bf16[576,768]{1,0:T(8,128)(2,1)}, f32[32,768]{1,0:T(8,128)}, s32[2,512]{1,0:T(...) custom-call(bf16[512,768]{1,0:T(8,128)(2,1)} %bitcast.18, bf16[96,2304]{1,0:T(8,128)(2,1)} %wq_ref.1, ...), custom_call_target="tpu_custom_call" | custom-call | tf_op jit(solution)/shard_map/start/pallas_call | solution.py:248
  50.2 0.0 copy-start.5
  50.2 5.4 %all-to-all-start = ((bf16[8,128,768]{2,1,0:T(8,128)(2,1)}), bf16[8,128,768]{2,1,0:T(8,128)(2,1)}, u32[]{:S(2)}, u32[]{:S(2)}) async-start(bf16[8,128,768]{2,1,0:T(8,128)(2,1)} %get-tuple-element.64), calls=%async_computation | async-start | bytes 3145728 | tf_op jit(solution)/shard_map/all_to_all | solution.py:1240
  55.6 0.0 copy-done.5
  55.6 0.1 convert_reduce_fusion
  55.7 0.1 select_reduce_fusion
  55.8 0.0 copy-start.7
  55.8 0.1 slice.3
  55.9 0.5 and_select_fusion.lo_ref
  56.5 0.0 copy-done.7
  56.5 19.9 %attend.1 = (bf16[4,192,512]{2,1,0:T(8,128)(2,1)}, f32[192,2048]{1,0:T(8,128)}, f32[3,2048]{1,0:T(4,128)}) custom-call(s32[8]{0:T(128)} %and_select_fusion.lo_ref, bf16[576,2048]{1,0:T(8,128)(2,1)} %get-tuple-element.57.qkv_ref, s32[1,2048]{1,0:T(1,128)} %bitcast.33), custom_call_target="tpu_custom_call" | custom-call | flops 16000000000 | bytes 16000000 | tf_op jit(solution)/shard_map/attend/pallas_call | solution.py:342
  76.4 18.4 %mid.1 = (bf16[4,192,512]{2,1,0:T(8,128)(2,1)}, f32[512,768]{1,0:T(8,128)}, f32[8,512]{1,0:T(8,128)}, bf16[8,128,768]{2,1,0:T(8,128)(2,1)}, f32[8,1,128]{2,1,0:T(1,128)}) custom-call(bf16[4,192,512]{2,1,0:T(8,128)(2,1)} %get-tuple-element.58.att_ref, bf16[512,768]{1,0:T(8,128)(2,1)} %bitcast.19, f32[12,1,512]{2,1,0:T(1,128)} %bitcast.25, ...), custom_call_target="tpu_custom_call" | custom-call | tf_op jit(solution)/shard_map/mid/pallas_call | solution.py:725
  94.8 0.0 all-to-all-done.g_ref
  94.9 100.1 %experts.1 = (bf16[8,128,768]{2,1,0:T(8,128)(2,1)}, f32[8,1,128]{2,1,0:T(1,128)}, bf16[8,128,768]{2,1,0:T(8,128)(2,1)}, bf16[3,256,768]{2,1,0:T(8,128)(2,1)}, bf...) custom-call(bf16[8,128,768]{2,1,0:T(8,128)(2,1)} %get-tuple-element., ...), custom_call_target="tpu_custom_call" | custom-call | tf_op jit(solution)/shard_map/experts/pallas_call | solution.py:633
  195.0 4.5 %all-to-all-start.1 = ((bf16[8,128,768]{2,1,0:T(8,128)(2,1)}), bf16[8,128,768]{2,1,0:T(8,128)(2,1)}, u32[]{:S(2)}, u32[]{:S(2)}) async-start(bf16[8,128,768]{2,1,0:T(8,128)(2,1)} %get-tuple-element.81), calls=%async_computation.1 | async-start | bytes 3145728 | tf_op jit(solution)/shard_map/all_to_all | solution.py:1245
  199.5 0.0 copy-start.2
  199.5 0.0 copy-start.1
  199.5 20.9 %mid_back.1 = (f32[512,768]{1,0:T(8,128)}, bf16[4,192,512]{2,1,0:T(8,128)(2,1)}, f32[512,768]{1,0:T(8,128)}, f32[12,1,512]{2,1,0:T(1,128)}, f32[8,40,96]{2,1,0:T(8,128)}, /*index=5*/bf16[2,768,192]{2,1,0:T(8,128)(2,1)}) custom-call(bf16[8,128,768]{2,1,0:T(8,128)(2,1)} %get-tuple-element.66.piece_ref, f32[8,1,128]{2,1,0:T(1,128)} %get-tuple-element.67.dots_ref, ...), custom_call_target="tpu_custom_call" | custom-call | tf_op jit(solution)/shard_map/mid_back/pallas_call | solution.py:870
  220.4 0.0 copy-done.2
  220.5 0.5 collective-permute-start.1
  221.0 1.0 collective-permute-start
  222.0 21.9 %attend_back.1.g_ref = bf16[576,2048]{1,0:T(8,128)(2,1)} custom-call(s32[8]{0:T(128)} %and_select_fusion.lo_ref, bf16[576,2048]{1,0:T(8,128)(2,1)} %get-tuple-element.57.qkv_ref, bf16[4,192,512]{2,1,0:T(8,128)(2,1)} %get-tuple-element.72.go_ref, f32[192,2048]{1,0:T(8,128)} %get-tuple-element.73.exact_ref, f32[3,2048]{1,0:T(4,128)} %get-tuple-element.74.log_ref, ...), custom_call_target="tpu_custom_call" | custom-call | flops 16000000000 | bytes 16000000 | tf_op jit(solution)/shard_map/attend_back/pallas_call | solution.py:446
  243.9 4.3 %collective-permute-done.1.refs_6_ = bf16[3,256,768]{2,1,0:T(8,128)(2,1)S(1)} collective-permute-done((bf16[3,256,768]{2,1,0:T(8,128)(2,1)S(1)}, bf16[3,256,768]{2,1,0:T(8,128)(2,1)S(1)}, u32[]{:S(2)}, u32[]{:S(2)}) %collective-permute-start.1) | collective-permute-done | bytes 1179680 | tf_op jit(solution)/shard_map/ppermute | solution.py:46
  248.2 25.4 %collective-permute-done.refs_5_ = bf16[3,256,768]{2,1,0:T(8,128)(2,1)} collective-permute-done((bf16[3,256,768]{2,1,0:T(8,128)(2,1)S(1)}, bf16[3,256,768]{2,1,0:T(8,128)(2,1)}, u32[]{:S(2)}, u32[]{:S(2)}) %collective-permute-start) | collective-permute-done | bytes 1179680 | tf_op jit(solution)/shard_map/ppermute | solution.py:46
  273.6 0.0 all-to-all-done.1.out_hbm
  273.6 60.0 %tail.1 = (f32[512,768]{1,0:T(8,128)}, bf16[4,96,768]{2,1,0:T(8,128)(2,1)}, f32[40,96]{1,0:T(8,128)}, bf16[512,768]{1,0:T(8,128)(2,1)}, bf16[2,4,3,256,768]{4,3,2,1,0:T(8,128)(2,1)}) custom-call(bf16[576,2048]{1,0:T(8,128)(2,1)} %attend_back.1.g_ref, bf16[576,768]{1,0:T(8,128)(2,1)} %get-tuple-element.75.wt_ref, ...), custom_call_target="tpu_custom_call" | custom-call | tf_op jit(solution)/shard_map/tail/pallas_call | solution.py:1091
  333.6 12.7 %finish.1 = (f32[3,2048,768]{2,1,0:T(8,128)}, f32[96,2304]{1,0:T(8,128)}, f32[96,768]{1,0:T(8,128)}, f32[1,96]{1,0:T(1,128)}, f32[1,96]{1,0:T(1,128)}, /*index=5...) custom-call(s32[1]{0:T(128)} %bitcast.14.me_ref, ...), custom_call_target="tpu_custom_call" | custom-call | tf_op jit(solution)/shard_map/finish/pallas_call | solution.py:1184
  346.3 0.9 copy.29
  347.2 0.8 copy-done
  348.0 1.1 copy.30
  349.1 0.6 copy.31
  (10 shorter events, 0.0 us)
Async XLA Ops:
  50.2 5.4 %copy-start.5 = (s32[1,2048]{1,0:T(1,128)S(1)}, s32[1,2048]{1,0:T(1,128)}, u32[]{:S(2)}) copy-start(s32[1,2048]{1,0:T(1,128)} %param.16) | copy-start | bytes 24580
  50.2 44.6 %all-to-all-start = ((bf16[8,128,768]{2,1,0:T(8,128)(2,1)}), bf16[8,128,768]{2,1,0:T(8,128)(2,1)}, u32[]{:S(2)}, u32[]{:S(2)}) async-start(bf16[8,128,768]{2,1,0:T(8,128)(2,1)} %get-tuple-element.64), calls=%async_computation | async-start | bytes 3145728 | tf_op jit(solution)/shard_map/all_to_all | solution.py:1240
  55.8 0.6 copy-start.7
  195.0 78.7 %all-to-all-start.1 = ((bf16[8,128,768]{2,1,0:T(8,128)(2,1)}), bf16[8,128,768]{2,1,0:T(8,128)(2,1)}, u32[]{:S(2)}, u32[]{:S(2)}) async-start(bf16[8,128,768]{2,1,0:T(8,128)(2,1)} %get-tuple-element.81), calls=%async_computation.1 | async-start | bytes 3145728 | tf_op jit(solution)/shard_map/all_to_all | solution.py:1245
  199.5 21.0 %copy-start.2 = (bf16[3,256,768]{2,1,0:T(8,128)(2,1)S(1)}, bf16[3,256,768]{2,1,0:T(8,128)(2,1)}, u32[]{:S(2)}) copy-start(bf16[3,256,768]{2,1,0:T(8,128)(2,1)} %get-tuple-element.86.refs_2_) | copy-start | bytes 3538948
  199.5 21.5 %copy-start.1 = (bf16[3,256,768]{2,1,0:T(8,128)(2,1)S(1)}, bf16[3,256,768]{2,1,0:T(8,128)(2,1)}, u32[]{:S(2)}) copy-start(bf16[3,256,768]{2,1,0:T(8,128)(2,1)} %get-tuple-element.83.refs_1_) | copy-start | bytes 3538948
  220.5 27.8 %collective-permute-start.1 = (bf16[3,256,768]{2,1,0:T(8,128)(2,1)S(1)}, bf16[3,256,768]{2,1,0:T(8,128)(2,1)S(1)}, u32[]{:S(2)}, u32[]{:S(2)}) collective-permute-start(bf16[3,256,768]{2,1,0:T(8,128)(2,1)S(1)} %copy-done.2), channel_id=1, source_target_pairs={{0,2},{1,3},{2,0},{3,1},{4,6},{5,7},{6,4},{7,5},{8,10},{9,11},{10,... | collective-permute-start | bytes 3538952 | tf_op jit(solution)/shard_map/ppermute | solution.py:46
  221.0 52.7 %collective-permute-start = (bf16[3,256,768]{2,1,0:T(8,128)(2,1)S(1)}, bf16[3,256,768]{2,1,0:T(8,128)(2,1)}, u32[]{:S(2)}, u32[]{:S(2)}) collective-permute-start(bf16[3,256,768]{2,1,0:T(8,128)(2,1)S(1)} %copy-done.1), channel_id=1, source_target_pairs={{0,2},{1,3},{2,0},{3,1},{4,6},{5,7},{6,4},{7,5},{8,10},{9,11},{10,... | collective-permute-start | bytes 3538952 | tf_op jit(solution)/shard_map/ppermute | solution.py:46
  248.2 25.4 %copy-start.3 = (bf16[3,256,768]{2,1,0:T(8,128)(2,1)}, bf16[3,256,768]{2,1,0:T(8,128)(2,1)S(1)}, u32[]{:S(2)}) copy-start(bf16[3,256,768]{2,1,0:T(8,128)(2,1)S(1)} %collective-permute-done.1.refs_6_) | copy-start | bytes 3538948
  333.6 12.7 %copy-start.4 = (bf16[512,768]{1,0:T(8,128)(2,1)S(1)}, bf16[512,768]{1,0:T(8,128)(2,1)}, u32[]{:S(2)}) copy-start(bf16[512,768]{1,0:T(8,128)(2,1)} %get-tuple-element.87) | copy-start | bytes 2359300
  346.3 1.7 copy-start
  348.0 1.1 copy-start.6

commit v5 on v4

--- a/solution.py
+++ b/solution.py
@@ -15,8 +15,8 @@
 CAP = 128
 BLK = 256
 PAIR = 2 * CAP
-TILE = 1024
 UNITS = 256
+PART = 128
 SMALL = 32
 LINES = 40
 
@@ -132,8 +132,8 @@
     n_seq, n_dp, h_ref, w_ref, again_ref, mgain_ref, vec_ref, mix_ref, router_ref,
     route_ref, cot_ref, cos_ref, sin_ref, wo_ref,
     attn_ref, qkv_ref, wt_ref, small_ref, slot_ref, g_ref, wo_all,
-    all_ref, slice_ref, small_buf, h_send, h_recv, w_send, w_recv, s_send, s_recv,
-    o_send, o_recv, c_send, c_recv,
+    all_ref, slice_ref, small_buf, h_send, h_recv, near_send, near_recv, next_send, next_recv,
+    c_send, c_recv,
 ):
     me, dp = lax.axis_index("seq"), lax.axis_index("dp")
     tok = h_ref.shape[0]
@@ -141,7 +141,8 @@
     seq_bits = list(bits_high_first(n_seq))
     greet(
         [{"seq": me ^ bit} for bit in seq_bits]
-        + [{"dp": lax.rem(dp + k, n_dp)} for k in range(1, n_dp)]
+        + [{"dp": dp ^ 1}]
+        + [{"dp": dp ^ (2 * j)} for j in range(1, n_dp // 2)]
     )
 
     plan, arrival = [], {}
@@ -177,24 +178,42 @@
     small_buf[dp, 4:6, :] = mix_ref[0]
     small_buf[dp, 6:8, :] = mix_ref[1]
     small_buf[dp, 8 : 8 + H, :] = router_ref[...]
-    small_copies, w_copies = [], []
-    for k in range(1, n_dp):
-        target = {"dp": lax.rem(dp + k, n_dp)}
-        small_copies.append(
-            remote(small_buf.at[dp], small_buf.at[dp], (s_send, s_recv), k, target)
-        )
-        w_copies.append(remote(slice_ref.at[dp], slice_ref.at[dp], (w_send, w_recv), k, target))
     cols = pl.ds(pl.multiple_of((me & 1) * (D // 2), D // 2), D // 2)
-    wo_copies = [
-        remote(
-            wo_ref.at[:, cols], wo_all.at[dp, :, cols], (o_send, o_recv), k,
-            {"dp": lax.rem(dp + k, n_dp)},
-        )
-        for k in range(1, n_dp)
-    ]
+    wo_all[dp, :, cols] = wo_ref[:, cols]
+
+    def rows_of(kind, source):
+        return (small_buf.at[source], slice_ref.at[source], wo_all.at[source, :, cols])[kind]
+
+    def first_copy(kind, j):
+        return remote_later(
+            rows_of(kind, dp), rows_of(kind, dp), (near_send.at[kind], near_recv.at[kind]), j,
+            {"dp": dp ^ (2 * j)},
+        )
+
+    def next_copy(kind, j):
+        return remote_later(
+            rows_of(kind, dp ^ (2 * j)), rows_of(kind, dp ^ (2 * j)),
+            (next_send.at[kind], next_recv.at[kind]), j, {"dp": dp ^ 1},
+        )
+
+    places = range(1, n_dp // 2)
+    for kind in range(3):
+        for j in places:
+            first_copy(kind, j).start()
+        next_copy(kind, 0).start()
     make_slots(route_ref, cot_ref, slot_ref, g_ref)
-    for copy in small_copies:
-        copy.wait()
+
+    def pass_on(kind):
+        for j in places:
+            first_copy(kind, j).wait_recv()
+            next_copy(kind, j).start()
+
+    def complete(kind):
+        for j in range(n_dp // 2):
+            next_copy(kind, j).wait_recv()
+
+    pass_on(0)
+    complete(0)
     small_ref[...] = jnp.concatenate([small_buf[i].astype(f32) for i in range(n_dp)], axis=1)
 
     def normalize(block, ref):
@@ -204,14 +223,15 @@
         attn_ref[rows, :] = (x * lax.rsqrt(mean_square + 1e-06) * small_ref[0:1]).astype(bf16)
 
     normalize(me, h_ref[...])
+    pass_on(1)
     for place in arrival:
         arrival[place].wait_recv()
         for source, copy in plan:
             if source == place:
                 copy.start()
         normalize(me ^ place, all_ref[me ^ place])
-    for copy in w_copies:
-        copy.wait()
+    complete(1)
+    pass_on(2)
     wt_ref[...] = slice_ref[...].reshape(D, 3 * width).T
     half = HD // 2
 
@@ -227,14 +247,17 @@
             qkv_ref[middle:high, rows] = (a * sin + b * cos).astype(bf16)
         qkv_ref[2 * width :, rows] = y[2 * width :].astype(bf16)
 
-    for copy in wo_copies:
-        copy.wait()
-    wo_all[dp, :, cols] = wo_ref[:, cols]
+    complete(2)
     trade = remote(
         wo_all.at[:, :, cols], wo_all.at[:, :, cols], (c_send, c_recv), 0, {"seq": me ^ 1}
     )
     for _, copy in plan:
         copy.wait_send()
+    for kind in range(3):
+        for j in places:
+            first_copy(kind, j).wait_send()
+        for j in range(n_dp // 2):
+            next_copy(kind, j).wait_send()
     trade.wait()
 
 
@@ -264,12 +287,10 @@
             pltpu.VMEM((n_dp, SMALL, shard), bf16),
             DMA((hops,)),
             DMA((hops,)),
-            DMA((n_dp,)),
-            DMA((n_dp,)),
-            DMA((n_dp,)),
-            DMA((n_dp,)),
-            DMA((n_dp,)),
-            DMA((n_dp,)),
+            DMA((3, n_dp // 2)),
+            DMA((3, n_dp // 2)),
+            DMA((3, n_dp // 2)),
+            DMA((3, n_dp // 2)),
             DMA((1,)),
             DMA((1,)),
         ],
@@ -473,21 +494,31 @@
     )(lows, qkv, grad_out, exact, logs, start_row, cos_t, sin_t)
 
 
-def moe_kernel(n_dp, n_cross, x_ref, gate_ref, w_hbm, g_ref, *refs):
+def gates_back(grad_hidden, gate_pre, up_pre):
+    sig = 1.0 / (1.0 + jnp.exp(-gate_pre))
+    silu = gate_pre * sig
+    grad_gate = grad_hidden * up_pre * sig * (1.0 + gate_pre * (1.0 - sig))
+    return (
+        (silu * up_pre).astype(bf16),
+        grad_gate.astype(bf16),
+        (grad_hidden * silu).astype(bf16),
+    )
+
+
+def moe_kernel(n_dp, parts, x_ref, gate_ref, w_hbm, g_ref, *refs):
     piece_ref, dots_ref, out_ref, refs = refs[0], refs[1], refs[2], refs[3:]
-    units = w_hbm.shape[1]
-    tile = min(TILE, units)
-    tiles = units // UNITS // 2
-    sum_hbm, refs = refs[:tiles], refs[tiles:]
-    far_refs, refs = refs[:n_cross], refs[n_cross:]
+    fin_hbm, refs = refs[:parts], refs[parts:]
     (
-        w_ref, x_in, gate_in, gs_ref, hid_ref, gg_ref, gu_ref, piece_out,
-        dot_out, dw_out, dw_in, dw_keep, w_sem, x_send, x_recv, t_send, t_recv, p_send, p_recv,
-        d_send, d_recv, c_send, c_recv, f_send, f_recv, keep_sem,
+        w_ref, x_in, x_far, g_far, gate_in, gate_far, gs_ref, gs_far, pair_ref, near_ref, far_ref,
+        own_ref, piece_out, dot_out, dw_out, dw_in, fin_ref,
+        w_sem, x_send, x_recv, t_send, t_recv, p_send, p_recv, d_send, d_recv,
+        xf_send, xf_recv, gf_send, gf_recv, tf_send, tf_recv, c_send, c_recv, keep_sem,
     ) = refs
     me, dp = lax.axis_index("seq"), lax.axis_index("dp")
     owners = n_dp // E
     pairs = n_dp // 2
+    half = near_ref.shape[2]
+    core, plane = me & 1, lax.div(me, 2)
     greet([{"dp": dp ^ k} for k in range(1, n_dp)] + [{"seq": me ^ 1}, {"seq": me ^ 2}])
 
     def x_copy(k):
@@ -508,11 +539,16 @@
     def dot_copy(k):
         return remote_later(dot_out.at[k], dots_ref.at[dp], (d_send, d_recv), k, {"dp": dp ^ k})
 
+    def far_copies(k):
+        across = {"seq": me ^ 2}
+        return [
+            remote_later(gate_in.at[k], gate_far.at[k], (tf_send, tf_recv), k, across),
+            remote_later(g_ref.at[dp ^ k], g_far.at[k], (gf_send, gf_recv), k, across),
+            remote_later(x_in.at[k], x_far.at[k], (xf_send, xf_recv), k, across),
+        ]
+
     def core_copy(t):
         return remote_later(dw_out.at[t], dw_in.at[t], (c_send, c_recv), t, {"seq": me ^ 1})
-
-    def far_copy(t):
-        return remote_later(dw_keep.at[t], far_refs[t], (f_send, f_recv), t, {"seq": me ^ 2})
 
     for p in [0, pairs - 1, *range(1, pairs - 1)]:
         for k in (2 * p, 2 * p + 1):
@@ -527,9 +563,17 @@
     for load in loads:
         load.wait()
 
+    def place(i):
+        return jnp.where(i == 0, 0, 1 + lax.rem(i + pairs - 3, pairs - 1))
+
+    def scale(ref, rows, gate, k):
+        column = jnp.broadcast_to(gate, (CAP, CAP)).T[:, 0:1]
+        here = pl.ds(pl.multiple_of(k * CAP, CAP), CAP)
+        ref[here] = (rows.astype(f32) * column).astype(bf16)
+
     @pl.loop(0, pairs)
     def _(i):
-        p = jnp.where(i == 0, 0, 1 + lax.rem(i + pairs - 3, pairs - 1))
+        p = place(i)
         rows = pl.ds(pl.multiple_of(p * PAIR, PAIR), PAIR)
 
         def arrive(k):
@@ -543,26 +587,27 @@
         arrive(2 * p + 1)
         for side in range(2):
             k = 2 * p + side
-            column = jnp.broadcast_to(gate_in[k], (CAP, CAP)).T[:, 0:1]
-            here = pl.ds(pl.multiple_of(k * CAP, CAP), CAP)
-            gs_ref[here] = (g_ref[dp ^ k].astype(f32) * column).astype(bf16)
-
-        @pl.loop(0, units // tile)
+            for copy in far_copies(k):
+                copy.start()
+            scale(gs_ref, g_ref[dp ^ k], gate_in[k], k)
+
+        @pl.loop(0, 2)
         def _(t):
-            part = pl.ds(pl.multiple_of(t * tile, tile), tile)
+            part = pl.ds(pl.multiple_of(t * half, half), half)
             x = x_in[pl.ds(2 * p, 2)].reshape(PAIR, D)
             gate_pre = mm(x, w_ref[0, part], NT)
             up_pre = mm(x, w_ref[1, part], NT)
             grad_hidden = mm(gs_ref[rows], w_ref[2, part], NT)
-            sig = 1.0 / (1.0 + jnp.exp(-gate_pre))
-            silu = gate_pre * sig
-            hid_ref[rows, part] = (silu * up_pre).astype(bf16)
-            gu_ref[rows, part] = (grad_hidden * silu).astype(bf16)
-            gg_ref[rows, part] = (
-                grad_hidden * up_pre * sig * (1.0 + gate_pre * (1.0 - sig))
-            ).astype(bf16)
-
-        pieces = mm(gg_ref[rows], w_ref[0], NN) + mm(gu_ref[rows], w_ref[1], NN)
+            results = gates_back(grad_hidden, gate_pre, up_pre)
+            for j in range(3):
+                pair_ref[j, :, part] = results[j]
+
+            @pl.when(t == plane)
+            def _():
+                for j in range(3):
+                    near_ref[j, rows] = results[j]
+
+        pieces = mm(pair_ref[1], w_ref[0], NN) + mm(pair_ref[2], w_ref[1], NN)
         piece_out[pl.ds(2 * p, 2)] = pieces.astype(bf16).reshape(2, CAP, D)
         piece_copy(2 * p + 1).start()
 
@@ -570,7 +615,7 @@
         def _():
             piece_copy(2 * p).start()
 
-        outs = mm(hid_ref[rows], w_ref[2], NN)
+        outs = mm(pair_ref[0], w_ref[2], NN)
         for side in range(2):
             k = 2 * p + side
             out = outs[side * CAP : (side + 1) * CAP].astype(bf16)
@@ -585,30 +630,58 @@
 
     piece_ref[dp] = piece_out[0]
     dots_ref[dp] = dot_out[0]
-    core = me & 1
-
-    def weight_grad(half, t, ref):
-        part = pl.ds(pl.multiple_of((half * tiles + t) * UNITS, UNITS), UNITS)
-        x_all = x_in[...].reshape(n_dp * CAP, D)
-        ref[0] = mm(gg_ref[:, part], x_all, TN).astype(ref.dtype)
-        ref[1] = mm(gu_ref[:, part], x_all, TN).astype(ref.dtype)
-        ref[2] = mm(hid_ref[:, part], gs_ref[...], TN).astype(ref.dtype)
+
+    def weight_grad(source, x, gs, j, part):
+        left = source[(1, 2, 0)[j], :, part]
+        return mm(left, gs[...] if j == 2 else x[...].reshape(n_dp * CAP, D), TN)
+
+    @pl.loop(0, half // UNITS)
+    def _(t):
+        part = pl.ds(pl.multiple_of(t * UNITS, UNITS), UNITS)
+        for j in range(3):
+            own_ref[j, part] = weight_grad(near_ref, x_in, gs_ref, j, part)
+
+    @pl.loop(0, pairs)
+    def _(i):
+        p = place(i)
+        rows = pl.ds(pl.multiple_of(p * PAIR, PAIR), PAIR)
+        for side in range(2):
+            k = 2 * p + side
+            for copy in far_copies(k):
+                copy.wait_recv()
+            scale(gs_far, g_far[k], gate_far[k], k)
+        part = pl.ds(pl.multiple_of(plane * half, half), half)
+        x = x_far[pl.ds(2 * p, 2)].reshape(PAIR, D)
+        results = gates_back(
+            mm(gs_far[rows], w_ref[2, part], NT),
+            mm(x, w_ref[0, part], NT),
+            mm(x, w_ref[1, part], NT),
+        )
+        for j in range(3):
+            far_ref[j, rows] = results[j]
+
+    tiles = half // UNITS // 2
+
+    def both_rows(side, t, j):
+        part = pl.ds(pl.multiple_of((side * tiles + t) * UNITS, UNITS), UNITS)
+        return own_ref[j, part] + weight_grad(far_ref, x_far, gs_far, j, part)
 
     @pl.loop(0, tiles)
     def _(t):
-        weight_grad(1 - core, t, dw_out.at[t])
+        for j in range(3):
+            dw_out[t, j] = both_rows(1 - core, t, j).astype(bf16)
         core_copy(t).start()
-        weight_grad(core, t, dw_keep.at[t])
+
+    @pl.loop(0, tiles)
+    def _(t):
         core_copy(t).wait_recv()
-        dw_keep[t] = (dw_keep[t].astype(f32) + dw_in[t].astype(f32)).astype(bf16)
-        for c in range(n_cross):
-
-            @pl.when(t == c)
-            def _():
-                far_copy(c).start()
+        for j in range(3):
+            total = (both_rows(core, t, j) + dw_in[t, j].astype(f32)).astype(bf16)
+            for u in range(UNITS // PART):
+                fin_ref[t * (UNITS // PART) + u, j] = total[u * PART : (u + 1) * PART]
 
     keeps = [
-        pltpu.make_async_copy(dw_keep.at[t], sum_hbm[t], keep_sem.at[t]) for t in range(tiles)
+        pltpu.make_async_copy(fin_ref.at[t], fin_hbm[t], keep_sem.at[t]) for t in range(parts)
     ]
     for keep in keeps:
         keep.start()
@@ -617,54 +690,81 @@
         dot_copy(k).wait()
         x_copy(k).wait_send()
         gate_copy(k).wait_send()
-    for t in range(n_cross):
-        far_copy(t).wait()
+    for k in range(n_dp):
+        for copy in far_copies(k):
+            copy.wait_send()
     for t in range(tiles):
         core_copy(t).wait_send()
     for keep in keeps:
         keep.wait()
 
 
-def moe_call(n_dp, n_cross, x_slots, gate_slots, weights, grads):
+def moe_call(n_dp, x_slots, gate_slots, weights, grads):
     units = weights.shape[1]
+    half = units // 2
     rows = n_dp * CAP
-    tiles = units // UNITS // 2
-    part = (3, UNITS, D)
+    parts = units // 4 // PART
+    tiles = half // UNITS // 2
     outs = pl.pallas_call(
-        functools.partial(moe_kernel, n_dp, n_cross),
+        functools.partial(moe_kernel, n_dp, parts),
         out_shape=(
             jax.ShapeDtypeStruct((n_dp, CAP, D), bf16),
             jax.ShapeDtypeStruct((n_dp, 1, CAP), f32),
             jax.ShapeDtypeStruct((n_dp, CAP, D), bf16),
         )
-        + (jax.ShapeDtypeStruct(part, bf16),) * (tiles + n_cross),
+        + (jax.ShapeDtypeStruct((3, PART, D), bf16),) * parts,
         in_specs=[HBM, VMEM, HBM, VMEM],
-        out_specs=[VMEM] * 3 + [HBM] * tiles + [VMEM] * n_cross,
+        out_specs=[VMEM] * 3 + [HBM] * parts,
         scratch_shapes=[
             pltpu.VMEM(weights.shape, bf16),
             pltpu.VMEM((n_dp, CAP, D), bf16),
+            pltpu.VMEM((n_dp, CAP, D), bf16),
+            pltpu.VMEM((n_dp, CAP, D), bf16),
+            pltpu.VMEM((n_dp, 1, CAP), f32),
             pltpu.VMEM((n_dp, 1, CAP), f32),
             pltpu.VMEM((rows, D), bf16),
-            pltpu.VMEM((rows, units), bf16),
-            pltpu.VMEM((rows, units), bf16),
-            pltpu.VMEM((rows, units), bf16),
+            pltpu.VMEM((rows, D), bf16),
+            pltpu.VMEM((3, PAIR, units), bf16),
+            pltpu.VMEM((3, rows, half), bf16),
+            pltpu.VMEM((3, rows, half), bf16),
+            pltpu.VMEM((3, half, D), f32),
             pltpu.VMEM((n_dp, CAP, D), bf16),
             pltpu.VMEM((n_dp, 1, CAP), f32),
-            pltpu.VMEM((tiles, *part), bf16),
-            pltpu.VMEM((tiles, *part), bf16),
-            pltpu.VMEM((tiles, *part), bf16),
+            pltpu.VMEM((tiles, 3, UNITS, D), bf16),
+            pltpu.VMEM((tiles, 3, UNITS, D), bf16),
+            pltpu.VMEM((parts, 3, PART, D), bf16),
             DMA((4,)),
         ]
-        + [DMA((n_dp,))] * 8
+        + [DMA((n_dp,))] * 14
         + [DMA((tiles,))] * 2
-        + [DMA((max(n_cross, 1),))] * 2
-        + [DMA((tiles,))],
+        + [DMA((parts,))],
         compiler_params=pltpu.CompilerParams(
             collective_id=4, has_side_effects=True, vmem_limit_bytes=67043328
         ),
         name="experts",
     )(x_slots, gate_slots, weights, grads)
-    return outs[0], outs[1], outs[2], outs[3 : 3 + tiles], outs[3 + tiles :]
+    return outs[0], outs[1], outs[2], list(outs[3:])
+
+
+def experts_plain(to_owners, to_sources, n_dp, x_slots, gate_slots, weights, grads):
+    rows = n_dp * CAP
+    x = to_owners(x_slots).reshape(rows, D)
+    gate = to_owners(gate_slots).reshape(rows, 1)
+    g = grads.reshape(rows, D)
+    gs = (g.astype(f32) * gate).astype(bf16)
+    hidden, grad_gate, grad_up = gates_back(
+        mm(gs, weights[2], NT), mm(x, weights[0], NT), mm(x, weights[1], NT)
+    )
+    out = mm(hidden, weights[2], NN).astype(bf16)
+    piece = (mm(grad_gate, weights[0], NN) + mm(grad_up, weights[1], NN)).astype(bf16)
+    dw = jnp.stack([mm(grad_gate, x, TN), mm(grad_up, x, TN), mm(hidden, gs, TN)])
+    dots = jnp.sum(out.astype(f32) * g.astype(f32), axis=-1)
+    return (
+        to_sources(piece.reshape(n_dp, CAP, D)),
+        to_sources(dots.reshape(n_dp, 1, CAP)),
+        out.reshape(n_dp, CAP, D),
+        lax.psum(dw, "seq"),
+    )
 
 
 def mid_kernel(
@@ -740,17 +840,23 @@
 
 
 def mid_back_kernel(
-    n_seq, n_dp, piece_ref, dots_ref, cot_ref, mid_ref, gate_ref, slot_ref, route_ref,
-    small_ref, heads_ref, w_ref, prev_ref, carry_ref,
-    resid_ref, go_ref, base_ref, dprev_ref, pack_ref, wo_sum_ref,
-    gh_ref, wo_ref, wo_in, a_send, a_recv, c_send, c_recv,
+    n_seq, n_dp, n_tile, piece_ref, dots_ref, cot_ref, mid_ref, gate_ref, slot_ref, route_ref,
+    small_ref, heads_ref, w_ref, prev_ref, carry_ref, *refs,
 ):
+    tile_refs, refs = refs[:n_tile], refs[n_tile:]
+    resid_ref, go_ref, base_ref, dprev_ref, pack_ref, wo_sum_ref, *refs = refs
+    far_refs, refs = refs[:n_tile], refs[n_tile:]
+    gh_ref, wo_ref, wo_in, a_send, a_recv, c_send, c_recv, t_send, t_recv = refs
     me = lax.axis_index("seq")
     tok = cot_ref.shape[0]
     width = heads_ref.shape[1]
     owners = n_dp // E
     pairs = n_seq // 2
     greet([{"seq": me ^ place} for place in range(1, n_seq)])
+    tile_copies = [
+        remote(tile_refs[t], far_refs[t], (t_send, t_recv), t, {"seq": me ^ 2})
+        for t in range(n_tile)
+    ]
     cot = cot_ref[...]
     grad_top = cot.astype(f32)
     resid_mid = mid_ref[...]
@@ -856,19 +962,21 @@
         wo_sum_ref[i] = (
             wo_ref[me ^ (2 * i)].astype(f32) + wo_in[i].astype(f32)
         ).astype(bf16)
-    for copy in copies:
+    for copy in copies + tile_copies:
         copy.wait()
     for copy in core_copies:
         copy.wait_send()
 
 
 def mid_back_call(
-    n_seq, n_dp, piece, dots, cot, mid, gates, slot_of, routes, small, heads, w, prev, carry
+    n_seq, n_dp, piece, dots, cot, mid, gates, slot_of, routes, small, heads, w, prev, carry,
+    parts,
 ):
     tok, width = cot.shape[0], heads.shape[1]
     pairs = n_seq // 2
-    return pl.pallas_call(
-        functools.partial(mid_back_kernel, n_seq, n_dp),
+    n_tile = len(parts)
+    outs = pl.pallas_call(
+        functools.partial(mid_back_kernel, n_seq, n_dp, n_tile),
         out_shape=(
             jax.ShapeDtypeStruct((tok, D), f32),
             jax.ShapeDtypeStruct((n_seq, width, tok), bf16),
@@ -876,9 +984,10 @@
             jax.ShapeDtypeStruct((H, 1, tok), f32),
             jax.ShapeDtypeStruct((n_dp, LINES, D // n_dp), f32),
             jax.ShapeDtypeStruct((pairs, D, width), bf16),
-        ),
-        in_specs=[VMEM] * 12,
-        out_specs=[VMEM] * 6,
+        )
+        + tuple(jax.ShapeDtypeStruct(part.shape, bf16) for part in parts),
+        in_specs=[VMEM] * 12 + [HBM] * n_tile,
+        out_specs=[VMEM] * 6 + [HBM] * n_tile,
         scratch_shapes=[
             pltpu.VMEM((n_seq, width, tok), bf16),
             pltpu.VMEM((n_seq, D, width), bf16),
@@ -887,22 +996,25 @@
             DMA((n_seq,)),
             DMA((pairs,)),
             DMA((pairs,)),
+            DMA((max(n_tile, 1),)),
+            DMA((max(n_tile, 1),)),
         ],
         compiler_params=pltpu.CompilerParams(collective_id=3, has_side_effects=True),
         name="mid_back",
-    )(piece, dots, cot, mid, gates, slot_of, routes, small, heads, w, prev, carry)
+    )(piece, dots, cot, mid, gates, slot_of, routes, small, heads, w, prev, carry, *parts)
+    return outs[:6], list(outs[6:])
 
 
 def tail_kernel(
-    n_seq, n_dp, tiles, g_ref, wt_ref, wo_ref, pack_ref, gate_ref, slot_ref, gain_ref,
+    n_seq, n_dp, parts, g_ref, wt_ref, wo_ref, pack_ref, gate_ref, slot_ref, gain_ref,
     a_hbm, h_hbm, resid_hbm, base_hbm, out_hbm, *refs,
 ):
-    sum_hbm, refs = refs[:tiles], refs[tiles:]
-    n_far = tiles - 1
+    n_far = max(parts - 1, 0)
+    fin_hbm, refs = refs[:parts], refs[parts:]
     far_hbm, refs = refs[:n_far], refs[n_far:]
     din_ref, row_in, line_ref, block_ref, both_ref, refs = *refs[:5], refs[5:]
     (
-        a_ref, h_ref, resid_ref, base_ref, rows_ref, far_ref, sum_ref, fin_ref,
+        a_ref, h_ref, resid_ref, base_ref, rows_ref, far_ref, fin_ref,
         core_out, core_in, x_out, x_in, part_ref, w_out_buf, w_in, wo_buf, wo_in, wo_x, wo_far,
         row_buf, pack_in, line_buf, line_in, load_sem, c_sems, x_sems, w_sems, r_sems, o_sems,
         p_sems, q_sems, l_sems, t_sems, f_sems, keep_sem,
@@ -929,8 +1041,8 @@
     for src, dst in [
         (a_hbm, a_ref), (out_hbm, rows_ref), (base_hbm, base_ref), (h_hbm, h_ref),
         (resid_hbm, resid_ref),
-    ] + [(far_hbm[t], far_ref.at[t]) for t in range(n_far)] + [
-        (sum_hbm[t], sum_ref.at[t]) for t in range(n_far)
+    ] + [(fin_hbm[t], fin_ref.at[t]) for t in range(parts)] + [
+        (far_hbm[t], far_ref.at[t]) for t in range(n_far)
     ]:
         load = pltpu.make_async_copy(src, dst, load_sem.at[len(loads)])
         load.start()
@@ -947,18 +1059,9 @@
         columns = pl.ds(pl.multiple_of((me ^ place) * tok, tok), tok)
         return mm(g_ref[:, columns], wt_ref[...], TN)
 
-    last, cut = sum_hbm[tiles - 1], UNITS // 2
-    tile_copies = []
-
-    def send_part(i):
-        part = pl.ds(i * cut, cut)
-        tile_copies.append(
-            remote(last.at[:, part], far_ref.at[tiles - 1, :, part], t_sems, i, {"seq": me ^ 2})
-        )
-
-    send_part(0)
-    last_load = pltpu.make_async_copy(last, sum_ref.at[tiles - 1], load_sem.at[len(loads)])
-    last_load.start()
+    part_copies = [
+        remote(fin_hbm[t], far_ref.at[t], t_sems, 0, {"seq": me ^ 2}) for t in range(n_far, parts)
+    ]
     pack_copies = [
         remote(pack_ref.at[there(k)], pack_in.at[dp], p_sems, k, {"dp": there(k)}) for k in others
     ]
@@ -981,7 +1084,6 @@
         x_copies.append(
             remote(x_out.at[i - 1], x_in.at[i - 1], x_sems, i - 1, {"seq": me ^ (2 * i)})
         )
-    send_part(1)
     loads[0].wait()
     turned = mm(g_ref[...], a_ref[...], NN)
     w_out_buf[...] = turned.T.astype(bf16).reshape(n_dp, shard, width3)
@@ -1004,17 +1106,21 @@
 
     fin_copies, keeps = [], []
 
-    def finish(t):
-        fin_ref[t] = (sum_ref[t].astype(f32) + far_ref[t].astype(f32)).astype(bf16)
-        fin_copies.append(remote(fin_ref.at[t], both_ref.at[1, t], f_sems, t, {"seq": me ^ 1}))
-        keep = pltpu.make_async_copy(fin_ref.at[t], both_ref.at[0, t], keep_sem.at[t])
+    def hand_over(ref, row, t):
+        index = row * parts + t
+        fin_copies.append(
+            remote(ref.at[t], both_ref.at[2 * row + 1, t], f_sems, index, {"seq": me ^ 1})
+        )
+        keep = pltpu.make_async_copy(ref.at[t], both_ref.at[2 * row, t], keep_sem.at[index])
         keep.start()
         keeps.append(keep)
 
+    for t in range(parts):
+        loads[5 + t].wait()
+        hand_over(fin_ref, 0, t)
     for t in range(n_far):
-        loads[5 + t].wait()
-        loads[5 + n_far + t].wait()
-        finish(t)
+        loads[5 + parts + t].wait()
+        hand_over(far_ref, 1, t)
 
     for copy in wo_copies:
         copy.wait_recv()
@@ -1063,15 +1169,14 @@
     for copy in line_copies:
         copy.wait_recv()
     line_ref[...] = jnp.sum(line_in[...], axis=0)
-    last_load.wait()
-    for copy in tile_copies:
+    for copy in part_copies:
         copy.wait_recv()
-    finish(tiles - 1)
+        hand_over(far_ref, 1, n_far)
     for copy in row_copies + fin_copies:
         copy.wait_recv()
     for copy in (
         core_copies + w_copies + x_copies + row_copies + wo_copies + pack_copies
-        + line_copies + wo_cross + tile_copies + fin_copies
+        + line_copies + wo_cross + part_copies + fin_copies
     ):
         copy.wait_send()
     for keep in keeps:
@@ -1080,24 +1185,24 @@
 
 def tail_call(
     n_seq, n_dp, grad_qkv, w_turned, wo_sum, pack, gates, slot_of, small,
-    attn_in, hidden, grad_resid, base, back_out, sums, far,
+    attn_in, hidden, grad_resid, base, back_out, fin, far,
 ):
     tok = hidden.shape[0]
     shard, width3 = D // n_dp, grad_qkv.shape[0]
     width = width3 // 3
     pairs = n_seq // 2
-    tiles = len(sums)
-    part = sums[0].shape
+    parts, room = len(fin), max(len(fin), 1)
+    part = (3, PART, D)
     return pl.pallas_call(
-        functools.partial(tail_kernel, n_seq, n_dp, tiles),
+        functools.partial(tail_kernel, n_seq, n_dp, parts),
         out_shape=(
             jax.ShapeDtypeStruct((tok, D), f32),
             jax.ShapeDtypeStruct((n_seq, shard, width3 + width), bf16),
             jax.ShapeDtypeStruct((LINES, shard), f32),
             jax.ShapeDtypeStruct((tok, D), bf16),
-            jax.ShapeDtypeStruct((2, tiles, *part), bf16),
+            jax.ShapeDtypeStruct((n_seq, room, *part), bf16),
         ),
-        in_specs=[VMEM] * 7 + [HBM] * (5 + tiles + len(far)),
+        in_specs=[VMEM] * 7 + [HBM] * (5 + parts + len(far)),
         out_specs=[VMEM] * 4 + [HBM],
         scratch_shapes=[
             pltpu.VMEM((n_seq * tok, D), bf16),
@@ -1105,9 +1210,8 @@
             pltpu.VMEM((tok, D), f32),
             pltpu.VMEM((tok, D), f32),
             pltpu.VMEM((n_dp, CAP, D), bf16),
-            pltpu.VMEM((tiles, *part), bf16),
-            pltpu.VMEM((tiles, *part), bf16),
-            pltpu.VMEM((tiles, *part), bf16),
+            pltpu.VMEM((room, *part), bf16),
+            pltpu.VMEM((room, *part), bf16),
             pltpu.VMEM((pairs, tok, D), bf16),
             pltpu.VMEM((pairs, tok, D), bf16),
             pltpu.VMEM((pairs - 1, tok, D), bf16),
@@ -1123,7 +1227,7 @@
             pltpu.VMEM((n_dp, LINES, shard), f32),
             pltpu.VMEM((LINES, shard), f32),
             pltpu.VMEM((n_seq, LINES, shard), f32),
-            DMA((4 + 2 * tiles,)),
+            DMA((5 + 2 * room,)),
             DMA((2, pairs)),
             DMA((2, pairs)),
             DMA((2, n_dp)),
@@ -1132,9 +1236,9 @@
             DMA((2, n_dp)),
             DMA((2, n_dp)),
             DMA((2, n_seq)),
-            DMA((2, 2)),
-            DMA((2, tiles)),
-            DMA((tiles,)),
+            DMA((2, 1)),
+            DMA((2, 2 * room)),
+            DMA((2 * room,)),
         ],
         compiler_params=pltpu.CompilerParams(
             collective_id=1, has_side_effects=True, vmem_limit_bytes=67043328
@@ -1142,7 +1246,7 @@
         name="tail",
     )(
         grad_qkv, w_turned, wo_sum, pack, gates, slot_of, small,
-        attn_in, hidden, grad_resid, base, back_out, *sums, *far,
+        attn_in, hidden, grad_resid, base, back_out, *fin, *far,
     )
 
 
@@ -1173,8 +1277,8 @@
 
 def finish_call(n_seq, me, both, row_in, lines, w_qkv, attn_gain):
     shard = w_qkv.shape[0]
-    _, tiles, three, step, _ = both.shape
-    units = 2 * tiles * step
+    _, parts, three, step, _ = both.shape
+    units = n_seq * parts * step
 
     def whole(shape):
         return pl.BlockSpec(shape, lambda i, me_ref: (0,) * len(shape))
@@ -1187,11 +1291,11 @@
         + [jax.ShapeDtypeStruct(shape, f32) for shape in shapes],
         grid_spec=pltpu.PrefetchScalarGridSpec(
             num_scalar_prefetch=1,
-            grid=(2 * tiles,),
+            grid=(n_seq * parts,),
             in_specs=[
                 pl.BlockSpec(
                     (1, 1, three, step, D),
-                    lambda i, me_ref: ((i // tiles) ^ (me_ref[0] & 1), i % tiles, 0, 0, 0),
+                    lambda i, me_ref: ((i // parts) ^ me_ref[0], i % parts, 0, 0, 0),
                 ),
                 whole(row_in.shape),
                 whole(lines.shape),
@@ -1262,30 +1366,35 @@
     heads_t, resid_mid, gates, x_slots, gate_slots = mid_call(
         n_seq, attended, hidden, prev_t, w_carry, small, slot_of, routes_t, out_weight
     )
-    tiles = experts.shape[1] // UNITS // 2
-    n_cross = 1 if tiles > 1 else 0
-    piece, dots, partial, sums, far = moe_call(
-        n_dp, n_cross, x_slots, gate_slots, experts, arrived_grad
-    )
-    far = list(far) + [swap(part, "seq", 2) for part in sums[n_cross : min(2, tiles - 1)]]
+    if n_dp * CAP > 1024:
+        piece, dots, partial, d_plain = experts_plain(
+            to_owners, to_sources, n_dp, x_slots, gate_slots, experts, arrived_grad
+        )
+        fin = []
+    else:
+        piece, dots, partial, fin = moe_call(
+            n_dp, x_slots, gate_slots, experts, arrived_grad
+        )
     back_out = to_sources(partial)
 
-    grad_resid, grad_out, base, d_prev, pack, wo_sum = mid_back_call(
+    (grad_resid, grad_out, base, d_prev, pack, wo_sum), far_back = mid_back_call(
         n_seq, n_dp, piece, dots, cot, resid_mid, gates, slot_of, routes_t, small, heads_t,
-        out_weight, prev_t, w_carry,
-    )
-    later, grad_out = lax.optimization_barrier((list(sums[2 : tiles - 1]), grad_out))
-    far += [swap(part, "seq", 2) for part in later]
+        out_weight, prev_t, w_carry, fin[:1],
+    )
+    later, grad_out = lax.optimization_barrier((fin[1:-1], grad_out))
+    far = far_back + [swap(part, "seq", 2) for part in later]
     grad_qkv = attn_back_call(
         lows, qkv, grad_out, attended_exact, logs, start_row, cos_t, sin_t
     )
     d_input, row_in, lines, block_out, both = tail_call(
         n_seq, n_dp, grad_qkv, w_turned, wo_sum, pack, gates, slot_of, small,
-        attn_in, hidden, grad_resid, base, back_out, sums, far,
+        attn_in, hidden, grad_resid, base, back_out, fin, far,
     )
     d_experts, d_qkv, d_out, again, mgain, router, carry, vec, mix = finish_call(
         n_seq, me.astype(jnp.int32).reshape(1), both, row_in, lines, w_qkv, attn_gain
     )
+    if not fin:
+        d_experts = d_plain
     return (
         block_out[None],
         d_input[None],

time: 353 us -> 319 us (0.904)
  waiting for transfers between devices: 29.7 us -> 0.83 us
  Pallas kernels: 302 us -> 298 us
    ppermute x2, waiting for transfers between devices: 29.7 us -> 0.82 us  [swap(): return lax.ppermute(value, axis, [(i, i ^ bit) for i in range(size)])]
    pallas_call x1, Pallas kernels: 47.7 us -> 37.9 us  [start_call(): pl.pallas_call(functools.partial(start_kernel, n_seq, n_dp), out_shape=(j...]
    pallas_call x3, Pallas kernels: 181 us -> 177 us  [the longest x1 92.5 us: moe_call(): pl.pallas_call(functools.partial(moe_kernel, n_dp, parts), out_shape=(jax...]
    pallas_call x1, Pallas kernels: 19.9 us -> 23.6 us  [attn_call(): pl.pallas_call(attn_kernel, out_shape=(jax.ShapeDtypeStruct((seq_len // t...]
    pallas_call x1, Pallas kernels: 21.9 us -> 25.5 us  [attn_back_call(): pl.pallas_call(attn_back_kernel, out_shape=jax.ShapeDtypeStruct((width3,...]
  transfers between devices with their start and end apart: 4 -> 4, of which waited for: 2 -> 1; matrix products, arithmetic and copies ran while one was open for 0% -> 0% of each run, Pallas kernels for 23% -> 30%
where the time goes in v5:
time: 319 us
  Pallas kernels  298 us (93%)
  starting transfers between devices  11.9 us (4%)
  local copies, waits for them, and re-layouts  4.35 us (1%)
    pallas_call x1, Pallas kernels, moe_call(): pl.pallas_call(functools.partial(moe_kernel, n_dp, parts), out_shape=(jax...  92.5 us
    pallas_call x1, Pallas kernels, tail_call(): pl.pallas_call(functools.partial(tail_kernel, n_seq, n_dp, parts), out_sh...  55.4 us
    pallas_call x1, Pallas kernels, start_call(): pl.pallas_call(functools.partial(start_kernel, n_seq, n_dp), out_shape=(j...  37.9 us
    pallas_call x1, Pallas kernels, mid_back_call(): pl.pallas_call(functools.partial(mid_back_kernel, n_seq, n_dp, n_tile), o...  29.3 us
    pallas_call x1, Pallas kernels, attn_back_call(): pl.pallas_call(attn_back_kernel, out_shape=jax.ShapeDtypeStruct((width3,...  25.5 us
    pallas_call x1, Pallas kernels, attn_call(): pl.pallas_call(attn_kernel, out_shape=(jax.ShapeDtypeStruct((seq_len // t...  23.6 us
    pallas_call x1, Pallas kernels, mid_call(): pl.pallas_call(functools.partial(mid_kernel, n_seq), out_shape=(jax.Shape...  18.3 us
    pallas_call x1, Pallas kernels, finish_call(): pl.pallas_call(functools.partial(finish_kernel, n_seq), out_shape=[jax.Sh...  15.6 us
  transfers between devices with their start and end apart: 4, of which 1 were waited for; matrix products, arithmetic and copies ran while one was open for 0% of the time, Pallas kernels for 30%

profile of v5, /device:TPU:13, one launch (start us, length us, event | category | flops | bytes accessed | tf_op | source)
XLA Modules:
  0.0 318.6 jit_solution(4650967611748982526)
XLA Ops:
  0.7 1.8 multiply_sine_fusion
  2.5 37.9 %start.1 = (bf16[2048,768]{1,0:T(8,128)(2,1)}, bf16[576,2048]{1,0:T(8,128)(2,1)}, bf16[576,768]{1,0:T(8,128)(2,1)}, f32[32,768]{1,0:T(8,128)}, s32[2,512]{1,0:T(...) custom-call(bf16[512,768]{1,0:T(8,128)(2,1)} %bitcast.18, bf16[96,2304]{1,0:T(8,128)(2,1)} %wq_ref.1, ...), custom_call_target="tpu_custom_call" | custom-call | tf_op jit(solution)/shard_map/start/pallas_call | solution.py:271
  40.4 0.0 copy-start.6
  40.4 4.9 %all-to-all-start = ((bf16[8,128,768]{2,1,0:T(8,128)(2,1)}), bf16[8,128,768]{2,1,0:T(8,128)(2,1)}, u32[]{:S(2)}, u32[]{:S(2)}) async-start(bf16[8,128,768]{2,1,0:T(8,128)(2,1)} %get-tuple-element.65), calls=%async_computation | async-start | bytes 3145728 | tf_op jit(solution)/shard_map/all_to_all | solution.py:1344
  45.4 0.0 copy-done.6
  45.4 0.1 convert_reduce_fusion
  45.5 0.1 select_reduce_fusion
  45.6 0.0 copy-start.8
  45.6 0.1 slice.3
  45.7 0.5 and_select_fusion.lo_ref
  46.2 0.0 copy-done.8
  46.2 23.6 %attend.1 = (bf16[4,192,512]{2,1,0:T(8,128)(2,1)}, f32[192,2048]{1,0:T(8,128)}, f32[3,2048]{1,0:T(4,128)}) custom-call(s32[8]{0:T(128)} %and_select_fusion.lo_ref, bf16[576,2048]{1,0:T(8,128)(2,1)} %get-tuple-element.58.qkv_ref, s32[1,2048]{1,0:T(1,128)} %bitcast.33), custom_call_target="tpu_custom_call" | custom-call | flops 16000000000 | bytes 16000000 | tf_op jit(solution)/shard_map/attend/pallas_call | solution.py:363
  69.9 18.3 %mid.1 = (bf16[4,192,512]{2,1,0:T(8,128)(2,1)}, f32[512,768]{1,0:T(8,128)}, f32[8,512]{1,0:T(8,128)}, bf16[8,128,768]{2,1,0:T(8,128)(2,1)}, f32[8,1,128]{2,1,0:T(1,128)}) custom-call(bf16[4,192,512]{2,1,0:T(8,128)(2,1)} %get-tuple-element.59.att_ref, bf16[512,768]{1,0:T(8,128)(2,1)} %bitcast.19, f32[12,1,512]{2,1,0:T(1,128)} %bitcast.25, ...), custom_call_target="tpu_custom_call" | custom-call | tf_op jit(solution)/shard_map/mid/pallas_call | solution.py:825
  88.2 0.0 all-to-all-done.g_ref
  88.2 92.5 %experts.1 = (bf16[8,128,768]{2,1,0:T(8,128)(2,1)}, f32[8,1,128]{2,1,0:T(1,128)}, bf16[8,128,768]{2,1,0:T(8,128)(2,1)}, bf16[3,128,768]{2,1,0:T(8,128)(2,1)}, bf...) custom-call(bf16[8,128,768]{2,1,0:T(8,128)(2,1)} %get-tuple-element.63.x_ref, ...), custom_call_target="tpu_custom_call" | custom-call | tf_op jit(solution)/shard_map/experts/pallas_call | solution.py:708
  180.8 5.4 %all-to-all-start.1 = ((bf16[8,128,768]{2,1,0:T(8,128)(2,1)}), bf16[8,128,768]{2,1,0:T(8,128)(2,1)}, u32[]{:S(2)}, u32[]{:S(2)}) async-start(bf16[8,128,768]{2,1,0:T(8,128)(2,1)} %get-tuple-element.84), calls=%async_computation.1 | async-start | bytes 3145728 | tf_op jit(solution)/shard_map/all_to_all | solution.py:1349
  186.2 29.3 %mid_back.1 = (f32[512,768]{1,0:T(8,128)}, bf16[4,192,512]{2,1,0:T(8,128)(2,1)}, f32[512,768]{1,0:T(8,128)}, f32[12,1,512]{2,1,0:T(1,128)}, f32[8,40,96]{2,1,0:T...) custom-call(bf16[8,128,768]{2,1,0:T(8,128)(2,1)} %get-tuple-element.68.piece_ref, ...), custom_call_target="tpu_custom_call" | custom-call | tf_op jit(solution)/shard_map/mid_back/pallas_call | solution.py:978
  215.4 0.0 copy-done.2
  215.5 1.3 collective-permute-start
  216.7 0.3 collective-permute-start.1
  217.0 25.5 %attend_back.1.g_ref = bf16[576,2048]{1,0:T(8,128)(2,1)} custom-call(s32[8]{0:T(128)} %and_select_fusion.lo_ref, bf16[576,2048]{1,0:T(8,128)(2,1)} %get-tuple-element.58.qkv_ref, bf16[4,192,512]{2,1,0:T(8,128)(2,1)} %get-tuple-element.75.go_ref, f32[192,2048]{1,0:T(8,128)} %get-tuple-element.76.exact_ref, f32[3,2048]{1,0:T(4,128)} %get-tuple-element.77.log_ref, ...), custom_call_target="tpu_custom_call" | custom-call | flops 16000000000 | bytes 16000000 | tf_op jit(solution)/shard_map/attend_back/pallas_call | solution.py:467
  242.5 0.0 collective-permute-done.refs_5_
  242.5 0.8 collective-permute-done.1.refs_6_
  243.3 0.0 all-to-all-done.1.out_hbm
  243.3 0.8 copy-done.5
  244.1 55.4 %tail.1 = (f32[512,768]{1,0:T(8,128)}, bf16[4,96,768]{2,1,0:T(8,128)(2,1)}, f32[40,96]{1,0:T(8,128)}, bf16[512,768]{1,0:T(8,128)(2,1)}, bf16[4,4,3,128,768]{4,3,2,1,0:T(8,128)(2,1)}) custom-call(bf16[576,2048]{1,0:T(8,128)(2,1)} %attend_back.1.g_ref, bf16[576,768]{1,0:T(8,128)(2,1)} %get-tuple-element.78.wt_ref, ...), custom_call_target="tpu_custom_call" | custom-call | tf_op jit(solution)/shard_map/tail/pallas_call | solution.py:1196
  299.5 15.6 %finish.1 = (f32[3,2048,768]{2,1,0:T(8,128)}, f32[96,2304]{1,0:T(8,128)}, f32[96,768]{1,0:T(8,128)}, f32[1,96]{1,0:T(1,128)}, f32[1,96]{1,0:T(1,128)}, /*index=5...) custom-call(s32[1]{0:T(128)} %bitcast.14.me_ref, ...), custom_call_target="tpu_custom_call" | custom-call | tf_op jit(solution)/shard_map/finish/pallas_call | solution.py:1288
  315.2 0.9 copy.29
  316.1 0.8 copy-done
  316.8 1.1 copy.30
  318.0 0.0 copy-done.7
  318.0 0.6 copy.31
  (12 shorter events, 0.0 us)
Async XLA Ops:
  40.4 4.9 %copy-start.6 = (s32[1,2048]{1,0:T(1,128)S(1)}, s32[1,2048]{1,0:T(1,128)}, u32[]{:S(2)}) copy-start(s32[1,2048]{1,0:T(1,128)} %param.16) | copy-start | bytes 24580
  40.4 47.8 %all-to-all-start = ((bf16[8,128,768]{2,1,0:T(8,128)(2,1)}), bf16[8,128,768]{2,1,0:T(8,128)(2,1)}, u32[]{:S(2)}, u32[]{:S(2)}) async-start(bf16[8,128,768]{2,1,0:T(8,128)(2,1)} %get-tuple-element.65), calls=%async_computation | async-start | bytes 3145728 | tf_op jit(solution)/shard_map/all_to_all | solution.py:1344
  45.6 0.6 copy-start.8
  180.8 62.6 %all-to-all-start.1 = ((bf16[8,128,768]{2,1,0:T(8,128)(2,1)}), bf16[8,128,768]{2,1,0:T(8,128)(2,1)}, u32[]{:S(2)}, u32[]{:S(2)}) async-start(bf16[8,128,768]{2,1,0:T(8,128)(2,1)} %get-tuple-element.84), calls=%async_computation.1 | async-start | bytes 3145728 | tf_op jit(solution)/shard_map/all_to_all | solution.py:1349
  186.2 29.3 %copy-start.2 = (bf16[3,128,768]{2,1,0:T(8,128)(2,1)S(1)}, bf16[3,128,768]{2,1,0:T(8,128)(2,1)}, u32[]{:S(2)}) copy-start(bf16[3,128,768]{2,1,0:T(8,128)(2,1)} %get-tuple-element.87.refs_1_) | copy-start | bytes 1769476
  186.2 30.6 %copy-start.3 = (bf16[3,128,768]{2,1,0:T(8,128)(2,1)S(1)}, bf16[3,128,768]{2,1,0:T(8,128)(2,1)}, u32[]{:S(2)}) copy-start(bf16[3,128,768]{2,1,0:T(8,128)(2,1)} %get-tuple-element.88.refs_2_) | copy-start | bytes 1769476
  215.5 27.0 %collective-permute-start = (bf16[3,128,768]{2,1,0:T(8,128)(2,1)S(1)}, bf16[3,128,768]{2,1,0:T(8,128)(2,1)S(1)}, u32[]{:S(2)}, u32[]{:S(2)}) collective-permute-start(bf16[3,128,768]{2,1,0:T(8,128)(2,1)S(1)} %copy-done.2), channel_id=1, source_target_pairs={{0,2},{1,3},{2,0},{3,1},{4,6},{5,7},{6,4},{7,5},{8,10},{9,11},{10,... | collective-permute-start | bytes 1769480 | tf_op jit(solution)/shard_map/ppermute | solution.py:46
  216.7 26.6 %collective-permute-start.1 = (bf16[3,128,768]{2,1,0:T(8,128)(2,1)S(1)}, bf16[3,128,768]{2,1,0:T(8,128)(2,1)S(1)}, u32[]{:S(2)}, u32[]{:S(2)}) collective-permute-start(bf16[3,128,768]{2,1,0:T(8,128)(2,1)S(1)} %copy-done.3), channel_id=1, source_target_pairs={{0,2},{1,3},{2,0},{3,1},{4,6},{5,7},{6,4},{7,5},{8,10},{9,11},{10,... | collective-permute-start | bytes 1769480 | tf_op jit(solution)/shard_map/ppermute | solution.py:46
  242.5 0.8 copy-start.4
  243.3 0.8 copy-start.5
  299.5 15.6 %copy-start.1 = (bf16[512,768]{1,0:T(8,128)(2,1)S(1)}, bf16[512,768]{1,0:T(8,128)(2,1)}, u32[]{:S(2)}) copy-start(bf16[512,768]{1,0:T(8,128)(2,1)} %get-tuple-element.89) | copy-start | bytes 2359300
  315.1 1.7 copy-start
  316.8 1.1 copy-start.7

commit v6 on v5

--- a/solution.py
+++ b/solution.py
@@ -16,7 +16,9 @@
 BLK = 256
 PAIR = 2 * CAP
 UNITS = 256
-PART = 128
+PART = 64
+EARLY = 2
+LATE = 2
 SMALL = 32
 LINES = 40
 
@@ -324,18 +326,25 @@
     def step(kb, carry):
         there = pl.ds(pl.multiple_of(kb * BLK, BLK), BLK)
         allowed = allowed_block(kb, qb, start_row)
+        scores = [
+            mm(keys_ref[h, there, :], qkv_ref[h * HD : (h + 1) * HD, here], NN)
+            for h in range(heads)
+        ]
+        stats, weights = [], []
+        for h in range(heads):
+            top, total, acc = carry[h]
+            masked = jnp.where(allowed, scores[h] * score_scale, neg_large)
+            new_top = jnp.maximum(top, jnp.max(masked, axis=0, keepdims=True))
+            fade = jnp.exp2(top - new_top)
+            weight = jnp.exp2(masked - new_top)
+            total = total * fade + jnp.sum(weight, axis=0, keepdims=True)
+            stats.append((new_top, total, acc * fade))
+            weights.append(weight.astype(bf16))
         new = []
         for h in range(heads):
-            top, total, acc = carry[h]
-            scores = mm(keys_ref[h, there, :], qkv_ref[h * HD : (h + 1) * HD, here], NN)
-            scores = jnp.where(allowed, scores * score_scale, neg_large)
-            new_top = jnp.maximum(top, jnp.max(scores, axis=0, keepdims=True))
-            fade = jnp.exp2(top - new_top)
-            weights = jnp.exp2(scores - new_top)
-            total = total * fade + jnp.sum(weights, axis=0, keepdims=True)
             values = qkv_ref[2 * width + h * HD : 2 * width + (h + 1) * HD, there]
-            acc = acc * fade + mm(values, weights.astype(bf16), NN)
-            new.append((new_top, total, acc))
+            top, total, acc = stats[h]
+            new.append((top, total, acc + mm(values, weights[h], NN)))
         return tuple(new)
 
     first = tuple(
@@ -420,19 +429,24 @@
     def step(kb, carry):
         there = pl.ds(pl.multiple_of(kb * BLK, BLK), BLK)
         allowed = allowed_block(kb, qb, start_row)
+        spans = [slice(h * HD, (h + 1) * HD) for h in range(heads)]
+        queries = [qkv_ref[rows, here] for rows in spans]
+        scores = [mm(keys_ref[h, there, :], queries[h], NN) for h in range(heads)]
+        grad_probs = [mm(values_ref[h, there, :], grad[spans[h]], NN) for h in range(heads)]
+        probs, grad_scores = [], []
+        for h in range(heads):
+            masked = jnp.where(allowed, scores[h] * score_scale, neg_large)
+            prob = jnp.exp2(masked - log_ref[h : h + 1, :])
+            probs.append(prob.astype(bf16))
+            grad_scores.append((prob * (grad_probs[h] - deltas[h])).astype(bf16))
         new = []
         for h in range(heads):
-            rows = slice(h * HD, (h + 1) * HD)
-            queries = qkv_ref[rows, here]
-            scores = mm(keys_ref[h, there, :], queries, NN)
-            scores = jnp.where(allowed, scores * score_scale, neg_large)
-            probs = jnp.exp2(scores - log_ref[h : h + 1, :])
-            grad_probs = mm(values_ref[h, there, :], grad[rows], NN)
-            grad_scores = (probs * (grad_probs - deltas[h])).astype(bf16)
-            dv_ref[rows, there] += mm(grad[rows], probs.astype(bf16), NT)
-            dk_ref[rows, there] += mm(queries, grad_scores, NT)
+            dv_ref[spans[h], there] += mm(grad[spans[h]], probs[h], NT)
+        for h in range(heads):
+            dk_ref[spans[h], there] += mm(queries[h], grad_scores[h], NT)
+        for h in range(heads):
             keys = qkv_ref[width + h * HD : width + (h + 1) * HD, there]
-            new.append(carry[h] + mm(keys, grad_scores, NN))
+            new.append(carry[h] + mm(keys, grad_scores[h], NN))
         return tuple(new)
 
     grads = lax.fori_loop(
@@ -508,11 +522,12 @@
 def moe_kernel(n_dp, parts, x_ref, gate_ref, w_hbm, g_ref, *refs):
     piece_ref, dots_ref, out_ref, refs = refs[0], refs[1], refs[2], refs[3:]
     fin_hbm, refs = refs[:parts], refs[parts:]
+    cross_hbm, refs = refs[:EARLY], refs[EARLY:]
     (
         w_ref, x_in, x_far, g_far, gate_in, gate_far, gs_ref, gs_far, pair_ref, near_ref, far_ref,
         own_ref, piece_out, dot_out, dw_out, dw_in, fin_ref,
         w_sem, x_send, x_recv, t_send, t_recv, p_send, p_recv, d_send, d_recv,
-        xf_send, xf_recv, gf_send, gf_recv, tf_send, tf_recv, c_send, c_recv, keep_sem,
+        xf_send, xf_recv, gf_send, gf_recv, tf_send, tf_recv, c_send, c_recv, e_send, e_recv, keep_sem,
     ) = refs
     me, dp = lax.axis_index("seq"), lax.axis_index("dp")
     owners = n_dp // E
@@ -640,6 +655,16 @@
         part = pl.ds(pl.multiple_of(t * UNITS, UNITS), UNITS)
         for j in range(3):
             own_ref[j, part] = weight_grad(near_ref, x_in, gs_ref, j, part)
+
+    def far_grad(rows, j, part):
+        left = far_ref[(1, 2, 0)[j], :, part]
+        if j == 2:
+            right = gs_far[rows]
+        elif isinstance(rows, slice):
+            right = x_far[rows.start // CAP : rows.stop // CAP].reshape(PAIR, D)
+        else:
+            right = x_far[pl.ds(lax.div(rows.start, CAP), 2)].reshape(PAIR, D)
+        return mm(left, right, TN)
 
     @pl.loop(0, pairs)
     def _(i):
@@ -658,19 +683,31 @@
             mm(x, w_ref[1, part], NT),
         )
         for j in range(3):
-            far_ref[j, rows] = results[j]
+            far_ref[j] = results[j]
+
+        @pl.when(i < pairs - 1)
+        def _():
+            @pl.loop(0, half // UNITS)
+            def _(t):
+                part = pl.ds(pl.multiple_of(t * UNITS, UNITS), UNITS)
+                for j in range(3):
+                    own_ref[j, part] += far_grad(rows, j, part)
 
     tiles = half // UNITS // 2
+    final = slice((pairs - 2) * PAIR, (pairs - 1) * PAIR)
 
     def both_rows(side, t, j):
         part = pl.ds(pl.multiple_of((side * tiles + t) * UNITS, UNITS), UNITS)
-        return own_ref[j, part] + weight_grad(far_ref, x_far, gs_far, j, part)
+        return own_ref[j, part] + far_grad(final, j, part)
 
     @pl.loop(0, tiles)
     def _(t):
         for j in range(3):
             dw_out[t, j] = both_rows(1 - core, t, j).astype(bf16)
         core_copy(t).start()
+
+    def early_copy(t):
+        return remote_later(fin_ref.at[t], cross_hbm[t], (e_send, e_recv), t, {"seq": me ^ 2})
 
     @pl.loop(0, tiles)
     def _(t):
@@ -679,6 +716,11 @@
             total = (both_rows(core, t, j) + dw_in[t, j].astype(f32)).astype(bf16)
             for u in range(UNITS // PART):
                 fin_ref[t * (UNITS // PART) + u, j] = total[u * PART : (u + 1) * PART]
+
+        @pl.when(t == 0)
+        def _():
+            for e in range(EARLY):
+                early_copy(e).start()
 
     keeps = [
         pltpu.make_async_copy(fin_ref.at[t], fin_hbm[t], keep_sem.at[t]) for t in range(parts)
@@ -695,6 +737,8 @@
             copy.wait_send()
     for t in range(tiles):
         core_copy(t).wait_send()
+    for t in range(EARLY):
+        early_copy(t).wait()
     for keep in keeps:
         keep.wait()
 
@@ -712,9 +756,9 @@
             jax.ShapeDtypeStruct((n_dp, 1, CAP), f32),
             jax.ShapeDtypeStruct((n_dp, CAP, D), bf16),
         )
-        + (jax.ShapeDtypeStruct((3, PART, D), bf16),) * parts,
+        + (jax.ShapeDtypeStruct((3, PART, D), bf16),) * (parts + EARLY),
         in_specs=[HBM, VMEM, HBM, VMEM],
-        out_specs=[VMEM] * 3 + [HBM] * parts,
+        out_specs=[VMEM] * 3 + [HBM] * (parts + EARLY),
         scratch_shapes=[
             pltpu.VMEM(weights.shape, bf16),
             pltpu.VMEM((n_dp, CAP, D), bf16),
@@ -726,7 +770,7 @@
             pltpu.VMEM((rows, D), bf16),
             pltpu.VMEM((3, PAIR, units), bf16),
             pltpu.VMEM((3, rows, half), bf16),
-            pltpu.VMEM((3, rows, half), bf16),
+            pltpu.VMEM((3, PAIR, half), bf16),
             pltpu.VMEM((3, half, D), f32),
             pltpu.VMEM((n_dp, CAP, D), bf16),
             pltpu.VMEM((n_dp, 1, CAP), f32),
@@ -737,13 +781,14 @@
         ]
         + [DMA((n_dp,))] * 14
         + [DMA((tiles,))] * 2
+        + [DMA((EARLY,))] * 2
         + [DMA((parts,))],
         compiler_params=pltpu.CompilerParams(
             collective_id=4, has_side_effects=True, vmem_limit_bytes=67043328
         ),
         name="experts",
     )(x_slots, gate_slots, weights, grads)
-    return outs[0], outs[1], outs[2], list(outs[3:])
+    return outs[0], outs[1], outs[2], list(outs[3 : 3 + parts]), list(outs[3 + parts :])
 
 
 def experts_plain(to_owners, to_sources, n_dp, x_slots, gate_slots, weights, grads):
@@ -1009,15 +1054,16 @@
     n_seq, n_dp, parts, g_ref, wt_ref, wo_ref, pack_ref, gate_ref, slot_ref, gain_ref,
     a_hbm, h_hbm, resid_hbm, base_hbm, out_hbm, *refs,
 ):
-    n_far = max(parts - 1, 0)
+    n_far = max(parts - LATE, 0)
     fin_hbm, refs = refs[:parts], refs[parts:]
     far_hbm, refs = refs[:n_far], refs[n_far:]
     din_ref, row_in, line_ref, block_ref, both_ref, refs = *refs[:5], refs[5:]
     (
         a_ref, h_ref, resid_ref, base_ref, rows_ref, far_ref, fin_ref,
         core_out, core_in, x_out, x_in, part_ref, w_out_buf, w_in, wo_buf, wo_in, wo_x, wo_far,
-        row_buf, pack_in, line_buf, line_in, load_sem, c_sems, x_sems, w_sems, r_sems, o_sems,
-        p_sems, q_sems, l_sems, t_sems, f_sems, keep_sem,
+        w_mid, wo_mid,
+        row_buf, pack_in, line_buf, line_in, load_sem, c_sems, x_sems, w_sems, v_sems, r_sems, o_sems,
+        p_sems, q_sems, u_sems, l_sems, t_sems, f_sems, keep_sem,
     ) = refs
     me, dp = lax.axis_index("seq"), lax.axis_index("dp")
     tok = h_ref.shape[0]
@@ -1030,10 +1076,11 @@
     def both(sems):
         return sems.at[0], sems.at[1]
 
-    c_sems, x_sems, w_sems, r_sems, o_sems, p_sems, q_sems, l_sems, t_sems, f_sems = (
+    c_sems, x_sems, w_sems, v_sems, r_sems, o_sems, p_sems, q_sems, u_sems, l_sems, t_sems, f_sems = (
         both(sems)
         for sems in (
-            c_sems, x_sems, w_sems, r_sems, o_sems, p_sems, q_sems, l_sems, t_sems, f_sems
+            c_sems, x_sems, w_sems, v_sems, r_sems, o_sems, p_sems, q_sems, u_sems, l_sems, t_sems,
+            f_sems,
         )
     )
 
@@ -1055,12 +1102,37 @@
     def there(k):
         return lax.rem(dp + k, n_dp)
 
+    spots = [*range(n_dp // 2 - 1, -1, -1)]
+
+    def to_neighbour(buf, near, sems):
+        return {
+            j: remote(buf.at[dp ^ (2 * j) ^ 1], near.at[j], sems, j, {"dp": dp ^ 1}) for j in spots
+        }
+
+    def pass_sums(copies, buf, near, mid, sems):
+        passed = []
+        for j in spots:
+            copies[j].wait_recv()
+            total = buf[dp ^ (2 * j)].astype(f32) + near[j].astype(f32)
+            mid[j] = total.astype(bf16)
+            if j:
+                passed.append(
+                    remote(mid.at[j], near.at[n_dp // 2 + j], sems, j, {"dp": dp ^ (2 * j)})
+                )
+        return passed
+
+    def collect(passed, near, mid):
+        for copy in passed:
+            copy.wait_recv()
+        return sum((near[n_dp // 2 + j].astype(f32) for j in spots[:-1]), mid[0].astype(f32))
+
     def term(place):
         columns = pl.ds(pl.multiple_of((me ^ place) * tok, tok), tok)
         return mm(g_ref[:, columns], wt_ref[...], TN)
 
     part_copies = [
-        remote(fin_hbm[t], far_ref.at[t], t_sems, 0, {"seq": me ^ 2}) for t in range(n_far, parts)
+        remote(fin_hbm[t], far_ref.at[t], t_sems, t - n_far, {"seq": me ^ 2})
+        for t in range(n_far, parts)
     ]
     pack_copies = [
         remote(pack_ref.at[there(k)], pack_in.at[dp], p_sems, k, {"dp": there(k)}) for k in others
@@ -1068,10 +1140,7 @@
     pack_in[dp] = pack_ref[dp]
     for i in range(pairs):
         wo_buf[:, :, i * width : (i + 1) * width] = wo_ref[i].reshape(n_dp, shard, width)
-    wo_in[dp] = wo_buf[dp]
-    wo_copies = [
-        remote(wo_buf.at[there(k)], wo_in.at[dp], q_sems, k, {"dp": there(k)}) for k in others
-    ]
+    wo_near = to_neighbour(wo_buf, wo_in, q_sems)
     core_copies = []
     for i in range(pairs - 1, -1, -1):
         core_out[i] = term(2 * i + 1).astype(bf16)
@@ -1087,10 +1156,9 @@
     loads[0].wait()
     turned = mm(g_ref[...], a_ref[...], NN)
     w_out_buf[...] = turned.T.astype(bf16).reshape(n_dp, shard, width3)
-    w_in[dp] = w_out_buf[dp]
-    w_copies = [
-        remote(w_out_buf.at[there(k)], w_in.at[dp], w_sems, k, {"dp": there(k)}) for k in others
-    ]
+    w_near = to_neighbour(w_out_buf, w_in, w_sems)
+    wo_copies = pass_sums(wo_near, wo_buf, wo_in, wo_mid, u_sems)
+    w_copies = pass_sums(w_near, w_out_buf, w_in, w_mid, v_sems)
     part = term(0)
     core_copies[0].wait_recv()
     part_ref[...] = part + core_in[0].astype(f32)
@@ -1122,9 +1190,7 @@
         loads[5 + parts + t].wait()
         hand_over(far_ref, 1, t)
 
-    for copy in wo_copies:
-        copy.wait_recv()
-    wo_total = jnp.sum(wo_in[...].astype(f32), axis=0)
+    wo_total = collect(wo_copies, wo_in, wo_mid)
     wo_cross = []
     for i in range(1, pairs):
         wo_x[i - 1] = wo_total[:, i * width : (i + 1) * width].astype(bf16)
@@ -1154,9 +1220,9 @@
     loads[4].wait()
     din_ref[...] = resid_ref[...] + norm_back(h_ref[...].astype(f32), gain_ref[0:1], grad)
 
-    for copy in w_copies + wo_cross:
+    row_buf[:, :width3] = collect(w_copies, w_in, w_mid).astype(bf16)
+    for copy in wo_cross:
         copy.wait_recv()
-    row_buf[:, :width3] = jnp.sum(w_in[...].astype(f32), axis=0).astype(bf16)
     wo_mine = wo_total[:, :width]
     for i in range(pairs - 1):
         wo_mine = wo_mine + wo_far[i].astype(f32)
@@ -1169,13 +1235,13 @@
     for copy in line_copies:
         copy.wait_recv()
     line_ref[...] = jnp.sum(line_in[...], axis=0)
-    for copy in part_copies:
+    for t, copy in enumerate(part_copies):
         copy.wait_recv()
-        hand_over(far_ref, 1, n_far)
+        hand_over(far_ref, 1, n_far + t)
     for copy in row_copies + fin_copies:
         copy.wait_recv()
     for copy in (
-        core_copies + w_copies + x_copies + row_copies + wo_copies + pack_copies
+        core_copies + [*w_near.values()] + [*wo_near.values()] + w_copies + x_copies + row_copies + wo_copies + pack_copies
         + line_copies + wo_cross + part_copies + fin_copies
     ):
         copy.wait_send()
@@ -1223,6 +1289,8 @@
             pltpu.VMEM((n_dp, shard, pairs * width), bf16),
             pltpu.VMEM((pairs - 1, shard, width), bf16),
             pltpu.VMEM((pairs - 1, shard, width), bf16),
+            pltpu.VMEM((n_dp // 2, shard, width3), bf16),
+            pltpu.VMEM((n_dp // 2, shard, pairs * width), bf16),
             pltpu.VMEM((shard, width3 + width), bf16),
             pltpu.VMEM((n_dp, LINES, shard), f32),
             pltpu.VMEM((LINES, shard), f32),
@@ -1230,13 +1298,15 @@
             DMA((5 + 2 * room,)),
             DMA((2, pairs)),
             DMA((2, pairs)),
-            DMA((2, n_dp)),
+            DMA((2, n_dp // 2)),
+            DMA((2, n_dp // 2)),
             DMA((2, n_seq)),
             DMA((2, pairs)),
             DMA((2, n_dp)),
-            DMA((2, n_dp)),
+            DMA((2, n_dp // 2)),
+            DMA((2, n_dp // 2)),
             DMA((2, n_seq)),
-            DMA((2, 1)),
+            DMA((2, LATE)),
             DMA((2, 2 * room)),
             DMA((2 * room,)),
         ],
@@ -1254,7 +1324,9 @@
     n_seq, me_ref, both_ref, row_ref, line_ref, wq_ref, gain_ref,
     de_ref, dw_ref, dwo_ref, again_ref, mgain_ref, router_ref, carry_ref, vec_ref, mix_ref,
 ):
-    de_ref[...] = both_ref[0, 0].astype(f32)
+    step = both_ref.shape[3]
+    for t in range(both_ref.shape[1]):
+        de_ref[:, t * step : (t + 1) * step] = both_ref[0, t].astype(f32)
 
     @pl.when(pl.program_id(0) == 0)
     def _():
@@ -1279,6 +1351,8 @@
     shard = w_qkv.shape[0]
     _, parts, three, step, _ = both.shape
     units = n_seq * parts * step
+    group = 4 if parts % 4 == 0 else 1
+    steps = parts // group
 
     def whole(shape):
         return pl.BlockSpec(shape, lambda i, me_ref: (0,) * len(shape))
@@ -1291,18 +1365,18 @@
         + [jax.ShapeDtypeStruct(shape, f32) for shape in shapes],
         grid_spec=pltpu.PrefetchScalarGridSpec(
             num_scalar_prefetch=1,
-            grid=(n_seq * parts,),
+            grid=(n_seq * steps,),
             in_specs=[
                 pl.BlockSpec(
-                    (1, 1, three, step, D),
-                    lambda i, me_ref: ((i // parts) ^ me_ref[0], i % parts, 0, 0, 0),
+                    (1, group, three, step, D),
+                    lambda i, me_ref: ((i // steps) ^ me_ref[0], i % steps, 0, 0, 0),
                 ),
                 whole(row_in.shape),
                 whole(lines.shape),
                 whole(w_qkv.shape),
                 whole((1, shard)),
             ],
-            out_specs=[pl.BlockSpec((three, step, D), lambda i, me_ref: (0, i, 0))]
+            out_specs=[pl.BlockSpec((three, group * step, D), lambda i, me_ref: (0, i, 0))]
             + [whole(shape) for shape in shapes],
         ),
         name="finish",
@@ -1370,19 +1444,19 @@
         piece, dots, partial, d_plain = experts_plain(
             to_owners, to_sources, n_dp, x_slots, gate_slots, experts, arrived_grad
         )
-        fin = []
+        fin, far = [], []
     else:
-        piece, dots, partial, fin = moe_call(
+        piece, dots, partial, fin, far = moe_call(
             n_dp, x_slots, gate_slots, experts, arrived_grad
         )
     back_out = to_sources(partial)
 
     (grad_resid, grad_out, base, d_prev, pack, wo_sum), far_back = mid_back_call(
         n_seq, n_dp, piece, dots, cot, resid_mid, gates, slot_of, routes_t, small, heads_t,
-        out_weight, prev_t, w_carry, fin[:1],
-    )
-    later, grad_out = lax.optimization_barrier((fin[1:-1], grad_out))
-    far = far_back + [swap(part, "seq", 2) for part in later]
+        out_weight, prev_t, w_carry, fin[EARLY : EARLY + 1],
+    )
+    later, grad_out = lax.optimization_barrier((fin[EARLY + 1 : -LATE], grad_out))
+    far = far + far_back + [swap(part, "seq", 2) for part in later]
     grad_qkv = attn_back_call(
         lows, qkv, grad_out, attended_exact, logs, start_row, cos_t, sin_t
     )

time: 319 us -> 308 us (0.966)
  Pallas kernels: 298 us -> 279 us
  starting transfers between devices: 11.9 us -> 21.8 us
    pallas_call x1, Pallas kernels: 92.5 us -> 103 us  [moe_call(): pl.pallas_call(functools.partial(moe_kernel, n_dp, parts), out_shape=(jax...]
    all_to_all x1, starting transfers between devices: 5.4 us -> 14.3 us  [to_sources(): return lax.all_to_all(values, 'dp', split_axis=0, concat_axis=0, tiled=True)]
    pallas_call x1, Pallas kernels: 23.6 us -> 15.7 us  [attn_call(): pl.pallas_call(attn_kernel, out_shape=(jax.ShapeDtypeStruct((seq_len // t...]
    pallas_call x1, Pallas kernels: 55.4 us -> 48.4 us  [tail_call(): pl.pallas_call(functools.partial(tail_kernel, n_seq, n_dp, parts), out_sh...]
    pallas_call x1, Pallas kernels: 29.3 us -> 23.5 us  [mid_back_call(): pl.pallas_call(functools.partial(mid_back_kernel, n_seq, n_dp, n_tile), o...]
    pallas_call x1, Pallas kernels: 25.5 us -> 20.2 us  [attn_back_call(): pl.pallas_call(attn_back_kernel, out_shape=jax.ShapeDtypeStruct((width3,...]
  transfers between devices with their start and end apart: 4 -> 5, of which waited for: 1 -> 0; matrix products, arithmetic and copies ran while one was open for 0% -> 0% of each run, Pallas kernels for 30% -> 25%
where the time goes in v6:
time: 308 us; the launch traced here: 310 us
  Pallas kernels  279 us (91%)
  starting transfers between devices  21.8 us (7%)
  local copies, waits for them, and re-layouts  4.93 us (2%)
    pallas_call x1, Pallas kernels, moe_call(): pl.pallas_call(functools.partial(moe_kernel, n_dp, parts), out_shape=(jax...  103 us
    pallas_call x1, Pallas kernels, tail_call(): pl.pallas_call(functools.partial(tail_kernel, n_seq, n_dp, parts), out_sh...  48.4 us
    pallas_call x1, Pallas kernels, start_call(): pl.pallas_call(functools.partial(start_kernel, n_seq, n_dp), out_shape=(j...  38 us
    pallas_call x1, Pallas kernels, mid_back_call(): pl.pallas_call(functools.partial(mid_back_kernel, n_seq, n_dp, n_tile), o...  23.5 us
    pallas_call x1, Pallas kernels, attn_back_call(): pl.pallas_call(attn_back_kernel, out_shape=jax.ShapeDtypeStruct((width3,...  20.2 us
    pallas_call x1, Pallas kernels, mid_call(): pl.pallas_call(functools.partial(mid_kernel, n_seq), out_shape=(jax.Shape...  18.3 us
    pallas_call x1, Pallas kernels, attn_call(): pl.pallas_call(attn_kernel, out_shape=(jax.ShapeDtypeStruct((seq_len // t...  15.7 us
    all_to_all x1, starting transfers between devices, to_sources(): return lax.all_to_all(values, 'dp', split_axis=0, concat_axis=0, tiled=True)  14.3 us
  transfers between devices with their start and end apart: 5, of which 0 were waited for; matrix products, arithmetic and copies ran while one was open for 0% of the time, Pallas kernels for 25%

profile of v6, /device:TPU:13, one launch (start us, length us, event | category | flops | bytes accessed | tf_op | source)
XLA Modules:
  0.0 309.6 jit_solution(16373584629246548768)
XLA Ops:
  0.7 1.8 multiply_sine_fusion
  2.5 38.0 %start.1 = (bf16[2048,768]{1,0:T(8,128)(2,1)}, bf16[576,2048]{1,0:T(8,128)(2,1)}, bf16[576,768]{1,0:T(8,128)(2,1)}, f32[32,768]{1,0:T(8,128)}, s32[2,512]{1,0:T(...) custom-call(bf16[512,768]{1,0:T(8,128)(2,1)} %bitcast.18, bf16[96,2304]{1,0:T(8,128)(2,1)} %wq_ref.1, ...), custom_call_target="tpu_custom_call" | custom-call | tf_op jit(solution)/shard_map/start/pallas_call | solution.py:273
  40.4 0.0 copy-start.8
  40.4 4.9 %all-to-all-start = ((bf16[8,128,768]{2,1,0:T(8,128)(2,1)}), bf16[8,128,768]{2,1,0:T(8,128)(2,1)}, u32[]{:S(2)}, u32[]{:S(2)}) async-start(bf16[8,128,768]{2,1,0:T(8,128)(2,1)} %get-tuple-element.72), calls=%async_computation | async-start | bytes 3145728 | tf_op jit(solution)/shard_map/all_to_all | solution.py:1418
  45.4 0.1 convert_reduce_fusion
  45.5 0.1 select_reduce_fusion
  45.6 0.0 copy-start.10
  45.6 0.1 slice.3
  45.7 0.5 and_select_fusion.lo_ref
  46.2 15.7 %attend.1 = (bf16[4,192,512]{2,1,0:T(8,128)(2,1)}, f32[192,2048]{1,0:T(8,128)}, f32[3,2048]{1,0:T(4,128)}) custom-call(s32[8]{0:T(128)} %and_select_fusion.lo_ref, bf16[576,2048]{1,0:T(8,128)(2,1)} %get-tuple-element.65.qkv_ref, s32[1,2048]{1,0:T(1,128)} %bitcast.33), custom_call_target="tpu_custom_call" | custom-call | flops 16000000000 | bytes 16000000 | tf_op jit(solution)/shard_map/attend/pallas_call | solution.py:372
  62.0 18.3 %mid.1 = (bf16[4,192,512]{2,1,0:T(8,128)(2,1)}, f32[512,768]{1,0:T(8,128)}, f32[8,512]{1,0:T(8,128)}, bf16[8,128,768]{2,1,0:T(8,128)(2,1)}, f32[8,1,128]{2,1,0:T(1,128)}) custom-call(bf16[4,192,512]{2,1,0:T(8,128)(2,1)} %get-tuple-element.66.att_ref, bf16[512,768]{1,0:T(8,128)(2,1)} %bitcast.19, f32[12,1,512]{2,1,0:T(1,128)} %bitcast.25, ...), custom_call_target="tpu_custom_call" | custom-call | tf_op jit(solution)/shard_map/mid/pallas_call | solution.py:870
  80.3 0.0 all-to-all-done.g_ref
  80.3 102.8 %experts.1 = (bf16[8,128,768]{2,1,0:T(8,128)(2,1)}, f32[8,1,128]{2,1,0:T(1,128)}, bf16[8,128,768]{2,1,0:T(8,128)(2,1)}, bf16[3,64,768]{2,1,0:T(8,128)(2,1)}, bf1...) custom-call(bf16[8,128,768]{2,1,0:T(8,128)(2,1)} %get-tuple-element., ...), custom_call_target="tpu_custom_call" | custom-call | tf_op jit(solution)/shard_map/experts/pallas_call | solution.py:752
  183.1 14.3 %all-to-all-start.1 = ((bf16[8,128,768]{2,1,0:T(8,128)(2,1)}), bf16[8,128,768]{2,1,0:T(8,128)(2,1)}, u32[]{:S(2)}, u32[]{:S(2)}) async-start(bf16[8,128,768]{2,1,0:T(8,128)(2,1)} %get-tuple-element.92), calls=%async_computation.1 | async-start | bytes 3145728 | tf_op jit(solution)/shard_map/all_to_all | solution.py:1423
  197.4 23.5 %mid_back.1 = (f32[512,768]{1,0:T(8,128)}, bf16[4,192,512]{2,1,0:T(8,128)(2,1)}, f32[512,768]{1,0:T(8,128)}, f32[12,1,512]{2,1,0:T(1,128)}, f32[8,40,96]{2,1,0:T...) custom-call(bf16[8,128,768]{2,1,0:T(8,128)(2,1)} %get-tuple-element.76.piece_ref, ...), custom_call_target="tpu_custom_call" | custom-call | tf_op jit(solution)/shard_map/mid_back/pallas_call | solution.py:1023
  220.9 1.1 collective-permute-start
  222.0 0.4 collective-permute-start.1
  222.4 1.1 collective-permute-start.2
  223.5 20.2 %attend_back.1.g_ref = bf16[576,2048]{1,0:T(8,128)(2,1)} custom-call(s32[8]{0:T(128)} %and_select_fusion.lo_ref, bf16[576,2048]{1,0:T(8,128)(2,1)} %get-tuple-element.65.qkv_ref, bf16[4,192,512]{2,1,0:T(8,128)(2,1)} %get-tuple-element.83.go_ref, f32[192,2048]{1,0:T(8,128)} %get-tuple-element.84.exact_ref, f32[3,2048]{1,0:T(4,128)} %get-tuple-element.85.log_ref, ...), custom_call_target="tpu_custom_call" | custom-call | flops 16000000000 | bytes 16000000 | tf_op jit(solution)/shard_map/attend_back/pallas_call | solution.py:481
  243.6 0.0 collective-permute-done.refs_11_
  243.7 0.0 collective-permute-done.1.refs_12_
  243.7 0.0 copy-start.6
  243.7 0.0 collective-permute-done.2.refs_13_
  243.7 0.7 copy-done.5
  244.4 0.1 copy-done.6
  244.5 0.6 copy-done.7
  245.1 48.4 %tail.1 = (f32[512,768]{1,0:T(8,128)}, bf16[4,96,768]{2,1,0:T(8,128)(2,1)}, f32[40,96]{1,0:T(8,128)}, bf16[512,768]{1,0:T(8,128)(2,1)}, bf16[4,8,3,64,768]{4,3,2,1,0:T(8,128)(2,1)}) custom-call(bf16[576,2048]{1,0:T(8,128)(2,1)} %attend_back.1.g_ref, bf16[576,768]{1,0:T(8,128)(2,1)} %get-tuple-element.86.wt_ref, ...), custom_call_target="tpu_custom_call" | custom-call | tf_op jit(solution)/shard_map/tail/pallas_call | solution.py:1262
  293.5 12.7 %finish.1 = (f32[3,2048,768]{2,1,0:T(8,128)}, f32[96,2304]{1,0:T(8,128)}, f32[96,768]{1,0:T(8,128)}, f32[1,96]{1,0:T(1,128)}, f32[1,96]{1,0:T(1,128)}, /*index=5...) custom-call(s32[1]{0:T(128)} %bitcast.14.me_ref, ...), custom_call_target="tpu_custom_call" | custom-call | tf_op jit(solution)/shard_map/finish/pallas_call | solution.py:1362
  306.2 0.9 copy.29
  307.1 0.8 copy-done
  307.9 1.1 copy.30
  309.0 0.6 copy.31
  (18 shorter events, 0.0 us)
Async XLA Ops:
  40.4 4.9 %copy-start.8 = (s32[1,2048]{1,0:T(1,128)S(1)}, s32[1,2048]{1,0:T(1,128)}, u32[]{:S(2)}) copy-start(s32[1,2048]{1,0:T(1,128)} %param.16) | copy-start | bytes 24580
  40.4 39.8 %all-to-all-start = ((bf16[8,128,768]{2,1,0:T(8,128)(2,1)}), bf16[8,128,768]{2,1,0:T(8,128)(2,1)}, u32[]{:S(2)}, u32[]{:S(2)}) async-start(bf16[8,128,768]{2,1,0:T(8,128)(2,1)} %get-tuple-element.72), calls=%async_computation | async-start | bytes 3145728 | tf_op jit(solution)/shard_map/all_to_all | solution.py:1418
  45.6 0.6 copy-start.10
  183.1 61.3 %all-to-all-start.1 = ((bf16[8,128,768]{2,1,0:T(8,128)(2,1)}), bf16[8,128,768]{2,1,0:T(8,128)(2,1)}, u32[]{:S(2)}, u32[]{:S(2)}) async-start(bf16[8,128,768]{2,1,0:T(8,128)(2,1)} %get-tuple-element.92), calls=%async_computation.1 | async-start | bytes 3145728 | tf_op jit(solution)/shard_map/all_to_all | solution.py:1423
  197.4 23.5 %copy-start.2 = (bf16[3,64,768]{2,1,0:T(8,128)(2,1)S(1)}, bf16[3,64,768]{2,1,0:T(8,128)(2,1)}, u32[]{:S(2)}) copy-start(bf16[3,64,768]{2,1,0:T(8,128)(2,1)} %get-tuple-element.100.refs_3_) | copy-start | bytes 884740
  197.4 24.6 %copy-start.3 = (bf16[3,64,768]{2,1,0:T(8,128)(2,1)S(1)}, bf16[3,64,768]{2,1,0:T(8,128)(2,1)}, u32[]{:S(2)}) copy-start(bf16[3,64,768]{2,1,0:T(8,128)(2,1)} %get-tuple-element.101.refs_4_) | copy-start | bytes 884740
  197.4 25.0 %copy-start.4 = (bf16[3,64,768]{2,1,0:T(8,128)(2,1)S(1)}, bf16[3,64,768]{2,1,0:T(8,128)(2,1)}, u32[]{:S(2)}) copy-start(bf16[3,64,768]{2,1,0:T(8,128)(2,1)} %get-tuple-element.102.refs_5_) | copy-start | bytes 884740
  220.9 22.8 %collective-permute-start = (bf16[3,64,768]{2,1,0:T(8,128)(2,1)S(1)}, bf16[3,64,768]{2,1,0:T(8,128)(2,1)S(1)}, u32[]{:S(2)}, u32[]{:S(2)}) collective-permute-start(bf16[3,64,768]{2,1,0:T(8,128)(2,1)S(1)} %copy-done.2), channel_id=1, source_target_pairs={{0,2},{1,3},{2,0},{3,1},{4,6},{5,7},{6,4},{7,5},{8,10},{9,11},{10,... | collective-permute-start | bytes 884744 | tf_op jit(solution)/shard_map/ppermute | solution.py:48
  222.0 21.6 %collective-permute-start.1 = (bf16[3,64,768]{2,1,0:T(8,128)(2,1)S(1)}, bf16[3,64,768]{2,1,0:T(8,128)(2,1)S(1)}, u32[]{:S(2)}, u32[]{:S(2)}) collective-permute-start(bf16[3,64,768]{2,1,0:T(8,128)(2,1)S(1)} %copy-done.3), channel_id=1, source_target_pairs={{0,2},{1,3},{2,0},{3,1},{4,6},{5,7},{6,4},{7,5},{8,10},{9,11},{10,... | collective-permute-start | bytes 884744 | tf_op jit(solution)/shard_map/ppermute | solution.py:48
  222.4 21.3 %collective-permute-start.2 = (bf16[3,64,768]{2,1,0:T(8,128)(2,1)S(1)}, bf16[3,64,768]{2,1,0:T(8,128)(2,1)S(1)}, u32[]{:S(2)}, u32[]{:S(2)}) collective-permute-start(bf16[3,64,768]{2,1,0:T(8,128)(2,1)S(1)} %copy-done.4), channel_id=1, source_target_pairs={{0,2},{1,3},{2,0},{3,1},{4,6},{5,7},{6,4},{7,5},{8,10},{9,11},{10,... | collective-permute-start | bytes 884744 | tf_op jit(solution)/shard_map/ppermute | solution.py:48
  243.6 0.7 copy-start.5
  243.7 0.8 copy-start.6
  244.4 0.7 copy-start.7
  293.5 12.7 %copy-start.1 = (bf16[512,768]{1,0:T(8,128)(2,1)S(1)}, bf16[512,768]{1,0:T(8,128)(2,1)}, u32[]{:S(2)}) copy-start(bf16[512,768]{1,0:T(8,128)(2,1)} %get-tuple-element.103) | copy-start | bytes 2359300
  306.2 1.7 copy-start
  307.9 1.1 copy-start.9

commit v7 on v6

--- a/solution.py
+++ b/solution.py
@@ -17,7 +17,7 @@
 PAIR = 2 * CAP
 UNITS = 256
 PART = 64
-EARLY = 2
+EARLY = 1
 LATE = 2
 SMALL = 32
 LINES = 40
@@ -565,7 +565,7 @@
     def core_copy(t):
         return remote_later(dw_out.at[t], dw_in.at[t], (c_send, c_recv), t, {"seq": me ^ 1})
 
-    for p in [0, pairs - 1, *range(1, pairs - 1)]:
+    for p in range(pairs):
         for k in (2 * p, 2 * p + 1):
             if k:
                 gate_copy(k).start()
@@ -579,7 +579,7 @@
         load.wait()
 
     def place(i):
-        return jnp.where(i == 0, 0, 1 + lax.rem(i + pairs - 3, pairs - 1))
+        return i + 0
 
     def scale(ref, rows, gate, k):
         column = jnp.broadcast_to(gate, (CAP, CAP)).T[:, 0:1]
@@ -694,7 +694,7 @@
                     own_ref[j, part] += far_grad(rows, j, part)
 
     tiles = half // UNITS // 2
-    final = slice((pairs - 2) * PAIR, (pairs - 1) * PAIR)
+    final = slice((pairs - 1) * PAIR, pairs * PAIR)
 
     def both_rows(side, t, j):
         part = pl.ds(pl.multiple_of((side * tiles + t) * UNITS, UNITS), UNITS)

time: 308 us -> 303 us (0.984); the launches traced: 310 us -> 300 us
  starting transfers between devices: 21.8 us -> 12.2 us
  waiting for transfers between devices: 0.01 us -> 8.32 us
  Pallas kernels: 279 us -> 272 us
    all_to_all x1, starting transfers between devices: 14.3 us -> 4.26 us  [to_sources(): return lax.all_to_all(values, 'dp', split_axis=0, concat_axis=0, tiled=True)]
    ppermute x3 -> x4, waiting for transfers between devices: 0.01 us -> 7.05 us  [swap(): return lax.ppermute(value, axis, [(i, i ^ bit) for i in range(size)])]
  transfers between devices with their start and end apart: 5 -> 6, of which waited for: 0 -> 3; matrix products, arithmetic and copies ran while one was open for 0% -> 0% of each run, Pallas kernels for 25% -> 24%
where the time goes in v7:
time: 303 us; the launch traced here: 300 us
  Pallas kernels  272 us (90%)
  starting transfers between devices  12.2 us (4%)
  waiting for transfers between devices  8.32 us (3%)
  local copies, waits for them, and re-layouts  4.25 us (1%)
    pallas_call x1, Pallas kernels, moe_call(): pl.pallas_call(functools.partial(moe_kernel, n_dp, parts), out_shape=(jax...  101 us
    pallas_call x1, Pallas kernels, tail_call(): pl.pallas_call(functools.partial(tail_kernel, n_seq, n_dp, parts), out_sh...  47.9 us
    pallas_call x1, Pallas kernels, start_call(): pl.pallas_call(functools.partial(start_kernel, n_seq, n_dp), out_shape=(j...  38 us
    pallas_call x1, Pallas kernels, mid_back_call(): pl.pallas_call(functools.partial(mid_back_kernel, n_seq, n_dp, n_tile), o...  22.9 us
    pallas_call x1, Pallas kernels, mid_call(): pl.pallas_call(functools.partial(mid_kernel, n_seq), out_shape=(jax.Shape...  18.7 us
    pallas_call x1, Pallas kernels, attn_back_call(): pl.pallas_call(attn_back_kernel, out_shape=jax.ShapeDtypeStruct((width3,...  17.8 us
    pallas_call x1, Pallas kernels, attn_call(): pl.pallas_call(attn_kernel, out_shape=(jax.ShapeDtypeStruct((seq_len // t...  13.6 us
    pallas_call x1, Pallas kernels, finish_call(): pl.pallas_call(functools.partial(finish_kernel, n_seq), out_shape=[jax.Sh...  12.7 us
  transfers between devices with their start and end apart: 6, of which 3 were waited for; matrix products, arithmetic and copies ran while one was open for 0% of the time, Pallas kernels for 24%

profile of v7, /device:TPU:13, one launch (start us, length us, event | category | flops | bytes accessed | tf_op | source)
XLA Modules:
  0.0 300.5 jit_solution(17160630142202171221)
XLA Ops:
  0.7 1.8 multiply_sine_fusion
  2.5 38.0 %start.1 = (bf16[2048,768]{1,0:T(8,128)(2,1)}, bf16[576,2048]{1,0:T(8,128)(2,1)}, bf16[576,768]{1,0:T(8,128)(2,1)}, f32[32,768]{1,0:T(8,128)}, s32[2,512]{1,0:T(...) custom-call(bf16[512,768]{1,0:T(8,128)(2,1)} %bitcast.18, bf16[96,2304]{1,0:T(8,128)(2,1)} %wq_ref.1, ...), custom_call_target="tpu_custom_call" | custom-call | tf_op jit(solution)/shard_map/start/pallas_call | solution.py:273
  40.5 0.0 copy-start.10
  40.5 4.9 %all-to-all-start = ((bf16[8,128,768]{2,1,0:T(8,128)(2,1)}), bf16[8,128,768]{2,1,0:T(8,128)(2,1)}, u32[]{:S(2)}, u32[]{:S(2)}) async-start(bf16[8,128,768]{2,1,0:T(8,128)(2,1)} %get-tuple-element.72), calls=%async_computation | async-start | bytes 3145728 | tf_op jit(solution)/shard_map/all_to_all | solution.py:1418
  45.4 0.1 convert_reduce_fusion
  45.5 0.1 select_reduce_fusion
  45.6 0.0 copy-start.12
  45.6 0.1 slice.3
  45.7 0.5 and_select_fusion.lo_ref
  46.3 13.6 %attend.1 = (bf16[4,192,512]{2,1,0:T(8,128)(2,1)}, f32[192,2048]{1,0:T(8,128)}, f32[3,2048]{1,0:T(4,128)}) custom-call(s32[8]{0:T(128)} %and_select_fusion.lo_ref, bf16[576,2048]{1,0:T(8,128)(2,1)} %get-tuple-element.65.qkv_ref, s32[1,2048]{1,0:T(1,128)} %bitcast.33), custom_call_target="tpu_custom_call" | custom-call | flops 16000000000 | bytes 16000000 | tf_op jit(solution)/shard_map/attend/pallas_call | solution.py:372
  59.9 18.7 %mid.1 = (bf16[4,192,512]{2,1,0:T(8,128)(2,1)}, f32[512,768]{1,0:T(8,128)}, f32[8,512]{1,0:T(8,128)}, bf16[8,128,768]{2,1,0:T(8,128)(2,1)}, f32[8,1,128]{2,1,0:T(1,128)}) custom-call(bf16[4,192,512]{2,1,0:T(8,128)(2,1)} %get-tuple-element.66.att_ref, bf16[512,768]{1,0:T(8,128)(2,1)} %bitcast.19, f32[12,1,512]{2,1,0:T(1,128)} %bitcast.25, ...), custom_call_target="tpu_custom_call" | custom-call | tf_op jit(solution)/shard_map/mid/pallas_call | solution.py:870
  78.6 1.3 all-to-all-done.g_ref
  79.9 100.8 %experts.1 = (bf16[8,128,768]{2,1,0:T(8,128)(2,1)}, f32[8,1,128]{2,1,0:T(1,128)}, bf16[8,128,768]{2,1,0:T(8,128)(2,1)}, bf16[3,64,768]{2,1,0:T(8,128)(2,1)}, bf1...) custom-call(bf16[8,128,768]{2,1,0:T(8,128)(2,1)} %get-tuple-element., ...), custom_call_target="tpu_custom_call" | custom-call | tf_op jit(solution)/shard_map/experts/pallas_call | solution.py:752
  180.6 4.3 %all-to-all-start.1 = ((bf16[8,128,768]{2,1,0:T(8,128)(2,1)}), bf16[8,128,768]{2,1,0:T(8,128)(2,1)}, u32[]{:S(2)}, u32[]{:S(2)}) async-start(bf16[8,128,768]{2,1,0:T(8,128)(2,1)} %get-tuple-element.93), calls=%async_computation.1 | async-start | bytes 3145728 | tf_op jit(solution)/shard_map/all_to_all | solution.py:1423
  184.9 22.9 %mid_back.1 = (f32[512,768]{1,0:T(8,128)}, bf16[4,192,512]{2,1,0:T(8,128)(2,1)}, f32[512,768]{1,0:T(8,128)}, f32[12,1,512]{2,1,0:T(1,128)}, f32[8,40,96]{2,1,0:T...) custom-call(bf16[8,128,768]{2,1,0:T(8,128)(2,1)} %get-tuple-element.77.piece_ref, ...), custom_call_target="tpu_custom_call" | custom-call | tf_op jit(solution)/shard_map/mid_back/pallas_call | solution.py:1023
  207.9 1.3 collective-permute-start
  209.1 0.3 collective-permute-start.1
  209.4 1.2 collective-permute-start.2
  210.6 0.3 collective-permute-start.3
  210.9 17.8 %attend_back.1.g_ref = bf16[576,2048]{1,0:T(8,128)(2,1)} custom-call(s32[8]{0:T(128)} %and_select_fusion.lo_ref, bf16[576,2048]{1,0:T(8,128)(2,1)} %get-tuple-element.65.qkv_ref, bf16[4,192,512]{2,1,0:T(8,128)(2,1)} %get-tuple-element.84.go_ref, f32[192,2048]{1,0:T(8,128)} %get-tuple-element.85.exact_ref, f32[3,2048]{1,0:T(4,128)} %get-tuple-element.86.log_ref, ...), custom_call_target="tpu_custom_call" | custom-call | flops 16000000000 | bytes 16000000 | tf_op jit(solution)/shard_map/attend_back/pallas_call | solution.py:481
  228.7 0.0 collective-permute-done.refs_10_
  228.7 0.0 collective-permute-done.1.refs_11_
  228.7 0.0 copy-start.7
  228.7 0.7 collective-permute-done.2.refs_12_
  229.4 6.3 %collective-permute-done.3.refs_13_ = bf16[3,64,768]{2,1,0:T(8,128)(2,1)S(1)} collective-permute-done((bf16[3,64,768]{2,1,0:T(8,128)(2,1)S(1)}, bf16[3,64,768]{2,1,0:T(8,128)(2,1)S(1)}, u32[]{:S(2)}, u32[]{:S(2)}) %collective-permute-start.3) | collective-permute-done | bytes 294944 | tf_op jit(solution)/shard_map/ppermute | solution.py:48
  235.8 0.7 copy-done.9
  236.5 47.9 %tail.1 = (f32[512,768]{1,0:T(8,128)}, bf16[4,96,768]{2,1,0:T(8,128)(2,1)}, f32[40,96]{1,0:T(8,128)}, bf16[512,768]{1,0:T(8,128)(2,1)}, bf16[4,8,3,64,768]{4,3,2,1,0:T(8,128)(2,1)}) custom-call(bf16[576,2048]{1,0:T(8,128)(2,1)} %attend_back.1.g_ref, bf16[576,768]{1,0:T(8,128)(2,1)} %get-tuple-element.87.wt_ref, ...), custom_call_target="tpu_custom_call" | custom-call | tf_op jit(solution)/shard_map/tail/pallas_call | solution.py:1262
  284.4 12.7 %finish.1 = (f32[3,2048,768]{2,1,0:T(8,128)}, f32[96,2304]{1,0:T(8,128)}, f32[96,768]{1,0:T(8,128)}, f32[1,96]{1,0:T(1,128)}, f32[1,96]{1,0:T(1,128)}, /*index=5...) custom-call(s32[1]{0:T(128)} %bitcast.14.me_ref, ...), custom_call_target="tpu_custom_call" | custom-call | tf_op jit(solution)/shard_map/finish/pallas_call | solution.py:1362
  297.1 0.9 copy.29
  297.9 0.8 copy-done
  298.7 1.1 copy.30
  299.9 0.6 copy.31
  (24 shorter events, 0.1 us)
Async XLA Ops:
  40.5 4.9 %copy-start.10 = (s32[1,2048]{1,0:T(1,128)S(1)}, s32[1,2048]{1,0:T(1,128)}, u32[]{:S(2)}) copy-start(s32[1,2048]{1,0:T(1,128)} %param.16) | copy-start | bytes 24580
  40.5 39.4 %all-to-all-start = ((bf16[8,128,768]{2,1,0:T(8,128)(2,1)}), bf16[8,128,768]{2,1,0:T(8,128)(2,1)}, u32[]{:S(2)}, u32[]{:S(2)}) async-start(bf16[8,128,768]{2,1,0:T(8,128)(2,1)} %get-tuple-element.72), calls=%async_computation | async-start | bytes 3145728 | tf_op jit(solution)/shard_map/all_to_all | solution.py:1418
  45.6 0.6 copy-start.12
  180.6 55.1 %all-to-all-start.1 = ((bf16[8,128,768]{2,1,0:T(8,128)(2,1)}), bf16[8,128,768]{2,1,0:T(8,128)(2,1)}, u32[]{:S(2)}, u32[]{:S(2)}) async-start(bf16[8,128,768]{2,1,0:T(8,128)(2,1)} %get-tuple-element.93), calls=%async_computation.1 | async-start | bytes 3145728 | tf_op jit(solution)/shard_map/all_to_all | solution.py:1423
  184.9 23.0 %copy-start.2 = (bf16[3,64,768]{2,1,0:T(8,128)(2,1)S(1)}, bf16[3,64,768]{2,1,0:T(8,128)(2,1)}, u32[]{:S(2)}) copy-start(bf16[3,64,768]{2,1,0:T(8,128)(2,1)} %get-tuple-element.99.refs_2_) | copy-start | bytes 884740
  184.9 24.2 %copy-start.3 = (bf16[3,64,768]{2,1,0:T(8,128)(2,1)S(1)}, bf16[3,64,768]{2,1,0:T(8,128)(2,1)}, u32[]{:S(2)}) copy-start(bf16[3,64,768]{2,1,0:T(8,128)(2,1)} %get-tuple-element.100.refs_3_) | copy-start | bytes 884740
  184.9 24.5 %copy-start.4 = (bf16[3,64,768]{2,1,0:T(8,128)(2,1)S(1)}, bf16[3,64,768]{2,1,0:T(8,128)(2,1)}, u32[]{:S(2)}) copy-start(bf16[3,64,768]{2,1,0:T(8,128)(2,1)} %get-tuple-element.101.refs_4_) | copy-start | bytes 884740
  184.9 25.7 %copy-start.5 = (bf16[3,64,768]{2,1,0:T(8,128)(2,1)S(1)}, bf16[3,64,768]{2,1,0:T(8,128)(2,1)}, u32[]{:S(2)}) copy-start(bf16[3,64,768]{2,1,0:T(8,128)(2,1)} %get-tuple-element.102.refs_5_) | copy-start | bytes 884740
  207.9 20.8 %collective-permute-start = (bf16[3,64,768]{2,1,0:T(8,128)(2,1)S(1)}, bf16[3,64,768]{2,1,0:T(8,128)(2,1)S(1)}, u32[]{:S(2)}, u32[]{:S(2)}) collective-permute-start(bf16[3,64,768]{2,1,0:T(8,128)(2,1)S(1)} %copy-done.2), channel_id=1, source_target_pairs={{0,2},{1,3},{2,0},{3,1},{4,6},{5,7},{6,4},{7,5},{8,10},{9,11},{10,... | collective-permute-start | bytes 884744 | tf_op jit(solution)/shard_map/ppermute | solution.py:48
  209.1 19.5 %collective-permute-start.1 = (bf16[3,64,768]{2,1,0:T(8,128)(2,1)S(1)}, bf16[3,64,768]{2,1,0:T(8,128)(2,1)S(1)}, u32[]{:S(2)}, u32[]{:S(2)}) collective-permute-start(bf16[3,64,768]{2,1,0:T(8,128)(2,1)S(1)} %copy-done.3), channel_id=1, source_target_pairs={{0,2},{1,3},{2,0},{3,1},{4,6},{5,7},{6,4},{7,5},{8,10},{9,11},{10,... | collective-permute-start | bytes 884744 | tf_op jit(solution)/shard_map/ppermute | solution.py:48
  209.4 20.0 %collective-permute-start.2 = (bf16[3,64,768]{2,1,0:T(8,128)(2,1)S(1)}, bf16[3,64,768]{2,1,0:T(8,128)(2,1)S(1)}, u32[]{:S(2)}, u32[]{:S(2)}) collective-permute-start(bf16[3,64,768]{2,1,0:T(8,128)(2,1)S(1)} %copy-done.4), channel_id=1, source_target_pairs={{0,2},{1,3},{2,0},{3,1},{4,6},{5,7},{6,4},{7,5},{8,10},{9,11},{10,... | collective-permute-start | bytes 884744 | tf_op jit(solution)/shard_map/ppermute | solution.py:48
  210.6 25.1 %collective-permute-start.3 = (bf16[3,64,768]{2,1,0:T(8,128)(2,1)S(1)}, bf16[3,64,768]{2,1,0:T(8,128)(2,1)S(1)}, u32[]{:S(2)}, u32[]{:S(2)}) collective-permute-start(bf16[3,64,768]{2,1,0:T(8,128)(2,1)S(1)} %copy-done.5), channel_id=1, source_target_pairs={{0,2},{1,3},{2,0},{3,1},{4,6},{5,7},{6,4},{7,5},{8,10},{9,11},{10,... | collective-permute-start | bytes 884744 | tf_op jit(solution)/shard_map/ppermute | solution.py:48
  228.7 7.1 %copy-start.6 = (bf16[3,64,768]{2,1,0:T(8,128)(2,1)}, bf16[3,64,768]{2,1,0:T(8,128)(2,1)S(1)}, u32[]{:S(2)}) copy-start(bf16[3,64,768]{2,1,0:T(8,128)(2,1)S(1)} %collective-permute-done.refs_10_) | copy-start | bytes 884740
  228.7 7.1 %copy-start.7 = (bf16[3,64,768]{2,1,0:T(8,128)(2,1)}, bf16[3,64,768]{2,1,0:T(8,128)(2,1)S(1)}, u32[]{:S(2)}) copy-start(bf16[3,64,768]{2,1,0:T(8,128)(2,1)S(1)} %collective-permute-done.1.refs_11_) | copy-start | bytes 884740
  229.4 6.3 %copy-start.8 = (bf16[3,64,768]{2,1,0:T(8,128)(2,1)}, bf16[3,64,768]{2,1,0:T(8,128)(2,1)S(1)}, u32[]{:S(2)}) copy-start(bf16[3,64,768]{2,1,0:T(8,128)(2,1)S(1)} %collective-permute-done.2.refs_12_) | copy-start | bytes 884740
  235.7 0.7 copy-start.9
  284.4 12.7 %copy-start.1 = (bf16[512,768]{1,0:T(8,128)(2,1)S(1)}, bf16[512,768]{1,0:T(8,128)(2,1)}, u32[]{:S(2)}) copy-start(bf16[512,768]{1,0:T(8,128)(2,1)} %get-tuple-element.103) | copy-start | bytes 2359300
  297.0 1.7 copy-start
  298.7 1.1 copy-start.11

commit v8 on v7

--- a/solution.py
+++ b/solution.py
@@ -133,8 +133,8 @@
 def start_kernel(
     n_seq, n_dp, h_ref, w_ref, again_ref, mgain_ref, vec_ref, mix_ref, router_ref,
     route_ref, cot_ref, cos_ref, sin_ref, wo_ref,
-    attn_ref, qkv_ref, wt_ref, small_ref, slot_ref, g_ref, wo_all,
-    all_ref, slice_ref, small_buf, h_send, h_recv, near_send, near_recv, next_send, next_recv,
+    attn_hbm, qkv_ref, wt_ref, small_ref, slot_ref, g_hbm, wo_all,
+    attn_ref, g_ref, out_sem, all_ref, slice_ref, small_buf, h_send, h_recv, near_send, near_recv, next_send, next_recv,
     c_send, c_recv,
 ):
     me, dp = lax.axis_index("seq"), lax.axis_index("dp")
@@ -204,6 +204,8 @@
             first_copy(kind, j).start()
         next_copy(kind, 0).start()
     make_slots(route_ref, cot_ref, slot_ref, g_ref)
+    outs = [pltpu.make_async_copy(g_ref, g_hbm, out_sem.at[0])]
+    outs[0].start()
 
     def pass_on(kind):
         for j in places:
@@ -223,6 +225,12 @@
         mean_square = jnp.mean(x * x, axis=-1, keepdims=True)
         rows = pl.ds(pl.multiple_of(block * tok, tok), tok)
         attn_ref[rows, :] = (x * lax.rsqrt(mean_square + 1e-06) * small_ref[0:1]).astype(bf16)
+        outs.append(
+            pltpu.make_async_copy(
+                attn_ref.at[rows, :], attn_hbm.at[rows, :], out_sem.at[len(outs)]
+            )
+        )
+        outs[-1].start()
 
     normalize(me, h_ref[...])
     pass_on(1)
@@ -260,6 +268,8 @@
             first_copy(kind, j).wait_send()
         for j in range(n_dp // 2):
             next_copy(kind, j).wait_send()
+    for copy in outs:
+        copy.wait()
     trade.wait()
 
 
@@ -282,8 +292,11 @@
             jax.ShapeDtypeStruct((n_dp, shard, D), bf16),
         ),
         in_specs=[VMEM] * 12,
-        out_specs=[VMEM] * 7,
+        out_specs=[HBM] + [VMEM] * 4 + [HBM, VMEM],
         scratch_shapes=[
+            pltpu.VMEM((n_seq * tok, D), bf16),
+            pltpu.VMEM((E, CAP, D), bf16),
+            DMA((1 + n_seq,)),
             pltpu.VMEM((n_seq, tok, D), bf16),
             pltpu.VMEM((n_dp, shard, width3), bf16),
             pltpu.VMEM((n_dp, SMALL, shard), bf16),

time: 303 us -> 302 us (level)
  waiting for transfers between devices: 8.32 us -> 4.02 us
    ppermute x4, waiting for transfers between devices: 7.05 us -> 4.01 us  [swap(): return lax.ppermute(value, axis, [(i, i ^ bit) for i in range(size)])]
  transfers between devices with their start and end apart: 6 -> 6, of which waited for: 3 -> 1; matrix products, arithmetic and copies ran while one was open for 0% -> 0% of each run, Pallas kernels for 24% -> 26%
where the time goes in v8:
time: 302 us; the launch traced here: 299 us
  Pallas kernels  275 us (91%)
  starting transfers between devices  12.2 us (4%)
  local copies, waits for them, and re-layouts  4.26 us (1%)
  waiting for transfers between devices  4.02 us (1%)
    pallas_call x1, Pallas kernels, moe_call(): pl.pallas_call(functools.partial(moe_kernel, n_dp, parts), out_shape=(jax...  99.8 us
    pallas_call x1, Pallas kernels, tail_call(): pl.pallas_call(functools.partial(tail_kernel, n_seq, n_dp, parts), out_sh...  47.9 us
    pallas_call x1, Pallas kernels, start_call(): pl.pallas_call(functools.partial(start_kernel, n_seq, n_dp), out_shape=(j...  36.7 us
    pallas_call x1, Pallas kernels, mid_back_call(): pl.pallas_call(functools.partial(mid_back_kernel, n_seq, n_dp, n_tile), o...  22.9 us
    pallas_call x1, Pallas kernels, attn_back_call(): pl.pallas_call(attn_back_kernel, out_shape=jax.ShapeDtypeStruct((width3,...  20.8 us
    pallas_call x1, Pallas kernels, mid_call(): pl.pallas_call(functools.partial(mid_kernel, n_seq), out_shape=(jax.Shape...  18.3 us
    pallas_call x1, Pallas kernels, attn_call(): pl.pallas_call(attn_kernel, out_shape=(jax.ShapeDtypeStruct((seq_len // t...  16.3 us
    pallas_call x1, Pallas kernels, finish_call(): pl.pallas_call(functools.partial(finish_kernel, n_seq), out_shape=[jax.Sh...  12.7 us
  transfers between devices with their start and end apart: 6, of which 1 were waited for; matrix products, arithmetic and copies ran while one was open for 0% of the time, Pallas kernels for 26%

profile of v8, /device:TPU:13, one launch (start us, length us, event | category | flops | bytes accessed | tf_op | source)
XLA Modules:
  0.0 299.2 jit_solution(1765771018878886754)
XLA Ops:
  0.7 1.8 multiply_sine_fusion
  2.5 36.7 %start.1 = (bf16[2048,768]{1,0:T(8,128)(2,1)}, bf16[576,2048]{1,0:T(8,128)(2,1)}, bf16[576,768]{1,0:T(8,128)(2,1)}, f32[32,768]{1,0:T(8,128)}, s32[2,512]{1,0:T(...) custom-call(bf16[512,768]{1,0:T(8,128)(2,1)} %bitcast.18, bf16[96,2304]{1,0:T(8,128)(2,1)} %wq_ref.1, ...), custom_call_target="tpu_custom_call" | custom-call | tf_op jit(solution)/shard_map/start/pallas_call | solution.py:283
  39.2 0.0 copy-start.10
  39.2 4.9 %all-to-all-start = ((bf16[8,128,768]{2,1,0:T(8,128)(2,1)}), bf16[8,128,768]{2,1,0:T(8,128)(2,1)}, u32[]{:S(2)}, u32[]{:S(2)}) async-start(bf16[8,128,768]{2,1,0:T(8,128)(2,1)} %get-tuple-element.72), calls=%async_computation | async-start | bytes 3145728 | tf_op jit(solution)/shard_map/all_to_all | solution.py:1431
  44.1 0.1 convert_reduce_fusion
  44.3 0.1 select_reduce_fusion
  44.4 0.0 copy-start.12
  44.4 0.1 slice.3
  44.5 0.5 and_select_fusion.lo_ref
  45.0 16.3 %attend.1 = (bf16[4,192,512]{2,1,0:T(8,128)(2,1)}, f32[192,2048]{1,0:T(8,128)}, f32[3,2048]{1,0:T(4,128)}) custom-call(s32[8]{0:T(128)} %and_select_fusion.lo_ref, bf16[576,2048]{1,0:T(8,128)(2,1)} %get-tuple-element.65.qkv_ref, s32[1,2048]{1,0:T(1,128)} %bitcast.33), custom_call_target="tpu_custom_call" | custom-call | flops 16000000000 | bytes 16000000 | tf_op jit(solution)/shard_map/attend/pallas_call | solution.py:385
  61.3 18.3 %mid.1 = (bf16[4,192,512]{2,1,0:T(8,128)(2,1)}, f32[512,768]{1,0:T(8,128)}, f32[8,512]{1,0:T(8,128)}, bf16[8,128,768]{2,1,0:T(8,128)(2,1)}, f32[8,1,128]{2,1,0:T(1,128)}) custom-call(bf16[4,192,512]{2,1,0:T(8,128)(2,1)} %get-tuple-element.66.att_ref, bf16[512,768]{1,0:T(8,128)(2,1)} %bitcast.19, f32[12,1,512]{2,1,0:T(1,128)} %bitcast.25, ...), custom_call_target="tpu_custom_call" | custom-call | tf_op jit(solution)/shard_map/mid/pallas_call | solution.py:883
  79.6 0.0 all-to-all-done.g_ref
  79.6 99.8 %experts.1 = (bf16[8,128,768]{2,1,0:T(8,128)(2,1)}, f32[8,1,128]{2,1,0:T(1,128)}, bf16[8,128,768]{2,1,0:T(8,128)(2,1)}, bf16[3,64,768]{2,1,0:T(8,128)(2,1)}, bf1...) custom-call(bf16[8,128,768]{2,1,0:T(8,128)(2,1)} %get-tuple-element., ...), custom_call_target="tpu_custom_call" | custom-call | tf_op jit(solution)/shard_map/experts/pallas_call | solution.py:765
  179.4 4.3 %all-to-all-start.1 = ((bf16[8,128,768]{2,1,0:T(8,128)(2,1)}), bf16[8,128,768]{2,1,0:T(8,128)(2,1)}, u32[]{:S(2)}, u32[]{:S(2)}) async-start(bf16[8,128,768]{2,1,0:T(8,128)(2,1)} %get-tuple-element.93), calls=%async_computation.1 | async-start | bytes 3145728 | tf_op jit(solution)/shard_map/all_to_all | solution.py:1436
  183.7 22.9 %mid_back.1 = (f32[512,768]{1,0:T(8,128)}, bf16[4,192,512]{2,1,0:T(8,128)(2,1)}, f32[512,768]{1,0:T(8,128)}, f32[12,1,512]{2,1,0:T(1,128)}, f32[8,40,96]{2,1,0:T...) custom-call(bf16[8,128,768]{2,1,0:T(8,128)(2,1)} %get-tuple-element.77.piece_ref, ...), custom_call_target="tpu_custom_call" | custom-call | tf_op jit(solution)/shard_map/mid_back/pallas_call | solution.py:1036
  206.6 1.2 collective-permute-start
  207.9 0.3 collective-permute-start.1
  208.2 1.2 collective-permute-start.2
  209.3 0.3 collective-permute-start.3
  209.6 20.8 %attend_back.1.g_ref = bf16[576,2048]{1,0:T(8,128)(2,1)} custom-call(s32[8]{0:T(128)} %and_select_fusion.lo_ref, bf16[576,2048]{1,0:T(8,128)(2,1)} %get-tuple-element.65.qkv_ref, bf16[4,192,512]{2,1,0:T(8,128)(2,1)} %get-tuple-element.84.go_ref, f32[192,2048]{1,0:T(8,128)} %get-tuple-element.85.exact_ref, f32[3,2048]{1,0:T(4,128)} %get-tuple-element.86.log_ref, ...), custom_call_target="tpu_custom_call" | custom-call | flops 16000000000 | bytes 16000000 | tf_op jit(solution)/shard_map/attend_back/pallas_call | solution.py:494
  230.4 0.0 collective-permute-done.1.refs_11_
  230.4 0.0 copy-start.7
  230.5 0.0 copy-start.8
  230.5 4.0 %collective-permute-done.3.refs_13_ = bf16[3,64,768]{2,1,0:T(8,128)(2,1)S(1)} collective-permute-done((bf16[3,64,768]{2,1,0:T(8,128)(2,1)S(1)}, bf16[3,64,768]{2,1,0:T(8,128)(2,1)S(1)}, u32[]{:S(2)}, u32[]{:S(2)}) %collective-permute-start.3) | collective-permute-done | bytes 294944 | tf_op jit(solution)/shard_map/ppermute | solution.py:48
  234.5 0.0 all-to-all-done.1.out_hbm
  234.5 0.7 copy-done.9
  235.2 47.9 %tail.1 = (f32[512,768]{1,0:T(8,128)}, bf16[4,96,768]{2,1,0:T(8,128)(2,1)}, f32[40,96]{1,0:T(8,128)}, bf16[512,768]{1,0:T(8,128)(2,1)}, bf16[4,8,3,64,768]{4,3,2,1,0:T(8,128)(2,1)}) custom-call(bf16[576,2048]{1,0:T(8,128)(2,1)} %attend_back.1.g_ref, bf16[576,768]{1,0:T(8,128)(2,1)} %get-tuple-element.87.wt_ref, ...), custom_call_target="tpu_custom_call" | custom-call | tf_op jit(solution)/shard_map/tail/pallas_call | solution.py:1275
  283.1 12.7 %finish.1 = (f32[3,2048,768]{2,1,0:T(8,128)}, f32[96,2304]{1,0:T(8,128)}, f32[96,768]{1,0:T(8,128)}, f32[1,96]{1,0:T(1,128)}, f32[1,96]{1,0:T(1,128)}, /*index=5...) custom-call(s32[1]{0:T(128)} %bitcast.14.me_ref, ...), custom_call_target="tpu_custom_call" | custom-call | tf_op jit(solution)/shard_map/finish/pallas_call | solution.py:1375
  295.8 0.9 copy.29
  296.7 0.8 copy-done
  297.5 1.1 copy.30
  298.6 0.6 copy.31
  (24 shorter events, 0.1 us)
Async XLA Ops:
  39.2 4.9 %copy-start.10 = (s32[1,2048]{1,0:T(1,128)S(1)}, s32[1,2048]{1,0:T(1,128)}, u32[]{:S(2)}) copy-start(s32[1,2048]{1,0:T(1,128)} %param.16) | copy-start | bytes 24580
  39.2 40.4 %all-to-all-start = ((bf16[8,128,768]{2,1,0:T(8,128)(2,1)}), bf16[8,128,768]{2,1,0:T(8,128)(2,1)}, u32[]{:S(2)}, u32[]{:S(2)}) async-start(bf16[8,128,768]{2,1,0:T(8,128)(2,1)} %get-tuple-element.72), calls=%async_computation | async-start | bytes 3145728 | tf_op jit(solution)/shard_map/all_to_all | solution.py:1431
  44.4 0.6 copy-start.12
  179.4 55.1 %all-to-all-start.1 = ((bf16[8,128,768]{2,1,0:T(8,128)(2,1)}), bf16[8,128,768]{2,1,0:T(8,128)(2,1)}, u32[]{:S(2)}, u32[]{:S(2)}) async-start(bf16[8,128,768]{2,1,0:T(8,128)(2,1)} %get-tuple-element.93), calls=%async_computation.1 | async-start | bytes 3145728 | tf_op jit(solution)/shard_map/all_to_all | solution.py:1436
  183.6 23.0 %copy-start.2 = (bf16[3,64,768]{2,1,0:T(8,128)(2,1)S(1)}, bf16[3,64,768]{2,1,0:T(8,128)(2,1)}, u32[]{:S(2)}) copy-start(bf16[3,64,768]{2,1,0:T(8,128)(2,1)} %get-tuple-element.99.refs_2_) | copy-start | bytes 884740
  183.7 24.2 %copy-start.3 = (bf16[3,64,768]{2,1,0:T(8,128)(2,1)S(1)}, bf16[3,64,768]{2,1,0:T(8,128)(2,1)}, u32[]{:S(2)}) copy-start(bf16[3,64,768]{2,1,0:T(8,128)(2,1)} %get-tuple-element.100.refs_3_) | copy-start | bytes 884740
  183.7 24.5 %copy-start.4 = (bf16[3,64,768]{2,1,0:T(8,128)(2,1)S(1)}, bf16[3,64,768]{2,1,0:T(8,128)(2,1)}, u32[]{:S(2)}) copy-start(bf16[3,64,768]{2,1,0:T(8,128)(2,1)} %get-tuple-element.101.refs_4_) | copy-start | bytes 884740
  183.7 25.7 %copy-start.5 = (bf16[3,64,768]{2,1,0:T(8,128)(2,1)S(1)}, bf16[3,64,768]{2,1,0:T(8,128)(2,1)}, u32[]{:S(2)}) copy-start(bf16[3,64,768]{2,1,0:T(8,128)(2,1)} %get-tuple-element.102.refs_5_) | copy-start | bytes 884740
  206.6 23.8 %collective-permute-start = (bf16[3,64,768]{2,1,0:T(8,128)(2,1)S(1)}, bf16[3,64,768]{2,1,0:T(8,128)(2,1)S(1)}, u32[]{:S(2)}, u32[]{:S(2)}) collective-permute-start(bf16[3,64,768]{2,1,0:T(8,128)(2,1)S(1)} %copy-done.2), channel_id=1, source_target_pairs={{0,2},{1,3},{2,0},{3,1},{4,6},{5,7},{6,4},{7,5},{8,10},{9,11},{10,... | collective-permute-start | bytes 884744 | tf_op jit(solution)/shard_map/ppermute | solution.py:48
  207.9 22.6 %collective-permute-start.1 = (bf16[3,64,768]{2,1,0:T(8,128)(2,1)S(1)}, bf16[3,64,768]{2,1,0:T(8,128)(2,1)S(1)}, u32[]{:S(2)}, u32[]{:S(2)}) collective-permute-start(bf16[3,64,768]{2,1,0:T(8,128)(2,1)S(1)} %copy-done.3), channel_id=1, source_target_pairs={{0,2},{1,3},{2,0},{3,1},{4,6},{5,7},{6,4},{7,5},{8,10},{9,11},{10,... | collective-permute-start | bytes 884744 | tf_op jit(solution)/shard_map/ppermute | solution.py:48
  208.2 22.3 %collective-permute-start.2 = (bf16[3,64,768]{2,1,0:T(8,128)(2,1)S(1)}, bf16[3,64,768]{2,1,0:T(8,128)(2,1)S(1)}, u32[]{:S(2)}, u32[]{:S(2)}) collective-permute-start(bf16[3,64,768]{2,1,0:T(8,128)(2,1)S(1)} %copy-done.4), channel_id=1, source_target_pairs={{0,2},{1,3},{2,0},{3,1},{4,6},{5,7},{6,4},{7,5},{8,10},{9,11},{10,... | collective-permute-start | bytes 884744 | tf_op jit(solution)/shard_map/ppermute | solution.py:48
  209.3 25.1 %collective-permute-start.3 = (bf16[3,64,768]{2,1,0:T(8,128)(2,1)S(1)}, bf16[3,64,768]{2,1,0:T(8,128)(2,1)S(1)}, u32[]{:S(2)}, u32[]{:S(2)}) collective-permute-start(bf16[3,64,768]{2,1,0:T(8,128)(2,1)S(1)} %copy-done.5), channel_id=1, source_target_pairs={{0,2},{1,3},{2,0},{3,1},{4,6},{5,7},{6,4},{7,5},{8,10},{9,11},{10,... | collective-permute-start | bytes 884744 | tf_op jit(solution)/shard_map/ppermute | solution.py:48
  230.4 4.1 %copy-start.6 = (bf16[3,64,768]{2,1,0:T(8,128)(2,1)}, bf16[3,64,768]{2,1,0:T(8,128)(2,1)S(1)}, u32[]{:S(2)}) copy-start(bf16[3,64,768]{2,1,0:T(8,128)(2,1)S(1)} %collective-permute-done.refs_10_) | copy-start | bytes 884740
  230.4 4.1 %copy-start.7 = (bf16[3,64,768]{2,1,0:T(8,128)(2,1)}, bf16[3,64,768]{2,1,0:T(8,128)(2,1)S(1)}, u32[]{:S(2)}) copy-start(bf16[3,64,768]{2,1,0:T(8,128)(2,1)S(1)} %collective-permute-done.1.refs_11_) | copy-start | bytes 884740
  230.5 4.0 %copy-start.8 = (bf16[3,64,768]{2,1,0:T(8,128)(2,1)}, bf16[3,64,768]{2,1,0:T(8,128)(2,1)S(1)}, u32[]{:S(2)}) copy-start(bf16[3,64,768]{2,1,0:T(8,128)(2,1)S(1)} %collective-permute-done.2.refs_12_) | copy-start | bytes 884740
  234.5 0.7 copy-start.9
  283.1 12.7 %copy-start.1 = (bf16[512,768]{1,0:T(8,128)(2,1)S(1)}, bf16[512,768]{1,0:T(8,128)(2,1)}, u32[]{:S(2)}) copy-start(bf16[512,768]{1,0:T(8,128)(2,1)} %get-tuple-element.103) | copy-start | bytes 2359300
  295.8 1.7 copy-start
  297.5 1.1 copy-start.11

commit v9 on v8

--- a/solution.py
+++ b/solution.py
@@ -3,6 +3,7 @@
 
 import jax
 import jax.numpy as jnp
+import numpy as np
 from jax import lax
 from jax.experimental import pallas as pl
 from jax.experimental.pallas import tpu as pltpu
@@ -132,8 +133,8 @@
 
 def start_kernel(
     n_seq, n_dp, h_ref, w_ref, again_ref, mgain_ref, vec_ref, mix_ref, router_ref,
-    route_ref, cot_ref, cos_ref, sin_ref, wo_ref,
-    attn_hbm, qkv_ref, wt_ref, small_ref, slot_ref, g_hbm, wo_all,
+    route_ref, cot_ref, fine_ref, coarse_ref, wo_ref,
+    attn_hbm, qkv_ref, wt_ref, small_ref, slot_ref, g_hbm, wo_all, cos_ref, sin_ref,
     attn_ref, g_ref, out_sem, all_ref, slice_ref, small_buf, h_send, h_recv, near_send, near_recv, next_send, next_recv,
     c_send, c_recv,
 ):
@@ -206,6 +207,12 @@
     make_slots(route_ref, cot_ref, slot_ref, g_ref)
     outs = [pltpu.make_async_copy(g_ref, g_hbm, out_sem.at[0])]
     outs[0].start()
+    rates = HD // 2
+    for b in range(coarse_ref.shape[1]):
+        there = slice(b * 128, (b + 1) * 128)
+        cos_b, sin_b = coarse_ref[:rates, b : b + 1], coarse_ref[rates:, b : b + 1]
+        cos_ref[:, there] = cos_b * fine_ref[:rates] - sin_b * fine_ref[rates:]
+        sin_ref[:, there] = sin_b * fine_ref[:rates] + cos_b * fine_ref[rates:]
 
     def pass_on(kind):
         for j in places:
@@ -274,8 +281,7 @@
 
 
 def start_call(
-    n_seq, n_dp, hidden, w_qkv, attn_gain, moe_gain, vec, mix, router, routes, cotangent, cos, sin,
-    w_out,
+    n_seq, n_dp, hidden, w_qkv, attn_gain, moe_gain, vec, mix, router, routes, cotangent, w_out,
 ):
     tok, shard = hidden.shape[0], w_qkv.shape[0]
     width3 = w_qkv.shape[1] // n_seq
@@ -290,9 +296,11 @@
             jax.ShapeDtypeStruct(routes.shape, jnp.int32),
             jax.ShapeDtypeStruct((E, CAP, D), bf16),
             jax.ShapeDtypeStruct((n_dp, shard, D), bf16),
+            jax.ShapeDtypeStruct((HD // 2, n_seq * tok), f32),
+            jax.ShapeDtypeStruct((HD // 2, n_seq * tok), f32),
         ),
         in_specs=[VMEM] * 12,
-        out_specs=[HBM] + [VMEM] * 4 + [HBM, VMEM],
+        out_specs=[HBM] + [VMEM] * 4 + [HBM] + [VMEM] * 3,
         scratch_shapes=[
             pltpu.VMEM((n_seq * tok, D), bf16),
             pltpu.VMEM((E, CAP, D), bf16),
@@ -313,7 +321,7 @@
         name="start",
     )(
         hidden, w_qkv, attn_gain[None], moe_gain[None], vec, mix, router, routes, cotangent,
-        cos, sin, w_out,
+        *rope_tables(n_seq * tok), w_out,
     )
 
 
@@ -1397,10 +1405,13 @@
 
 
 def rope_tables(seq_len):
-    freq_index = jnp.arange(HD // 2, dtype=f32)
-    inv_freq = jnp.exp(freq_index * (-2.0 * math.log(10000.0) / HD))
-    angles = jnp.arange(seq_len, dtype=jnp.int32).astype(f32)[None, :] * inv_freq[:, None]
-    return jnp.cos(angles), jnp.sin(angles)
+    rates = 10000.0 ** (np.arange(HD // 2) * (-2.0 / HD))
+
+    def table(positions):
+        angles = rates[:, None] * positions[None, :]
+        return jnp.asarray(np.concatenate([np.cos(angles), np.sin(angles)]), f32)
+
+    return table(np.arange(128.0)), table(np.arange(0.0, seq_len, 128.0))
 
 
 def per_device(
@@ -1435,10 +1446,9 @@
     def to_sources(values):
         return lax.all_to_all(values, "dp", split_axis=0, concat_axis=0, tiled=True)
 
-    cos_t, sin_t = rope_tables(tok * n_seq)
-    attn_in, qkv, w_turned, small, slot_of, grad_slots, out_weight = start_call(
+    attn_in, qkv, w_turned, small, slot_of, grad_slots, out_weight, cos_t, sin_t = start_call(
         n_seq, n_dp, hidden, w_qkv, attn_gain, moe_gain, const_vec, const_mix, w_router.T,
-        routes_t, cot, cos_t, sin_t, w_out,
+        routes_t, cot, w_out,
     )
     arrived_grad = to_owners(grad_slots)
 

time: 302 us -> 300 us (level)
  no operation moved by 1% of the time
where the time goes in v9:
time: 300 us; the launch traced here: 297 us
  Pallas kernels  275 us (92%)
  starting transfers between devices  12.2 us (4%)
  waiting for transfers between devices  4.65 us (2%)
  local copies, waits for them, and re-layouts  4.26 us (1%)
    pallas_call x1, Pallas kernels, moe_call(): pl.pallas_call(functools.partial(moe_kernel, n_dp, parts), out_shape=(jax...  100 us
    pallas_call x1, Pallas kernels, tail_call(): pl.pallas_call(functools.partial(tail_kernel, n_seq, n_dp, parts), out_sh...  47.9 us
    pallas_call x1, Pallas kernels, start_call(): pl.pallas_call(functools.partial(start_kernel, n_seq, n_dp), out_shape=(j...  36.7 us
    pallas_call x1, Pallas kernels, mid_back_call(): pl.pallas_call(functools.partial(mid_back_kernel, n_seq, n_dp, n_tile), o...  22.9 us
    pallas_call x1, Pallas kernels, attn_back_call(): pl.pallas_call(attn_back_kernel, out_shape=jax.ShapeDtypeStruct((width3,...  20.2 us
    pallas_call x1, Pallas kernels, mid_call(): pl.pallas_call(functools.partial(mid_kernel, n_seq), out_shape=(jax.Shape...  18.3 us
    pallas_call x1, Pallas kernels, attn_call(): pl.pallas_call(attn_kernel, out_shape=(jax.ShapeDtypeStruct((seq_len // t...  15.7 us
    pallas_call x1, Pallas kernels, finish_call(): pl.pallas_call(functools.partial(finish_kernel, n_seq), out_shape=[jax.Sh...  12.7 us
  transfers between devices with their start and end apart: 6, of which 1 were waited for; matrix products, arithmetic and copies ran while one was open for 0% of the time, Pallas kernels for 26%

profile of v9, /device:TPU:13, one launch (start us, length us, event | category | flops | bytes accessed | tf_op | source)
XLA Modules:
  0.0 297.4 jit_solution(17374087963049801373)
XLA Ops:
  0.6 36.7 %start.1 = (bf16[2048,768]{1,0:T(8,128)(2,1)}, bf16[576,2048]{1,0:T(8,128)(2,1)}, bf16[576,768]{1,0:T(8,128)(2,1)}, f32[32,768]{1,0:T(8,128)}, s32[2,512]{1,0:T(...) custom-call(bf16[512,768]{1,0:T(8,128)(2,1)} %bitcast.18, ...), custom_call_target="tpu_custom_call" | custom-call | tf_op jit(solution)/shard_map/start/pallas_call | solution.py:289
  37.4 0.0 copy-start.10
  37.4 4.9 %all-to-all-start = ((bf16[8,128,768]{2,1,0:T(8,128)(2,1)}), bf16[8,128,768]{2,1,0:T(8,128)(2,1)}, u32[]{:S(2)}, u32[]{:S(2)}) async-start(bf16[8,128,768]{2,1,0:T(8,128)(2,1)} %get-tuple-element.74), calls=%async_computation | async-start | bytes 3145728 | tf_op jit(solution)/shard_map/all_to_all | solution.py:1442
  42.3 0.1 convert_reduce_fusion
  42.5 0.1 select_reduce_fusion
  42.6 0.0 copy-start.12
  42.6 0.1 slice.3
  42.7 0.5 and_select_fusion.lo_ref
  43.2 15.7 %attend.1 = (bf16[4,192,512]{2,1,0:T(8,128)(2,1)}, f32[192,2048]{1,0:T(8,128)}, f32[3,2048]{1,0:T(4,128)}) custom-call(s32[8]{0:T(128)} %and_select_fusion.lo_ref, bf16[576,2048]{1,0:T(8,128)(2,1)} %get-tuple-element.67.qkv_ref, s32[1,2048]{1,0:T(1,128)} %bitcast.33), custom_call_target="tpu_custom_call" | custom-call | flops 16000000000 | bytes 16000000 | tf_op jit(solution)/shard_map/attend/pallas_call | solution.py:393
  58.9 18.3 %mid.1 = (bf16[4,192,512]{2,1,0:T(8,128)(2,1)}, f32[512,768]{1,0:T(8,128)}, f32[8,512]{1,0:T(8,128)}, bf16[8,128,768]{2,1,0:T(8,128)(2,1)}, f32[8,1,128]{2,1,0:T(1,128)}) custom-call(bf16[4,192,512]{2,1,0:T(8,128)(2,1)} %get-tuple-element.68.att_ref, bf16[512,768]{1,0:T(8,128)(2,1)} %bitcast.19, f32[12,1,512]{2,1,0:T(1,128)} %bitcast.25, ...), custom_call_target="tpu_custom_call" | custom-call | tf_op jit(solution)/shard_map/mid/pallas_call | solution.py:891
  77.3 0.0 all-to-all-done.g_ref
  77.3 100.3 %experts.1 = (bf16[8,128,768]{2,1,0:T(8,128)(2,1)}, f32[8,1,128]{2,1,0:T(1,128)}, bf16[8,128,768]{2,1,0:T(8,128)(2,1)}, bf16[3,64,768]{2,1,0:T(8,128)(2,1)}, bf1...) custom-call(bf16[8,128,768]{2,1,0:T(8,128)(2,1)} %get-tuple-element., ...), custom_call_target="tpu_custom_call" | custom-call | tf_op jit(solution)/shard_map/experts/pallas_call | solution.py:773
  177.6 4.3 %all-to-all-start.1 = ((bf16[8,128,768]{2,1,0:T(8,128)(2,1)}), bf16[8,128,768]{2,1,0:T(8,128)(2,1)}, u32[]{:S(2)}, u32[]{:S(2)}) async-start(bf16[8,128,768]{2,1,0:T(8,128)(2,1)} %get-tuple-element.97), calls=%async_computation.1 | async-start | bytes 3145728 | tf_op jit(solution)/shard_map/all_to_all | solution.py:1447
  181.9 22.9 %mid_back.1 = (f32[512,768]{1,0:T(8,128)}, bf16[4,192,512]{2,1,0:T(8,128)(2,1)}, f32[512,768]{1,0:T(8,128)}, f32[12,1,512]{2,1,0:T(1,128)}, f32[8,40,96]{2,1,0:T...) custom-call(bf16[8,128,768]{2,1,0:T(8,128)(2,1)} %get-tuple-element.79.piece_ref, ...), custom_call_target="tpu_custom_call" | custom-call | tf_op jit(solution)/shard_map/mid_back/pallas_call | solution.py:1044
  204.8 1.3 collective-permute-start
  206.1 0.3 collective-permute-start.1
  206.3 1.2 collective-permute-start.2
  207.5 0.3 collective-permute-start.3
  207.8 20.2 %attend_back.1.g_ref = bf16[576,2048]{1,0:T(8,128)(2,1)} custom-call(s32[8]{0:T(128)} %and_select_fusion.lo_ref, bf16[576,2048]{1,0:T(8,128)(2,1)} %get-tuple-element.67.qkv_ref, bf16[4,192,512]{2,1,0:T(8,128)(2,1)} %get-tuple-element.86.go_ref, f32[192,2048]{1,0:T(8,128)} %get-tuple-element.87.exact_ref, f32[3,2048]{1,0:T(4,128)} %get-tuple-element.88.log_ref, ...), custom_call_target="tpu_custom_call" | custom-call | flops 16000000000 | bytes 16000000 | tf_op jit(solution)/shard_map/attend_back/pallas_call | solution.py:502
  228.0 0.0 collective-permute-done.refs_10_
  228.0 0.0 collective-permute-done.1.refs_11_
  228.0 0.0 copy-start.7
  228.0 0.0 copy-start.8
  228.0 4.6 %collective-permute-done.3.refs_13_ = bf16[3,64,768]{2,1,0:T(8,128)(2,1)S(1)} collective-permute-done((bf16[3,64,768]{2,1,0:T(8,128)(2,1)S(1)}, bf16[3,64,768]{2,1,0:T(8,128)(2,1)S(1)}, u32[]{:S(2)}, u32[]{:S(2)}) %collective-permute-start.3) | collective-permute-done | bytes 294944 | tf_op jit(solution)/shard_map/ppermute | solution.py:49
  232.7 0.0 all-to-all-done.1.out_hbm
  232.7 0.7 copy-done.9
  233.4 47.9 %tail.1 = (f32[512,768]{1,0:T(8,128)}, bf16[4,96,768]{2,1,0:T(8,128)(2,1)}, f32[40,96]{1,0:T(8,128)}, bf16[512,768]{1,0:T(8,128)(2,1)}, bf16[4,8,3,64,768]{4,3,2,1,0:T(8,128)(2,1)}) custom-call(bf16[576,2048]{1,0:T(8,128)(2,1)} %attend_back.1.g_ref, bf16[576,768]{1,0:T(8,128)(2,1)} %get-tuple-element.91.wt_ref, ...), custom_call_target="tpu_custom_call" | custom-call | tf_op jit(solution)/shard_map/tail/pallas_call | solution.py:1283
  281.3 12.7 %finish.1 = (f32[3,2048,768]{2,1,0:T(8,128)}, f32[96,2304]{1,0:T(8,128)}, f32[96,768]{1,0:T(8,128)}, f32[1,96]{1,0:T(1,128)}, f32[1,96]{1,0:T(1,128)}, /*index=5...) custom-call(s32[1]{0:T(128)} %bitcast.14.me_ref, ...), custom_call_target="tpu_custom_call" | custom-call | tf_op jit(solution)/shard_map/finish/pallas_call | solution.py:1383
  294.0 0.9 copy.31
  294.9 0.8 copy-done
  295.7 1.1 copy.32
  296.8 0.6 copy.33
  (21 shorter events, 0.0 us)
Async XLA Ops:
  37.4 4.9 %copy-start.10 = (s32[1,2048]{1,0:T(1,128)S(1)}, s32[1,2048]{1,0:T(1,128)}, u32[]{:S(2)}) copy-start(s32[1,2048]{1,0:T(1,128)} %param.18) | copy-start | bytes 24580
  37.4 39.9 %all-to-all-start = ((bf16[8,128,768]{2,1,0:T(8,128)(2,1)}), bf16[8,128,768]{2,1,0:T(8,128)(2,1)}, u32[]{:S(2)}, u32[]{:S(2)}) async-start(bf16[8,128,768]{2,1,0:T(8,128)(2,1)} %get-tuple-element.74), calls=%async_computation | async-start | bytes 3145728 | tf_op jit(solution)/shard_map/all_to_all | solution.py:1442
  42.6 0.6 copy-start.12
  177.6 55.1 %all-to-all-start.1 = ((bf16[8,128,768]{2,1,0:T(8,128)(2,1)}), bf16[8,128,768]{2,1,0:T(8,128)(2,1)}, u32[]{:S(2)}, u32[]{:S(2)}) async-start(bf16[8,128,768]{2,1,0:T(8,128)(2,1)} %get-tuple-element.97), calls=%async_computation.1 | async-start | bytes 3145728 | tf_op jit(solution)/shard_map/all_to_all | solution.py:1447
  181.8 23.0 %copy-start.2 = (bf16[3,64,768]{2,1,0:T(8,128)(2,1)S(1)}, bf16[3,64,768]{2,1,0:T(8,128)(2,1)}, u32[]{:S(2)}) copy-start(bf16[3,64,768]{2,1,0:T(8,128)(2,1)} %get-tuple-element.103.refs_2_) | copy-start | bytes 884740
  181.8 24.2 %copy-start.3 = (bf16[3,64,768]{2,1,0:T(8,128)(2,1)S(1)}, bf16[3,64,768]{2,1,0:T(8,128)(2,1)}, u32[]{:S(2)}) copy-start(bf16[3,64,768]{2,1,0:T(8,128)(2,1)} %get-tuple-element.104.refs_3_) | copy-start | bytes 884740
  181.9 24.5 %copy-start.4 = (bf16[3,64,768]{2,1,0:T(8,128)(2,1)S(1)}, bf16[3,64,768]{2,1,0:T(8,128)(2,1)}, u32[]{:S(2)}) copy-start(bf16[3,64,768]{2,1,0:T(8,128)(2,1)} %get-tuple-element.105.refs_4_) | copy-start | bytes 884740
  181.9 25.7 %copy-start.5 = (bf16[3,64,768]{2,1,0:T(8,128)(2,1)S(1)}, bf16[3,64,768]{2,1,0:T(8,128)(2,1)}, u32[]{:S(2)}) copy-start(bf16[3,64,768]{2,1,0:T(8,128)(2,1)} %get-tuple-element.106.refs_5_) | copy-start | bytes 884740
  204.8 23.2 %collective-permute-start = (bf16[3,64,768]{2,1,0:T(8,128)(2,1)S(1)}, bf16[3,64,768]{2,1,0:T(8,128)(2,1)S(1)}, u32[]{:S(2)}, u32[]{:S(2)}) collective-permute-start(bf16[3,64,768]{2,1,0:T(8,128)(2,1)S(1)} %copy-done.2), channel_id=1, source_target_pairs={{0,2},{1,3},{2,0},{3,1},{4,6},{5,7},{6,4},{7,5},{8,10},{9,11},{10,... | collective-permute-start | bytes 884744 | tf_op jit(solution)/shard_map/ppermute | solution.py:49
  206.1 21.9 %collective-permute-start.1 = (bf16[3,64,768]{2,1,0:T(8,128)(2,1)S(1)}, bf16[3,64,768]{2,1,0:T(8,128)(2,1)S(1)}, u32[]{:S(2)}, u32[]{:S(2)}) collective-permute-start(bf16[3,64,768]{2,1,0:T(8,128)(2,1)S(1)} %copy-done.3), channel_id=1, source_target_pairs={{0,2},{1,3},{2,0},{3,1},{4,6},{5,7},{6,4},{7,5},{8,10},{9,11},{10,... | collective-permute-start | bytes 884744 | tf_op jit(solution)/shard_map/ppermute | solution.py:49
  206.3 21.7 %collective-permute-start.2 = (bf16[3,64,768]{2,1,0:T(8,128)(2,1)S(1)}, bf16[3,64,768]{2,1,0:T(8,128)(2,1)S(1)}, u32[]{:S(2)}, u32[]{:S(2)}) collective-permute-start(bf16[3,64,768]{2,1,0:T(8,128)(2,1)S(1)} %copy-done.4), channel_id=1, source_target_pairs={{0,2},{1,3},{2,0},{3,1},{4,6},{5,7},{6,4},{7,5},{8,10},{9,11},{10,... | collective-permute-start | bytes 884744 | tf_op jit(solution)/shard_map/ppermute | solution.py:49
  207.5 25.1 %collective-permute-start.3 = (bf16[3,64,768]{2,1,0:T(8,128)(2,1)S(1)}, bf16[3,64,768]{2,1,0:T(8,128)(2,1)S(1)}, u32[]{:S(2)}, u32[]{:S(2)}) collective-permute-start(bf16[3,64,768]{2,1,0:T(8,128)(2,1)S(1)} %copy-done.5), channel_id=1, source_target_pairs={{0,2},{1,3},{2,0},{3,1},{4,6},{5,7},{6,4},{7,5},{8,10},{9,11},{10,... | collective-permute-start | bytes 884744 | tf_op jit(solution)/shard_map/ppermute | solution.py:49
  228.0 4.7 %copy-start.6 = (bf16[3,64,768]{2,1,0:T(8,128)(2,1)}, bf16[3,64,768]{2,1,0:T(8,128)(2,1)S(1)}, u32[]{:S(2)}) copy-start(bf16[3,64,768]{2,1,0:T(8,128)(2,1)S(1)} %collective-permute-done.refs_10_) | copy-start | bytes 884740
  228.0 4.7 %copy-start.7 = (bf16[3,64,768]{2,1,0:T(8,128)(2,1)}, bf16[3,64,768]{2,1,0:T(8,128)(2,1)S(1)}, u32[]{:S(2)}) copy-start(bf16[3,64,768]{2,1,0:T(8,128)(2,1)S(1)} %collective-permute-done.1.refs_11_) | copy-start | bytes 884740
  228.0 4.7 %copy-start.8 = (bf16[3,64,768]{2,1,0:T(8,128)(2,1)}, bf16[3,64,768]{2,1,0:T(8,128)(2,1)S(1)}, u32[]{:S(2)}) copy-start(bf16[3,64,768]{2,1,0:T(8,128)(2,1)S(1)} %collective-permute-done.2.refs_12_) | copy-start | bytes 884740
  232.7 0.7 copy-start.9
  281.3 12.7 %copy-start.1 = (bf16[512,768]{1,0:T(8,128)(2,1)S(1)}, bf16[512,768]{1,0:T(8,128)(2,1)}, u32[]{:S(2)}) copy-start(bf16[512,768]{1,0:T(8,128)(2,1)} %get-tuple-element.107) | copy-start | bytes 2359300
  294.0 1.7 copy-start
  295.7 1.1 copy-start.11
